TPU v7x, 256 devices: a whole 4x4x8 slice. The times are simulated.
256 devices in a mesh: dp: 64 (over x, z_lo, y, core), tensor: 4 (over z_hi).
Axes of the slice: x: 4, y: 4, z: 8 (z_hi: 4, z_lo: 2; z = z_hi * 2 + z_lo), core: 2. Of those that a mesh axis runs over, the one named last changes fastest.
Arguments:
- activations: bfloat16 [1, 8192, 4096], P(None, ('dp', 'tensor')), may hold values from -6 to 6
- out_grad: bfloat16 [1, 8192, 512], P(None, 'dp', 'tensor'), may hold values from -0.5 to 0.5
- value_weight: bfloat16 [1, 512, 4096], P(None, 'tensor'), may hold values from -6 to 6
- error_feedback: bfloat16 [1, 64, 512, 4096], P(None, 'dp', 'tensor'), may hold values from -8 to 8
- warm_right: bfloat16 [1, 4, 4096, 32], P(None, 'tensor'), may hold values from -6 to 6
Outputs:
- new_error: bfloat16 [1, 64, 512, 4096], P(None, 'dp', 'tensor')
- left_basis: float32 [1, 512, 32], P(None, 'tensor')
- right_factor: bfloat16 [1, 4, 4096, 32], P(None, 'tensor')
- input_grad: bfloat16 [1, 8192, 4096], P(None, ('dp', 'tensor'))
All inputs are finite; a program needn't handle non-finite values.
Results may differ from a plain program's by a relative error of at most 0.00065.
Values may be sent and summed in bfloat16 or wider, within the bound.
No kernel may reach another device: no remote copies, remote signals or barrier semaphores. Data moves between devices by JAX's collectives and lax.ppermute only.
A program may use at most 64 MiB of HBM per device.

v0:
```python
import jax
import jax.numpy as jnp
from jax import lax
from jax.sharding import PartitionSpec as P

HIGH = lax.Precision.HIGHEST


def laid_out(pieces, dim):
    pieces = jnp.moveaxis(pieces, 0, dim)
    dims = pieces.shape
    return pieces.reshape(*dims[:dim], dims[dim] * dims[dim + 1], *dims[dim + 2 :])


def copy_for_each(shard, axis):
    length = lax.axis_size(axis)
    return lax.all_to_all(
        jnp.broadcast_to(shard[None], (length, *shard.shape)), axis, 0, 0, tiled=True
    )


def gathered_copies(shard, axis, dim):
    return laid_out(copy_for_each(shard, axis), dim)


def cut_along(shard, dim, length):
    before, after = (shard.shape[:dim], shard.shape[dim + 1 :])
    return jnp.moveaxis(shard.reshape(*before, length, -1, *after), dim, 0)


def sum_at_owner(shard, axis, dim):
    length = lax.axis_size(axis)
    pieces = lax.all_to_all(cut_along(shard, dim, length), axis, 0, 0, tiled=True)
    return jnp.sum(pieces, axis=0)


def of_everyone(shard, axis):
    everything = copy_for_each(shard, axis)
    return jnp.sum(everything, axis=0)


def rows_for(lines, length):
    spare = -len(lines) % length
    return jnp.pad(lines, [(0, spare)] + [(0, 0)] * (lines.ndim - 1))


def nested_sum(shard, axes):
    lines = shard.reshape(-1, shard.shape[-1])
    own = sum_at_owner(rows_for(lines, lax.axis_size(axes)), axes, 0)
    whole = gathered_copies(own, axes, 0)
    return whole[: len(lines)].reshape(shard.shape)


def orthonormal(left):
    gram = jnp.einsum("...hk,...hj->...kj", left, left, precision=HIGH)
    lower = jnp.linalg.cholesky(gram)
    return lax.linalg.triangular_solve(lower, left, left_side=False, lower=True, transpose_a=True)


def layer_merged(tokens, grads, error):
    weight_grad = lax.dot_general(
        grads,
        gathered_copies(tokens, "tensor", 0),
        (((0,), (0,)), ((), ())),
        preferred_element_type=jnp.float32,
    )
    return weight_grad + error.astype(jnp.float32)


def right_part(merged, basis):
    return lax.dot_general(
        merged, basis, (((0,), (0,)), ((), ())), precision=HIGH, preferred_element_type=jnp.float32
    )


def finish(merged, basis, right):
    approx = lax.dot_general(
        basis, right, (((1,), (1,)), ((), ())), precision=HIGH, preferred_element_type=jnp.float32
    )
    return ((merged - approx).astype(jnp.bfloat16), right.astype(jnp.bfloat16))


def backprop_input(grads, weight):
    total = sum_at_owner(jnp.dot(grads, weight, preferred_element_type=jnp.float32), "tensor", 0)
    return total.astype(jnp.bfloat16)


def local(activations, out_grad, value_weight, error_feedback, warm_right):
    replicas = float(lax.axis_size("dp"))
    merged = layer_merged(activations[0], out_grad[0], error_feedback[0, 0])
    warm = warm_right[0, 0].astype(jnp.float32)
    left = jnp.dot(merged, warm, precision=HIGH, preferred_element_type=jnp.float32)
    left = of_everyone(left, "dp") / replicas
    basis = orthonormal(left)
    right = nested_sum(right_part(merged, basis), "dp") / replicas
    residual, right_low = finish(merged, basis, right)
    errors = [residual]
    bases = [basis]
    rights = [right_low]
    inputs = [backprop_input(out_grad[0], value_weight[0])]
    new_error = jnp.stack(errors)[:, None]
    left_basis = jnp.stack(bases)
    right_factor = jnp.stack(rights)[:, None]
    input_grad = jnp.stack(inputs)
    return (new_error, left_basis, right_factor, input_grad)


def solution(mesh):
    return jax.shard_map(
        local,
        mesh=mesh,
        in_specs=(
            P(None, ("dp", "tensor"), None),
            P(None, "dp", "tensor"),
            P(None, "tensor", None),
            P(None, "dp", "tensor", None),
            P(None, "tensor", None, None),
        ),
        out_specs=(
            P(None, "dp", "tensor", None),
            P(None, "tensor", None),
            P(None, "tensor", None, None),
            P(None, ("dp", "tensor"), None),
        ),
        check_vma=False,
    )
```

profile of v0, /device:TPU:1, one launch (start us, length us, event | category | flops | bytes accessed | tf_op | source)
XLA Modules:
  0.0 197.3 jit_solution(825288019451803567)
XLA Ops:
  0.6 0.0 copy-start
  0.6 0.0 copy-start.3
  0.7 0.0 copy-start.1
  0.7 1.2 broadcast_in_dim.11
  1.9 34.1 %all_to_all.25 = bf16[4,32,4096]{2,1,0:T(8,128)(2,1)S(1)} all-to-all(bf16[4,32,4096]{2,1,0:T(8,128)(2,1)S(1)} %broadcast_in_dim.11), channel_id=1, replica_groups=mesh['dp'=64,'tensor'=4] {'tensor'}, dimensions={0} | all-to-all | bytes 2097152 | tf_op jit(solution)/shard_map/all_to_all | solution.py:17
  36.0 0.0 copy-done.3
  36.0 0.0 copy-done.1
  36.0 0.0 copy-start.2
  36.0 0.5 convolution_add_fusion
  36.5 0.5 copy-done.2
  37.0 1.3 fusion.4
  38.2 0.1 broadcast_in_dim.12
  38.3 28.9 %all_to_all.26 = f32[64,128,32]{1,2,0:T(8,128)} all-to-all(f32[64,128,32]{1,2,0:T(8,128)S(1)} %broadcast_in_dim.12), channel_id=1, replica_groups=mesh['dp'=64,'tensor'=4] {'dp'}, dimensions={0} | all-to-all | bytes 2097152 | tf_op jit(solution)/shard_map/all_to_all | solution.py:17
  67.2 1.3 reduce_sum.27
  68.5 0.1 fusion.12
  68.7 0.1 copy.17
  68.7 2.9 %cholesky.16 = f32[32,32]{1,0:T(8,128)S(1)} custom-call(f32[32,32]{1,0:T(8,128)S(1)} %fusion.10), custom_call_target="Cholesky" | custom-call | tf_op jit(solution)/shard_map/jit(cholesky)/cholesky | solution.py:56
  71.7 0.6 compare_reduce_fusion
  72.3 0.7 fusion.7
  73.0 2.4 %custom-call.6 = f32[1,32,32]{1,2,0:T(8,128)S(1)} custom-call(f32[1,32,32]{2,1,0:T(8,128)S(1)} %fusion.7), custom_call_target="InvertDiagBlocksLowerTriangular" | custom-call | tf_op jit(solution)/shard_map/triangular_solve | solution.py:57
  75.4 0.2 fusion.8
  75.7 0.0 copy-start.4
  75.7 2.1 %fusion.19 = f32[4096,32]{0,1:T(8,128)} fusion(f32[128,4096]{1,0:T(8,128)S(1)} %convolution_add_fusion, f32[128,32]{0,1:T(8,128)S(1)} %fusion.8), kind=kOutput, calls=%fused_computation.32 | convolution fusion | flops 201326592 | bytes 2637824 | tf_op jit(solution)/shard_map/dot_general | solution.py:71
  77.8 2.4 %reshape.58 = f32[64,64,32]{1,0,2:T(8,128)} reshape(f32[4096,32]{0,1:T(8,128)} %fusion.19) | data formatting | bytes 1048576 | tf_op jit(solution)/shard_map/reshape | solution.py:28
  80.2 2.8 %copy.22 = f32[64,64,32]{1,2,0:T(8,128)} copy(f32[64,64,32]{1,0,2:T(8,128)} %reshape.58) | data formatting | bytes 1048576 | tf_op jit(solution)/shard_map/reshape | solution.py:28
  83.0 2.7 %reshape.61 = f32[64,1,2048]{2,1,0:T(1,128)} reshape(f32[64,32,64]{2,1,0:T(8,128)} %bitcast.53) | data formatting | bytes 1048576
  85.7 5.2 %all-to-all-start.2 = ((f32[64,1,2048]{2,1,0:T(1,128)}), f32[64,1,2048]{2,1,0:T(1,128)}, u32[]{:S(2)}, u32[]{:S(2)}) async-start(f32[64,1,2048]{2,1,0:T(1,128)} %reshape.61), calls=%async_computation.2 | async-start | bytes 1048576 | tf_op jit(solution)/shard_map/all_to_all | solution.py:33
  90.9 0.0 copy-done
  90.9 1.7 fusion.2
  92.6 10.7 %all-to-all-done.2 = f32[64,1,2048]{2,1,0:T(1,128)} async-done(((f32[64,1,2048]{2,1,0:T(1,128)}), f32[64,1,2048]{2,1,0:T(1,128)}, u32[]{:S(2)}, u32[]{:S(2)}) %all-to-all-start.2) | async-done | bytes 524320 | tf_op jit(solution)/shard_map/all_to_all | solution.py:33
  103.3 4.4 %all-to-all-start.4 = ((f32[4,32,4096]{2,1,0:T(8,128)}), f32[4,32,4096]{2,1,0:T(8,128)}, u32[]{:S(2)}, u32[]{:S(2)}) async-start(f32[4,32,4096]{2,1,0:T(8,128)} %fusion.2), calls=%async_computation.4 | async-start | bytes 4194304 | tf_op jit(solution)/shard_map/all_to_all | solution.py:33
  107.8 0.5 broadcast.62
  108.3 3.7 %reduce.6 = f32[64,2048]{1,0:T(8,128)} reduce(f32[64,1,2048]{2,1,0:T(1,128)} %all-to-all-done.2, f32[]{:T(128)} %broadcast.62), dimensions={1}, to_apply=%all_to_all.17.reduce_sub_computation | reduce | bytes 1048580 | tf_op jit(solution)/shard_map/all_to_all | solution.py:33
  112.0 2.4 %reshape.62 = f32[64,32,64]{2,1,0:T(8,128)} reshape(f32[64,2048]{1,0:T(8,128)} %reduce.6) | data formatting | bytes 1048576
  114.5 1.3 bitcast_reduce_fusion
  115.8 1.1 broadcast_bitcast_fusion
  116.9 2.7 %reshape.63 = f32[64,1,2048]{2,1,0:T(1,128)} reshape(f32[64,32,64]{2,1,0:T(8,128)} %broadcast_bitcast_fusion) | data formatting | bytes 1048576
  119.6 36.7 %all-to-all-done.4 = f32[4,32,4096]{2,1,0:T(8,128)} async-done(((f32[4,32,4096]{2,1,0:T(8,128)}), f32[4,32,4096]{2,1,0:T(8,128)}, u32[]{:S(2)}, u32[]{:S(2)}) %all-to-all-start.4) | async-done | bytes 2097184 | tf_op jit(solution)/shard_map/all_to_all | solution.py:33
  156.3 7.6 %all-to-all-start.3 = ((f32[64,1,2048]{2,1,0:T(1,128)}), f32[64,1,2048]{2,1,0:T(1,128)}, u32[]{:S(2)}, u32[]{:S(2)}) async-start(f32[64,1,2048]{2,1,0:T(1,128)} %reshape.63), calls=%async_computation.3 | async-start | bytes 1048576 | tf_op jit(solution)/shard_map/all_to_all | solution.py:17
  164.0 2.5 %reduce_sum.29 = bf16[32,4096]{1,0:T(8,128)(2,1)} reduce(f32[4,32,4096]{2,1,0:T(8,128)} %all-to-all-done.4, f32[]{:T(128)} %constant.43.clone.1), dimensions={0}, to_apply=%region_4.5 | reduce | flops 393216 | bytes 2359300 | tf_op jit(solution)/shard_map/reduce_sum | solution.py:34
  166.4 10.0 %all-to-all-done.3 = f32[64,1,2048]{2,1,0:T(1,128)} async-done(((f32[64,1,2048]{2,1,0:T(1,128)}), f32[64,1,2048]{2,1,0:T(1,128)}, u32[]{:S(2)}, u32[]{:S(2)}) %all-to-all-start.3) | async-done | bytes 524320 | tf_op jit(solution)/shard_map/all_to_all | solution.py:17
  176.4 3.7 %reduce.7 = f32[64,2048]{1,0:T(8,128)} reduce(f32[64,1,2048]{2,1,0:T(1,128)} %all-to-all-done.3, f32[]{:T(128)} %broadcast.62), dimensions={1}, to_apply=%all_to_all.18.reduce_sub_computation | reduce | bytes 1048580 | tf_op jit(solution)/shard_map/all_to_all | solution.py:17
  180.1 2.4 %reshape.64 = f32[64,32,64]{2,1,0:T(8,128)} reshape(f32[64,2048]{1,0:T(8,128)} %reduce.7) | data formatting | bytes 1048576
  182.6 2.4 %fusion.18 = (bf16[64,64,32]{1,2,0:T(8,128)(2,1)S(1)}, f32[64,64,32]{1,2,0:T(8,128)}) fusion(f32[64,32,64]{2,1,0:T(8,128)} %reshape.64), kind=kLoop, calls=%fused_computation.28 | loop fusion | flops 262144 | bytes 1310720 | tf_op jit(solution)/shard_map/convert_element_type | solution.py:80
  185.0 1.0 copy.20
  186.0 2.2 %convert_element_type.40 = bf16[1,1,4096,32]{2,3,1,0:T(8,128)(2,1)} reshape(bf16[64,64,32]{1,0,2:T(8,128)(2,1)} %copy.20) | data formatting | bytes 524288 | tf_op jit(solution)/shard_map/convert_element_type | solution.py:80
  188.2 2.8 %copy.19 = f32[64,64,32]{1,0,2:T(8,128)} copy(f32[64,64,32]{1,2,0:T(8,128)} %get-tuple-element.5) | data formatting | bytes 1048576 | tf_op jit(solution)/shard_map/div | solution.py:95
  191.0 2.4 %div.28 = f32[4096,32]{0,1:T(8,128)} reshape(f32[64,64,32]{1,0,2:T(8,128)} %copy.19) | data formatting | bytes 1048576 | tf_op jit(solution)/shard_map/div | solution.py:95
  193.4 0.0 copy-done.4
  193.4 3.9 %fusion.1 = bf16[1,1,128,4096]{3,2,1,0:T(8,128)(2,1)} fusion(f32[128,4096]{1,0:T(8,128)S(1)} %convolution_add_fusion, f32[128,32]{0,1:T(8,128)S(1)} %fusion.8, f32[4096,32]{0,1:T(8,128)} %div.28), kind=kOutput, calls=%fused_computation.3 | convolution fusion | flops 202375168 | bytes 3686400 | tf_op jit(solution)/shard_map/dot_general | solution.py:77
  (2 shorter events, 0.0 us)
Async XLA Ops:
  0.6 90.2 %copy-start = (bf16[1,128,4096]{2,1,0:T(8,128)(2,1)S(1)}, bf16[1,128,4096]{2,1,0:T(8,128)(2,1)}, u32[]{:S(2)}) copy-start(bf16[1,128,4096]{2,1,0:T(8,128)(2,1)} %param.7) | copy-start | bytes 3145732
  0.6 35.4 %copy-start.3 = (bf16[1,128,128]{2,1,0:T(8,128)(2,1)S(1)}, bf16[1,128,128]{2,1,0:T(8,128)(2,1)}, u32[]{:S(2)}) copy-start(bf16[1,128,128]{2,1,0:T(8,128)(2,1)} %param.6) | copy-start | bytes 98308
  0.7 35.3 %copy-start.1 = (bf16[1,1,128,4096]{3,2,1,0:T(8,128)(2,1)S(1)}, bf16[1,1,128,4096]{3,2,1,0:T(8,128)(2,1)}, u32[]{:S(2)}) copy-start(bf16[1,1,128,4096]{3,2,1,0:T(8,128)(2,1)} %param.8) | copy-start | bytes 3145732
  36.0 1.0 copy-start.2
  75.7 117.7 %copy-start.4 = (f32[128,32]{0,1:T(8,128)}, f32[128,32]{0,1:T(8,128)S(1)}, u32[]{:S(2)}) copy-start(f32[128,32]{0,1:T(8,128)S(1)} %fusion.8) | copy-start | bytes 49156
  85.7 17.6 %all-to-all-start.2 = ((f32[64,1,2048]{2,1,0:T(1,128)}), f32[64,1,2048]{2,1,0:T(1,128)}, u32[]{:S(2)}, u32[]{:S(2)}) async-start(f32[64,1,2048]{2,1,0:T(1,128)} %reshape.61), calls=%async_computation.2 | async-start | bytes 1048576 | tf_op jit(solution)/shard_map/all_to_all | solution.py:33
  103.3 53.0 %all-to-all-start.4 = ((f32[4,32,4096]{2,1,0:T(8,128)}), f32[4,32,4096]{2,1,0:T(8,128)}, u32[]{:S(2)}, u32[]{:S(2)}) async-start(f32[4,32,4096]{2,1,0:T(8,128)} %fusion.2), calls=%async_computation.4 | async-start | bytes 4194304 | tf_op jit(solution)/shard_map/all_to_all | solution.py:33
  156.3 20.1 %all-to-all-start.3 = ((f32[64,1,2048]{2,1,0:T(1,128)}), f32[64,1,2048]{2,1,0:T(1,128)}, u32[]{:S(2)}, u32[]{:S(2)}) async-start(f32[64,1,2048]{2,1,0:T(1,128)} %reshape.63), calls=%async_computation.3 | async-start | bytes 1048576 | tf_op jit(solution)/shard_map/all_to_all | solution.py:17
where the time goes:
time: 198 us; the launch traced here: 197 us
  blocking collectives  63 us (32%)
  waiting for transfers between devices  57.4 us (29%)
  local copies, waits for them, and re-layouts  27.4 us (14%)
  other arithmetic  21.7 us (11%)
  starting transfers between devices  17.2 us (9%)
  matrix products  9.73 us (5%)
    all_to_all x2, blocking collectives, copy_for_each(): lax.all_to_all(jnp.broadcast_to(shard[None], (length, *shard.shape)), axi...  63 us
    all_to_all x2, waiting for transfers between devices, sum_at_owner(): lax.all_to_all(cut_along(shard, dim, length), axis, 0, 0, tiled=True)  47.5 us
    unnamed x15, local copies, waits for them, and re-layouts  11.8 us
    all_to_all x1, waiting for transfers between devices, copy_for_each(): lax.all_to_all(jnp.broadcast_to(shard[None], (length, *shard.shape)), axi...  9.97 us
    all_to_all x2, starting transfers between devices, sum_at_owner(): lax.all_to_all(cut_along(shard, dim, length), axis, 0, 0, tiled=True)  9.61 us
    all_to_all x1, starting transfers between devices, copy_for_each(): lax.all_to_all(jnp.broadcast_to(shard[None], (length, *shard.shape)), axi...  7.64 us
    reshape x2, local copies, waits for them, and re-layouts, cut_along(): return jnp.moveaxis(shard.reshape(*before, length, -1, *after), dim, 0)  5.26 us
    div x2, local copies, waits for them, and re-layouts, local(): right = nested_sum(right_part(merged, basis), 'dp') / replicas  5.22 us
  transfers between devices with their start and end apart: 3, of which 3 were waited for; matrix products, arithmetic and copies ran while one was open for 8% of the time, Pallas kernels for 0%

commit v1 on v0

v1 whole, which is shorter than its diff:
```python
import jax
import jax.numpy as jnp
from jax import lax
from jax.experimental import pallas as pl
from jax.experimental.pallas import tpu as pltpu
from jax.sharding import Mesh
from jax.sharding import PartitionSpec as P

F32 = jnp.float32
BF16 = jnp.bfloat16
HIGH = lax.Precision.HIGHEST
CHIPS = ("x", "zl", "y")
DP = ("x", "zl", "y", "core")
EVERY = DP + ("t",)

TENSOR = 4
REPLICAS = 64
WIDE = 4096
HEAD = 128
RANK = 32
HALF = RANK // 2
OWN = 32
PART = WIDE // TENSOR
N_CHIPS = REPLICAS // 2
STEP = 512
NT = (((1,), (1,)), ((), ()))


def split3(x):
    hi = x.astype(BF16)
    rest = x - hi.astype(F32)
    mid = rest.astype(BF16)
    low = (rest - mid.astype(F32)).astype(BF16)
    return (hi, mid, low)


def split2(x):
    hi = x.astype(BF16)
    return (hi, (x - hi.astype(F32)).astype(BF16))


def turned(ref, t):
    blocks = [ref[pl.ds(((t - k + TENSOR) % TENSOR) * OWN, OWN), :] for k in range(TENSOR)]
    return jnp.concatenate(blocks, axis=0)


def call(kernel, outs, scratch=(), flops=10**6, moved=10**6):
    vmem = pl.BlockSpec(memory_space=pltpu.VMEM)

    def run(*args):
        return pl.pallas_call(
            kernel,
            out_shape=[jax.ShapeDtypeStruct(s, d) for s, d in outs],
            in_specs=[vmem] * len(args),
            out_specs=[vmem] * len(outs),
            scratch_shapes=list(scratch),
            compiler_params=pltpu.CompilerParams(vmem_limit_bytes=40 * 2**20),
            cost_estimate=pl.CostEstimate(flops=flops, bytes_accessed=moved, transcendentals=0),
        )(*args)

    return run


def pack_kernel(w, og, *sends):
    t, core = lax.axis_index("t"), lax.axis_index("core")
    rows = pl.ds(pl.multiple_of(core * 64, 64), 64)
    for k, send in enumerate(sends, 1):
        target = lax.rem(t + k, TENSOR)
        send[0:64, :] = w[rows, pl.ds(pl.multiple_of(target * PART, PART), PART)]
        for m in range(8):
            send[64:80, 128 * m : 128 * m + 128] = og[16 * m : 16 * m + 16, :]


def left_kernel(a0, a1, a2, a3, og, ef, warm, keep, send, held):
    t, core = lax.axis_index("t"), lax.axis_index("core")
    lines = warm[...]
    ogp = turned(og, t)
    inner = jnp.concatenate(
        [lax.dot_general(lines, a[...], NT, preferred_element_type=F32) for a in (a0, a1, a2, a3)],
        axis=1,
    )
    parts = jnp.concatenate(split3(inner), axis=0)
    prod = jnp.dot(parts, ogp, preferred_element_type=F32)
    fed = lax.dot_general(lines, ef[...], NT, preferred_element_type=F32)
    held[...] = prod[0:RANK] + prod[RANK : 2 * RANK] + prod[2 * RANK :] + fed
    keep[...] = held[pl.ds(pl.multiple_of(core * HALF, HALF), HALF), :]
    send[...] = held[pl.ds(pl.multiple_of((1 - core) * HALF, HALF), HALF), :]


def basis_kernel(lown, loth, a0, a1, a2, a3, og, ef, qt, keep, send, held, heldo):
    t, core = lax.axis_index("t"), lax.axis_index("core")
    mine = pl.ds(pl.multiple_of(core * HALF, HALF), HALF)
    other = pl.ds(pl.multiple_of((1 - core) * HALF, HALF), HALF)
    held[mine, :] = lown[...]
    held[other, :] = loth[...]
    left = held[...]
    gram = lax.dot_general(left, left, NT, precision=HIGH, preferred_element_type=F32)
    row = lax.broadcasted_iota(jnp.int32, (RANK, 1), 0)
    for k in range(RANK - 1):
        scale = 1.0 / gram[k : k + 1, k : k + 1]
        factor = jnp.where(row > k, gram[:, k : k + 1] * scale, 0.0)
        pivot_g, pivot_l = gram[k : k + 1, :], left[k : k + 1, :]
        gram = gram - factor * pivot_g
        left = left - factor * pivot_l
    eye = row == lax.broadcasted_iota(jnp.int32, (RANK, RANK), 1)
    diagonal = jnp.sum(jnp.where(eye, gram, 0.0), axis=1, keepdims=True)
    basis = left * (1.0 / jnp.sqrt(diagonal))
    qt[...] = basis
    ogp = turned(og, t)
    prod = lax.dot_general(
        jnp.concatenate(split3(basis), axis=0), ogp, NT, preferred_element_type=F32
    )
    held[...] = basis
    heldo[...] = prod[0:RANK] + prod[RANK : 2 * RANK] + prod[2 * RANK :]
    q = jnp.concatenate([held[mine, :], held[other, :]], axis=0)
    qo = jnp.concatenate([heldo[mine, :], heldo[other, :]], axis=0)
    lhs = jnp.concatenate(
        [jnp.concatenate(split3(qo), axis=0), jnp.concatenate(split3(q), axis=0)], axis=1
    )
    for c in range(0, WIDE, STEP):
        cols = slice(c, c + STEP)
        rhs = jnp.concatenate([a[:, cols] for a in (a0, a1, a2, a3, ef)], axis=0)
        p = jnp.dot(lhs, rhs, preferred_element_type=F32)
        r = p[0:RANK] + p[RANK : 2 * RANK] + p[2 * RANK :]
        for j in range(STEP // 128):
            chip = c // 128 + j
            keep[chip] = r[0:HALF, 128 * j : 128 * j + 128]
            send[chip] = r[HALF:, 128 * j : 128 * j + 128]


def spread_kernel(pieces, out):
    total = jnp.sum(pieces[...], axis=0) * (1.0 / REPLICAS)
    out[...] = jnp.broadcast_to(total[None], out.shape)


def finish_kernel(rown, roth, qt, og, a0, a1, a2, a3, ef, i0, i1, i2, i3, err, fac, igrad, held):
    t, core = lax.axis_index("t"), lax.axis_index("core")
    mine = pl.ds(pl.multiple_of(core * HALF, HALF), HALF)
    other = pl.ds(pl.multiple_of((1 - core) * HALF, HALF), HALF)
    for k, block in enumerate((i0, i1, i2, i3)):
        source = lax.rem(t - k + TENSOR, TENSOR)
        igrad[:, pl.ds(pl.multiple_of(source * PART, PART), PART)] = block[...]
    q = jnp.concatenate([qt[mine, :], qt[other, :]], axis=0)
    hi, mid = split2(q)
    hi, mid = hi.astype(F32), mid.astype(F32)
    ogp = turned(og, t).astype(F32)
    lhs = jnp.concatenate([ogp, -hi, -hi, -mid, -mid], axis=0).T.astype(BF16)
    for c in range(0, WIDE, STEP):
        cols = slice(c, c + STEP)
        ro = jnp.concatenate([rown[c // 128 + j] for j in range(STEP // 128)], axis=1)
        rt = jnp.concatenate([roth[c // 128 + j] for j in range(STEP // 128)], axis=1)
        fac[mine, cols] = ro.astype(BF16)
        fac[other, cols] = rt.astype(BF16)
        rhi, rmid = split2(jnp.concatenate([ro, rt], axis=0))
        rhs = jnp.concatenate([a[:, cols] for a in (a0, a1, a2, a3)] + [rhi, rmid, rhi, rmid], axis=0)
        total = jnp.dot(lhs, rhs, preferred_element_type=F32) + ef[:, cols].astype(F32)
        err[:, cols] = total.astype(BF16)


def input_kernel(w, og, r1, r2, r3, e1, e2, e3, o0, o1, o2, o3, weights, feats):
    t, core = lax.axis_index("t"), lax.axis_index("core")
    weights[0:128, :] = w[:, pl.ds(pl.multiple_of(t * PART, PART), PART)]
    feats[:, 0:128] = og[...]
    for k, (r, e) in enumerate(((r1, e1), (r2, e2), (r3, e3)), 1):
        weights[pl.ds(pl.multiple_of(128 * k + 64 * core, 64), 64), :] = r[0:64, :]
        weights[pl.ds(pl.multiple_of(128 * k + 64 * (1 - core), 64), 64), :] = e[0:64, :]
        for m in range(8):
            feats[16 * m : 16 * m + 16, 128 * k : 128 * k + 128] = r[64:80, 128 * m : 128 * m + 128]
    for k, out in enumerate((o0, o1, o2, o3)):
        target = lax.rem(t + k, TENSOR)
        rows = feats[pl.ds(pl.multiple_of(target * OWN, OWN), OWN), :]
        out[...] = jnp.dot(rows, weights[...], preferred_element_type=F32).astype(BF16)


def moved(x, k):
    return lax.ppermute(x, "t", [(i, (i + k) % TENSOR) for i in range(TENSOR)])


def swapped(x):
    return lax.ppermute(x, "core", [(0, 1), (1, 0)])


def exchanged(x):
    return lax.all_to_all(x, CHIPS, 0, 0, tiled=True)


def local(activations, out_grad, value_weight, error_feedback, warm_right):
    act, og, weight = activations[0], out_grad[0], value_weight[0]
    ef = error_feedback[0, 0]
    warm = warm_right[0, 0].T

    acts = [act] + [moved(act, k) for k in (1, 2, 3)]
    packed = ((OWN * 2 + 16, PART), BF16)
    sends = call(pack_kernel, [packed] * 3)(weight, og)

    half = ((HALF, HEAD), F32)
    left_keep, left_send = call(
        left_kernel, [half, half], [pltpu.VMEM((RANK, HEAD), F32)], flops=10**8, moved=3 * 10**6
    )(*acts, og, ef, warm)

    sends, left_send = lax.optimization_barrier((sends, left_send))
    got = [moved(s, k) for k, s in zip((1, 2, 3), sends)]

    left_half = left_keep + swapped(left_send)
    pieces = exchanged(jnp.broadcast_to(left_half[None], (N_CHIPS, HALF, HEAD)))
    left_own = jnp.sum(pieces, axis=0)
    left_other = swapped(left_own)
    left_other, got = lax.optimization_barrier((left_other, got))

    traded = [swapped(g) for g in got]
    block = ((N_CHIPS, HALF, 128), F32)
    basis, right_keep, right_send = call(
        basis_kernel,
        [((RANK, HEAD), F32), block, block],
        [pltpu.VMEM((RANK, HEAD), F32), pltpu.VMEM((RANK, HEAD), F32)],
        flops=10**8,
        moved=3 * 10**6,
    )(left_own, left_other, *acts, og, ef)

    outs = call(
        input_kernel,
        [((OWN, PART), BF16)] * 4,
        [pltpu.VMEM((512, PART), BF16), pltpu.VMEM((128, 512), BF16)],
        flops=2 * 10**8,
        moved=2 * 10**6,
    )(weight, og, *got, *traded)
    inputs = [outs[0]] + [moved(o, k) for k, o in zip((1, 2, 3), outs[1:])]

    pieces = exchanged(right_keep + swapped(right_send))
    pieces, outs = lax.optimization_barrier((pieces, outs))
    (mean,) = call(spread_kernel, [block])(pieces)
    right_own = exchanged(mean)
    right_own, inputs = lax.optimization_barrier((right_own, inputs))
    right_other = swapped(right_own)

    err, fac, igrad = call(
        finish_kernel,
        [((HEAD, WIDE), BF16), ((RANK, WIDE), BF16), ((OWN, WIDE), BF16)],
        [pltpu.VMEM((RANK, HEAD), F32)],
        flops=3 * 10**8,
        moved=5 * 10**6,
    )(right_own, right_other, basis, og, *acts, ef, *inputs)

    return (err[None, None], basis.T[None], fac.T[None, None], igrad[None])


def solution(mesh):
    parted = Mesh(
        mesh.devices.reshape(4, 2, 4, 2, 4), EVERY
    )
    return jax.shard_map(
        local,
        mesh=parted,
        in_specs=(
            P(None, EVERY, None),
            P(None, DP, "t"),
            P(None, "t", None),
            P(None, DP, "t", None),
            P(None, "t", None, None),
        ),
        out_specs=(
            P(None, DP, "t", None),
            P(None, "t", None),
            P(None, "t", None, None),
            P(None, EVERY, None),
        ),
        check_vma=False,
    )
```

time: 198 us -> 116 us (0.59)
  blocking collectives: 63 us -> 0 us
  starting transfers between devices: 17.2 us -> 61.4 us
  waiting for transfers between devices: 57.4 us -> 34.8 us
  other arithmetic: 21.7 us -> 0.78 us
  local copies, waits for them, and re-layouts: 27.4 us -> 9.93 us
  matrix products: 9.73 us -> 0 us
  Pallas kernels: 0 us -> 7.82 us
    all_to_all x2 -> x0, blocking collectives: 63 us -> none  [copy_for_each(): lax.all_to_all(jnp.broadcast_to(shard[None], (length, *shard.shape)), axi...]
    all_to_all x3, waiting for transfers between devices: 57.4 us -> 0.01 us  [exchanged(): return lax.all_to_all(x, CHIPS, 0, 0, tiled=True)]
    ppermute x0 -> x16, starting transfers between devices: none -> 36.7 us  [the longest x9 26.5 us: moved(): return lax.ppermute(x, 't', [(i, (i + k) % TENSOR) for i in range(TENSOR)])]
    ppermute x0 -> x16, waiting for transfers between devices: none -> 34.8 us  [the longest x9 30.3 us: moved(): return lax.ppermute(x, 't', [(i, (i + k) % TENSOR) for i in range(TENSOR)])]
    dot_general x6 -> x0, matrix products: 9.5 us -> none  [the longest x1 3.87 us: finish(): lax.dot_general(basis, right, (((1,), (1,)), ((), ())), precision=HIGH, p...]
    pallas_call x0 -> x6, Pallas kernels: none -> 7.82 us  [run(): pl.pallas_call(kernel, out_shape=[jax.ShapeDtypeStruct(s, d) for s, d in...]
    all_to_all x2 -> x0, other arithmetic: 7.47 us -> none  [the longest x1 3.75 us: sum_at_owner(): lax.all_to_all(cut_along(shard, dim, length), axis, 0, 0, tiled=True)]
    all_to_all x3, starting transfers between devices: 17.2 us -> 24.7 us  [exchanged(): return lax.all_to_all(x, CHIPS, 0, 0, tiled=True)]
  transfers between devices with their start and end apart: 3 -> 19, of which waited for: 3 -> 14; matrix products, arithmetic and copies ran while one was open for 8% -> 0% of each run, Pallas kernels for 0% -> 1%
where the time goes in v1:
time: 116 us; the launch traced here: 115 us
  starting transfers between devices  61.4 us (53%)
  waiting for transfers between devices  34.8 us (30%)
  local copies, waits for them, and re-layouts  9.93 us (9%)
  Pallas kernels  7.82 us (7%)
    ppermute x9, waiting for transfers between devices, moved(): return lax.ppermute(x, 't', [(i, (i + k) % TENSOR) for i in range(TENSOR)])  30.3 us
    ppermute x9, starting transfers between devices, moved(): return lax.ppermute(x, 't', [(i, (i + k) % TENSOR) for i in range(TENSOR)])  26.5 us
    all_to_all x3, starting transfers between devices, exchanged(): return lax.all_to_all(x, CHIPS, 0, 0, tiled=True)  24.7 us
    ppermute x7, starting transfers between devices, swapped(): return lax.ppermute(x, 'core', [(0, 1), (1, 0)])  10.2 us
    unnamed x42, local copies, waits for them, and re-layouts  9.21 us
    pallas_call x6, Pallas kernels, run(): pl.pallas_call(kernel, out_shape=[jax.ShapeDtypeStruct(s, d) for s, d in...  7.82 us
    ppermute x7, waiting for transfers between devices, swapped(): return lax.ppermute(x, 'core', [(0, 1), (1, 0)])  4.48 us
  transfers between devices with their start and end apart: 19, of which 14 were waited for; matrix products, arithmetic and copies ran while one was open for 0% of the time, Pallas kernels for 1%

profile of v1, /device:TPU:1, one launch (start us, length us, event | category | flops | bytes accessed | tf_op | source)
XLA Modules:
  0.0 115.4 jit_solution(7672257498192467224)
XLA Ops:
  0.6 0.0 copy-start
  0.6 6.9 %collective-permute-start.2 = (bf16[32,4096]{1,0:T(8,128)(2,1)}, bf16[32,4096]{1,0:T(8,128)(2,1)S(1)}, u32[]{:S(2)}, u32[]{:S(2)}) collective-permute-start(bf16[32,4096]{1,0:T(8,128)(2,1)} %bitcast.20), channel_id=1, source_target_pairs={{0,3},{1,0},{2,1},{3,2},{4,7},{5,4},{6,5},{7,6},{8,11},{9,8},{10,9... | collective-permute-start | bytes 786440 | tf_op jit(solution)/shard_map/ppermute | solution.py:176
  7.6 1.0 collective-permute-start.1
  8.6 2.3 %collective-permute-start = (bf16[32,4096]{1,0:T(8,128)(2,1)}, bf16[32,4096]{1,0:T(8,128)(2,1)S(1)}, u32[]{:S(2)}, u32[]{:S(2)}) collective-permute-start(bf16[32,4096]{1,0:T(8,128)(2,1)} %bitcast.22), channel_id=1, source_target_pairs={{0,1},{1,2},{2,3},{3,0},{4,5},{5,6},{6,7},{7,4},{8,9},{9,10},{10,1... | collective-permute-start | bytes 786440 | tf_op jit(solution)/shard_map/ppermute | solution.py:176
  10.8 1.2 %copy-done.1 = bf16[1,128,4096]{2,1,0:T(8,128)(2,1)S(1)} copy-done((bf16[1,128,4096]{2,1,0:T(8,128)(2,1)S(1)}, bf16[1,128,4096]{2,1,0:T(8,128)(2,1)}, u32[]{:S(2)}) %copy-start.1) | copy-done | bytes 1048600
  12.1 0.8 copy-done.5
  12.9 6.9 %collective-permute-done.2.a3 = bf16[32,4096]{1,0:T(8,128)(2,1)S(1)} collective-permute-done((bf16[32,4096]{1,0:T(8,128)(2,1)}, bf16[32,4096]{1,0:T(8,128)(2,1)S(1)}, u32[]{:S(2)}, u32[]{:S(2)}) %collective-permute-start.2) | collective-permute-done | bytes 262176 | tf_op jit(solution)/shard_map/ppermute | solution.py:176
  19.7 4.5 %collective-permute-done.1.a2 = bf16[32,4096]{1,0:T(8,128)(2,1)S(1)} collective-permute-done((bf16[32,4096]{1,0:T(8,128)(2,1)}, bf16[32,4096]{1,0:T(8,128)(2,1)S(1)}, u32[]{:S(2)}, u32[]{:S(2)}) %collective-permute-start.1) | collective-permute-done | bytes 262176 | tf_op jit(solution)/shard_map/ppermute | solution.py:176
  24.2 2.8 %collective-permute-done.a1 = bf16[32,4096]{1,0:T(8,128)(2,1)S(1)} collective-permute-done((bf16[32,4096]{1,0:T(8,128)(2,1)}, bf16[32,4096]{1,0:T(8,128)(2,1)S(1)}, u32[]{:S(2)}, u32[]{:S(2)}) %collective-permute-start) | collective-permute-done | bytes 262176 | tf_op jit(solution)/shard_map/ppermute | solution.py:176
  27.1 0.0 copy-done
  27.1 0.0 copy-done.6
  27.1 0.9 copy-done.3
  28.0 0.9 copy-done.7
  29.0 0.9 shard_map.84
  29.8 4.3 %collective-permute-start.3 = (f32[16,128]{1,0:T(8,128)S(1)}, f32[16,128]{1,0:T(8,128)S(1)}, u32[]{:S(2)}, u32[]{:S(2)}) collective-permute-start(f32[16,128]{1,0:T(8,128)S(1)} %get-tuple-element.38), channel_id=1, source_target_pairs={{0,4},{4,0},{1,5},{5,1},{2,6},{6,2},{3,7},{7,3},{8,12},{12,8},{9,1... | collective-permute-start | bytes 24584 | tf_op jit(solution)/shard_map/ppermute | solution.py:180
  34.1 0.8 collective-permute-done.3
  34.9 0.7 broadcast_in_dim.18
  35.7 9.8 %all-to-all-start = ((f32[32,16,128]{2,1,0:T(8,128)}), f32[32,16,128]{2,1,0:T(8,128)S(1)}, u32[]{:S(2)}, u32[]{:S(2)}) async-start(f32[32,16,128]{2,1,0:T(8,128)} %broadcast_in_dim.18), calls=%async_computation | async-start | bytes 524288 | tf_op jit(solution)/shard_map/all_to_all | solution.py:184
  45.4 0.0 copy-start.4
  45.5 2.3 %collective-permute-start.5 = (bf16[80,1024]{1,0:T(8,128)(2,1)S(1)}, bf16[80,1024]{1,0:T(8,128)(2,1)S(1)}, u32[]{:S(2)}, u32[]{:S(2)}) collective-permute-start(bf16[80,1024]{1,0:T(8,128)(2,1)S(1)} %get-tuple-element.39), channel_id=1, source_target_pairs={{0,1},{1,2},{2,3},{3,0},{4,5},{5,6},{6,7},{7,4},{8,9},{9,10},{10,1... | collective-permute-start | bytes 491528 | tf_op jit(solution)/shard_map/ppermute | solution.py:176
  47.7 4.0 %collective-permute-start.6 = (bf16[80,1024]{1,0:T(8,128)(2,1)S(1)}, bf16[80,1024]{1,0:T(8,128)(2,1)S(1)}, u32[]{:S(2)}, u32[]{:S(2)}) collective-permute-start(bf16[80,1024]{1,0:T(8,128)(2,1)S(1)} %get-tuple-element.40), channel_id=1, source_target_pairs={{0,2},{1,3},{2,0},{3,1},{4,6},{5,7},{6,4},{7,5},{8,10},{9,11},{10,... | collective-permute-start | bytes 491528 | tf_op jit(solution)/shard_map/ppermute | solution.py:176
  51.7 2.6 %collective-permute-start.7 = (bf16[80,1024]{1,0:T(8,128)(2,1)S(1)}, bf16[80,1024]{1,0:T(8,128)(2,1)S(1)}, u32[]{:S(2)}, u32[]{:S(2)}) collective-permute-start(bf16[80,1024]{1,0:T(8,128)(2,1)S(1)} %get-tuple-element.41), channel_id=1, source_target_pairs={{0,3},{1,0},{2,1},{3,2},{4,7},{5,4},{6,5},{7,6},{8,11},{9,8},{10,9... | collective-permute-start | bytes 491528 | tf_op jit(solution)/shard_map/ppermute | solution.py:176
  54.3 0.0 all-to-all-done
  54.4 1.6 %collective-permute-start.4 = (f32[16,128]{1,0:T(8,128)S(1)}, f32[16,128]{1,0:T(8,128)S(1)}, u32[]{:S(2)}, u32[]{:S(2)}) collective-permute-start(f32[16,128]{1,0:T(8,128)S(1)} %reduce_sum.9.lown), channel_id=1, source_target_pairs={{0,4},{4,0},{1,5},{5,1},{2,6},{6,2},{3,7},{7,3},{8,12},{12,8},{9,1... | collective-permute-start | bytes 24584 | tf_op jit(solution)/shard_map/ppermute | solution.py:180
  55.9 3.9 %collective-permute-done.5.r1 = bf16[80,1024]{1,0:T(8,128)(2,1)S(1)} collective-permute-done((bf16[80,1024]{1,0:T(8,128)(2,1)S(1)}, bf16[80,1024]{1,0:T(8,128)(2,1)S(1)}, u32[]{:S(2)}, u32[]{:S(2)}) %collective-permute-start.5) | collective-permute-done | bytes 163872 | tf_op jit(solution)/shard_map/ppermute | solution.py:176
  59.8 4.4 %collective-permute-done.6.r2 = bf16[80,1024]{1,0:T(8,128)(2,1)S(1)} collective-permute-done((bf16[80,1024]{1,0:T(8,128)(2,1)S(1)}, bf16[80,1024]{1,0:T(8,128)(2,1)S(1)}, u32[]{:S(2)}, u32[]{:S(2)}) %collective-permute-start.6) | collective-permute-done | bytes 163872 | tf_op jit(solution)/shard_map/ppermute | solution.py:176
  64.2 3.8 %collective-permute-done.7.r3 = bf16[80,1024]{1,0:T(8,128)(2,1)S(1)} collective-permute-done((bf16[80,1024]{1,0:T(8,128)(2,1)S(1)}, bf16[80,1024]{1,0:T(8,128)(2,1)S(1)}, u32[]{:S(2)}, u32[]{:S(2)}) %collective-permute-start.7) | collective-permute-done | bytes 163872 | tf_op jit(solution)/shard_map/ppermute | solution.py:176
  68.0 0.0 copy-done.8
  68.0 0.0 copy-done.10
  68.0 0.0 collective-permute-done.4.loth
  68.0 0.7 copy-done.12
  68.6 0.0 copy-done.4
  68.6 3.8 %shard_map.86 = (f32[32,128]{1,0:T(8,128)}, f32[32,16,128]{2,1,0:T(8,128)S(1)}, f32[32,16,128]{2,1,0:T(8,128)S(1)}) custom-call(f32[16,128]{1,0:T(8,128)S(1)} %reduce_sum.9.lown, f32[16,128]{1,0:T(8,128)S(1)} %collective-permute-done.4.loth, bf16[32,4096]{1,0:T(8,128)(2,1)S(1)} %bitcast.24, bf16[32,4096]{1,0:T(8,128)(2,1)S(1)} %collective-permute-done.a1, ...), custom_call_target="tpu_custom_call" | custom-call | flops 100000000 | bytes 3000000 | tf_op jit(solution)/shard_map/pallas_call | solution.py:51
  72.4 0.5 collective-permute-start.8
  72.9 1.2 %collective-permute-done.8 = f32[32,16,128]{2,1,0:T(8,128)S(1)} collective-permute-done((f32[32,16,128]{2,1,0:T(8,128)S(1)}, f32[32,16,128]{2,1,0:T(8,128)S(1)}, u32[]{:S(2)}, u32[]{:S(2)}) %collective-permute-start.8) | collective-permute-done | bytes 262176 | tf_op jit(solution)/shard_map/ppermute | solution.py:180
  74.1 0.7 add.7
  74.8 6.8 %all-to-all-start.1 = ((f32[32,16,128]{2,1,0:T(8,128)}), f32[32,16,128]{2,1,0:T(8,128)S(1)}, u32[]{:S(2)}, u32[]{:S(2)}) async-start(f32[32,16,128]{2,1,0:T(8,128)} %add.7), calls=%async_computation.1 | async-start | bytes 524288 | tf_op jit(solution)/shard_map/all_to_all | solution.py:184
  81.6 0.7 collective-permute-start.9
  82.3 0.1 collective-permute-start.10
  82.4 0.4 collective-permute-start.11
  82.9 0.7 collective-permute-done.9.e1
  83.6 0.4 collective-permute-done.10.e2
  84.0 0.2 collective-permute-done.11.e3
  84.2 0.9 copy-done.9
  85.1 0.9 copy-done.11
  86.0 0.9 copy-done.13
  86.9 0.9 shard_map.87
  87.9 0.6 copy-done.15
  88.5 0.6 copy-done.17
  89.1 0.6 copy-done.19
  89.7 0.0 all-to-all-done.1.pieces
  89.8 0.8 shard_map.88
  90.5 8.2 %all-to-all-start.2 = ((f32[32,16,128]{2,1,0:T(8,128)}), f32[32,16,128]{2,1,0:T(8,128)S(1)}, u32[]{:S(2)}, u32[]{:S(2)}) async-start(f32[32,16,128]{2,1,0:T(8,128)} %shard_map.88), calls=%async_computation.2 | async-start | bytes 524288 | tf_op jit(solution)/shard_map/all_to_all | solution.py:184
  98.7 2.5 %collective-permute-start.12 = (bf16[32,1024]{1,0:T(8,128)(2,1)S(1)}, bf16[32,1024]{1,0:T(8,128)(2,1)S(1)}, u32[]{:S(2)}, u32[]{:S(2)}) collective-permute-start(bf16[32,1024]{1,0:T(8,128)(2,1)S(1)} %copy-done.20), channel_id=1, source_target_pairs={{0,1},{1,2},{2,3},{3,0},{4,5},{5,6},{6,7},{7,4},{8,9},{9,10},{10,1... | collective-permute-start | bytes 196616 | tf_op jit(solution)/shard_map/ppermute | solution.py:176
  101.2 3.0 %collective-permute-start.13 = (bf16[32,1024]{1,0:T(8,128)(2,1)S(1)}, bf16[32,1024]{1,0:T(8,128)(2,1)S(1)}, u32[]{:S(2)}, u32[]{:S(2)}) collective-permute-start(bf16[32,1024]{1,0:T(8,128)(2,1)S(1)} %copy-done.18), channel_id=1, source_target_pairs={{0,2},{1,3},{2,0},{3,1},{4,6},{5,7},{6,4},{7,5},{8,10},{9,11},{10,... | collective-permute-start | bytes 196616 | tf_op jit(solution)/shard_map/ppermute | solution.py:176
  104.2 0.0 copy-done.16
  104.2 1.9 %collective-permute-start.14 = (bf16[32,1024]{1,0:T(8,128)(2,1)S(1)}, bf16[32,1024]{1,0:T(8,128)(2,1)S(1)}, u32[]{:S(2)}, u32[]{:S(2)}) collective-permute-start(bf16[32,1024]{1,0:T(8,128)(2,1)S(1)} %copy-done.16), channel_id=1, source_target_pairs={{0,3},{1,0},{2,1},{3,2},{4,7},{5,4},{6,5},{7,6},{8,11},{9,8},{10,9... | collective-permute-start | bytes 196616 | tf_op jit(solution)/shard_map/ppermute | solution.py:176
  106.1 2.1 %collective-permute-done.12.i1 = bf16[32,1024]{1,0:T(8,128)(2,1)S(1)} collective-permute-done((bf16[32,1024]{1,0:T(8,128)(2,1)S(1)}, bf16[32,1024]{1,0:T(8,128)(2,1)S(1)}, u32[]{:S(2)}, u32[]{:S(2)}) %collective-permute-start.12) | collective-permute-done | bytes 65568 | tf_op jit(solution)/shard_map/ppermute | solution.py:176
  108.2 1.9 %collective-permute-done.13.i2 = bf16[32,1024]{1,0:T(8,128)(2,1)S(1)} collective-permute-done((bf16[32,1024]{1,0:T(8,128)(2,1)S(1)}, bf16[32,1024]{1,0:T(8,128)(2,1)S(1)}, u32[]{:S(2)}, u32[]{:S(2)}) %collective-permute-start.13) | collective-permute-done | bytes 65568 | tf_op jit(solution)/shard_map/ppermute | solution.py:176
  110.1 0.0 collective-permute-done.14.i3
  110.1 0.0 all-to-all-done.2.rown
  110.1 2.6 %collective-permute-start.15 = (f32[32,16,128]{2,1,0:T(8,128)S(1)}, f32[32,16,128]{2,1,0:T(8,128)S(1)}, u32[]{:S(2)}, u32[]{:S(2)}) collective-permute-start(f32[32,16,128]{2,1,0:T(8,128)S(1)} %all-to-all-done.2.rown), channel_id=1, source_target_pairs={{0,4},{4,0},{1,5},{5,1},{2,6},{6,2},{3,7},{7,3},{8,12},{12,8},{9,1... | collective-permute-start | bytes 786440 | tf_op jit(solution)/shard_map/ppermute | solution.py:180
  112.8 1.2 %collective-permute-done.15.roth = f32[32,16,128]{2,1,0:T(8,128)S(1)} collective-permute-done((f32[32,16,128]{2,1,0:T(8,128)S(1)}, f32[32,16,128]{2,1,0:T(8,128)S(1)}, u32[]{:S(2)}, u32[]{:S(2)}) %collective-permute-start.15) | collective-permute-done | bytes 262176 | tf_op jit(solution)/shard_map/ppermute | solution.py:180
  113.9 1.5 %shard_map.89 = (bf16[128,4096]{1,0:T(8,128)(2,1)}, bf16[32,4096]{1,0:T(8,128)(2,1)}, bf16[32,4096]{1,0:T(8,128)(2,1)}) custom-call(f32[32,16,128]{2,1,0:T(8,128)S(1)} %all-to-all-done.2.rown, f32[32,16,128]{2,1,0:T(8,128)S(1)} %collective-permute-done.15.roth, f32[32,128]{1,0:T(8,128)S(1)} %copy-done.14, bf16[128,128]{1,0:T(8,128)(2,1)S(1)} %bitcast.30, ...), custom_call_target="tpu_custom_call" | custom-call | flops 300000000 | bytes 5000000 | tf_op jit(solution)/shard_map/pallas_call | solution.py:51
  (26 shorter events, 0.1 us)
Async XLA Ops:
  0.6 26.4 %copy-start = (bf16[1,1,128,4096]{3,2,1,0:T(8,128)(2,1)S(1)}, bf16[1,1,128,4096]{3,2,1,0:T(8,128)(2,1)}, u32[]{:S(2)}) copy-start(bf16[1,1,128,4096]{3,2,1,0:T(8,128)(2,1)} %param.8) | copy-start | bytes 3145732
  0.6 19.1 %collective-permute-start.2 = (bf16[32,4096]{1,0:T(8,128)(2,1)}, bf16[32,4096]{1,0:T(8,128)(2,1)S(1)}, u32[]{:S(2)}, u32[]{:S(2)}) collective-permute-start(bf16[32,4096]{1,0:T(8,128)(2,1)} %bitcast.20), channel_id=1, source_target_pairs={{0,3},{1,0},{2,1},{3,2},{4,7},{5,4},{6,5},{7,6},{8,11},{9,8},{10,9... | collective-permute-start | bytes 786440 | tf_op jit(solution)/shard_map/ppermute | solution.py:176
  7.6 16.7 %collective-permute-start.1 = (bf16[32,4096]{1,0:T(8,128)(2,1)}, bf16[32,4096]{1,0:T(8,128)(2,1)S(1)}, u32[]{:S(2)}, u32[]{:S(2)}) collective-permute-start(bf16[32,4096]{1,0:T(8,128)(2,1)} %bitcast.21), channel_id=1, source_target_pairs={{0,2},{1,3},{2,0},{3,1},{4,6},{5,7},{6,4},{7,5},{8,10},{9,11},{10,... | collective-permute-start | bytes 786440 | tf_op jit(solution)/shard_map/ppermute | solution.py:176
  8.6 18.5 %collective-permute-start = (bf16[32,4096]{1,0:T(8,128)(2,1)}, bf16[32,4096]{1,0:T(8,128)(2,1)S(1)}, u32[]{:S(2)}, u32[]{:S(2)}) collective-permute-start(bf16[32,4096]{1,0:T(8,128)(2,1)} %bitcast.22), channel_id=1, source_target_pairs={{0,1},{1,2},{2,3},{3,0},{4,5},{5,6},{6,7},{7,4},{8,9},{9,10},{10,1... | collective-permute-start | bytes 786440 | tf_op jit(solution)/shard_map/ppermute | solution.py:176
  10.8 1.2 %copy-start.1 = (bf16[1,128,4096]{2,1,0:T(8,128)(2,1)S(1)}, bf16[1,128,4096]{2,1,0:T(8,128)(2,1)}, u32[]{:S(2)}) copy-start(bf16[1,128,4096]{2,1,0:T(8,128)(2,1)} %param.7) | copy-start | bytes 3145732
  12.0 0.8 copy-start.5
  12.8 14.3 %copy-start.6 = (bf16[1,128,128]{2,1,0:T(8,128)(2,1)S(1)}, bf16[1,128,128]{2,1,0:T(8,128)(2,1)}, u32[]{:S(2)}) copy-start(bf16[1,128,128]{2,1,0:T(8,128)(2,1)} %param.6) | copy-start | bytes 98308
  27.1 1.0 copy-start.3
  28.0 0.9 copy-start.7
  29.8 5.1 %collective-permute-start.3 = (f32[16,128]{1,0:T(8,128)S(1)}, f32[16,128]{1,0:T(8,128)S(1)}, u32[]{:S(2)}, u32[]{:S(2)}) collective-permute-start(f32[16,128]{1,0:T(8,128)S(1)} %get-tuple-element.38), channel_id=1, source_target_pairs={{0,4},{4,0},{1,5},{5,1},{2,6},{6,2},{3,7},{7,3},{8,12},{12,8},{9,1... | collective-permute-start | bytes 24584 | tf_op jit(solution)/shard_map/ppermute | solution.py:180
  35.7 18.7 %all-to-all-start = ((f32[32,16,128]{2,1,0:T(8,128)}), f32[32,16,128]{2,1,0:T(8,128)S(1)}, u32[]{:S(2)}, u32[]{:S(2)}) async-start(f32[32,16,128]{2,1,0:T(8,128)} %broadcast_in_dim.18), calls=%async_computation | async-start | bytes 524288 | tf_op jit(solution)/shard_map/all_to_all | solution.py:184
  45.4 23.2 %copy-start.4 = (bf16[1,32,4096]{2,1,0:T(8,128)(2,1)S(1)}, bf16[1,32,4096]{2,1,0:T(8,128)(2,1)}, u32[]{:S(2)}) copy-start(bf16[1,32,4096]{2,1,0:T(8,128)(2,1)} %param.5) | copy-start | bytes 786436
  45.5 14.3 %collective-permute-start.5 = (bf16[80,1024]{1,0:T(8,128)(2,1)S(1)}, bf16[80,1024]{1,0:T(8,128)(2,1)S(1)}, u32[]{:S(2)}, u32[]{:S(2)}) collective-permute-start(bf16[80,1024]{1,0:T(8,128)(2,1)S(1)} %get-tuple-element.39), channel_id=1, source_target_pairs={{0,1},{1,2},{2,3},{3,0},{4,5},{5,6},{6,7},{7,4},{8,9},{9,10},{10,1... | collective-permute-start | bytes 491528 | tf_op jit(solution)/shard_map/ppermute | solution.py:176
  47.7 16.5 %collective-permute-start.6 = (bf16[80,1024]{1,0:T(8,128)(2,1)S(1)}, bf16[80,1024]{1,0:T(8,128)(2,1)S(1)}, u32[]{:S(2)}, u32[]{:S(2)}) collective-permute-start(bf16[80,1024]{1,0:T(8,128)(2,1)S(1)} %get-tuple-element.40), channel_id=1, source_target_pairs={{0,2},{1,3},{2,0},{3,1},{4,6},{5,7},{6,4},{7,5},{8,10},{9,11},{10,... | collective-permute-start | bytes 491528 | tf_op jit(solution)/shard_map/ppermute | solution.py:176
  51.7 16.3 %collective-permute-start.7 = (bf16[80,1024]{1,0:T(8,128)(2,1)S(1)}, bf16[80,1024]{1,0:T(8,128)(2,1)S(1)}, u32[]{:S(2)}, u32[]{:S(2)}) collective-permute-start(bf16[80,1024]{1,0:T(8,128)(2,1)S(1)} %get-tuple-element.41), channel_id=1, source_target_pairs={{0,3},{1,0},{2,1},{3,2},{4,7},{5,4},{6,5},{7,6},{8,11},{9,8},{10,9... | collective-permute-start | bytes 491528 | tf_op jit(solution)/shard_map/ppermute | solution.py:176
  54.4 13.6 %collective-permute-start.4 = (f32[16,128]{1,0:T(8,128)S(1)}, f32[16,128]{1,0:T(8,128)S(1)}, u32[]{:S(2)}, u32[]{:S(2)}) collective-permute-start(f32[16,128]{1,0:T(8,128)S(1)} %reduce_sum.9.lown), channel_id=1, source_target_pairs={{0,4},{4,0},{1,5},{5,1},{2,6},{6,2},{3,7},{7,3},{8,12},{12,8},{9,1... | collective-permute-start | bytes 24584 | tf_op jit(solution)/shard_map/ppermute | solution.py:180
  59.8 8.2 %copy-start.8 = (bf16[80,1024]{1,0:T(8,128)(2,1)}, bf16[80,1024]{1,0:T(8,128)(2,1)S(1)}, u32[]{:S(2)}) copy-start(bf16[80,1024]{1,0:T(8,128)(2,1)S(1)} %collective-permute-done.5.r1) | copy-start | bytes 491524
  64.2 3.8 %copy-start.10 = (bf16[80,1024]{1,0:T(8,128)(2,1)}, bf16[80,1024]{1,0:T(8,128)(2,1)S(1)}, u32[]{:S(2)}) copy-start(bf16[80,1024]{1,0:T(8,128)(2,1)S(1)} %collective-permute-done.6.r2) | copy-start | bytes 491524
  68.0 0.7 copy-start.12
  72.4 11.8 %copy-start.2 = (bf16[1,128,4096]{2,1,0:T(8,128)(2,1)S(1)}, bf16[1,128,4096]{2,1,0:T(8,128)(2,1)}, u32[]{:S(2)}) copy-start(bf16[1,128,4096]{2,1,0:T(8,128)(2,1)} %param.7) | copy-start | bytes 3145732
  72.4 1.7 %collective-permute-start.8 = (f32[32,16,128]{2,1,0:T(8,128)S(1)}, f32[32,16,128]{2,1,0:T(8,128)S(1)}, u32[]{:S(2)}, u32[]{:S(2)}) collective-permute-start(f32[32,16,128]{2,1,0:T(8,128)S(1)} %get-tuple-element.44), channel_id=1, source_target_pairs={{0,4},{4,0},{1,5},{5,1},{2,6},{6,2},{3,7},{7,3},{8,12},{12,8},{9,1... | collective-permute-start | bytes 786440 | tf_op jit(solution)/shard_map/ppermute | solution.py:180
  74.8 14.9 %all-to-all-start.1 = ((f32[32,16,128]{2,1,0:T(8,128)}), f32[32,16,128]{2,1,0:T(8,128)S(1)}, u32[]{:S(2)}, u32[]{:S(2)}) async-start(f32[32,16,128]{2,1,0:T(8,128)} %add.7), calls=%async_computation.1 | async-start | bytes 524288 | tf_op jit(solution)/shard_map/all_to_all | solution.py:184
  81.6 2.0 %collective-permute-start.9 = (bf16[80,1024]{1,0:T(8,128)(2,1)}, bf16[80,1024]{1,0:T(8,128)(2,1)S(1)}, u32[]{:S(2)}, u32[]{:S(2)}) collective-permute-start(bf16[80,1024]{1,0:T(8,128)(2,1)} %copy-done.8), channel_id=1, source_target_pairs={{0,4},{4,0},{1,5},{5,1},{2,6},{6,2},{3,7},{7,3},{8,12},{12,8},{9,1... | collective-permute-start | bytes 491528 | tf_op jit(solution)/shard_map/ppermute | solution.py:180
  82.3 1.6 %collective-permute-start.10 = (bf16[80,1024]{1,0:T(8,128)(2,1)}, bf16[80,1024]{1,0:T(8,128)(2,1)S(1)}, u32[]{:S(2)}, u32[]{:S(2)}) collective-permute-start(bf16[80,1024]{1,0:T(8,128)(2,1)} %copy-done.10), channel_id=1, source_target_pairs={{0,4},{4,0},{1,5},{5,1},{2,6},{6,2},{3,7},{7,3},{8,12},{12,8},{9,1... | collective-permute-start | bytes 491528 | tf_op jit(solution)/shard_map/ppermute | solution.py:180
  82.4 1.7 %collective-permute-start.11 = (bf16[80,1024]{1,0:T(8,128)(2,1)}, bf16[80,1024]{1,0:T(8,128)(2,1)S(1)}, u32[]{:S(2)}, u32[]{:S(2)}) collective-permute-start(bf16[80,1024]{1,0:T(8,128)(2,1)} %copy-done.12), channel_id=1, source_target_pairs={{0,4},{4,0},{1,5},{5,1},{2,6},{6,2},{3,7},{7,3},{8,12},{12,8},{9,1... | collective-permute-start | bytes 491528 | tf_op jit(solution)/shard_map/ppermute | solution.py:180
  84.2 0.9 copy-start.9
  85.1 0.9 copy-start.11
  86.0 0.9 copy-start.13
  87.9 0.6 copy-start.15
  88.5 0.6 copy-start.17
  89.1 0.6 copy-start.19
  90.5 8.2 %copy-start.20 = (bf16[32,1024]{1,0:T(8,128)(2,1)S(1)}, bf16[32,1024]{1,0:T(8,128)(2,1)}, u32[]{:S(2)}) copy-start(bf16[32,1024]{1,0:T(8,128)(2,1)} %copy-done.19) | copy-start | bytes 196612
  90.5 10.7 %copy-start.18 = (bf16[32,1024]{1,0:T(8,128)(2,1)S(1)}, bf16[32,1024]{1,0:T(8,128)(2,1)}, u32[]{:S(2)}) copy-start(bf16[32,1024]{1,0:T(8,128)(2,1)} %copy-done.17) | copy-start | bytes 196612
  90.5 13.6 %copy-start.16 = (bf16[32,1024]{1,0:T(8,128)(2,1)S(1)}, bf16[32,1024]{1,0:T(8,128)(2,1)}, u32[]{:S(2)}) copy-start(bf16[32,1024]{1,0:T(8,128)(2,1)} %copy-done.15) | copy-start | bytes 196612
  90.5 23.4 %copy-start.14 = (f32[32,128]{1,0:T(8,128)S(1)}, f32[32,128]{1,0:T(8,128)}, u32[]{:S(2)}) copy-start(f32[32,128]{1,0:T(8,128)} %get-tuple-element.54.qt) | copy-start | bytes 49156
  90.5 19.6 %all-to-all-start.2 = ((f32[32,16,128]{2,1,0:T(8,128)}), f32[32,16,128]{2,1,0:T(8,128)S(1)}, u32[]{:S(2)}, u32[]{:S(2)}) async-start(f32[32,16,128]{2,1,0:T(8,128)} %shard_map.88), calls=%async_computation.2 | async-start | bytes 524288 | tf_op jit(solution)/shard_map/all_to_all | solution.py:184
  98.7 9.5 %collective-permute-start.12 = (bf16[32,1024]{1,0:T(8,128)(2,1)S(1)}, bf16[32,1024]{1,0:T(8,128)(2,1)S(1)}, u32[]{:S(2)}, u32[]{:S(2)}) collective-permute-start(bf16[32,1024]{1,0:T(8,128)(2,1)S(1)} %copy-done.20), channel_id=1, source_target_pairs={{0,1},{1,2},{2,3},{3,0},{4,5},{5,6},{6,7},{7,4},{8,9},{9,10},{10,1... | collective-permute-start | bytes 196616 | tf_op jit(solution)/shard_map/ppermute | solution.py:176
  101.2 8.9 %collective-permute-start.13 = (bf16[32,1024]{1,0:T(8,128)(2,1)S(1)}, bf16[32,1024]{1,0:T(8,128)(2,1)S(1)}, u32[]{:S(2)}, u32[]{:S(2)}) collective-permute-start(bf16[32,1024]{1,0:T(8,128)(2,1)S(1)} %copy-done.18), channel_id=1, source_target_pairs={{0,2},{1,3},{2,0},{3,1},{4,6},{5,7},{6,4},{7,5},{8,10},{9,11},{10,... | collective-permute-start | bytes 196616 | tf_op jit(solution)/shard_map/ppermute | solution.py:176
  104.2 6.0 %collective-permute-start.14 = (bf16[32,1024]{1,0:T(8,128)(2,1)S(1)}, bf16[32,1024]{1,0:T(8,128)(2,1)S(1)}, u32[]{:S(2)}, u32[]{:S(2)}) collective-permute-start(bf16[32,1024]{1,0:T(8,128)(2,1)S(1)} %copy-done.16), channel_id=1, source_target_pairs={{0,3},{1,0},{2,1},{3,2},{4,7},{5,4},{6,5},{7,6},{8,11},{9,8},{10,9... | collective-permute-start | bytes 196616 | tf_op jit(solution)/shard_map/ppermute | solution.py:176
  110.1 3.8 %collective-permute-start.15 = (f32[32,16,128]{2,1,0:T(8,128)S(1)}, f32[32,16,128]{2,1,0:T(8,128)S(1)}, u32[]{:S(2)}, u32[]{:S(2)}) collective-permute-start(f32[32,16,128]{2,1,0:T(8,128)S(1)} %all-to-all-done.2.rown), channel_id=1, source_target_pairs={{0,4},{4,0},{1,5},{5,1},{2,6},{6,2},{3,7},{7,3},{8,12},{12,8},{9,1... | collective-permute-start | bytes 786440 | tf_op jit(solution)/shard_map/ppermute | solution.py:180

commit v2 on v1

--- a/solution.py
+++ b/solution.py
@@ -22,6 +22,7 @@
 OWN = 32
 PART = WIDE // TENSOR
 N_CHIPS = REPLICAS // 2
+GROUP = 8
 STEP = 512
 NT = (((1,), (1,)), ((), ()))
 
@@ -61,39 +62,42 @@
     return run
 
 
-def pack_kernel(w, og, *sends):
+def early_kernel(w, og, a0, ef, warm, packed, inner, fed, lines):
     t, core = lax.axis_index("t"), lax.axis_index("core")
     rows = pl.ds(pl.multiple_of(core * 64, 64), 64)
-    for k, send in enumerate(sends, 1):
-        target = lax.rem(t + k, TENSOR)
-        send[0:64, :] = w[rows, pl.ds(pl.multiple_of(target * PART, PART), PART)]
+    for target in range(TENSOR):
+        packed[target, 0:64, :] = w[rows, target * PART : target * PART + PART]
         for m in range(8):
-            send[64:80, 128 * m : 128 * m + 128] = og[16 * m : 16 * m + 16, :]
-
-
-def left_kernel(a0, a1, a2, a3, og, ef, warm, keep, send, held):
-    t, core = lax.axis_index("t"), lax.axis_index("core")
-    lines = warm[...]
+            packed[target, 64:80, 128 * m : 128 * m + 128] = og[16 * m : 16 * m + 16, :]
+    lines[...] = warm[...]
+    inner[...] = lax.dot_general(warm[...], a0[...], NT, preferred_element_type=F32)
+    fed[...] = lax.dot_general(warm[...], ef[...], NT, preferred_element_type=F32)
+
+
+def left_kernel(a1, a2, a3, og, lines, inner0, fed, out):
+    t = lax.axis_index("t")
     ogp = turned(og, t)
-    inner = jnp.concatenate(
-        [lax.dot_general(lines, a[...], NT, preferred_element_type=F32) for a in (a0, a1, a2, a3)],
-        axis=1,
-    )
-    parts = jnp.concatenate(split3(inner), axis=0)
-    prod = jnp.dot(parts, ogp, preferred_element_type=F32)
-    fed = lax.dot_general(lines, ef[...], NT, preferred_element_type=F32)
-    held[...] = prod[0:RANK] + prod[RANK : 2 * RANK] + prod[2 * RANK :] + fed
-    keep[...] = held[pl.ds(pl.multiple_of(core * HALF, HALF), HALF), :]
-    send[...] = held[pl.ds(pl.multiple_of((1 - core) * HALF, HALF), HALF), :]
-
-
-def basis_kernel(lown, loth, a0, a1, a2, a3, og, ef, qt, keep, send, held, heldo):
+    rest = [
+        lax.dot_general(lines[...], a[...], NT, preferred_element_type=F32) for a in (a1, a2, a3)
+    ]
+    inner = jnp.concatenate([inner0[...]] + rest, axis=1)
+    prod = jnp.dot(jnp.concatenate(split3(inner), axis=0), ogp, preferred_element_type=F32)
+    left = prod[0:RANK] + prod[RANK : 2 * RANK] + prod[2 * RANK :] + fed[...]
+    for k in range(GROUP):
+        out[k] = left
+
+
+def add_kernel(pieces, out):
+    total = jnp.sum(pieces[...], axis=0)
+    for k in range(GROUP):
+        out[k] = total
+
+
+def basis_kernel(lefts, a0, a1, a2, a3, og, ef, qt, keep, send, held, heldo):
     t, core = lax.axis_index("t"), lax.axis_index("core")
     mine = pl.ds(pl.multiple_of(core * HALF, HALF), HALF)
     other = pl.ds(pl.multiple_of((1 - core) * HALF, HALF), HALF)
-    held[mine, :] = lown[...]
-    held[other, :] = loth[...]
-    left = held[...]
+    left = jnp.sum(lefts[...], axis=0)
     gram = lax.dot_general(left, left, NT, precision=HIGH, preferred_element_type=F32)
     row = lax.broadcasted_iota(jnp.int32, (RANK, 1), 0)
     for k in range(RANK - 1):
@@ -133,13 +137,12 @@
     out[...] = jnp.broadcast_to(total[None], out.shape)
 
 
-def finish_kernel(rown, roth, qt, og, a0, a1, a2, a3, ef, i0, i1, i2, i3, err, fac, igrad, held):
+def finish_kernel(rown, roth, qt, og, a0, a1, a2, a3, ef, parts, err, fac, igrad):
     t, core = lax.axis_index("t"), lax.axis_index("core")
     mine = pl.ds(pl.multiple_of(core * HALF, HALF), HALF)
     other = pl.ds(pl.multiple_of((1 - core) * HALF, HALF), HALF)
-    for k, block in enumerate((i0, i1, i2, i3)):
-        source = lax.rem(t - k + TENSOR, TENSOR)
-        igrad[:, pl.ds(pl.multiple_of(source * PART, PART), PART)] = block[...]
+    for source in range(TENSOR):
+        igrad[:, source * PART : source * PART + PART] = parts[source]
     q = jnp.concatenate([qt[mine, :], qt[other, :]], axis=0)
     hi, mid = split2(q)
     hi, mid = hi.astype(F32), mid.astype(F32)
@@ -157,19 +160,18 @@
         err[:, cols] = total.astype(BF16)
 
 
-def input_kernel(w, og, r1, r2, r3, e1, e2, e3, o0, o1, o2, o3, weights, feats):
-    t, core = lax.axis_index("t"), lax.axis_index("core")
-    weights[0:128, :] = w[:, pl.ds(pl.multiple_of(t * PART, PART), PART)]
-    feats[:, 0:128] = og[...]
-    for k, (r, e) in enumerate(((r1, e1), (r2, e2), (r3, e3)), 1):
-        weights[pl.ds(pl.multiple_of(128 * k + 64 * core, 64), 64), :] = r[0:64, :]
-        weights[pl.ds(pl.multiple_of(128 * k + 64 * (1 - core), 64), 64), :] = e[0:64, :]
+def input_kernel(got, traded, outs, weights, feats):
+    core = lax.axis_index("core")
+    for k in range(TENSOR):
+        weights[pl.ds(pl.multiple_of(128 * k + 64 * core, 64), 64), :] = got[k, 0:64, :]
+        weights[pl.ds(pl.multiple_of(128 * k + 64 * (1 - core), 64), 64), :] = traded[k, 0:64, :]
         for m in range(8):
-            feats[16 * m : 16 * m + 16, 128 * k : 128 * k + 128] = r[64:80, 128 * m : 128 * m + 128]
-    for k, out in enumerate((o0, o1, o2, o3)):
-        target = lax.rem(t + k, TENSOR)
-        rows = feats[pl.ds(pl.multiple_of(target * OWN, OWN), OWN), :]
-        out[...] = jnp.dot(rows, weights[...], preferred_element_type=F32).astype(BF16)
+            feats[16 * m : 16 * m + 16, 128 * k : 128 * k + 128] = got[
+                k, 64:80, 128 * m : 128 * m + 128
+            ]
+    total = jnp.dot(feats[...], weights[...], preferred_element_type=F32).astype(BF16)
+    for k in range(TENSOR):
+        outs[k] = total[OWN * k : OWN * k + OWN]
 
 
 def moved(x, k):
@@ -180,8 +182,8 @@
     return lax.ppermute(x, "core", [(0, 1), (1, 0)])
 
 
-def exchanged(x):
-    return lax.all_to_all(x, CHIPS, 0, 0, tiled=True)
+def exchanged(x, axes):
+    return lax.all_to_all(x, axes, 0, 0, tiled=True)
 
 
 def local(activations, out_grad, value_weight, error_feedback, warm_right):
@@ -190,24 +192,27 @@
     warm = warm_right[0, 0].T
 
     acts = [act] + [moved(act, k) for k in (1, 2, 3)]
-    packed = ((OWN * 2 + 16, PART), BF16)
-    sends = call(pack_kernel, [packed] * 3)(weight, og)
-
-    half = ((HALF, HEAD), F32)
-    left_keep, left_send = call(
-        left_kernel, [half, half], [pltpu.VMEM((RANK, HEAD), F32)], flops=10**8, moved=3 * 10**6
-    )(*acts, og, ef, warm)
-
-    sends, left_send = lax.optimization_barrier((sends, left_send))
-    got = [moved(s, k) for k, s in zip((1, 2, 3), sends)]
-
-    left_half = left_keep + swapped(left_send)
-    pieces = exchanged(jnp.broadcast_to(left_half[None], (N_CHIPS, HALF, HEAD)))
-    left_own = jnp.sum(pieces, axis=0)
-    left_other = swapped(left_own)
-    left_other, got = lax.optimization_barrier((left_other, got))
-
-    traded = [swapped(g) for g in got]
+    packed, inner, fed, lines = call(
+        early_kernel,
+        [
+            ((TENSOR, OWN * 2 + 16, PART), BF16),
+            ((RANK, OWN), F32),
+            ((RANK, HEAD), F32),
+            ((RANK, WIDE), BF16),
+        ],
+        flops=5 * 10**7,
+        moved=4 * 10**6,
+    )(weight, og, act, ef, warm)
+
+    group = ((GROUP, RANK, HEAD), F32)
+    (left,) = call(left_kernel, [group], flops=5 * 10**7, moved=10**6)(
+        *acts[1:], og, lines, inner, fed
+    )
+    left, packed = lax.optimization_barrier((left, packed))
+    got = exchanged(packed, "t")
+    (left,) = call(add_kernel, [group])(exchanged(left, ("y", "core")))
+    left = exchanged(left, ("x", "zl"))
+
     block = ((N_CHIPS, HALF, 128), F32)
     basis, right_keep, right_send = call(
         basis_kernel,
@@ -215,31 +220,31 @@
         [pltpu.VMEM((RANK, HEAD), F32), pltpu.VMEM((RANK, HEAD), F32)],
         flops=10**8,
         moved=3 * 10**6,
-    )(left_own, left_other, *acts, og, ef)
-
-    outs = call(
+    )(left, *acts, og, ef)
+
+    pieces = exchanged(right_keep + swapped(right_send), CHIPS)
+    pieces, got = lax.optimization_barrier((pieces, got))
+    (mean,) = call(spread_kernel, [block])(pieces)
+
+    (outs,) = call(
         input_kernel,
-        [((OWN, PART), BF16)] * 4,
+        [((TENSOR, OWN, PART), BF16)],
         [pltpu.VMEM((512, PART), BF16), pltpu.VMEM((128, 512), BF16)],
         flops=2 * 10**8,
         moved=2 * 10**6,
-    )(weight, og, *got, *traded)
-    inputs = [outs[0]] + [moved(o, k) for k, o in zip((1, 2, 3), outs[1:])]
-
-    pieces = exchanged(right_keep + swapped(right_send))
-    pieces, outs = lax.optimization_barrier((pieces, outs))
-    (mean,) = call(spread_kernel, [block])(pieces)
-    right_own = exchanged(mean)
-    right_own, inputs = lax.optimization_barrier((right_own, inputs))
+    )(got, swapped(got))
+    mean, outs = lax.optimization_barrier((mean, outs))
+    inputs = exchanged(outs, "t")
+
+    right_own = exchanged(mean, CHIPS)
     right_other = swapped(right_own)
 
     err, fac, igrad = call(
         finish_kernel,
         [((HEAD, WIDE), BF16), ((RANK, WIDE), BF16), ((OWN, WIDE), BF16)],
-        [pltpu.VMEM((RANK, HEAD), F32)],
         flops=3 * 10**8,
         moved=5 * 10**6,
-    )(right_own, right_other, basis, og, *acts, ef, *inputs)
+    )(right_own, right_other, basis, og, *acts, ef, inputs)
 
     return (err[None, None], basis.T[None], fac.T[None, None], igrad[None])
 

time: 116 us -> 123 us (1.060)
  the two profiles are of different devices: /device:TPU:1 before, /device:TPU:8 now
where the time goes in v2:
time: 123 us
  blocking collectives  50.4 us (41%)
  waiting for transfers between devices  37.4 us (30%)
  starting transfers between devices  20.8 us (17%)
  Pallas kernels  8.36 us (7%)
  local copies, waits for them, and re-layouts  5.12 us (4%)
    all_to_all x4, blocking collectives, exchanged(): return lax.all_to_all(x, axes, 0, 0, tiled=True)  50.4 us
    all_to_all x2, waiting for transfers between devices, exchanged(): return lax.all_to_all(x, axes, 0, 0, tiled=True)  21.3 us
    ppermute x3, waiting for transfers between devices, moved(): return lax.ppermute(x, 't', [(i, (i + k) % TENSOR) for i in range(TENSOR)])  12.6 us
    all_to_all x2, starting transfers between devices, exchanged(): return lax.all_to_all(x, axes, 0, 0, tiled=True)  10.5 us
    ppermute x3, starting transfers between devices, moved(): return lax.ppermute(x, 't', [(i, (i + k) % TENSOR) for i in range(TENSOR)])  10.2 us
    pallas_call x7, Pallas kernels, run(): pl.pallas_call(kernel, out_shape=[jax.ShapeDtypeStruct(s, d) for s, d in...  8.36 us
    unnamed x18, local copies, waits for them, and re-layouts  5.12 us
    ppermute x3, waiting for transfers between devices, swapped(): return lax.ppermute(x, 'core', [(0, 1), (1, 0)])  3.57 us
  transfers between devices with their start and end apart: 8, of which 5 were waited for; matrix products, arithmetic and copies ran while one was open for 0% of the time, Pallas kernels for 4%

profile of v2, /device:TPU:8, one launch (start us, length us, event | category | flops | bytes accessed | tf_op | source)
XLA Modules:
  0.0 122.8 jit_solution(1694792197900341653)
XLA Ops:
  0.6 6.4 %collective-permute-start.2 = (bf16[32,4096]{1,0:T(8,128)(2,1)}, bf16[32,4096]{1,0:T(8,128)(2,1)S(1)}, u32[]{:S(2)}, u32[]{:S(2)}) collective-permute-start(bf16[32,4096]{1,0:T(8,128)(2,1)} %bitcast.18), channel_id=1, source_target_pairs={{0,3},{1,0},{2,1},{3,2},{4,7},{5,4},{6,5},{7,6},{8,11},{9,8},{10,9... | collective-permute-start | bytes 786440 | tf_op jit(solution)/shard_map/ppermute | solution.py:178
  7.0 1.0 collective-permute-start.1
  8.0 2.8 %collective-permute-start = (bf16[32,4096]{1,0:T(8,128)(2,1)}, bf16[32,4096]{1,0:T(8,128)(2,1)S(1)}, u32[]{:S(2)}, u32[]{:S(2)}) collective-permute-start(bf16[32,4096]{1,0:T(8,128)(2,1)} %bitcast.20), channel_id=1, source_target_pairs={{0,1},{1,2},{2,3},{3,0},{4,5},{5,6},{6,7},{7,4},{8,9},{9,10},{10,1... | collective-permute-start | bytes 786440 | tf_op jit(solution)/shard_map/ppermute | solution.py:178
  10.8 0.0 copy-start
  10.8 1.2 copy-done
  12.0 0.0 copy-start.2
  12.1 0.9 copy-done.2
  13.0 0.0 copy-start.4
  13.0 1.2 copy-done.4
  14.2 0.0 copy-start.5
  14.2 0.8 copy-done.5
  15.0 0.0 copy-start.7
  15.0 0.9 copy-done.7
  15.9 1.3 %shard_map.84 = (bf16[4,80,1024]{2,1,0:T(8,128)(2,1)}, f32[32,32]{1,0:T(8,128)S(1)}, f32[32,128]{1,0:T(8,128)S(1)}, bf16[32,4096]{1,0:T(8,128)(2,1)S(1)}) custom-call(bf16[128,4096]{1,0:T(8,128)(2,1)S(1)} %bitcast.24, bf16[128,128]{1,0:T(8,128)(2,1)S(1)} %bitcast.25, bf16[32,4096]{1,0:T(8,128)(2,1)S(1)} %bitcast.21, bf16[128,4096]{1,0:T(8,128)(2,1)S(1)} %bitcast.15, ...), custom_call_target="tpu_custom_call" | custom-call | flops 50000000 | bytes 4000000 | tf_op jit(solution)/shard_map/pallas_call | solution.py:52
  17.2 12.6 %collective-permute-done.2.a3 = bf16[32,4096]{1,0:T(8,128)(2,1)S(1)} collective-permute-done((bf16[32,4096]{1,0:T(8,128)(2,1)}, bf16[32,4096]{1,0:T(8,128)(2,1)S(1)}, u32[]{:S(2)}, u32[]{:S(2)}) %collective-permute-start.2) | collective-permute-done | bytes 262176 | tf_op jit(solution)/shard_map/ppermute | solution.py:178
  29.8 0.0 collective-permute-done.1.a2
  29.8 0.0 collective-permute-done.a1
  29.8 0.6 shard_map.85
  30.3 0.0 copy-start.1
  30.4 9.5 %all_to_all.30.pieces = f32[8,32,128]{2,1,0:T(8,128)S(1)} all-to-all(f32[8,32,128]{2,1,0:T(8,128)S(1)} %shard_map.85), channel_id=1, replica_groups=mesh['x'=4,'zl'=2,'y'=4,'core'=2,'t'=4] {'y','core'}, dimensions={0} | all-to-all | bytes 262144 | tf_op jit(solution)/shard_map/all_to_all | solution.py:186
  39.9 13.5 %all_to_all.31.lefts = f32[8,32,128]{2,1,0:T(8,128)S(1)} all-to-all(f32[8,32,128]{2,1,0:T(8,128)S(1)} %shard_map.86), channel_id=1, replica_groups=mesh['x'=4,'zl'=2,'y'=4,'core'=2,'t'=4] {'x','zl'}, dimensions={0} | all-to-all | bytes 262144 | tf_op jit(solution)/shard_map/all_to_all | solution.py:186
  53.4 0.0 copy-start.3
  53.4 0.0 copy-start.6
  53.4 6.9 %all-to-all-start.3 = ((bf16[4,80,1024]{2,1,0:T(8,128)(2,1)}), bf16[4,80,1024]{2,1,0:T(8,128)(2,1)S(1)}, u32[]{:S(2)}, u32[]{:S(2)}) async-start(bf16[4,80,1024]{2,1,0:T(8,128)(2,1)} %get-tuple-element.27), calls=%async_computation.3 | async-start | bytes 1310720 | tf_op jit(solution)/shard_map/all_to_all | solution.py:186
  60.4 0.0 copy-done.1
  60.4 0.0 copy-done.3
  60.4 0.0 copy-done.6
  60.4 3.8 %shard_map.87 = (f32[32,128]{1,0:T(8,128)}, f32[32,16,128]{2,1,0:T(8,128)S(1)}, f32[32,16,128]{2,1,0:T(8,128)S(1)}) custom-call(f32[8,32,128]{2,1,0:T(8,128)S(1)} %all_to_all.31.lefts, bf16[32,4096]{1,0:T(8,128)(2,1)S(1)} %bitcast.22, bf16[32,4096]{1,0:T(8,128)(2,1)S(1)} %collective-permute-done.a1, bf16[32,4096]{1,0:T(8,128)(2,1)S(1)} %collective-permute-done.1.a2, ...), custom_call_target="tpu_custom_call" | custom-call | flops 100000000 | bytes 3000000 | tf_op jit(solution)/shard_map/pallas_call | solution.py:52
  64.1 0.0 collective-permute-start.3
  64.2 1.5 %collective-permute-done.3 = f32[32,16,128]{2,1,0:T(8,128)S(1)} collective-permute-done((f32[32,16,128]{2,1,0:T(8,128)S(1)}, f32[32,16,128]{2,1,0:T(8,128)S(1)}, u32[]{:S(2)}, u32[]{:S(2)}) %collective-permute-start.3) | collective-permute-done | bytes 262176 | tf_op jit(solution)/shard_map/ppermute | solution.py:182
  65.7 10.9 %all-to-all-done.3.got = bf16[4,80,1024]{2,1,0:T(8,128)(2,1)S(1)} async-done(((bf16[4,80,1024]{2,1,0:T(8,128)(2,1)}), bf16[4,80,1024]{2,1,0:T(8,128)(2,1)S(1)}, u32[]{:S(2)}, u32[]{:S(2)}) %all-to-all-start.3) | async-done | bytes 655392 | tf_op jit(solution)/shard_map/all_to_all | solution.py:186
  76.6 14.3 %all_to_all.32.pieces = f32[32,16,128]{2,1,0:T(8,128)S(1)} all-to-all(f32[32,16,128]{2,1,0:T(8,128)S(1)} %add.3), channel_id=1, replica_groups=mesh['x'=4,'zl'=2,'y'=4,'core'=2,'t'=4] {'x','zl','y'}, dimensions={0} | all-to-all | bytes 524288 | tf_op jit(solution)/shard_map/all_to_all | solution.py:186
  91.0 0.0 collective-permute-start.4
  91.0 0.1 shard_map.88
  91.0 2.0 %collective-permute-done.4.traded = bf16[4,80,1024]{2,1,0:T(8,128)(2,1)S(1)} collective-permute-done((bf16[4,80,1024]{2,1,0:T(8,128)(2,1)S(1)}, bf16[4,80,1024]{2,1,0:T(8,128)(2,1)S(1)}, u32[]{:S(2)}, u32[]{:S(2)}) %collective-permute-start.4) | collective-permute-done | bytes 655392 | tf_op jit(solution)/shard_map/ppermute | solution.py:182
  93.1 1.2 shard_map.89
  94.2 13.0 %all_to_all.33.rown = f32[32,16,128]{2,1,0:T(8,128)S(1)} all-to-all(f32[32,16,128]{2,1,0:T(8,128)S(1)} %shard_map.88), channel_id=1, replica_groups=mesh['x'=4,'zl'=2,'y'=4,'core'=2,'t'=4] {'x','zl','y'}, dimensions={0} | all-to-all | bytes 524288 | tf_op jit(solution)/shard_map/all_to_all | solution.py:186
  107.3 0.0 copy-start.8
  107.3 3.5 %all-to-all-start.5 = ((bf16[4,32,1024]{2,1,0:T(8,128)(2,1)}), bf16[4,32,1024]{2,1,0:T(8,128)(2,1)S(1)}, u32[]{:S(2)}, u32[]{:S(2)}) async-start(bf16[4,32,1024]{2,1,0:T(8,128)(2,1)} %shard_map.89), calls=%async_computation.5 | async-start | bytes 524288 | tf_op jit(solution)/shard_map/all_to_all | solution.py:186
  110.8 0.1 collective-permute-start.5
  110.9 10.3 %all-to-all-done.5.parts = bf16[4,32,1024]{2,1,0:T(8,128)(2,1)S(1)} async-done(((bf16[4,32,1024]{2,1,0:T(8,128)(2,1)}), bf16[4,32,1024]{2,1,0:T(8,128)(2,1)S(1)}, u32[]{:S(2)}, u32[]{:S(2)}) %all-to-all-start.5) | async-done | bytes 262176 | tf_op jit(solution)/shard_map/all_to_all | solution.py:186
  121.3 0.0 collective-permute-done.5.roth
  121.3 0.0 copy-done.8
  121.3 1.5 %shard_map.90 = (bf16[128,4096]{1,0:T(8,128)(2,1)}, bf16[32,4096]{1,0:T(8,128)(2,1)}, bf16[32,4096]{1,0:T(8,128)(2,1)}) custom-call(f32[32,16,128]{2,1,0:T(8,128)S(1)} %all_to_all.33.rown, f32[32,16,128]{2,1,0:T(8,128)S(1)} %collective-permute-done.5.roth, f32[32,128]{1,0:T(8,128)S(1)} %copy-done.8, bf16[128,128]{1,0:T(8,128)(2,1)S(1)} %bitcast.28, ...), custom_call_target="tpu_custom_call" | custom-call | flops 300000000 | bytes 5000000 | tf_op jit(solution)/shard_map/pallas_call | solution.py:52
  (2 shorter events, 0.1 us)
Async XLA Ops:
  0.6 29.1 %collective-permute-start.2 = (bf16[32,4096]{1,0:T(8,128)(2,1)}, bf16[32,4096]{1,0:T(8,128)(2,1)S(1)}, u32[]{:S(2)}, u32[]{:S(2)}) collective-permute-start(bf16[32,4096]{1,0:T(8,128)(2,1)} %bitcast.18), channel_id=1, source_target_pairs={{0,3},{1,0},{2,1},{3,2},{4,7},{5,4},{6,5},{7,6},{8,11},{9,8},{10,9... | collective-permute-start | bytes 786440 | tf_op jit(solution)/shard_map/ppermute | solution.py:178
  7.0 22.8 %collective-permute-start.1 = (bf16[32,4096]{1,0:T(8,128)(2,1)}, bf16[32,4096]{1,0:T(8,128)(2,1)S(1)}, u32[]{:S(2)}, u32[]{:S(2)}) collective-permute-start(bf16[32,4096]{1,0:T(8,128)(2,1)} %bitcast.19), channel_id=1, source_target_pairs={{0,2},{1,3},{2,0},{3,1},{4,6},{5,7},{6,4},{7,5},{8,10},{9,11},{10,... | collective-permute-start | bytes 786440 | tf_op jit(solution)/shard_map/ppermute | solution.py:178
  8.0 21.8 %collective-permute-start = (bf16[32,4096]{1,0:T(8,128)(2,1)}, bf16[32,4096]{1,0:T(8,128)(2,1)S(1)}, u32[]{:S(2)}, u32[]{:S(2)}) collective-permute-start(bf16[32,4096]{1,0:T(8,128)(2,1)} %bitcast.20), channel_id=1, source_target_pairs={{0,1},{1,2},{2,3},{3,0},{4,5},{5,6},{6,7},{7,4},{8,9},{9,10},{10,1... | collective-permute-start | bytes 786440 | tf_op jit(solution)/shard_map/ppermute | solution.py:178
  10.8 1.2 copy-start
  12.0 0.9 copy-start.2
  13.0 1.2 copy-start.4
  14.2 0.8 copy-start.5
  15.0 0.9 copy-start.7
  30.3 30.0 %copy-start.1 = (bf16[1,1,128,4096]{3,2,1,0:T(8,128)(2,1)S(1)}, bf16[1,1,128,4096]{3,2,1,0:T(8,128)(2,1)}, u32[]{:S(2)}) copy-start(bf16[1,1,128,4096]{3,2,1,0:T(8,128)(2,1)} %param.8) | copy-start | bytes 3145732
  53.4 6.9 %copy-start.3 = (bf16[1,32,4096]{2,1,0:T(8,128)(2,1)S(1)}, bf16[1,32,4096]{2,1,0:T(8,128)(2,1)}, u32[]{:S(2)}) copy-start(bf16[1,32,4096]{2,1,0:T(8,128)(2,1)} %param.5) | copy-start | bytes 786436
  53.4 6.9 %copy-start.6 = (bf16[1,128,128]{2,1,0:T(8,128)(2,1)S(1)}, bf16[1,128,128]{2,1,0:T(8,128)(2,1)}, u32[]{:S(2)}) copy-start(bf16[1,128,128]{2,1,0:T(8,128)(2,1)} %param.6) | copy-start | bytes 98308
  53.4 23.2 %all-to-all-start.3 = ((bf16[4,80,1024]{2,1,0:T(8,128)(2,1)}), bf16[4,80,1024]{2,1,0:T(8,128)(2,1)S(1)}, u32[]{:S(2)}, u32[]{:S(2)}) async-start(bf16[4,80,1024]{2,1,0:T(8,128)(2,1)} %get-tuple-element.27), calls=%async_computation.3 | async-start | bytes 1310720 | tf_op jit(solution)/shard_map/all_to_all | solution.py:186
  64.1 1.5 %collective-permute-start.3 = (f32[32,16,128]{2,1,0:T(8,128)S(1)}, f32[32,16,128]{2,1,0:T(8,128)S(1)}, u32[]{:S(2)}, u32[]{:S(2)}) collective-permute-start(f32[32,16,128]{2,1,0:T(8,128)S(1)} %get-tuple-element.26), channel_id=1, source_target_pairs={{0,4},{4,0},{1,5},{5,1},{2,6},{6,2},{3,7},{7,3},{8,12},{12,8},{9,1... | collective-permute-start | bytes 786440 | tf_op jit(solution)/shard_map/ppermute | solution.py:182
  91.0 2.1 %collective-permute-start.4 = (bf16[4,80,1024]{2,1,0:T(8,128)(2,1)S(1)}, bf16[4,80,1024]{2,1,0:T(8,128)(2,1)S(1)}, u32[]{:S(2)}, u32[]{:S(2)}) collective-permute-start(bf16[4,80,1024]{2,1,0:T(8,128)(2,1)S(1)} %all-to-all-done.3.got), channel_id=1, source_target_pairs={{0,4},{4,0},{1,5},{5,1},{2,6},{6,2},{3,7},{7,3},{8,12},{12,8},{9,1... | collective-permute-start | bytes 1966088 | tf_op jit(solution)/shard_map/ppermute | solution.py:182
  107.3 14.0 %copy-start.8 = (f32[32,128]{1,0:T(8,128)S(1)}, f32[32,128]{1,0:T(8,128)}, u32[]{:S(2)}) copy-start(f32[32,128]{1,0:T(8,128)} %get-tuple-element.31.qt) | copy-start | bytes 49156
  107.3 14.0 %all-to-all-start.5 = ((bf16[4,32,1024]{2,1,0:T(8,128)(2,1)}), bf16[4,32,1024]{2,1,0:T(8,128)(2,1)S(1)}, u32[]{:S(2)}, u32[]{:S(2)}) async-start(bf16[4,32,1024]{2,1,0:T(8,128)(2,1)} %shard_map.89), calls=%async_computation.5 | async-start | bytes 524288 | tf_op jit(solution)/shard_map/all_to_all | solution.py:186
  110.8 10.4 %collective-permute-start.5 = (f32[32,16,128]{2,1,0:T(8,128)S(1)}, f32[32,16,128]{2,1,0:T(8,128)S(1)}, u32[]{:S(2)}, u32[]{:S(2)}) collective-permute-start(f32[32,16,128]{2,1,0:T(8,128)S(1)} %all_to_all.33.rown), channel_id=1, source_target_pairs={{0,4},{4,0},{1,5},{5,1},{2,6},{6,2},{3,7},{7,3},{8,12},{12,8},{9,1... | collective-permute-start | bytes 786440 | tf_op jit(solution)/shard_map/ppermute | solution.py:182

commit v3 on v1

--- a/solution.py
+++ b/solution.py
@@ -20,7 +20,6 @@
 RANK = 32
 HALF = RANK // 2
 OWN = 32
-PART = WIDE // TENSOR
 N_CHIPS = REPLICAS // 2
 STEP = 512
 NT = (((1,), (1,)), ((), ()))
@@ -61,28 +60,29 @@
     return run
 
 
-def pack_kernel(w, og, *sends):
+def early_kernel(w, og, a0, ef, warm, p0, p1, p2, p3, inner, fed, lines):
+    t = lax.axis_index("t")
+    lines[...] = warm[...]
+    inner[...] = lax.dot_general(warm[...], a0[...], NT, preferred_element_type=F32)
+    fed[...] = lax.dot_general(warm[...], ef[...], NT, preferred_element_type=F32)
+    targets = jnp.concatenate(
+        [og[pl.ds(lax.rem(t + k, TENSOR) * OWN, OWN), :] for k in range(TENSOR)], axis=0
+    )
+    for c in range(0, WIDE, STEP):
+        share = jnp.dot(targets, w[:, c : c + STEP], preferred_element_type=F32)
+        for k, out in enumerate((p0, p1, p2, p3)):
+            out[:, c : c + STEP] = share[OWN * k : OWN * k + OWN]
+
+
+def left_kernel(a1, a2, a3, og, lines, inner0, fed, keep, send, held):
     t, core = lax.axis_index("t"), lax.axis_index("core")
-    rows = pl.ds(pl.multiple_of(core * 64, 64), 64)
-    for k, send in enumerate(sends, 1):
-        target = lax.rem(t + k, TENSOR)
-        send[0:64, :] = w[rows, pl.ds(pl.multiple_of(target * PART, PART), PART)]
-        for m in range(8):
-            send[64:80, 128 * m : 128 * m + 128] = og[16 * m : 16 * m + 16, :]
-
-
-def left_kernel(a0, a1, a2, a3, og, ef, warm, keep, send, held):
-    t, core = lax.axis_index("t"), lax.axis_index("core")
-    lines = warm[...]
     ogp = turned(og, t)
-    inner = jnp.concatenate(
-        [lax.dot_general(lines, a[...], NT, preferred_element_type=F32) for a in (a0, a1, a2, a3)],
-        axis=1,
-    )
-    parts = jnp.concatenate(split3(inner), axis=0)
-    prod = jnp.dot(parts, ogp, preferred_element_type=F32)
-    fed = lax.dot_general(lines, ef[...], NT, preferred_element_type=F32)
-    held[...] = prod[0:RANK] + prod[RANK : 2 * RANK] + prod[2 * RANK :] + fed
+    rest = [
+        lax.dot_general(lines[...], a[...], NT, preferred_element_type=F32) for a in (a1, a2, a3)
+    ]
+    inner = jnp.concatenate([inner0[...]] + rest, axis=1)
+    prod = jnp.dot(jnp.concatenate(split3(inner), axis=0), ogp, preferred_element_type=F32)
+    held[...] = prod[0:RANK] + prod[RANK : 2 * RANK] + prod[2 * RANK :] + fed[...]
     keep[...] = held[pl.ds(pl.multiple_of(core * HALF, HALF), HALF), :]
     send[...] = held[pl.ds(pl.multiple_of((1 - core) * HALF, HALF), HALF), :]
 
@@ -133,13 +133,10 @@
     out[...] = jnp.broadcast_to(total[None], out.shape)
 
 
-def finish_kernel(rown, roth, qt, og, a0, a1, a2, a3, ef, i0, i1, i2, i3, err, fac, igrad, held):
+def finish_kernel(rown, roth, qt, og, a0, a1, a2, a3, ef, err, fac):
     t, core = lax.axis_index("t"), lax.axis_index("core")
     mine = pl.ds(pl.multiple_of(core * HALF, HALF), HALF)
     other = pl.ds(pl.multiple_of((1 - core) * HALF, HALF), HALF)
-    for k, block in enumerate((i0, i1, i2, i3)):
-        source = lax.rem(t - k + TENSOR, TENSOR)
-        igrad[:, pl.ds(pl.multiple_of(source * PART, PART), PART)] = block[...]
     q = jnp.concatenate([qt[mine, :], qt[other, :]], axis=0)
     hi, mid = split2(q)
     hi, mid = hi.astype(F32), mid.astype(F32)
@@ -157,21 +154,6 @@
         err[:, cols] = total.astype(BF16)
 
 
-def input_kernel(w, og, r1, r2, r3, e1, e2, e3, o0, o1, o2, o3, weights, feats):
-    t, core = lax.axis_index("t"), lax.axis_index("core")
-    weights[0:128, :] = w[:, pl.ds(pl.multiple_of(t * PART, PART), PART)]
-    feats[:, 0:128] = og[...]
-    for k, (r, e) in enumerate(((r1, e1), (r2, e2), (r3, e3)), 1):
-        weights[pl.ds(pl.multiple_of(128 * k + 64 * core, 64), 64), :] = r[0:64, :]
-        weights[pl.ds(pl.multiple_of(128 * k + 64 * (1 - core), 64), 64), :] = e[0:64, :]
-        for m in range(8):
-            feats[16 * m : 16 * m + 16, 128 * k : 128 * k + 128] = r[64:80, 128 * m : 128 * m + 128]
-    for k, out in enumerate((o0, o1, o2, o3)):
-        target = lax.rem(t + k, TENSOR)
-        rows = feats[pl.ds(pl.multiple_of(target * OWN, OWN), OWN), :]
-        out[...] = jnp.dot(rows, weights[...], preferred_element_type=F32).astype(BF16)
-
-
 def moved(x, k):
     return lax.ppermute(x, "t", [(i, (i + k) % TENSOR) for i in range(TENSOR)])
 
@@ -180,8 +162,8 @@
     return lax.ppermute(x, "core", [(0, 1), (1, 0)])
 
 
-def exchanged(x):
-    return lax.all_to_all(x, CHIPS, 0, 0, tiled=True)
+def exchanged(x, axes):
+    return lax.all_to_all(x, axes, 0, 0, tiled=True)
 
 
 def local(activations, out_grad, value_weight, error_feedback, warm_right):
@@ -190,24 +172,26 @@
     warm = warm_right[0, 0].T
 
     acts = [act] + [moved(act, k) for k in (1, 2, 3)]
-    packed = ((OWN * 2 + 16, PART), BF16)
-    sends = call(pack_kernel, [packed] * 3)(weight, og)
+    share = ((OWN, WIDE), F32)
+    *shares, inner, fed, lines = call(
+        early_kernel,
+        [share] * 4 + [((RANK, OWN), F32), ((RANK, HEAD), F32), ((RANK, WIDE), BF16)],
+        flops=2 * 10**8,
+        moved=6 * 10**6,
+    )(weight, og, act, ef, warm)
 
     half = ((HALF, HEAD), F32)
     left_keep, left_send = call(
-        left_kernel, [half, half], [pltpu.VMEM((RANK, HEAD), F32)], flops=10**8, moved=3 * 10**6
-    )(*acts, og, ef, warm)
-
-    sends, left_send = lax.optimization_barrier((sends, left_send))
-    got = [moved(s, k) for k, s in zip((1, 2, 3), sends)]
+        left_kernel, [half, half], [pltpu.VMEM((RANK, HEAD), F32)], flops=5 * 10**7, moved=10**6
+    )(*acts[1:], og, lines, inner, fed)
+    shares, left_send = lax.optimization_barrier((shares, left_send))
+    near = [moved(shares[1], 1), moved(shares[3], 3)]
 
     left_half = left_keep + swapped(left_send)
-    pieces = exchanged(jnp.broadcast_to(left_half[None], (N_CHIPS, HALF, HEAD)))
+    pieces = exchanged(jnp.broadcast_to(left_half[None], (N_CHIPS, HALF, HEAD)), CHIPS)
     left_own = jnp.sum(pieces, axis=0)
     left_other = swapped(left_own)
-    left_other, got = lax.optimization_barrier((left_other, got))
-
-    traded = [swapped(g) for g in got]
+
     block = ((N_CHIPS, HALF, 128), F32)
     basis, right_keep, right_send = call(
         basis_kernel,
@@ -217,29 +201,20 @@
         moved=3 * 10**6,
     )(left_own, left_other, *acts, og, ef)
 
-    outs = call(
-        input_kernel,
-        [((OWN, PART), BF16)] * 4,
-        [pltpu.VMEM((512, PART), BF16), pltpu.VMEM((128, 512), BF16)],
-        flops=2 * 10**8,
-        moved=2 * 10**6,
-    )(weight, og, *got, *traded)
-    inputs = [outs[0]] + [moved(o, k) for k, o in zip((1, 2, 3), outs[1:])]
-
-    pieces = exchanged(right_keep + swapped(right_send))
-    pieces, outs = lax.optimization_barrier((pieces, outs))
+    right_send, near, far = lax.optimization_barrier((right_send, near, shares[2]))
+    far = moved(far, 2)
+    pieces = exchanged(right_keep + swapped(right_send), CHIPS)
     (mean,) = call(spread_kernel, [block])(pieces)
-    right_own = exchanged(mean)
-    right_own, inputs = lax.optimization_barrier((right_own, inputs))
+    right_own = exchanged(mean, CHIPS)
     right_other = swapped(right_own)
 
-    err, fac, igrad = call(
+    err, fac = call(
         finish_kernel,
-        [((HEAD, WIDE), BF16), ((RANK, WIDE), BF16), ((OWN, WIDE), BF16)],
-        [pltpu.VMEM((RANK, HEAD), F32)],
+        [((HEAD, WIDE), BF16), ((RANK, WIDE), BF16)],
         flops=3 * 10**8,
         moved=5 * 10**6,
-    )(right_own, right_other, basis, og, *acts, ef, *inputs)
+    )(right_own, right_other, basis, og, *acts, ef)
+    igrad = (shares[0] + near[0] + near[1] + far).astype(BF16)
 
     return (err[None, None], basis.T[None], fac.T[None, None], igrad[None])
 

time: 116 us -> 123 us (1.060)
  blocking collectives: 0 us -> 24.5 us
  starting transfers between devices: 61.4 us -> 39.1 us
  waiting for transfers between devices: 34.8 us -> 42.5 us
  local copies, waits for them, and re-layouts: 9.93 us -> 5.86 us
  other arithmetic: 0.78 us -> 2.93 us
    all_to_all x0 -> x1, blocking collectives: none -> 24.5 us  [exchanged(): return lax.all_to_all(x, axes, 0, 0, tiled=True)]
    all_to_all x3 -> x2, starting transfers between devices: 24.7 us -> 14.1 us  [exchanged(): return lax.all_to_all(x, axes, 0, 0, tiled=True)]
    all_to_all x3 -> x2, waiting for transfers between devices: 0.01 us -> 9.27 us  [exchanged(): return lax.all_to_all(x, axes, 0, 0, tiled=True)]
    ppermute x9 -> x6, starting transfers between devices: 26.5 us -> 18.3 us  [moved(): return lax.ppermute(x, 't', [(i, (i + k) % TENSOR) for i in range(TENSOR)])]
    unnamed x42 -> x22, local copies, waits for them, and re-layouts: 9.21 us -> 5.14 us
    ppermute x7 -> x4, starting transfers between devices: 10.2 us -> 6.77 us  [swapped(): return lax.ppermute(x, 'core', [(0, 1), (1, 0)])]
    broadcast_in_dim x0 -> x1, other arithmetic: none -> 2.16 us  [local(): return (err[None, None], basis.T[None], fac.T[None, None], igrad[None])]
    ppermute x7 -> x4, waiting for transfers between devices: 4.48 us -> 2.82 us  [swapped(): return lax.ppermute(x, 'core', [(0, 1), (1, 0)])]
  transfers between devices with their start and end apart: 19 -> 12, of which waited for: 14 -> 8; matrix products, arithmetic and copies ran while one was open for 0% -> 2% of each run, Pallas kernels for 1% -> 4%
where the time goes in v3:
time: 123 us; the launch traced here: 122 us
  waiting for transfers between devices  42.5 us (35%)
  starting transfers between devices  39.1 us (32%)
  blocking collectives  24.5 us (20%)
  Pallas kernels  6.63 us (5%)
  local copies, waits for them, and re-layouts  5.86 us (5%)
  other arithmetic  2.93 us (2%)
    ppermute x6, waiting for transfers between devices, moved(): return lax.ppermute(x, 't', [(i, (i + k) % TENSOR) for i in range(TENSOR)])  30.4 us
    all_to_all x1, blocking collectives, exchanged(): return lax.all_to_all(x, axes, 0, 0, tiled=True)  24.5 us
    ppermute x6, starting transfers between devices, moved(): return lax.ppermute(x, 't', [(i, (i + k) % TENSOR) for i in range(TENSOR)])  18.3 us
    all_to_all x2, starting transfers between devices, exchanged(): return lax.all_to_all(x, axes, 0, 0, tiled=True)  14.1 us
    all_to_all x2, waiting for transfers between devices, exchanged(): return lax.all_to_all(x, axes, 0, 0, tiled=True)  9.27 us
    ppermute x4, starting transfers between devices, swapped(): return lax.ppermute(x, 'core', [(0, 1), (1, 0)])  6.77 us
    pallas_call x5, Pallas kernels, run(): pl.pallas_call(kernel, out_shape=[jax.ShapeDtypeStruct(s, d) for s, d in...  6.63 us
    unnamed x22, local copies, waits for them, and re-layouts  5.14 us
  transfers between devices with their start and end apart: 12, of which 8 were waited for; matrix products, arithmetic and copies ran while one was open for 2% of the time, Pallas kernels for 4%

profile of v3, /device:TPU:1, one launch (start us, length us, event | category | flops | bytes accessed | tf_op | source)
XLA Modules:
  0.0 122.3 jit_solution(11800343979354800274)
XLA Ops:
  0.6 3.9 %collective-permute-start = (bf16[32,4096]{1,0:T(8,128)(2,1)}, bf16[32,4096]{1,0:T(8,128)(2,1)S(1)}, u32[]{:S(2)}, u32[]{:S(2)}) collective-permute-start(bf16[32,4096]{1,0:T(8,128)(2,1)} %bitcast.19), channel_id=1, source_target_pairs={{0,1},{1,2},{2,3},{3,0},{4,5},{5,6},{6,7},{7,4},{8,9},{9,10},{10,1... | collective-permute-start | bytes 786440 | tf_op jit(solution)/shard_map/ppermute | solution.py:158
  4.5 5.1 %collective-permute-start.1 = (bf16[32,4096]{1,0:T(8,128)(2,1)}, bf16[32,4096]{1,0:T(8,128)(2,1)S(1)}, u32[]{:S(2)}, u32[]{:S(2)}) collective-permute-start(bf16[32,4096]{1,0:T(8,128)(2,1)} %bitcast.20), channel_id=1, source_target_pairs={{0,2},{1,3},{2,0},{3,1},{4,6},{5,7},{6,4},{7,5},{8,10},{9,11},{10,... | collective-permute-start | bytes 786440 | tf_op jit(solution)/shard_map/ppermute | solution.py:158
  9.6 2.4 %collective-permute-start.2 = (bf16[32,4096]{1,0:T(8,128)(2,1)}, bf16[32,4096]{1,0:T(8,128)(2,1)S(1)}, u32[]{:S(2)}, u32[]{:S(2)}) collective-permute-start(bf16[32,4096]{1,0:T(8,128)(2,1)} %bitcast.21), channel_id=1, source_target_pairs={{0,3},{1,0},{2,1},{3,2},{4,7},{5,4},{6,5},{7,6},{8,11},{9,8},{10,9... | collective-permute-start | bytes 786440 | tf_op jit(solution)/shard_map/ppermute | solution.py:158
  12.0 0.0 copy-start
  12.0 1.2 %copy-done = bf16[1,1,128,4096]{3,2,1,0:T(8,128)(2,1)S(1)} copy-done((bf16[1,1,128,4096]{3,2,1,0:T(8,128)(2,1)S(1)}, bf16[1,1,128,4096]{3,2,1,0:T(8,128)(2,1)}, u32[]{:S(2)}) %copy-start) | copy-done | bytes 1048600
  13.2 0.0 copy-start.2
  13.3 0.9 copy-done.2
  14.2 0.0 copy-start.4
  14.2 1.2 %copy-done.4 = bf16[1,128,4096]{2,1,0:T(8,128)(2,1)S(1)} copy-done((bf16[1,128,4096]{2,1,0:T(8,128)(2,1)S(1)}, bf16[1,128,4096]{2,1,0:T(8,128)(2,1)}, u32[]{:S(2)}) %copy-start.4) | copy-done | bytes 1048600
  15.4 0.0 copy-start.5
  15.4 0.8 copy-done.5
  16.2 0.0 copy-start.7
  16.2 0.9 copy-done.7
  17.1 0.8 shard_map.84
  17.9 0.0 copy-start.9
  17.9 0.0 copy-start.10
  17.9 0.0 collective-permute-done.a1
  17.9 7.3 %collective-permute-done.1.a2 = bf16[32,4096]{1,0:T(8,128)(2,1)S(1)} collective-permute-done((bf16[32,4096]{1,0:T(8,128)(2,1)}, bf16[32,4096]{1,0:T(8,128)(2,1)S(1)}, u32[]{:S(2)}, u32[]{:S(2)}) %collective-permute-start.1) | collective-permute-done | bytes 262176 | tf_op jit(solution)/shard_map/ppermute | solution.py:158
  25.2 8.9 %collective-permute-done.2.a3 = bf16[32,4096]{1,0:T(8,128)(2,1)S(1)} collective-permute-done((bf16[32,4096]{1,0:T(8,128)(2,1)}, bf16[32,4096]{1,0:T(8,128)(2,1)S(1)}, u32[]{:S(2)}, u32[]{:S(2)}) %collective-permute-start.2) | collective-permute-done | bytes 262176 | tf_op jit(solution)/shard_map/ppermute | solution.py:158
  34.1 0.0 copy-start.1
  34.1 0.6 shard_map.85
  34.6 0.0 copy-done.9
  34.6 0.0 copy-done.10
  34.6 0.6 collective-permute-start.3
  35.2 0.8 collective-permute-done.3
  36.1 0.7 broadcast_in_dim.18
  36.8 0.0 copy-start.6
  36.8 7.2 %all-to-all-start = ((f32[32,16,128]{2,1,0:T(8,128)}), f32[32,16,128]{2,1,0:T(8,128)S(1)}, u32[]{:S(2)}, u32[]{:S(2)}) async-start(f32[32,16,128]{2,1,0:T(8,128)} %broadcast_in_dim.18), calls=%async_computation | async-start | bytes 524288 | tf_op jit(solution)/shard_map/all_to_all | solution.py:166
  44.0 0.0 copy-start.3
  44.0 1.4 %collective-permute-start.5 = (f32[32,4096]{1,0:T(8,128)}, f32[32,4096]{1,0:T(8,128)}, u32[]{:S(2)}, u32[]{:S(2)}) collective-permute-start(f32[32,4096]{1,0:T(8,128)} %copy-done.10), channel_id=1, source_target_pairs={{0,1},{1,2},{2,3},{3,0},{4,5},{5,6},{6,7},{7,4},{8,9},{9,10},{10,1... | collective-permute-start | bytes 1572872 | tf_op jit(solution)/shard_map/ppermute | solution.py:158
  45.4 2.3 %collective-permute-start.6 = (f32[32,4096]{1,0:T(8,128)}, f32[32,4096]{1,0:T(8,128)}, u32[]{:S(2)}, u32[]{:S(2)}) collective-permute-start(f32[32,4096]{1,0:T(8,128)} %copy-done.9), channel_id=1, source_target_pairs={{0,3},{1,0},{2,1},{3,2},{4,7},{5,4},{6,5},{7,6},{8,11},{9,8},{10,9... | collective-permute-start | bytes 1572872 | tf_op jit(solution)/shard_map/ppermute | solution.py:158
  47.6 4.4 %all-to-all-done = f32[32,16,128]{2,1,0:T(8,128)S(1)} async-done(((f32[32,16,128]{2,1,0:T(8,128)}), f32[32,16,128]{2,1,0:T(8,128)S(1)}, u32[]{:S(2)}, u32[]{:S(2)}) %all-to-all-start) | async-done | bytes 262176 | tf_op jit(solution)/shard_map/all_to_all | solution.py:166
  52.1 2.1 %collective-permute-start.4 = (f32[16,128]{1,0:T(8,128)S(1)}, f32[16,128]{1,0:T(8,128)S(1)}, u32[]{:S(2)}, u32[]{:S(2)}) collective-permute-start(f32[16,128]{1,0:T(8,128)S(1)} %reduce_sum.9.lown), channel_id=1, source_target_pairs={{0,4},{4,0},{1,5},{5,1},{2,6},{6,2},{3,7},{7,3},{8,12},{12,8},{9,1... | collective-permute-start | bytes 24584 | tf_op jit(solution)/shard_map/ppermute | solution.py:162
  54.2 0.8 collective-permute-done.4.loth
  55.0 0.0 copy-done.1
  55.0 0.0 copy-done.6
  55.0 0.0 copy-done.3
  55.0 3.8 %shard_map.86 = (f32[32,128]{1,0:T(8,128)}, f32[32,16,128]{2,1,0:T(8,128)S(1)}, f32[32,16,128]{2,1,0:T(8,128)S(1)}) custom-call(f32[16,128]{1,0:T(8,128)S(1)} %reduce_sum.9.lown, f32[16,128]{1,0:T(8,128)S(1)} %collective-permute-done.4.loth, bf16[32,4096]{1,0:T(8,128)(2,1)S(1)} %bitcast.23, bf16[32,4096]{1,0:T(8,128)(2,1)S(1)} %collective-permute-done.a1, ...), custom_call_target="tpu_custom_call" | custom-call | flops 100000000 | bytes 3000000 | tf_op jit(solution)/shard_map/pallas_call | solution.py:50
  58.8 14.3 %collective-permute-done.5 = f32[32,4096]{1,0:T(8,128)} collective-permute-done((f32[32,4096]{1,0:T(8,128)}, f32[32,4096]{1,0:T(8,128)}, u32[]{:S(2)}, u32[]{:S(2)}) %collective-permute-start.5) | collective-permute-done | bytes 524320 | tf_op jit(solution)/shard_map/ppermute | solution.py:158
  73.1 0.0 collective-permute-done.6
  73.1 1.2 collective-permute-start.7
  74.2 1.2 collective-permute-done.7
  75.4 0.7 add.16
  76.1 6.9 %all-to-all-start.1 = ((f32[32,16,128]{2,1,0:T(8,128)}), f32[32,16,128]{2,1,0:T(8,128)S(1)}, u32[]{:S(2)}, u32[]{:S(2)}) async-start(f32[32,16,128]{2,1,0:T(8,128)} %add.16), calls=%async_computation.1 | async-start | bytes 524288 | tf_op jit(solution)/shard_map/all_to_all | solution.py:166
  83.1 3.2 %collective-permute-start.9 = (f32[32,4096]{1,0:T(8,128)S(1)}, f32[32,4096]{1,0:T(8,128)}, u32[]{:S(2)}, u32[]{:S(2)}) collective-permute-start(f32[32,4096]{1,0:T(8,128)S(1)} %get-tuple-element.49), channel_id=1, source_target_pairs={{0,2},{1,3},{2,0},{3,1},{4,6},{5,7},{6,4},{7,5},{8,10},{9,11},{10,... | collective-permute-start | bytes 1572872 | tf_op jit(solution)/shard_map/ppermute | solution.py:158
  86.3 4.8 %all-to-all-done.1.pieces = f32[32,16,128]{2,1,0:T(8,128)S(1)} async-done(((f32[32,16,128]{2,1,0:T(8,128)}), f32[32,16,128]{2,1,0:T(8,128)S(1)}, u32[]{:S(2)}, u32[]{:S(2)}) %all-to-all-start.1) | async-done | bytes 262176 | tf_op jit(solution)/shard_map/all_to_all | solution.py:166
  91.1 0.1 shard_map.87
  91.2 24.5 %all_to_all.15.rown = f32[32,16,128]{2,1,0:T(8,128)S(1)} all-to-all(f32[32,16,128]{2,1,0:T(8,128)S(1)} %shard_map.87), channel_id=1, replica_groups=mesh['x'=4,'zl'=2,'y'=4,'core'=2,'t'=4] {'x','zl','y'}, dimensions={0} | all-to-all | bytes 524288 | tf_op jit(solution)/shard_map/all_to_all | solution.py:166
  115.7 0.0 copy-start.8
  115.7 3.0 %collective-permute-start.8 = (f32[32,16,128]{2,1,0:T(8,128)S(1)}, f32[32,16,128]{2,1,0:T(8,128)S(1)}, u32[]{:S(2)}, u32[]{:S(2)}) collective-permute-start(f32[32,16,128]{2,1,0:T(8,128)S(1)} %all_to_all.15.rown), channel_id=1, source_target_pairs={{0,4},{4,0},{1,5},{5,1},{2,6},{6,2},{3,7},{7,3},{8,12},{12,8},{9,1... | collective-permute-start | bytes 786440 | tf_op jit(solution)/shard_map/ppermute | solution.py:162
  118.6 0.0 collective-permute-done.9
  118.6 2.2 %fusion = bf16[1,32,4096]{2,1,0:T(8,128)(2,1)} fusion(f32[32,4096]{1,0:T(8,128)} %collective-permute-done.9, f32[32,4096]{1,0:T(8,128)} %collective-permute-done.6, f32[32,4096]{1,0:T(8,128)S(1)} %get-tuple-element.46, f32[32,4096]{1,0:T(8,128)} %collective-permute-done.5), kind=kLoop, calls=%fused_computation.1 | loop fusion | flops 524288 | bytes 2359296 | tf_op jit(solution)/shard_map/broadcast_in_dim | solution.py:219
  120.8 0.0 collective-permute-done.8.roth
  120.8 0.0 copy-done.8
  120.8 1.5 %shard_map.88 = (bf16[128,4096]{1,0:T(8,128)(2,1)}, bf16[32,4096]{1,0:T(8,128)(2,1)}) custom-call(f32[32,16,128]{2,1,0:T(8,128)S(1)} %all_to_all.15.rown, f32[32,16,128]{2,1,0:T(8,128)S(1)} %collective-permute-done.8.roth, f32[32,128]{1,0:T(8,128)S(1)} %copy-done.8, bf16[128,128]{1,0:T(8,128)(2,1)S(1)} %bitcast.29, bf16[32,4096]{1,0:T(8,128)(2,1)S(1)} %bitcast.24, ...), custom_call_target="tpu_custom_call" | custom-call | flops 300000000 | bytes 5000000 | tf_op jit(solution)/shard_map/pallas_call | solution.py:50
  (2 shorter events, 0.0 us)
Async XLA Ops:
  0.6 17.3 %collective-permute-start = (bf16[32,4096]{1,0:T(8,128)(2,1)}, bf16[32,4096]{1,0:T(8,128)(2,1)S(1)}, u32[]{:S(2)}, u32[]{:S(2)}) collective-permute-start(bf16[32,4096]{1,0:T(8,128)(2,1)} %bitcast.19), channel_id=1, source_target_pairs={{0,1},{1,2},{2,3},{3,0},{4,5},{5,6},{6,7},{7,4},{8,9},{9,10},{10,1... | collective-permute-start | bytes 786440 | tf_op jit(solution)/shard_map/ppermute | solution.py:158
  4.5 20.7 %collective-permute-start.1 = (bf16[32,4096]{1,0:T(8,128)(2,1)}, bf16[32,4096]{1,0:T(8,128)(2,1)S(1)}, u32[]{:S(2)}, u32[]{:S(2)}) collective-permute-start(bf16[32,4096]{1,0:T(8,128)(2,1)} %bitcast.20), channel_id=1, source_target_pairs={{0,2},{1,3},{2,0},{3,1},{4,6},{5,7},{6,4},{7,5},{8,10},{9,11},{10,... | collective-permute-start | bytes 786440 | tf_op jit(solution)/shard_map/ppermute | solution.py:158
  9.6 24.4 %collective-permute-start.2 = (bf16[32,4096]{1,0:T(8,128)(2,1)}, bf16[32,4096]{1,0:T(8,128)(2,1)S(1)}, u32[]{:S(2)}, u32[]{:S(2)}) collective-permute-start(bf16[32,4096]{1,0:T(8,128)(2,1)} %bitcast.21), channel_id=1, source_target_pairs={{0,3},{1,0},{2,1},{3,2},{4,7},{5,4},{6,5},{7,6},{8,11},{9,8},{10,9... | collective-permute-start | bytes 786440 | tf_op jit(solution)/shard_map/ppermute | solution.py:158
  12.0 1.2 %copy-start = (bf16[1,1,128,4096]{3,2,1,0:T(8,128)(2,1)S(1)}, bf16[1,1,128,4096]{3,2,1,0:T(8,128)(2,1)}, u32[]{:S(2)}) copy-start(bf16[1,1,128,4096]{3,2,1,0:T(8,128)(2,1)} %param.8) | copy-start | bytes 3145732
  13.2 0.9 copy-start.2
  14.2 1.2 %copy-start.4 = (bf16[1,128,4096]{2,1,0:T(8,128)(2,1)S(1)}, bf16[1,128,4096]{2,1,0:T(8,128)(2,1)}, u32[]{:S(2)}) copy-start(bf16[1,128,4096]{2,1,0:T(8,128)(2,1)} %param.7) | copy-start | bytes 3145732
  15.4 0.8 copy-start.5
  16.2 0.9 copy-start.7
  17.9 16.7 %copy-start.9 = (f32[32,4096]{1,0:T(8,128)}, f32[32,4096]{1,0:T(8,128)S(1)}, u32[]{:S(2)}) copy-start(f32[32,4096]{1,0:T(8,128)S(1)} %get-tuple-element.40) | copy-start | bytes 1572868
  17.9 16.7 %copy-start.10 = (f32[32,4096]{1,0:T(8,128)}, f32[32,4096]{1,0:T(8,128)S(1)}, u32[]{:S(2)}) copy-start(f32[32,4096]{1,0:T(8,128)S(1)} %get-tuple-element.39) | copy-start | bytes 1572868
  34.1 20.9 %copy-start.1 = (bf16[1,1,128,4096]{3,2,1,0:T(8,128)(2,1)S(1)}, bf16[1,1,128,4096]{3,2,1,0:T(8,128)(2,1)}, u32[]{:S(2)}) copy-start(bf16[1,1,128,4096]{3,2,1,0:T(8,128)(2,1)} %param.8) | copy-start | bytes 3145732
  34.6 1.4 %collective-permute-start.3 = (f32[16,128]{1,0:T(8,128)S(1)}, f32[16,128]{1,0:T(8,128)S(1)}, u32[]{:S(2)}, u32[]{:S(2)}) collective-permute-start(f32[16,128]{1,0:T(8,128)S(1)} %get-tuple-element.36), channel_id=1, source_target_pairs={{0,4},{4,0},{1,5},{5,1},{2,6},{6,2},{3,7},{7,3},{8,12},{12,8},{9,1... | collective-permute-start | bytes 24584 | tf_op jit(solution)/shard_map/ppermute | solution.py:162
  36.8 18.2 %copy-start.6 = (bf16[1,128,128]{2,1,0:T(8,128)(2,1)S(1)}, bf16[1,128,128]{2,1,0:T(8,128)(2,1)}, u32[]{:S(2)}) copy-start(bf16[1,128,128]{2,1,0:T(8,128)(2,1)} %param.6) | copy-start | bytes 98308
  36.8 15.3 %all-to-all-start = ((f32[32,16,128]{2,1,0:T(8,128)}), f32[32,16,128]{2,1,0:T(8,128)S(1)}, u32[]{:S(2)}, u32[]{:S(2)}) async-start(f32[32,16,128]{2,1,0:T(8,128)} %broadcast_in_dim.18), calls=%async_computation | async-start | bytes 524288 | tf_op jit(solution)/shard_map/all_to_all | solution.py:166
  44.0 11.0 %copy-start.3 = (bf16[1,32,4096]{2,1,0:T(8,128)(2,1)S(1)}, bf16[1,32,4096]{2,1,0:T(8,128)(2,1)}, u32[]{:S(2)}) copy-start(bf16[1,32,4096]{2,1,0:T(8,128)(2,1)} %param.5) | copy-start | bytes 786436
  44.0 29.1 %collective-permute-start.5 = (f32[32,4096]{1,0:T(8,128)}, f32[32,4096]{1,0:T(8,128)}, u32[]{:S(2)}, u32[]{:S(2)}) collective-permute-start(f32[32,4096]{1,0:T(8,128)} %copy-done.10), channel_id=1, source_target_pairs={{0,1},{1,2},{2,3},{3,0},{4,5},{5,6},{6,7},{7,4},{8,9},{9,10},{10,1... | collective-permute-start | bytes 1572872 | tf_op jit(solution)/shard_map/ppermute | solution.py:158
  45.4 27.7 %collective-permute-start.6 = (f32[32,4096]{1,0:T(8,128)}, f32[32,4096]{1,0:T(8,128)}, u32[]{:S(2)}, u32[]{:S(2)}) collective-permute-start(f32[32,4096]{1,0:T(8,128)} %copy-done.9), channel_id=1, source_target_pairs={{0,3},{1,0},{2,1},{3,2},{4,7},{5,4},{6,5},{7,6},{8,11},{9,8},{10,9... | collective-permute-start | bytes 1572872 | tf_op jit(solution)/shard_map/ppermute | solution.py:158
  52.1 2.9 %collective-permute-start.4 = (f32[16,128]{1,0:T(8,128)S(1)}, f32[16,128]{1,0:T(8,128)S(1)}, u32[]{:S(2)}, u32[]{:S(2)}) collective-permute-start(f32[16,128]{1,0:T(8,128)S(1)} %reduce_sum.9.lown), channel_id=1, source_target_pairs={{0,4},{4,0},{1,5},{5,1},{2,6},{6,2},{3,7},{7,3},{8,12},{12,8},{9,1... | collective-permute-start | bytes 24584 | tf_op jit(solution)/shard_map/ppermute | solution.py:162
  73.1 2.3 %collective-permute-start.7 = (f32[32,16,128]{2,1,0:T(8,128)S(1)}, f32[32,16,128]{2,1,0:T(8,128)S(1)}, u32[]{:S(2)}, u32[]{:S(2)}) collective-permute-start(f32[32,16,128]{2,1,0:T(8,128)S(1)} %get-tuple-element.42), channel_id=1, source_target_pairs={{0,4},{4,0},{1,5},{5,1},{2,6},{6,2},{3,7},{7,3},{8,12},{12,8},{9,1... | collective-permute-start | bytes 786440 | tf_op jit(solution)/shard_map/ppermute | solution.py:162
  76.1 15.0 %all-to-all-start.1 = ((f32[32,16,128]{2,1,0:T(8,128)}), f32[32,16,128]{2,1,0:T(8,128)S(1)}, u32[]{:S(2)}, u32[]{:S(2)}) async-start(f32[32,16,128]{2,1,0:T(8,128)} %add.16), calls=%async_computation.1 | async-start | bytes 524288 | tf_op jit(solution)/shard_map/all_to_all | solution.py:166
  83.1 35.5 %collective-permute-start.9 = (f32[32,4096]{1,0:T(8,128)S(1)}, f32[32,4096]{1,0:T(8,128)}, u32[]{:S(2)}, u32[]{:S(2)}) collective-permute-start(f32[32,4096]{1,0:T(8,128)S(1)} %get-tuple-element.49), channel_id=1, source_target_pairs={{0,2},{1,3},{2,0},{3,1},{4,6},{5,7},{6,4},{7,5},{8,10},{9,11},{10,... | collective-permute-start | bytes 1572872 | tf_op jit(solution)/shard_map/ppermute | solution.py:158
  115.7 5.1 %copy-start.8 = (f32[32,128]{1,0:T(8,128)S(1)}, f32[32,128]{1,0:T(8,128)}, u32[]{:S(2)}) copy-start(f32[32,128]{1,0:T(8,128)} %get-tuple-element.43.qt) | copy-start | bytes 49156
  115.7 5.1 %collective-permute-start.8 = (f32[32,16,128]{2,1,0:T(8,128)S(1)}, f32[32,16,128]{2,1,0:T(8,128)S(1)}, u32[]{:S(2)}, u32[]{:S(2)}) collective-permute-start(f32[32,16,128]{2,1,0:T(8,128)S(1)} %all_to_all.15.rown), channel_id=1, source_target_pairs={{0,4},{4,0},{1,5},{5,1},{2,6},{6,2},{3,7},{7,3},{8,12},{12,8},{9,1... | collective-permute-start | bytes 786440 | tf_op jit(solution)/shard_map/ppermute | solution.py:162

commit v4 on v3

--- a/solution.py
+++ b/solution.py
@@ -20,6 +20,8 @@
 RANK = 32
 HALF = RANK // 2
 OWN = 32
+CUT = 16
+PART = WIDE // TENSOR
 N_CHIPS = REPLICAS // 2
 STEP = 512
 NT = (((1,), (1,)), ((), ()))
@@ -60,18 +62,20 @@
     return run
 
 
-def early_kernel(w, og, a0, ef, warm, p0, p1, p2, p3, inner, fed, lines):
-    t = lax.axis_index("t")
+def pack_kernel(w, og, *sends):
+    t, y, core = lax.axis_index("t"), lax.axis_index("y"), lax.axis_index("core")
+    rows = pl.ds(pl.multiple_of((2 * y + core) * CUT, CUT), CUT)
+    for k, send in enumerate(sends, 1):
+        target = lax.rem(t + k, TENSOR)
+        send[0:CUT, :] = w[rows, pl.ds(pl.multiple_of(target * PART, PART), PART)]
+        for m in range(8):
+            send[CUT : 2 * CUT, 128 * m : 128 * m + 128] = og[16 * m : 16 * m + 16, :]
+
+
+def early_kernel(a0, ef, warm, inner, fed, lines):
     lines[...] = warm[...]
     inner[...] = lax.dot_general(warm[...], a0[...], NT, preferred_element_type=F32)
     fed[...] = lax.dot_general(warm[...], ef[...], NT, preferred_element_type=F32)
-    targets = jnp.concatenate(
-        [og[pl.ds(lax.rem(t + k, TENSOR) * OWN, OWN), :] for k in range(TENSOR)], axis=0
-    )
-    for c in range(0, WIDE, STEP):
-        share = jnp.dot(targets, w[:, c : c + STEP], preferred_element_type=F32)
-        for k, out in enumerate((p0, p1, p2, p3)):
-            out[:, c : c + STEP] = share[OWN * k : OWN * k + OWN]
 
 
 def left_kernel(a1, a2, a3, og, lines, inner0, fed, keep, send, held):
@@ -133,10 +137,13 @@
     out[...] = jnp.broadcast_to(total[None], out.shape)
 
 
-def finish_kernel(rown, roth, qt, og, a0, a1, a2, a3, ef, err, fac):
+def finish_kernel(rown, roth, qt, og, a0, a1, a2, a3, ef, i0, i1, i2, i3, err, fac, igrad):
     t, core = lax.axis_index("t"), lax.axis_index("core")
     mine = pl.ds(pl.multiple_of(core * HALF, HALF), HALF)
     other = pl.ds(pl.multiple_of((1 - core) * HALF, HALF), HALF)
+    for k, block in enumerate((i0, i1, i2, i3)):
+        source = lax.rem(t - k + TENSOR, TENSOR)
+        igrad[:, pl.ds(pl.multiple_of(source * PART, PART), PART)] = block[...]
     q = jnp.concatenate([qt[mine, :], qt[other, :]], axis=0)
     hi, mid = split2(q)
     hi, mid = hi.astype(F32), mid.astype(F32)
@@ -154,8 +161,29 @@
         err[:, cols] = total.astype(BF16)
 
 
-def moved(x, k):
-    return lax.ppermute(x, "t", [(i, (i + k) % TENSOR) for i in range(TENSOR)])
+def input_kernel(w, og, r1, r2, r3, h0, h1, h2, h3, c0, c1, c2, c3, o0, o1, o2, o3, weights, feats):
+    t, y, core = lax.axis_index("t"), lax.axis_index("y"), lax.axis_index("core")
+    weights[0:128, :] = w[:, pl.ds(pl.multiple_of(t * PART, PART), PART)]
+    feats[:, 0:128] = og[...]
+    for k, r in enumerate((r1, r2, r3), 1):
+        for m in range(8):
+            feats[16 * m : 16 * m + 16, 128 * k : 128 * k + 128] = r[
+                CUT : 2 * CUT, 128 * m : 128 * m + 128
+            ]
+        for j, (h, c) in enumerate(((h0, c0), (h1, c1), (h2, c2), (h3, c3))):
+            first = 128 * k + 2 * CUT * lax.rem(y - j + 4, 4)
+            here = pl.ds(pl.multiple_of(first + CUT * core, CUT), CUT)
+            there = pl.ds(pl.multiple_of(first + CUT * (1 - core), CUT), CUT)
+            weights[here, :] = h[CUT * (k - 1) : CUT * k, :]
+            weights[there, :] = c[CUT * (k - 1) : CUT * k, :]
+    for k, out in enumerate((o0, o1, o2, o3)):
+        target = lax.rem(t + k, TENSOR)
+        rows = feats[pl.ds(pl.multiple_of(target * OWN, OWN), OWN), :]
+        out[...] = jnp.dot(rows, weights[...], preferred_element_type=F32).astype(BF16)
+
+
+def moved(x, k, axis="t"):
+    return lax.ppermute(x, axis, [(i, (i + k) % 4) for i in range(4)])
 
 
 def swapped(x):
@@ -171,23 +199,35 @@
     ef = error_feedback[0, 0]
     warm = warm_right[0, 0].T
 
+    sends = call(pack_kernel, [((2 * CUT, PART), BF16)] * 3)(weight, og)
+    got = [moved(x, k) for k, x in zip((1, 2, 3), sends)]
+    act, got = lax.optimization_barrier((act, got))
     acts = [act] + [moved(act, k) for k in (1, 2, 3)]
-    share = ((OWN, WIDE), F32)
-    *shares, inner, fed, lines = call(
+    inner, fed, lines = call(
         early_kernel,
-        [share] * 4 + [((RANK, OWN), F32), ((RANK, HEAD), F32), ((RANK, WIDE), BF16)],
-        flops=2 * 10**8,
-        moved=6 * 10**6,
-    )(weight, og, act, ef, warm)
+        [((RANK, OWN), F32), ((RANK, HEAD), F32), ((RANK, WIDE), BF16)],
+        flops=0,
+        moved=0,
+    )(act, ef, warm)
+
+    shares = [jnp.concatenate([g[:CUT] for g in got], axis=0)]
+    shares += [moved(shares[0], j, "y") for j in (1, 2, 3)]
+    outs = call(
+        input_kernel,
+        [((OWN, PART), BF16)] * 4,
+        [pltpu.VMEM((512, PART), BF16), pltpu.VMEM((128, 512), BF16)],
+        flops=0,
+        moved=0,
+    )(weight, og, *got, *shares, *[swapped(x) for x in shares])
+    inputs = [outs[0]] + [moved(o, k) for k, o in zip((1, 2, 3), outs[1:])]
 
     half = ((HALF, HEAD), F32)
     left_keep, left_send = call(
         left_kernel, [half, half], [pltpu.VMEM((RANK, HEAD), F32)], flops=5 * 10**7, moved=10**6
     )(*acts[1:], og, lines, inner, fed)
-    shares, left_send = lax.optimization_barrier((shares, left_send))
-    near = [moved(shares[1], 1), moved(shares[3], 3)]
 
     left_half = left_keep + swapped(left_send)
+    left_half, inputs = lax.optimization_barrier((left_half, inputs))
     pieces = exchanged(jnp.broadcast_to(left_half[None], (N_CHIPS, HALF, HEAD)), CHIPS)
     left_own = jnp.sum(pieces, axis=0)
     left_other = swapped(left_own)
@@ -201,20 +241,17 @@
         moved=3 * 10**6,
     )(left_own, left_other, *acts, og, ef)
 
-    right_send, near, far = lax.optimization_barrier((right_send, near, shares[2]))
-    far = moved(far, 2)
     pieces = exchanged(right_keep + swapped(right_send), CHIPS)
     (mean,) = call(spread_kernel, [block])(pieces)
     right_own = exchanged(mean, CHIPS)
     right_other = swapped(right_own)
 
-    err, fac = call(
+    err, fac, igrad = call(
         finish_kernel,
-        [((HEAD, WIDE), BF16), ((RANK, WIDE), BF16)],
+        [((HEAD, WIDE), BF16), ((RANK, WIDE), BF16), ((OWN, WIDE), BF16)],
         flops=3 * 10**8,
         moved=5 * 10**6,
-    )(right_own, right_other, basis, og, *acts, ef)
-    igrad = (shares[0] + near[0] + near[1] + far).astype(BF16)
+    )(right_own, right_other, basis, og, *acts, ef, *inputs)
 
     return (err[None, None], basis.T[None], fac.T[None, None], igrad[None])
 

time: 123 us -> 113 us (0.919)
  waiting for transfers between devices: 42.5 us -> 16.9 us
  blocking collectives: 24.5 us -> 41.5 us
  starting transfers between devices: 39.1 us -> 43.8 us
  local copies, waits for them, and re-layouts: 5.86 us -> 2.03 us
  other arithmetic: 2.93 us -> 0.08 us
    ppermute x6 -> x12, waiting for transfers between devices: 30.4 us -> 11.6 us  [moved(): return lax.ppermute(x, axis, [(i, (i + k) % 4) for i in range(4)])]
    all_to_all x1 -> x3, blocking collectives: 24.5 us -> 41.5 us  [exchanged(): return lax.all_to_all(x, axes, 0, 0, tiled=True)]
    all_to_all x2 -> x0, starting transfers between devices: 14.1 us -> none  [exchanged(): return lax.all_to_all(x, axes, 0, 0, tiled=True)]
    ppermute x6 -> x12, starting transfers between devices: 18.3 us -> 29.2 us  [moved(): return lax.ppermute(x, axis, [(i, (i + k) % 4) for i in range(4)])]
    all_to_all x2 -> x0, waiting for transfers between devices: 9.27 us -> none  [exchanged(): return lax.all_to_all(x, axes, 0, 0, tiled=True)]
    ppermute x4 -> x8, starting transfers between devices: 6.77 us -> 14.6 us  [swapped(): return lax.ppermute(x, 'core', [(0, 1), (1, 0)])]
    unnamed x22 -> x14, local copies, waits for them, and re-layouts: 5.14 us -> 2 us
    ppermute x4 -> x8, waiting for transfers between devices: 2.82 us -> 5.31 us  [swapped(): return lax.ppermute(x, 'core', [(0, 1), (1, 0)])]
  transfers between devices with their start and end apart: 12 -> 20, of which waited for: 8 -> 12; matrix products, arithmetic and copies ran while one was open for 2% -> 0% of each run, Pallas kernels for 4% -> 2%
where the time goes in v4:
time: 113 us; the launch traced here: 112 us
  starting transfers between devices  43.8 us (39%)
  blocking collectives  41.5 us (37%)
  waiting for transfers between devices  16.9 us (15%)
  Pallas kernels  7.29 us (6%)
  local copies, waits for them, and re-layouts  2.03 us (2%)
    all_to_all x3, blocking collectives, exchanged(): return lax.all_to_all(x, axes, 0, 0, tiled=True)  41.5 us
    ppermute x12, starting transfers between devices, moved(): return lax.ppermute(x, axis, [(i, (i + k) % 4) for i in range(4)])  29.2 us
    ppermute x8, starting transfers between devices, swapped(): return lax.ppermute(x, 'core', [(0, 1), (1, 0)])  14.6 us
    ppermute x12, waiting for transfers between devices, moved(): return lax.ppermute(x, axis, [(i, (i + k) % 4) for i in range(4)])  11.6 us
    pallas_call x7, Pallas kernels, run(): pl.pallas_call(kernel, out_shape=[jax.ShapeDtypeStruct(s, d) for s, d in...  7.29 us
    ppermute x8, waiting for transfers between devices, swapped(): return lax.ppermute(x, 'core', [(0, 1), (1, 0)])  5.31 us
  transfers between devices with their start and end apart: 20, of which 12 were waited for; matrix products, arithmetic and copies ran while one was open for 0% of the time, Pallas kernels for 2%

profile of v4, /device:TPU:1, one launch (start us, length us, event | category | flops | bytes accessed | tf_op | source)
XLA Modules:
  0.0 112.3 jit_solution(3529294399825375635)
XLA Ops:
  0.6 0.0 copy-start.1
  0.6 1.2 %copy-done.1 = bf16[1,128,4096]{2,1,0:T(8,128)(2,1)S(1)} copy-done((bf16[1,128,4096]{2,1,0:T(8,128)(2,1)S(1)}, bf16[1,128,4096]{2,1,0:T(8,128)(2,1)}, u32[]{:S(2)}) %copy-start.1) | copy-done | bytes 1048600
  1.9 0.0 copy-start.3
  1.9 0.8 copy-done.3
  2.6 0.0 copy-start.2
  2.7 3.9 %collective-permute-start = (bf16[32,1024]{1,0:T(8,128)(2,1)S(1)}, bf16[32,1024]{1,0:T(8,128)(2,1)S(1)}, u32[]{:S(2)}, u32[]{:S(2)}) collective-permute-start(bf16[32,1024]{1,0:T(8,128)(2,1)S(1)} %get-tuple-element.31), channel_id=1, source_target_pairs={{0,1},{1,2},{2,3},{3,0},{4,5},{5,6},{6,7},{7,4},{8,9},{9,10},{10,1... | collective-permute-start | bytes 196616 | tf_op jit(solution)/shard_map/ppermute | solution.py:186
  6.6 5.1 %collective-permute-start.1 = (bf16[32,1024]{1,0:T(8,128)(2,1)S(1)}, bf16[32,1024]{1,0:T(8,128)(2,1)S(1)}, u32[]{:S(2)}, u32[]{:S(2)}) collective-permute-start(bf16[32,1024]{1,0:T(8,128)(2,1)S(1)} %get-tuple-element.32), channel_id=1, source_target_pairs={{0,2},{1,3},{2,0},{3,1},{4,6},{5,7},{6,4},{7,5},{8,10},{9,11},{10,... | collective-permute-start | bytes 196616 | tf_op jit(solution)/shard_map/ppermute | solution.py:186
  11.7 2.4 %collective-permute-start.2 = (bf16[32,1024]{1,0:T(8,128)(2,1)S(1)}, bf16[32,1024]{1,0:T(8,128)(2,1)S(1)}, u32[]{:S(2)}, u32[]{:S(2)}) collective-permute-start(bf16[32,1024]{1,0:T(8,128)(2,1)S(1)} %get-tuple-element.33), channel_id=1, source_target_pairs={{0,3},{1,0},{2,1},{3,2},{4,7},{5,4},{6,5},{7,6},{8,11},{9,8},{10,9... | collective-permute-start | bytes 196616 | tf_op jit(solution)/shard_map/ppermute | solution.py:186
  14.1 0.0 collective-permute-done.r1
  14.1 0.4 collective-permute-done.1.r2
  14.4 4.9 %collective-permute-done.2.r3 = bf16[32,1024]{1,0:T(8,128)(2,1)S(1)} collective-permute-done((bf16[32,1024]{1,0:T(8,128)(2,1)S(1)}, bf16[32,1024]{1,0:T(8,128)(2,1)S(1)}, u32[]{:S(2)}, u32[]{:S(2)}) %collective-permute-start.2) | collective-permute-done | bytes 65568 | tf_op jit(solution)/shard_map/ppermute | solution.py:186
  19.4 0.0 copy-start
  19.4 0.0 copy-start.5
  19.4 0.6 collective-permute-start.10
  20.0 2.7 %collective-permute-start.9 = (bf16[48,1024]{1,0:T(8,128)(2,1)S(1)}, bf16[48,1024]{1,0:T(8,128)(2,1)S(1)}, u32[]{:S(2)}, u32[]{:S(2)}) collective-permute-start(bf16[48,1024]{1,0:T(8,128)(2,1)S(1)} %pad_maximum_fusion.h0), channel_id=1, source_target_pairs={{0,24},{8,0},{16,8},{24,16},{1,25},{9,1},{17,9},{25,17},{2,26},{10... | collective-permute-start | bytes 294920 | tf_op jit(solution)/shard_map/ppermute | solution.py:186
  22.7 0.3 collective-permute-start.8
  23.1 0.0 copy-done.2
  23.1 3.1 %collective-permute-start.5 = (bf16[32,4096]{1,0:T(8,128)(2,1)S(1)}, bf16[32,4096]{1,0:T(8,128)(2,1)S(1)}, u32[]{:S(2)}, u32[]{:S(2)}) collective-permute-start(bf16[32,4096]{1,0:T(8,128)(2,1)S(1)} %bitcast.20), channel_id=1, source_target_pairs={{0,3},{1,0},{2,1},{3,2},{4,7},{5,4},{6,5},{7,6},{8,11},{9,8},{10,9... | collective-permute-start | bytes 786440 | tf_op jit(solution)/shard_map/ppermute | solution.py:186
  26.2 1.9 %collective-permute-start.4 = (bf16[32,4096]{1,0:T(8,128)(2,1)S(1)}, bf16[32,4096]{1,0:T(8,128)(2,1)S(1)}, u32[]{:S(2)}, u32[]{:S(2)}) collective-permute-start(bf16[32,4096]{1,0:T(8,128)(2,1)S(1)} %bitcast.21), channel_id=1, source_target_pairs={{0,2},{1,3},{2,0},{3,1},{4,6},{5,7},{6,4},{7,5},{8,10},{9,11},{10,... | collective-permute-start | bytes 786440 | tf_op jit(solution)/shard_map/ppermute | solution.py:186
  28.1 0.0 collective-permute-done.10.c0
  28.1 1.0 collective-permute-start.3
  29.1 0.0 collective-permute-done.9.h3
  29.1 0.7 collective-permute-start.7
  29.7 0.0 collective-permute-done.8.h2
  29.8 1.8 %collective-permute-start.13 = (bf16[48,1024]{1,0:T(8,128)(2,1)S(1)}, bf16[48,1024]{1,0:T(8,128)(2,1)S(1)}, u32[]{:S(2)}, u32[]{:S(2)}) collective-permute-start(bf16[48,1024]{1,0:T(8,128)(2,1)S(1)} %collective-permute-done.9.h3), channel_id=1, source_target_pairs={{0,4},{4,0},{1,5},{5,1},{2,6},{6,2},{3,7},{7,3},{8,12},{12,8},{9,1... | collective-permute-start | bytes 294920 | tf_op jit(solution)/shard_map/ppermute | solution.py:190
  31.5 2.4 %collective-permute-done.7.h1 = bf16[48,1024]{1,0:T(8,128)(2,1)S(1)} collective-permute-done((bf16[48,1024]{1,0:T(8,128)(2,1)S(1)}, bf16[48,1024]{1,0:T(8,128)(2,1)S(1)}, u32[]{:S(2)}, u32[]{:S(2)}) %collective-permute-start.7) | collective-permute-done | bytes 98336 | tf_op jit(solution)/shard_map/ppermute | solution.py:186
  33.9 2.5 %collective-permute-start.12 = (bf16[48,1024]{1,0:T(8,128)(2,1)S(1)}, bf16[48,1024]{1,0:T(8,128)(2,1)S(1)}, u32[]{:S(2)}, u32[]{:S(2)}) collective-permute-start(bf16[48,1024]{1,0:T(8,128)(2,1)S(1)} %collective-permute-done.8.h2), channel_id=1, source_target_pairs={{0,4},{4,0},{1,5},{5,1},{2,6},{6,2},{3,7},{7,3},{8,12},{12,8},{9,1... | collective-permute-start | bytes 294920 | tf_op jit(solution)/shard_map/ppermute | solution.py:190
  36.4 0.0 collective-permute-done.13.c3
  36.4 0.0 collective-permute-start.11
  36.4 0.9 collective-permute-done.12.c2
  37.3 0.4 collective-permute-done.11.c1
  37.7 0.9 shard_map.87
  38.6 2.8 %collective-permute-start.14 = (bf16[32,1024]{1,0:T(8,128)(2,1)S(1)}, bf16[32,1024]{1,0:T(8,128)(2,1)S(1)}, u32[]{:S(2)}, u32[]{:S(2)}) collective-permute-start(bf16[32,1024]{1,0:T(8,128)(2,1)S(1)} %get-tuple-element.44), channel_id=1, source_target_pairs={{0,1},{1,2},{2,3},{3,0},{4,5},{5,6},{6,7},{7,4},{8,9},{9,10},{10,1... | collective-permute-start | bytes 196616 | tf_op jit(solution)/shard_map/ppermute | solution.py:186
  41.4 1.9 %collective-permute-start.15 = (bf16[32,1024]{1,0:T(8,128)(2,1)S(1)}, bf16[32,1024]{1,0:T(8,128)(2,1)S(1)}, u32[]{:S(2)}, u32[]{:S(2)}) collective-permute-start(bf16[32,1024]{1,0:T(8,128)(2,1)S(1)} %get-tuple-element.45), channel_id=1, source_target_pairs={{0,2},{1,3},{2,0},{3,1},{4,6},{5,7},{6,4},{7,5},{8,10},{9,11},{10,... | collective-permute-start | bytes 196616 | tf_op jit(solution)/shard_map/ppermute | solution.py:186
  43.3 0.2 collective-permute-done.5.a3
  43.5 3.3 %collective-permute-start.16 = (bf16[32,1024]{1,0:T(8,128)(2,1)S(1)}, bf16[32,1024]{1,0:T(8,128)(2,1)S(1)}, u32[]{:S(2)}, u32[]{:S(2)}) collective-permute-start(bf16[32,1024]{1,0:T(8,128)(2,1)S(1)} %get-tuple-element.46), channel_id=1, source_target_pairs={{0,3},{1,0},{2,1},{3,2},{4,7},{5,4},{6,5},{7,6},{8,11},{9,8},{10,9... | collective-permute-start | bytes 196616 | tf_op jit(solution)/shard_map/ppermute | solution.py:186
  46.8 0.0 copy-done
  46.8 0.0 copy-done.5
  46.8 0.0 copy-start.4
  46.8 0.5 shard_map.85
  47.3 0.0 collective-permute-done.4.a2
  47.3 3.3 %collective-permute-done.3.a1 = bf16[32,4096]{1,0:T(8,128)(2,1)S(1)} collective-permute-done((bf16[32,4096]{1,0:T(8,128)(2,1)S(1)}, bf16[32,4096]{1,0:T(8,128)(2,1)S(1)}, u32[]{:S(2)}, u32[]{:S(2)}) %collective-permute-start.3) | collective-permute-done | bytes 262176 | tf_op jit(solution)/shard_map/ppermute | solution.py:186
  50.7 0.0 copy-done.4
  50.7 0.6 shard_map.86
  51.2 4.4 %collective-permute-start.6 = (f32[16,128]{1,0:T(8,128)S(1)}, f32[16,128]{1,0:T(8,128)S(1)}, u32[]{:S(2)}, u32[]{:S(2)}) collective-permute-start(f32[16,128]{1,0:T(8,128)S(1)} %get-tuple-element.39), channel_id=1, source_target_pairs={{0,4},{4,0},{1,5},{5,1},{2,6},{6,2},{3,7},{7,3},{8,12},{12,8},{9,1... | collective-permute-start | bytes 24584 | tf_op jit(solution)/shard_map/ppermute | solution.py:190
  55.7 0.8 collective-permute-done.6
  56.5 0.0 collective-permute-done.14.i1
  56.5 0.0 collective-permute-done.15.i2
  56.5 0.4 collective-permute-done.16.i3
  56.9 18.3 %all_to_all.15 = f32[32,16,128]{2,1,0:T(8,128)S(1)} all-to-all(f32[32,16,128]{2,1,0:T(8,128)S(1)} %broadcast_in_dim.18), channel_id=1, replica_groups=mesh['x'=4,'zl'=2,'y'=4,'core'=2,'t'=4] {'x','zl','y'}, dimensions={0} | all-to-all | bytes 524288 | tf_op jit(solution)/shard_map/all_to_all | solution.py:194
  75.2 2.1 %collective-permute-start.17 = (f32[16,128]{1,0:T(8,128)S(1)}, f32[16,128]{1,0:T(8,128)S(1)}, u32[]{:S(2)}, u32[]{:S(2)}) collective-permute-start(f32[16,128]{1,0:T(8,128)S(1)} %reduce_sum.9.lown), channel_id=1, source_target_pairs={{0,4},{4,0},{1,5},{5,1},{2,6},{6,2},{3,7},{7,3},{8,12},{12,8},{9,1... | collective-permute-start | bytes 24584 | tf_op jit(solution)/shard_map/ppermute | solution.py:190
  77.3 0.8 collective-permute-done.17.loth
  78.1 3.8 %shard_map.88 = (f32[32,128]{1,0:T(8,128)}, f32[32,16,128]{2,1,0:T(8,128)S(1)}, f32[32,16,128]{2,1,0:T(8,128)S(1)}) custom-call(f32[16,128]{1,0:T(8,128)S(1)} %reduce_sum.9.lown, f32[16,128]{1,0:T(8,128)S(1)} %collective-permute-done.17.loth, bf16[32,4096]{1,0:T(8,128)(2,1)S(1)} %bitcast.24, bf16[32,4096]{1,0:T(8,128)(2,1)S(1)} %collective-permute-done.3.a1, ...), custom_call_target="tpu_custom_call" | custom-call | flops 100000000 | bytes 3000000 | tf_op jit(solution)/shard_map/pallas_call | solution.py:52
  81.9 0.3 collective-permute-start.18
  82.2 1.2 %collective-permute-done.18 = f32[32,16,128]{2,1,0:T(8,128)S(1)} collective-permute-done((f32[32,16,128]{2,1,0:T(8,128)S(1)}, f32[32,16,128]{2,1,0:T(8,128)S(1)}, u32[]{:S(2)}, u32[]{:S(2)}) %collective-permute-start.18) | collective-permute-done | bytes 262176 | tf_op jit(solution)/shard_map/ppermute | solution.py:190
  83.5 11.4 %all_to_all.16.pieces = f32[32,16,128]{2,1,0:T(8,128)S(1)} all-to-all(f32[32,16,128]{2,1,0:T(8,128)S(1)} %add.7), channel_id=1, replica_groups=mesh['x'=4,'zl'=2,'y'=4,'core'=2,'t'=4] {'x','zl','y'}, dimensions={0} | all-to-all | bytes 524288 | tf_op jit(solution)/shard_map/all_to_all | solution.py:194
  94.9 0.1 shard_map.89
  95.0 0.0 copy-start.6
  95.0 11.8 %all_to_all.17.rown = f32[32,16,128]{2,1,0:T(8,128)S(1)} all-to-all(f32[32,16,128]{2,1,0:T(8,128)S(1)} %shard_map.89), channel_id=1, replica_groups=mesh['x'=4,'zl'=2,'y'=4,'core'=2,'t'=4] {'x','zl','y'}, dimensions={0} | all-to-all | bytes 524288 | tf_op jit(solution)/shard_map/all_to_all | solution.py:194
  106.7 3.0 %collective-permute-start.19 = (f32[32,16,128]{2,1,0:T(8,128)S(1)}, f32[32,16,128]{2,1,0:T(8,128)S(1)}, u32[]{:S(2)}, u32[]{:S(2)}) collective-permute-start(f32[32,16,128]{2,1,0:T(8,128)S(1)} %all_to_all.17.rown), channel_id=1, source_target_pairs={{0,4},{4,0},{1,5},{5,1},{2,6},{6,2},{3,7},{7,3},{8,12},{12,8},{9,1... | collective-permute-start | bytes 786440 | tf_op jit(solution)/shard_map/ppermute | solution.py:190
  109.7 1.2 %collective-permute-done.19.roth = f32[32,16,128]{2,1,0:T(8,128)S(1)} collective-permute-done((f32[32,16,128]{2,1,0:T(8,128)S(1)}, f32[32,16,128]{2,1,0:T(8,128)S(1)}, u32[]{:S(2)}, u32[]{:S(2)}) %collective-permute-start.19) | collective-permute-done | bytes 262176 | tf_op jit(solution)/shard_map/ppermute | solution.py:190
  110.9 0.0 copy-done.6
  110.9 1.5 %shard_map.90 = (bf16[128,4096]{1,0:T(8,128)(2,1)}, bf16[32,4096]{1,0:T(8,128)(2,1)}, bf16[32,4096]{1,0:T(8,128)(2,1)}) custom-call(f32[32,16,128]{2,1,0:T(8,128)S(1)} %all_to_all.17.rown, f32[32,16,128]{2,1,0:T(8,128)S(1)} %collective-permute-done.19.roth, f32[32,128]{1,0:T(8,128)S(1)} %copy-done.6, bf16[128,128]{1,0:T(8,128)(2,1)S(1)} %bitcast.30, ...), custom_call_target="tpu_custom_call" | custom-call | flops 300000000 | bytes 5000000 | tf_op jit(solution)/shard_map/pallas_call | solution.py:52
  (9 shorter events, 0.1 us)
Async XLA Ops:
  0.6 1.2 %copy-start.1 = (bf16[1,128,4096]{2,1,0:T(8,128)(2,1)S(1)}, bf16[1,128,4096]{2,1,0:T(8,128)(2,1)}, u32[]{:S(2)}) copy-start(bf16[1,128,4096]{2,1,0:T(8,128)(2,1)} %param.7) | copy-start | bytes 3145732
  1.9 0.8 copy-start.3
  2.6 20.4 %copy-start.2 = (bf16[1,32,4096]{2,1,0:T(8,128)(2,1)S(1)}, bf16[1,32,4096]{2,1,0:T(8,128)(2,1)}, u32[]{:S(2)}) copy-start(bf16[1,32,4096]{2,1,0:T(8,128)(2,1)} %param.5) | copy-start | bytes 786436
  2.7 11.4 %collective-permute-start = (bf16[32,1024]{1,0:T(8,128)(2,1)S(1)}, bf16[32,1024]{1,0:T(8,128)(2,1)S(1)}, u32[]{:S(2)}, u32[]{:S(2)}) collective-permute-start(bf16[32,1024]{1,0:T(8,128)(2,1)S(1)} %get-tuple-element.31), channel_id=1, source_target_pairs={{0,1},{1,2},{2,3},{3,0},{4,5},{5,6},{6,7},{7,4},{8,9},{9,10},{10,1... | collective-permute-start | bytes 196616 | tf_op jit(solution)/shard_map/ppermute | solution.py:186
  6.6 7.9 %collective-permute-start.1 = (bf16[32,1024]{1,0:T(8,128)(2,1)S(1)}, bf16[32,1024]{1,0:T(8,128)(2,1)S(1)}, u32[]{:S(2)}, u32[]{:S(2)}) collective-permute-start(bf16[32,1024]{1,0:T(8,128)(2,1)S(1)} %get-tuple-element.32), channel_id=1, source_target_pairs={{0,2},{1,3},{2,0},{3,1},{4,6},{5,7},{6,4},{7,5},{8,10},{9,11},{10,... | collective-permute-start | bytes 196616 | tf_op jit(solution)/shard_map/ppermute | solution.py:186
  11.7 7.7 %collective-permute-start.2 = (bf16[32,1024]{1,0:T(8,128)(2,1)S(1)}, bf16[32,1024]{1,0:T(8,128)(2,1)S(1)}, u32[]{:S(2)}, u32[]{:S(2)}) collective-permute-start(bf16[32,1024]{1,0:T(8,128)(2,1)S(1)} %get-tuple-element.33), channel_id=1, source_target_pairs={{0,3},{1,0},{2,1},{3,2},{4,7},{5,4},{6,5},{7,6},{8,11},{9,8},{10,9... | collective-permute-start | bytes 196616 | tf_op jit(solution)/shard_map/ppermute | solution.py:186
  19.4 27.4 %copy-start = (bf16[1,1,128,4096]{3,2,1,0:T(8,128)(2,1)S(1)}, bf16[1,1,128,4096]{3,2,1,0:T(8,128)(2,1)}, u32[]{:S(2)}) copy-start(bf16[1,1,128,4096]{3,2,1,0:T(8,128)(2,1)} %param.8) | copy-start | bytes 3145732
  19.4 27.4 %copy-start.5 = (bf16[1,1,4096,32]{2,3,1,0:T(8,128)(2,1)S(1)}, bf16[1,1,4096,32]{2,3,1,0:T(8,128)(2,1)}, u32[]{:S(2)}) copy-start(bf16[1,1,4096,32]{2,3,1,0:T(8,128)(2,1)} %param.9) | copy-start | bytes 786436
  19.4 8.7 %collective-permute-start.10 = (bf16[48,1024]{1,0:T(8,128)(2,1)S(1)}, bf16[48,1024]{1,0:T(8,128)(2,1)S(1)}, u32[]{:S(2)}, u32[]{:S(2)}) collective-permute-start(bf16[48,1024]{1,0:T(8,128)(2,1)S(1)} %pad_maximum_fusion.h0), channel_id=1, source_target_pairs={{0,4},{4,0},{1,5},{5,1},{2,6},{6,2},{3,7},{7,3},{8,12},{12,8},{9,1... | collective-permute-start | bytes 294920 | tf_op jit(solution)/shard_map/ppermute | solution.py:190
  20.0 9.1 %collective-permute-start.9 = (bf16[48,1024]{1,0:T(8,128)(2,1)S(1)}, bf16[48,1024]{1,0:T(8,128)(2,1)S(1)}, u32[]{:S(2)}, u32[]{:S(2)}) collective-permute-start(bf16[48,1024]{1,0:T(8,128)(2,1)S(1)} %pad_maximum_fusion.h0), channel_id=1, source_target_pairs={{0,24},{8,0},{16,8},{24,16},{1,25},{9,1},{17,9},{25,17},{2,26},{10... | collective-permute-start | bytes 294920 | tf_op jit(solution)/shard_map/ppermute | solution.py:186
  22.7 7.0 %collective-permute-start.8 = (bf16[48,1024]{1,0:T(8,128)(2,1)S(1)}, bf16[48,1024]{1,0:T(8,128)(2,1)S(1)}, u32[]{:S(2)}, u32[]{:S(2)}) collective-permute-start(bf16[48,1024]{1,0:T(8,128)(2,1)S(1)} %pad_maximum_fusion.h0), channel_id=1, source_target_pairs={{0,16},{8,24},{16,0},{24,8},{1,17},{9,25},{17,1},{25,9},{2,18},{10... | collective-permute-start | bytes 294920 | tf_op jit(solution)/shard_map/ppermute | solution.py:186
  23.1 20.4 %collective-permute-start.5 = (bf16[32,4096]{1,0:T(8,128)(2,1)S(1)}, bf16[32,4096]{1,0:T(8,128)(2,1)S(1)}, u32[]{:S(2)}, u32[]{:S(2)}) collective-permute-start(bf16[32,4096]{1,0:T(8,128)(2,1)S(1)} %bitcast.20), channel_id=1, source_target_pairs={{0,3},{1,0},{2,1},{3,2},{4,7},{5,4},{6,5},{7,6},{8,11},{9,8},{10,9... | collective-permute-start | bytes 786440 | tf_op jit(solution)/shard_map/ppermute | solution.py:186
  26.2 21.1 %collective-permute-start.4 = (bf16[32,4096]{1,0:T(8,128)(2,1)S(1)}, bf16[32,4096]{1,0:T(8,128)(2,1)S(1)}, u32[]{:S(2)}, u32[]{:S(2)}) collective-permute-start(bf16[32,4096]{1,0:T(8,128)(2,1)S(1)} %bitcast.21), channel_id=1, source_target_pairs={{0,2},{1,3},{2,0},{3,1},{4,6},{5,7},{6,4},{7,5},{8,10},{9,11},{10,... | collective-permute-start | bytes 786440 | tf_op jit(solution)/shard_map/ppermute | solution.py:186
  28.1 22.6 %collective-permute-start.3 = (bf16[32,4096]{1,0:T(8,128)(2,1)S(1)}, bf16[32,4096]{1,0:T(8,128)(2,1)S(1)}, u32[]{:S(2)}, u32[]{:S(2)}) collective-permute-start(bf16[32,4096]{1,0:T(8,128)(2,1)S(1)} %bitcast.22), channel_id=1, source_target_pairs={{0,1},{1,2},{2,3},{3,0},{4,5},{5,6},{6,7},{7,4},{8,9},{9,10},{10,1... | collective-permute-start | bytes 786440 | tf_op jit(solution)/shard_map/ppermute | solution.py:186
  29.1 4.8 %collective-permute-start.7 = (bf16[48,1024]{1,0:T(8,128)(2,1)S(1)}, bf16[48,1024]{1,0:T(8,128)(2,1)S(1)}, u32[]{:S(2)}, u32[]{:S(2)}) collective-permute-start(bf16[48,1024]{1,0:T(8,128)(2,1)S(1)} %pad_maximum_fusion.h0), channel_id=1, source_target_pairs={{0,8},{8,16},{16,24},{24,0},{1,9},{9,17},{17,25},{25,1},{2,10},{10... | collective-permute-start | bytes 294920 | tf_op jit(solution)/shard_map/ppermute | solution.py:186
  29.8 6.6 %collective-permute-start.13 = (bf16[48,1024]{1,0:T(8,128)(2,1)S(1)}, bf16[48,1024]{1,0:T(8,128)(2,1)S(1)}, u32[]{:S(2)}, u32[]{:S(2)}) collective-permute-start(bf16[48,1024]{1,0:T(8,128)(2,1)S(1)} %collective-permute-done.9.h3), channel_id=1, source_target_pairs={{0,4},{4,0},{1,5},{5,1},{2,6},{6,2},{3,7},{7,3},{8,12},{12,8},{9,1... | collective-permute-start | bytes 294920 | tf_op jit(solution)/shard_map/ppermute | solution.py:190
  33.9 3.4 %collective-permute-start.12 = (bf16[48,1024]{1,0:T(8,128)(2,1)S(1)}, bf16[48,1024]{1,0:T(8,128)(2,1)S(1)}, u32[]{:S(2)}, u32[]{:S(2)}) collective-permute-start(bf16[48,1024]{1,0:T(8,128)(2,1)S(1)} %collective-permute-done.8.h2), channel_id=1, source_target_pairs={{0,4},{4,0},{1,5},{5,1},{2,6},{6,2},{3,7},{7,3},{8,12},{12,8},{9,1... | collective-permute-start | bytes 294920 | tf_op jit(solution)/shard_map/ppermute | solution.py:190
  36.4 1.3 %collective-permute-start.11 = (bf16[48,1024]{1,0:T(8,128)(2,1)S(1)}, bf16[48,1024]{1,0:T(8,128)(2,1)S(1)}, u32[]{:S(2)}, u32[]{:S(2)}) collective-permute-start(bf16[48,1024]{1,0:T(8,128)(2,1)S(1)} %collective-permute-done.7.h1), channel_id=1, source_target_pairs={{0,4},{4,0},{1,5},{5,1},{2,6},{6,2},{3,7},{7,3},{8,12},{12,8},{9,1... | collective-permute-start | bytes 294920 | tf_op jit(solution)/shard_map/ppermute | solution.py:190
  38.6 17.9 %collective-permute-start.14 = (bf16[32,1024]{1,0:T(8,128)(2,1)S(1)}, bf16[32,1024]{1,0:T(8,128)(2,1)S(1)}, u32[]{:S(2)}, u32[]{:S(2)}) collective-permute-start(bf16[32,1024]{1,0:T(8,128)(2,1)S(1)} %get-tuple-element.44), channel_id=1, source_target_pairs={{0,1},{1,2},{2,3},{3,0},{4,5},{5,6},{6,7},{7,4},{8,9},{9,10},{10,1... | collective-permute-start | bytes 196616 | tf_op jit(solution)/shard_map/ppermute | solution.py:186
  41.4 15.1 %collective-permute-start.15 = (bf16[32,1024]{1,0:T(8,128)(2,1)S(1)}, bf16[32,1024]{1,0:T(8,128)(2,1)S(1)}, u32[]{:S(2)}, u32[]{:S(2)}) collective-permute-start(bf16[32,1024]{1,0:T(8,128)(2,1)S(1)} %get-tuple-element.45), channel_id=1, source_target_pairs={{0,2},{1,3},{2,0},{3,1},{4,6},{5,7},{6,4},{7,5},{8,10},{9,11},{10,... | collective-permute-start | bytes 196616 | tf_op jit(solution)/shard_map/ppermute | solution.py:186
  43.5 13.4 %collective-permute-start.16 = (bf16[32,1024]{1,0:T(8,128)(2,1)S(1)}, bf16[32,1024]{1,0:T(8,128)(2,1)S(1)}, u32[]{:S(2)}, u32[]{:S(2)}) collective-permute-start(bf16[32,1024]{1,0:T(8,128)(2,1)S(1)} %get-tuple-element.46), channel_id=1, source_target_pairs={{0,3},{1,0},{2,1},{3,2},{4,7},{5,4},{6,5},{7,6},{8,11},{9,8},{10,9... | collective-permute-start | bytes 196616 | tf_op jit(solution)/shard_map/ppermute | solution.py:186
  46.8 3.9 %copy-start.4 = (bf16[1,128,128]{2,1,0:T(8,128)(2,1)S(1)}, bf16[1,128,128]{2,1,0:T(8,128)(2,1)}, u32[]{:S(2)}) copy-start(bf16[1,128,128]{2,1,0:T(8,128)(2,1)} %param.6) | copy-start | bytes 98308
  51.2 5.3 %collective-permute-start.6 = (f32[16,128]{1,0:T(8,128)S(1)}, f32[16,128]{1,0:T(8,128)S(1)}, u32[]{:S(2)}, u32[]{:S(2)}) collective-permute-start(f32[16,128]{1,0:T(8,128)S(1)} %get-tuple-element.39), channel_id=1, source_target_pairs={{0,4},{4,0},{1,5},{5,1},{2,6},{6,2},{3,7},{7,3},{8,12},{12,8},{9,1... | collective-permute-start | bytes 24584 | tf_op jit(solution)/shard_map/ppermute | solution.py:190
  75.2 2.9 %collective-permute-start.17 = (f32[16,128]{1,0:T(8,128)S(1)}, f32[16,128]{1,0:T(8,128)S(1)}, u32[]{:S(2)}, u32[]{:S(2)}) collective-permute-start(f32[16,128]{1,0:T(8,128)S(1)} %reduce_sum.9.lown), channel_id=1, source_target_pairs={{0,4},{4,0},{1,5},{5,1},{2,6},{6,2},{3,7},{7,3},{8,12},{12,8},{9,1... | collective-permute-start | bytes 24584 | tf_op jit(solution)/shard_map/ppermute | solution.py:190
  81.9 1.5 %collective-permute-start.18 = (f32[32,16,128]{2,1,0:T(8,128)S(1)}, f32[32,16,128]{2,1,0:T(8,128)S(1)}, u32[]{:S(2)}, u32[]{:S(2)}) collective-permute-start(f32[32,16,128]{2,1,0:T(8,128)S(1)} %get-tuple-element.49), channel_id=1, source_target_pairs={{0,4},{4,0},{1,5},{5,1},{2,6},{6,2},{3,7},{7,3},{8,12},{12,8},{9,1... | collective-permute-start | bytes 786440 | tf_op jit(solution)/shard_map/ppermute | solution.py:190
  95.0 15.9 %copy-start.6 = (f32[32,128]{1,0:T(8,128)S(1)}, f32[32,128]{1,0:T(8,128)}, u32[]{:S(2)}) copy-start(f32[32,128]{1,0:T(8,128)} %get-tuple-element.50.qt) | copy-start | bytes 49156
  106.7 4.1 %collective-permute-start.19 = (f32[32,16,128]{2,1,0:T(8,128)S(1)}, f32[32,16,128]{2,1,0:T(8,128)S(1)}, u32[]{:S(2)}, u32[]{:S(2)}) collective-permute-start(f32[32,16,128]{2,1,0:T(8,128)S(1)} %all_to_all.17.rown), channel_id=1, source_target_pairs={{0,4},{4,0},{1,5},{5,1},{2,6},{6,2},{3,7},{7,3},{8,12},{12,8},{9,1... | collective-permute-start | bytes 786440 | tf_op jit(solution)/shard_map/ppermute | solution.py:190

commit v5 on v4

--- a/solution.py
+++ b/solution.py
@@ -201,25 +201,13 @@
 
     sends = call(pack_kernel, [((2 * CUT, PART), BF16)] * 3)(weight, og)
     got = [moved(x, k) for k, x in zip((1, 2, 3), sends)]
-    act, got = lax.optimization_barrier((act, got))
     acts = [act] + [moved(act, k) for k in (1, 2, 3)]
     inner, fed, lines = call(
         early_kernel,
         [((RANK, OWN), F32), ((RANK, HEAD), F32), ((RANK, WIDE), BF16)],
-        flops=0,
-        moved=0,
+        flops=10**8,
+        moved=3 * 10**6,
     )(act, ef, warm)
-
-    shares = [jnp.concatenate([g[:CUT] for g in got], axis=0)]
-    shares += [moved(shares[0], j, "y") for j in (1, 2, 3)]
-    outs = call(
-        input_kernel,
-        [((OWN, PART), BF16)] * 4,
-        [pltpu.VMEM((512, PART), BF16), pltpu.VMEM((128, 512), BF16)],
-        flops=0,
-        moved=0,
-    )(weight, og, *got, *shares, *[swapped(x) for x in shares])
-    inputs = [outs[0]] + [moved(o, k) for k, o in zip((1, 2, 3), outs[1:])]
 
     half = ((HALF, HEAD), F32)
     left_keep, left_send = call(
@@ -227,7 +215,10 @@
     )(*acts[1:], og, lines, inner, fed)
 
     left_half = left_keep + swapped(left_send)
-    left_half, inputs = lax.optimization_barrier((left_half, inputs))
+    left_half, got = lax.optimization_barrier((left_half, got))
+    shares = [jnp.concatenate([g[:CUT] for g in got], axis=0)]
+    shares += [moved(shares[0], j, "y") for j in (1, 2, 3)]
+    traded = [swapped(x) for x in shares]
     pieces = exchanged(jnp.broadcast_to(left_half[None], (N_CHIPS, HALF, HEAD)), CHIPS)
     left_own = jnp.sum(pieces, axis=0)
     left_other = swapped(left_own)
@@ -241,9 +232,20 @@
         moved=3 * 10**6,
     )(left_own, left_other, *acts, og, ef)
 
+    right_send, shares, traded = lax.optimization_barrier((right_send, shares, traded))
+    outs = call(
+        input_kernel,
+        [((OWN, PART), BF16)] * 4,
+        [pltpu.VMEM((512, PART), BF16), pltpu.VMEM((128, 512), BF16)],
+        flops=2 * 10**8,
+        moved=2 * 10**6,
+    )(weight, og, *got, *shares, *traded)
     pieces = exchanged(right_keep + swapped(right_send), CHIPS)
+    pieces, outs = lax.optimization_barrier((pieces, outs))
     (mean,) = call(spread_kernel, [block])(pieces)
+    inputs = [outs[0]] + [moved(o, k) for k, o in zip((1, 2, 3), outs[1:])]
     right_own = exchanged(mean, CHIPS)
+    right_own, inputs = lax.optimization_barrier((right_own, inputs))
     right_other = swapped(right_own)
 
     err, fac, igrad = call(

time: 113 us -> 110 us (0.973)
  blocking collectives: 41.5 us -> 0 us
  starting transfers between devices: 43.8 us -> 71.4 us
  local copies, waits for them, and re-layouts: 2.03 us -> 10.8 us
  Pallas kernels: 7.29 us -> 9.01 us
    all_to_all x3 -> x0, blocking collectives: 41.5 us -> none  [exchanged(): return lax.all_to_all(x, axes, 0, 0, tiled=True)]
    all_to_all x0 -> x3, starting transfers between devices: none -> 18 us  [exchanged(): return lax.all_to_all(x, axes, 0, 0, tiled=True)]
    unnamed x14 -> x50, local copies, waits for them, and re-layouts: 2 us -> 9.37 us
    ppermute x8, starting transfers between devices: 14.6 us -> 20.4 us  [swapped(): return lax.ppermute(x, 'core', [(0, 1), (1, 0)])]
    ppermute x12, starting transfers between devices: 29.2 us -> 33.1 us  [moved(): return lax.ppermute(x, axis, [(i, (i + k) % 4) for i in range(4)])]
    pallas_call x7, Pallas kernels: 7.29 us -> 9.01 us  [run(): pl.pallas_call(kernel, out_shape=[jax.ShapeDtypeStruct(s, d) for s, d in...]
    ppermute x12, waiting for transfers between devices: 11.6 us -> 9.99 us  [moved(): return lax.ppermute(x, axis, [(i, (i + k) % 4) for i in range(4)])]
    all_to_all x0 -> x3, waiting for transfers between devices: none -> 1.54 us  [exchanged(): return lax.all_to_all(x, axes, 0, 0, tiled=True)]
  transfers between devices with their start and end apart: 20 -> 23, of which waited for: 12 -> 10; matrix products, arithmetic and copies ran while one was open for 0% -> 0% of each run, Pallas kernels for 2% -> 6%
where the time goes in v5:
time: 110 us; the launch traced here: 109 us
  starting transfers between devices  71.4 us (65%)
  waiting for transfers between devices  16.1 us (15%)
  local copies, waits for them, and re-layouts  10.8 us (10%)
  Pallas kernels  9.01 us (8%)
    ppermute x12, starting transfers between devices, moved(): return lax.ppermute(x, axis, [(i, (i + k) % 4) for i in range(4)])  33.1 us
    ppermute x8, starting transfers between devices, swapped(): return lax.ppermute(x, 'core', [(0, 1), (1, 0)])  20.4 us
    all_to_all x3, starting transfers between devices, exchanged(): return lax.all_to_all(x, axes, 0, 0, tiled=True)  18 us
    ppermute x12, waiting for transfers between devices, moved(): return lax.ppermute(x, axis, [(i, (i + k) % 4) for i in range(4)])  9.99 us
    unnamed x50, local copies, waits for them, and re-layouts  9.37 us
    pallas_call x7, Pallas kernels, run(): pl.pallas_call(kernel, out_shape=[jax.ShapeDtypeStruct(s, d) for s, d in...  9.01 us
    ppermute x8, waiting for transfers between devices, swapped(): return lax.ppermute(x, 'core', [(0, 1), (1, 0)])  4.53 us
  transfers between devices with their start and end apart: 23, of which 10 were waited for; matrix products, arithmetic and copies ran while one was open for 0% of the time, Pallas kernels for 6%

profile of v5, /device:TPU:1, one launch (start us, length us, event | category | flops | bytes accessed | tf_op | source)
XLA Modules:
  0.0 109.0 jit_solution(653919644653432044)
XLA Ops:
  0.6 6.9 %collective-permute-start.2 = (bf16[32,4096]{1,0:T(8,128)(2,1)}, bf16[32,4096]{1,0:T(8,128)(2,1)S(1)}, u32[]{:S(2)}, u32[]{:S(2)}) collective-permute-start(bf16[32,4096]{1,0:T(8,128)(2,1)} %bitcast.20), channel_id=1, source_target_pairs={{0,3},{1,0},{2,1},{3,2},{4,7},{5,4},{6,5},{7,6},{8,11},{9,8},{10,9... | collective-permute-start | bytes 786440 | tf_op jit(solution)/shard_map/ppermute | solution.py:186
  7.6 1.0 collective-permute-start.1
  8.6 2.3 %collective-permute-start = (bf16[32,4096]{1,0:T(8,128)(2,1)}, bf16[32,4096]{1,0:T(8,128)(2,1)S(1)}, u32[]{:S(2)}, u32[]{:S(2)}) collective-permute-start(bf16[32,4096]{1,0:T(8,128)(2,1)} %bitcast.22), channel_id=1, source_target_pairs={{0,1},{1,2},{2,3},{3,0},{4,5},{5,6},{6,7},{7,4},{8,9},{9,10},{10,1... | collective-permute-start | bytes 786440 | tf_op jit(solution)/shard_map/ppermute | solution.py:186
  10.8 1.2 %copy-done.1 = bf16[1,128,4096]{2,1,0:T(8,128)(2,1)S(1)} copy-done((bf16[1,128,4096]{2,1,0:T(8,128)(2,1)S(1)}, bf16[1,128,4096]{2,1,0:T(8,128)(2,1)}, u32[]{:S(2)}) %copy-start.1) | copy-done | bytes 1048600
  12.1 0.8 copy-done.5
  12.8 2.5 %collective-permute-start.4 = (bf16[32,1024]{1,0:T(8,128)(2,1)S(1)}, bf16[32,1024]{1,0:T(8,128)(2,1)S(1)}, u32[]{:S(2)}, u32[]{:S(2)}) collective-permute-start(bf16[32,1024]{1,0:T(8,128)(2,1)S(1)} %get-tuple-element.50), channel_id=1, source_target_pairs={{0,1},{1,2},{2,3},{3,0},{4,5},{5,6},{6,7},{7,4},{8,9},{9,10},{10,1... | collective-permute-start | bytes 196616 | tf_op jit(solution)/shard_map/ppermute | solution.py:186
  15.3 1.0 collective-permute-start.5
  16.3 3.4 %collective-permute-done.2.a3 = bf16[32,4096]{1,0:T(8,128)(2,1)S(1)} collective-permute-done((bf16[32,4096]{1,0:T(8,128)(2,1)}, bf16[32,4096]{1,0:T(8,128)(2,1)S(1)}, u32[]{:S(2)}, u32[]{:S(2)}) %collective-permute-start.2) | collective-permute-done | bytes 262176 | tf_op jit(solution)/shard_map/ppermute | solution.py:186
  19.7 11.6 %collective-permute-start.6 = (bf16[32,1024]{1,0:T(8,128)(2,1)S(1)}, bf16[32,1024]{1,0:T(8,128)(2,1)S(1)}, u32[]{:S(2)}, u32[]{:S(2)}) collective-permute-start(bf16[32,1024]{1,0:T(8,128)(2,1)S(1)} %get-tuple-element.52), channel_id=1, source_target_pairs={{0,3},{1,0},{2,1},{3,2},{4,7},{5,4},{6,5},{7,6},{8,11},{9,8},{10,9... | collective-permute-start | bytes 196616 | tf_op jit(solution)/shard_map/ppermute | solution.py:186
  31.4 0.9 copy-done.3
  32.3 0.9 copy-done.7
  33.3 0.5 shard_map.84
  33.8 0.0 collective-permute-done.a1
  33.8 0.2 copy-done.6
  34.0 0.5 shard_map.85
  34.6 8.9 %collective-permute-start.3 = (f32[16,128]{1,0:T(8,128)S(1)}, f32[16,128]{1,0:T(8,128)S(1)}, u32[]{:S(2)}, u32[]{:S(2)}) collective-permute-start(f32[16,128]{1,0:T(8,128)S(1)} %get-tuple-element.49), channel_id=1, source_target_pairs={{0,4},{4,0},{1,5},{5,1},{2,6},{6,2},{3,7},{7,3},{8,12},{12,8},{9,1... | collective-permute-start | bytes 24584 | tf_op jit(solution)/shard_map/ppermute | solution.py:190
  43.4 0.8 collective-permute-done.3
  44.3 0.0 collective-permute-done.4.r1
  44.3 0.0 collective-permute-done.5.r2
  44.3 0.7 broadcast_in_dim.18
  45.0 7.0 %all-to-all-start = ((f32[32,16,128]{2,1,0:T(8,128)}), f32[32,16,128]{2,1,0:T(8,128)S(1)}, u32[]{:S(2)}, u32[]{:S(2)}) async-start(f32[32,16,128]{2,1,0:T(8,128)} %broadcast_in_dim.18), calls=%async_computation | async-start | bytes 524288 | tf_op jit(solution)/shard_map/all_to_all | solution.py:194
  52.1 0.0 slice-start.1
  52.1 0.7 slice-done
  52.8 0.0 slice-done.1
  52.9 2.5 %collective-permute-start.10 = (bf16[48,1024]{1,0:T(8,128)(2,1)S(1)}, bf16[48,1024]{1,0:T(8,128)(2,1)S(1)}, u32[]{:S(2)}, u32[]{:S(2)}) collective-permute-start(bf16[48,1024]{1,0:T(8,128)(2,1)S(1)} %pad_maximum_fusion.h0), channel_id=1, source_target_pairs={{0,24},{8,0},{16,8},{24,16},{1,25},{9,1},{17,9},{25,17},{2,26},{10... | collective-permute-start | bytes 294920 | tf_op jit(solution)/shard_map/ppermute | solution.py:186
  55.4 0.6 collective-permute-start.9
  55.9 0.6 collective-permute-start.8
  56.5 1.7 %collective-permute-start.11 = (bf16[48,1024]{1,0:T(8,128)(2,1)S(1)}, bf16[48,1024]{1,0:T(8,128)(2,1)}, u32[]{:S(2)}, u32[]{:S(2)}) collective-permute-start(bf16[48,1024]{1,0:T(8,128)(2,1)S(1)} %pad_maximum_fusion.h0), channel_id=1, source_target_pairs={{0,4},{4,0},{1,5},{5,1},{2,6},{6,2},{3,7},{7,3},{8,12},{12,8},{9,1... | collective-permute-start | bytes 294920 | tf_op jit(solution)/shard_map/ppermute | solution.py:190
  58.3 1.4 %collective-permute-done.10.h3 = bf16[48,1024]{1,0:T(8,128)(2,1)S(1)} collective-permute-done((bf16[48,1024]{1,0:T(8,128)(2,1)S(1)}, bf16[48,1024]{1,0:T(8,128)(2,1)S(1)}, u32[]{:S(2)}, u32[]{:S(2)}) %collective-permute-start.10) | collective-permute-done | bytes 98336 | tf_op jit(solution)/shard_map/ppermute | solution.py:186
  59.6 2.6 %collective-permute-start.14 = (bf16[48,1024]{1,0:T(8,128)(2,1)S(1)}, bf16[48,1024]{1,0:T(8,128)(2,1)}, u32[]{:S(2)}, u32[]{:S(2)}) collective-permute-start(bf16[48,1024]{1,0:T(8,128)(2,1)S(1)} %collective-permute-done.10.h3), channel_id=1, source_target_pairs={{0,4},{4,0},{1,5},{5,1},{2,6},{6,2},{3,7},{7,3},{8,12},{12,8},{9,1... | collective-permute-start | bytes 294920 | tf_op jit(solution)/shard_map/ppermute | solution.py:190
  62.3 1.9 %collective-permute-start.13 = (bf16[48,1024]{1,0:T(8,128)(2,1)S(1)}, bf16[48,1024]{1,0:T(8,128)(2,1)}, u32[]{:S(2)}, u32[]{:S(2)}) collective-permute-start(bf16[48,1024]{1,0:T(8,128)(2,1)S(1)} %collective-permute-done.9.h2), channel_id=1, source_target_pairs={{0,4},{4,0},{1,5},{5,1},{2,6},{6,2},{3,7},{7,3},{8,12},{12,8},{9,1... | collective-permute-start | bytes 294920 | tf_op jit(solution)/shard_map/ppermute | solution.py:190
  64.2 0.6 collective-permute-done.8.h1
  64.8 0.5 collective-permute-start.12
  65.3 0.6 copy-done.16
  65.9 0.0 all-to-all-done
  66.0 0.1 collective-permute-start.7
  66.1 1.2 %collective-permute-done.7.loth = f32[16,128]{1,0:T(8,128)S(1)} collective-permute-done((f32[16,128]{1,0:T(8,128)S(1)}, f32[16,128]{1,0:T(8,128)S(1)}, u32[]{:S(2)}, u32[]{:S(2)}) %collective-permute-start.7) | collective-permute-done | bytes 8224 | tf_op jit(solution)/shard_map/ppermute | solution.py:190
  67.3 3.8 %shard_map.87 = (f32[32,128]{1,0:T(8,128)}, f32[32,16,128]{2,1,0:T(8,128)S(1)}, f32[32,16,128]{2,1,0:T(8,128)S(1)}) custom-call(f32[16,128]{1,0:T(8,128)S(1)} %reduce_sum.9.lown, f32[16,128]{1,0:T(8,128)S(1)} %collective-permute-done.7.loth, bf16[32,4096]{1,0:T(8,128)(2,1)S(1)} %bitcast.24, bf16[32,4096]{1,0:T(8,128)(2,1)S(1)} %collective-permute-done.a1, ...), custom_call_target="tpu_custom_call" | custom-call | flops 100000000 | bytes 3000000 | tf_op jit(solution)/shard_map/pallas_call | solution.py:52
  71.0 0.0 collective-permute-done.11.c0
  71.0 0.0 collective-permute-done.13.c2
  71.1 0.4 collective-permute-start.15
  71.5 1.4 %collective-permute-done.15 = f32[32,16,128]{2,1,0:T(8,128)S(1)} collective-permute-done((f32[32,16,128]{2,1,0:T(8,128)S(1)}, f32[32,16,128]{2,1,0:T(8,128)S(1)}, u32[]{:S(2)}, u32[]{:S(2)}) %collective-permute-start.15) | collective-permute-done | bytes 262176 | tf_op jit(solution)/shard_map/ppermute | solution.py:190
  72.9 0.7 add.7
  73.6 4.6 %all-to-all-start.1 = ((f32[32,16,128]{2,1,0:T(8,128)}), f32[32,16,128]{2,1,0:T(8,128)S(1)}, u32[]{:S(2)}, u32[]{:S(2)}) async-start(f32[32,16,128]{2,1,0:T(8,128)} %add.7), calls=%async_computation.1 | async-start | bytes 524288 | tf_op jit(solution)/shard_map/all_to_all | solution.py:194
  78.2 0.9 copy-done.13
  79.1 0.9 copy-done.15
  80.0 0.9 copy-done.17
  80.9 1.9 %shard_map.88 = (bf16[32,1024]{1,0:T(8,128)(2,1)S(1)}, bf16[32,1024]{1,0:T(8,128)(2,1)S(1)}, bf16[32,1024]{1,0:T(8,128)(2,1)S(1)}, bf16[32,1024]{1,0:T(8,128)(2,1)S(1)}) custom-call(bf16[128,4096]{1,0:T(8,128)(2,1)S(1)} %bitcast.19, bf16[128,128]{1,0:T(8,128)(2,1)S(1)} %bitcast.29, bf16[32,1024]{1,0:T(8,128)(2,1)S(1)} %copy-done.9, ...), custom_call_target="tpu_custom_call" | custom-call | flops 200000000 | bytes 2000000 | tf_op jit(solution)/shard_map/pallas_call | solution.py:52
  82.8 0.0 copy-start.19
  82.9 0.6 copy-done.19
  83.5 0.6 copy-done.21
  84.1 0.6 copy-done.23
  84.8 1.5 %all-to-all-done.1.pieces = f32[32,16,128]{2,1,0:T(8,128)S(1)} async-done(((f32[32,16,128]{2,1,0:T(8,128)}), f32[32,16,128]{2,1,0:T(8,128)S(1)}, u32[]{:S(2)}, u32[]{:S(2)}) %all-to-all-start.1) | async-done | bytes 262176 | tf_op jit(solution)/shard_map/all_to_all | solution.py:194
  86.3 0.8 shard_map.89
  87.1 0.0 copy-start.18
  87.1 6.3 %all-to-all-start.2 = ((f32[32,16,128]{2,1,0:T(8,128)}), f32[32,16,128]{2,1,0:T(8,128)S(1)}, u32[]{:S(2)}, u32[]{:S(2)}) async-start(f32[32,16,128]{2,1,0:T(8,128)} %shard_map.89), calls=%async_computation.2 | async-start | bytes 524288 | tf_op jit(solution)/shard_map/all_to_all | solution.py:194
  93.4 0.1 collective-permute-start.16
  93.5 3.4 %collective-permute-start.17 = (bf16[32,1024]{1,0:T(8,128)(2,1)S(1)}, bf16[32,1024]{1,0:T(8,128)(2,1)S(1)}, u32[]{:S(2)}, u32[]{:S(2)}) collective-permute-start(bf16[32,1024]{1,0:T(8,128)(2,1)S(1)} %copy-done.22), channel_id=1, source_target_pairs={{0,2},{1,3},{2,0},{3,1},{4,6},{5,7},{6,4},{7,5},{8,10},{9,11},{10,... | collective-permute-start | bytes 196616 | tf_op jit(solution)/shard_map/ppermute | solution.py:186
  96.9 0.7 collective-permute-start.18
  97.6 3.1 %collective-permute-done.16.i1 = bf16[32,1024]{1,0:T(8,128)(2,1)S(1)} collective-permute-done((bf16[32,1024]{1,0:T(8,128)(2,1)S(1)}, bf16[32,1024]{1,0:T(8,128)(2,1)S(1)}, u32[]{:S(2)}, u32[]{:S(2)}) %collective-permute-start.16) | collective-permute-done | bytes 65568 | tf_op jit(solution)/shard_map/ppermute | solution.py:186
  100.8 1.4 %collective-permute-done.17.i2 = bf16[32,1024]{1,0:T(8,128)(2,1)S(1)} collective-permute-done((bf16[32,1024]{1,0:T(8,128)(2,1)S(1)}, bf16[32,1024]{1,0:T(8,128)(2,1)S(1)}, u32[]{:S(2)}, u32[]{:S(2)}) %collective-permute-start.17) | collective-permute-done | bytes 65568 | tf_op jit(solution)/shard_map/ppermute | solution.py:186
  102.2 4.2 %collective-permute-start.19 = (f32[32,16,128]{2,1,0:T(8,128)S(1)}, f32[32,16,128]{2,1,0:T(8,128)S(1)}, u32[]{:S(2)}, u32[]{:S(2)}) collective-permute-start(f32[32,16,128]{2,1,0:T(8,128)S(1)} %all-to-all-done.2.rown), channel_id=1, source_target_pairs={{0,4},{4,0},{1,5},{5,1},{2,6},{6,2},{3,7},{7,3},{8,12},{12,8},{9,1... | collective-permute-start | bytes 786440 | tf_op jit(solution)/shard_map/ppermute | solution.py:190
  106.4 1.2 %collective-permute-done.19.roth = f32[32,16,128]{2,1,0:T(8,128)S(1)} collective-permute-done((f32[32,16,128]{2,1,0:T(8,128)S(1)}, f32[32,16,128]{2,1,0:T(8,128)S(1)}, u32[]{:S(2)}, u32[]{:S(2)}) %collective-permute-start.19) | collective-permute-done | bytes 262176 | tf_op jit(solution)/shard_map/ppermute | solution.py:190
  107.5 1.5 %shard_map.90 = (bf16[128,4096]{1,0:T(8,128)(2,1)}, bf16[32,4096]{1,0:T(8,128)(2,1)}, bf16[32,4096]{1,0:T(8,128)(2,1)}) custom-call(f32[32,16,128]{2,1,0:T(8,128)S(1)} %all-to-all-done.2.rown, f32[32,16,128]{2,1,0:T(8,128)S(1)} %collective-permute-done.19.roth, f32[32,128]{1,0:T(8,128)S(1)} %copy-done.18, bf16[128,128]{1,0:T(8,128)(2,1)S(1)} %bitcast.30, ...), custom_call_target="tpu_custom_call" | custom-call | flops 300000000 | bytes 5000000 | tf_op jit(solution)/shard_map/pallas_call | solution.py:52
  (49 shorter events, 0.2 us)
Async XLA Ops:
  0.6 30.7 %copy-start = (bf16[1,1,128,4096]{3,2,1,0:T(8,128)(2,1)S(1)}, bf16[1,1,128,4096]{3,2,1,0:T(8,128)(2,1)}, u32[]{:S(2)}) copy-start(bf16[1,1,128,4096]{3,2,1,0:T(8,128)(2,1)} %param.8) | copy-start | bytes 3145732
  0.6 19.1 %collective-permute-start.2 = (bf16[32,4096]{1,0:T(8,128)(2,1)}, bf16[32,4096]{1,0:T(8,128)(2,1)S(1)}, u32[]{:S(2)}, u32[]{:S(2)}) collective-permute-start(bf16[32,4096]{1,0:T(8,128)(2,1)} %bitcast.20), channel_id=1, source_target_pairs={{0,3},{1,0},{2,1},{3,2},{4,7},{5,4},{6,5},{7,6},{8,11},{9,8},{10,9... | collective-permute-start | bytes 786440 | tf_op jit(solution)/shard_map/ppermute | solution.py:186
  7.6 26.2 %collective-permute-start.1 = (bf16[32,4096]{1,0:T(8,128)(2,1)}, bf16[32,4096]{1,0:T(8,128)(2,1)S(1)}, u32[]{:S(2)}, u32[]{:S(2)}) collective-permute-start(bf16[32,4096]{1,0:T(8,128)(2,1)} %bitcast.21), channel_id=1, source_target_pairs={{0,2},{1,3},{2,0},{3,1},{4,6},{5,7},{6,4},{7,5},{8,10},{9,11},{10,... | collective-permute-start | bytes 786440 | tf_op jit(solution)/shard_map/ppermute | solution.py:186
  8.6 25.2 %collective-permute-start = (bf16[32,4096]{1,0:T(8,128)(2,1)}, bf16[32,4096]{1,0:T(8,128)(2,1)S(1)}, u32[]{:S(2)}, u32[]{:S(2)}) collective-permute-start(bf16[32,4096]{1,0:T(8,128)(2,1)} %bitcast.22), channel_id=1, source_target_pairs={{0,1},{1,2},{2,3},{3,0},{4,5},{5,6},{6,7},{7,4},{8,9},{9,10},{10,1... | collective-permute-start | bytes 786440 | tf_op jit(solution)/shard_map/ppermute | solution.py:186
  10.8 1.2 %copy-start.1 = (bf16[1,128,4096]{2,1,0:T(8,128)(2,1)S(1)}, bf16[1,128,4096]{2,1,0:T(8,128)(2,1)}, u32[]{:S(2)}) copy-start(bf16[1,128,4096]{2,1,0:T(8,128)(2,1)} %param.7) | copy-start | bytes 3145732
  12.0 0.8 copy-start.5
  12.8 31.4 %collective-permute-start.4 = (bf16[32,1024]{1,0:T(8,128)(2,1)S(1)}, bf16[32,1024]{1,0:T(8,128)(2,1)S(1)}, u32[]{:S(2)}, u32[]{:S(2)}) collective-permute-start(bf16[32,1024]{1,0:T(8,128)(2,1)S(1)} %get-tuple-element.50), channel_id=1, source_target_pairs={{0,1},{1,2},{2,3},{3,0},{4,5},{5,6},{6,7},{7,4},{8,9},{9,10},{10,1... | collective-permute-start | bytes 196616 | tf_op jit(solution)/shard_map/ppermute | solution.py:186
  15.3 29.0 %collective-permute-start.5 = (bf16[32,1024]{1,0:T(8,128)(2,1)S(1)}, bf16[32,1024]{1,0:T(8,128)(2,1)S(1)}, u32[]{:S(2)}, u32[]{:S(2)}) collective-permute-start(bf16[32,1024]{1,0:T(8,128)(2,1)S(1)} %get-tuple-element.51), channel_id=1, source_target_pairs={{0,2},{1,3},{2,0},{3,1},{4,6},{5,7},{6,4},{7,5},{8,10},{9,11},{10,... | collective-permute-start | bytes 196616 | tf_op jit(solution)/shard_map/ppermute | solution.py:186
  19.7 24.5 %collective-permute-start.6 = (bf16[32,1024]{1,0:T(8,128)(2,1)S(1)}, bf16[32,1024]{1,0:T(8,128)(2,1)S(1)}, u32[]{:S(2)}, u32[]{:S(2)}) collective-permute-start(bf16[32,1024]{1,0:T(8,128)(2,1)S(1)} %get-tuple-element.52), channel_id=1, source_target_pairs={{0,3},{1,0},{2,1},{3,2},{4,7},{5,4},{6,5},{7,6},{8,11},{9,8},{10,9... | collective-permute-start | bytes 196616 | tf_op jit(solution)/shard_map/ppermute | solution.py:186
  31.4 1.0 copy-start.3
  32.3 0.9 copy-start.7
  33.3 0.8 copy-start.6
  34.6 9.7 %collective-permute-start.3 = (f32[16,128]{1,0:T(8,128)S(1)}, f32[16,128]{1,0:T(8,128)S(1)}, u32[]{:S(2)}, u32[]{:S(2)}) collective-permute-start(f32[16,128]{1,0:T(8,128)S(1)} %get-tuple-element.49), channel_id=1, source_target_pairs={{0,4},{4,0},{1,5},{5,1},{2,6},{6,2},{3,7},{7,3},{8,12},{12,8},{9,1... | collective-permute-start | bytes 24584 | tf_op jit(solution)/shard_map/ppermute | solution.py:190
  44.3 7.8 %copy-start.8 = (bf16[32,1024]{1,0:T(8,128)(2,1)}, bf16[32,1024]{1,0:T(8,128)(2,1)S(1)}, u32[]{:S(2)}) copy-start(bf16[32,1024]{1,0:T(8,128)(2,1)S(1)} %collective-permute-done.4.r1) | copy-start | bytes 196612
  44.3 7.8 %copy-start.10 = (bf16[32,1024]{1,0:T(8,128)(2,1)}, bf16[32,1024]{1,0:T(8,128)(2,1)S(1)}, u32[]{:S(2)}) copy-start(bf16[32,1024]{1,0:T(8,128)(2,1)S(1)} %collective-permute-done.5.r2) | copy-start | bytes 196612
  45.0 20.9 %all-to-all-start = ((f32[32,16,128]{2,1,0:T(8,128)}), f32[32,16,128]{2,1,0:T(8,128)S(1)}, u32[]{:S(2)}, u32[]{:S(2)}) async-start(f32[32,16,128]{2,1,0:T(8,128)} %broadcast_in_dim.18), calls=%async_computation | async-start | bytes 524288 | tf_op jit(solution)/shard_map/all_to_all | solution.py:194
  52.1 0.8 slice-start
  52.1 0.8 slice-start.1
  52.9 6.8 %collective-permute-start.10 = (bf16[48,1024]{1,0:T(8,128)(2,1)S(1)}, bf16[48,1024]{1,0:T(8,128)(2,1)S(1)}, u32[]{:S(2)}, u32[]{:S(2)}) collective-permute-start(bf16[48,1024]{1,0:T(8,128)(2,1)S(1)} %pad_maximum_fusion.h0), channel_id=1, source_target_pairs={{0,24},{8,0},{16,8},{24,16},{1,25},{9,1},{17,9},{25,17},{2,26},{10... | collective-permute-start | bytes 294920 | tf_op jit(solution)/shard_map/ppermute | solution.py:186
  55.4 6.9 %collective-permute-start.9 = (bf16[48,1024]{1,0:T(8,128)(2,1)S(1)}, bf16[48,1024]{1,0:T(8,128)(2,1)S(1)}, u32[]{:S(2)}, u32[]{:S(2)}) collective-permute-start(bf16[48,1024]{1,0:T(8,128)(2,1)S(1)} %pad_maximum_fusion.h0), channel_id=1, source_target_pairs={{0,16},{8,24},{16,0},{24,8},{1,17},{9,25},{17,1},{25,9},{2,18},{10... | collective-permute-start | bytes 294920 | tf_op jit(solution)/shard_map/ppermute | solution.py:186
  55.9 8.8 %collective-permute-start.8 = (bf16[48,1024]{1,0:T(8,128)(2,1)S(1)}, bf16[48,1024]{1,0:T(8,128)(2,1)S(1)}, u32[]{:S(2)}, u32[]{:S(2)}) collective-permute-start(bf16[48,1024]{1,0:T(8,128)(2,1)S(1)} %pad_maximum_fusion.h0), channel_id=1, source_target_pairs={{0,8},{8,16},{16,24},{24,0},{1,9},{9,17},{17,25},{25,1},{2,10},{10... | collective-permute-start | bytes 294920 | tf_op jit(solution)/shard_map/ppermute | solution.py:186
  56.5 14.5 %collective-permute-start.11 = (bf16[48,1024]{1,0:T(8,128)(2,1)S(1)}, bf16[48,1024]{1,0:T(8,128)(2,1)}, u32[]{:S(2)}, u32[]{:S(2)}) collective-permute-start(bf16[48,1024]{1,0:T(8,128)(2,1)S(1)} %pad_maximum_fusion.h0), channel_id=1, source_target_pairs={{0,4},{4,0},{1,5},{5,1},{2,6},{6,2},{3,7},{7,3},{8,12},{12,8},{9,1... | collective-permute-start | bytes 294920 | tf_op jit(solution)/shard_map/ppermute | solution.py:190
  59.6 6.3 %copy-start.12 = (bf16[48,1024]{1,0:T(8,128)(2,1)}, bf16[48,1024]{1,0:T(8,128)(2,1)S(1)}, u32[]{:S(2)}) copy-start(bf16[48,1024]{1,0:T(8,128)(2,1)S(1)} %collective-permute-done.10.h3) | copy-start | bytes 294916
  59.6 11.4 %collective-permute-start.14 = (bf16[48,1024]{1,0:T(8,128)(2,1)S(1)}, bf16[48,1024]{1,0:T(8,128)(2,1)}, u32[]{:S(2)}, u32[]{:S(2)}) collective-permute-start(bf16[48,1024]{1,0:T(8,128)(2,1)S(1)} %collective-permute-done.10.h3), channel_id=1, source_target_pairs={{0,4},{4,0},{1,5},{5,1},{2,6},{6,2},{3,7},{7,3},{8,12},{12,8},{9,1... | collective-permute-start | bytes 294920 | tf_op jit(solution)/shard_map/ppermute | solution.py:190
  62.3 3.7 %copy-start.14 = (bf16[48,1024]{1,0:T(8,128)(2,1)}, bf16[48,1024]{1,0:T(8,128)(2,1)S(1)}, u32[]{:S(2)}) copy-start(bf16[48,1024]{1,0:T(8,128)(2,1)S(1)} %collective-permute-done.9.h2) | copy-start | bytes 294916
  62.3 8.8 %collective-permute-start.13 = (bf16[48,1024]{1,0:T(8,128)(2,1)S(1)}, bf16[48,1024]{1,0:T(8,128)(2,1)}, u32[]{:S(2)}, u32[]{:S(2)}) collective-permute-start(bf16[48,1024]{1,0:T(8,128)(2,1)S(1)} %collective-permute-done.9.h2), channel_id=1, source_target_pairs={{0,4},{4,0},{1,5},{5,1},{2,6},{6,2},{3,7},{7,3},{8,12},{12,8},{9,1... | collective-permute-start | bytes 294920 | tf_op jit(solution)/shard_map/ppermute | solution.py:190
  64.8 6.3 %collective-permute-start.12 = (bf16[48,1024]{1,0:T(8,128)(2,1)S(1)}, bf16[48,1024]{1,0:T(8,128)(2,1)}, u32[]{:S(2)}, u32[]{:S(2)}) collective-permute-start(bf16[48,1024]{1,0:T(8,128)(2,1)S(1)} %collective-permute-done.8.h1), channel_id=1, source_target_pairs={{0,4},{4,0},{1,5},{5,1},{2,6},{6,2},{3,7},{7,3},{8,12},{12,8},{9,1... | collective-permute-start | bytes 294920 | tf_op jit(solution)/shard_map/ppermute | solution.py:190
  65.3 0.6 copy-start.16
  66.0 1.3 %collective-permute-start.7 = (f32[16,128]{1,0:T(8,128)S(1)}, f32[16,128]{1,0:T(8,128)S(1)}, u32[]{:S(2)}, u32[]{:S(2)}) collective-permute-start(f32[16,128]{1,0:T(8,128)S(1)} %reduce_sum.9.lown), channel_id=1, source_target_pairs={{0,4},{4,0},{1,5},{5,1},{2,6},{6,2},{3,7},{7,3},{8,12},{12,8},{9,1... | collective-permute-start | bytes 24584 | tf_op jit(solution)/shard_map/ppermute | solution.py:190
  71.0 7.2 %copy-start.2 = (bf16[1,128,4096]{2,1,0:T(8,128)(2,1)S(1)}, bf16[1,128,4096]{2,1,0:T(8,128)(2,1)}, u32[]{:S(2)}) copy-start(bf16[1,128,4096]{2,1,0:T(8,128)(2,1)} %param.7) | copy-start | bytes 3145732
  71.1 1.8 %collective-permute-start.15 = (f32[32,16,128]{2,1,0:T(8,128)S(1)}, f32[32,16,128]{2,1,0:T(8,128)S(1)}, u32[]{:S(2)}, u32[]{:S(2)}) collective-permute-start(f32[32,16,128]{2,1,0:T(8,128)S(1)} %get-tuple-element.59), channel_id=1, source_target_pairs={{0,4},{4,0},{1,5},{5,1},{2,6},{6,2},{3,7},{7,3},{8,12},{12,8},{9,1... | collective-permute-start | bytes 786440 | tf_op jit(solution)/shard_map/ppermute | solution.py:190
  73.6 4.6 %copy-start.9 = (bf16[32,1024]{1,0:T(8,128)(2,1)S(1)}, bf16[32,1024]{1,0:T(8,128)(2,1)}, u32[]{:S(2)}) copy-start(bf16[32,1024]{1,0:T(8,128)(2,1)} %copy-done.8) | copy-start | bytes 196612
  73.6 4.6 %copy-start.11 = (bf16[32,1024]{1,0:T(8,128)(2,1)S(1)}, bf16[32,1024]{1,0:T(8,128)(2,1)}, u32[]{:S(2)}) copy-start(bf16[32,1024]{1,0:T(8,128)(2,1)} %copy-done.10) | copy-start | bytes 196612
  73.6 12.7 %all-to-all-start.1 = ((f32[32,16,128]{2,1,0:T(8,128)}), f32[32,16,128]{2,1,0:T(8,128)S(1)}, u32[]{:S(2)}, u32[]{:S(2)}) async-start(f32[32,16,128]{2,1,0:T(8,128)} %add.7), calls=%async_computation.1 | async-start | bytes 524288 | tf_op jit(solution)/shard_map/all_to_all | solution.py:194
  78.2 0.9 copy-start.13
  79.1 0.9 copy-start.15
  80.0 0.9 copy-start.17
  82.8 0.7 copy-start.19
  83.5 0.6 copy-start.21
  84.1 0.6 copy-start.23
  87.0 6.4 %copy-start.24 = (bf16[32,1024]{1,0:T(8,128)(2,1)S(1)}, bf16[32,1024]{1,0:T(8,128)(2,1)}, u32[]{:S(2)}) copy-start(bf16[32,1024]{1,0:T(8,128)(2,1)} %copy-done.23) | copy-start | bytes 196612
  87.0 6.5 %copy-start.22 = (bf16[32,1024]{1,0:T(8,128)(2,1)S(1)}, bf16[32,1024]{1,0:T(8,128)(2,1)}, u32[]{:S(2)}) copy-start(bf16[32,1024]{1,0:T(8,128)(2,1)} %copy-done.21) | copy-start | bytes 196612
  87.1 9.9 %copy-start.20 = (bf16[32,1024]{1,0:T(8,128)(2,1)S(1)}, bf16[32,1024]{1,0:T(8,128)(2,1)}, u32[]{:S(2)}) copy-start(bf16[32,1024]{1,0:T(8,128)(2,1)} %copy-done.19) | copy-start | bytes 196612
  87.1 20.5 %copy-start.4 = (bf16[1,32,4096]{2,1,0:T(8,128)(2,1)S(1)}, bf16[1,32,4096]{2,1,0:T(8,128)(2,1)}, u32[]{:S(2)}) copy-start(bf16[1,32,4096]{2,1,0:T(8,128)(2,1)} %param.5) | copy-start | bytes 786436
  87.1 20.5 %copy-start.18 = (f32[32,128]{1,0:T(8,128)S(1)}, f32[32,128]{1,0:T(8,128)}, u32[]{:S(2)}) copy-start(f32[32,128]{1,0:T(8,128)} %get-tuple-element.78.qt) | copy-start | bytes 49156
  87.1 15.1 %all-to-all-start.2 = ((f32[32,16,128]{2,1,0:T(8,128)}), f32[32,16,128]{2,1,0:T(8,128)S(1)}, u32[]{:S(2)}, u32[]{:S(2)}) async-start(f32[32,16,128]{2,1,0:T(8,128)} %shard_map.89), calls=%async_computation.2 | async-start | bytes 524288 | tf_op jit(solution)/shard_map/all_to_all | solution.py:194
  93.4 7.3 %collective-permute-start.16 = (bf16[32,1024]{1,0:T(8,128)(2,1)S(1)}, bf16[32,1024]{1,0:T(8,128)(2,1)S(1)}, u32[]{:S(2)}, u32[]{:S(2)}) collective-permute-start(bf16[32,1024]{1,0:T(8,128)(2,1)S(1)} %copy-done.24), channel_id=1, source_target_pairs={{0,1},{1,2},{2,3},{3,0},{4,5},{5,6},{6,7},{7,4},{8,9},{9,10},{10,1... | collective-permute-start | bytes 196616 | tf_op jit(solution)/shard_map/ppermute | solution.py:186
  93.5 8.6 %collective-permute-start.17 = (bf16[32,1024]{1,0:T(8,128)(2,1)S(1)}, bf16[32,1024]{1,0:T(8,128)(2,1)S(1)}, u32[]{:S(2)}, u32[]{:S(2)}) collective-permute-start(bf16[32,1024]{1,0:T(8,128)(2,1)S(1)} %copy-done.22), channel_id=1, source_target_pairs={{0,2},{1,3},{2,0},{3,1},{4,6},{5,7},{6,4},{7,5},{8,10},{9,11},{10,... | collective-permute-start | bytes 196616 | tf_op jit(solution)/shard_map/ppermute | solution.py:186
  96.9 5.2 %collective-permute-start.18 = (bf16[32,1024]{1,0:T(8,128)(2,1)S(1)}, bf16[32,1024]{1,0:T(8,128)(2,1)S(1)}, u32[]{:S(2)}, u32[]{:S(2)}) collective-permute-start(bf16[32,1024]{1,0:T(8,128)(2,1)S(1)} %copy-done.20), channel_id=1, source_target_pairs={{0,3},{1,0},{2,1},{3,2},{4,7},{5,4},{6,5},{7,6},{8,11},{9,8},{10,9... | collective-permute-start | bytes 196616 | tf_op jit(solution)/shard_map/ppermute | solution.py:186
  102.2 5.4 %collective-permute-start.19 = (f32[32,16,128]{2,1,0:T(8,128)S(1)}, f32[32,16,128]{2,1,0:T(8,128)S(1)}, u32[]{:S(2)}, u32[]{:S(2)}) collective-permute-start(f32[32,16,128]{2,1,0:T(8,128)S(1)} %all-to-all-done.2.rown), channel_id=1, source_target_pairs={{0,4},{4,0},{1,5},{5,1},{2,6},{6,2},{3,7},{7,3},{8,12},{12,8},{9,1... | collective-permute-start | bytes 786440 | tf_op jit(solution)/shard_map/ppermute | solution.py:190

commit v6 on v4

--- a/solution.py
+++ b/solution.py
@@ -45,31 +45,40 @@
     return jnp.concatenate(blocks, axis=0)
 
 
-def call(kernel, outs, scratch=(), flops=10**6, moved=10**6):
-    vmem = pl.BlockSpec(memory_space=pltpu.VMEM)
+def call(kernel, outs, scratch=(), flops=10**6, moved=10**6, space=pltpu.VMEM, dest=pltpu.VMEM, room=8):
 
     def run(*args):
         return pl.pallas_call(
             kernel,
             out_shape=[jax.ShapeDtypeStruct(s, d) for s, d in outs],
-            in_specs=[vmem] * len(args),
-            out_specs=[vmem] * len(outs),
+            in_specs=[pl.BlockSpec(memory_space=space)] * len(args),
+            out_specs=[pl.BlockSpec(memory_space=dest)] * len(outs),
             scratch_shapes=list(scratch),
-            compiler_params=pltpu.CompilerParams(vmem_limit_bytes=40 * 2**20),
+            compiler_params=pltpu.CompilerParams(vmem_limit_bytes=room * 2**20),
             cost_estimate=pl.CostEstimate(flops=flops, bytes_accessed=moved, transcendentals=0),
         )(*args)
 
     return run
 
 
-def pack_kernel(w, og, *sends):
+def fetched(pairs, sems):
+    copies = [pltpu.make_async_copy(a, b, sems.at[i]) for i, (a, b) in enumerate(pairs)]
+    for copy in copies:
+        copy.start()
+    for copy in copies:
+        copy.wait()
+
+
+def pack_kernel(w, og, s1, s2, s3, lines, feats, packed, sems):
     t, y, core = lax.axis_index("t"), lax.axis_index("y"), lax.axis_index("core")
     rows = pl.ds(pl.multiple_of((2 * y + core) * CUT, CUT), CUT)
-    for k, send in enumerate(sends, 1):
+    fetched([(w.at[rows, :], lines), (og, feats)], sems)
+    for k in range(1, TENSOR):
         target = lax.rem(t + k, TENSOR)
-        send[0:CUT, :] = w[rows, pl.ds(pl.multiple_of(target * PART, PART), PART)]
+        packed[k - 1, 0:CUT, :] = lines[:, pl.ds(pl.multiple_of(target * PART, PART), PART)]
         for m in range(8):
-            send[CUT : 2 * CUT, 128 * m : 128 * m + 128] = og[16 * m : 16 * m + 16, :]
+            packed[k - 1, CUT : 2 * CUT, 128 * m : 128 * m + 128] = feats[16 * m : 16 * m + 16, :]
+    fetched([(packed.at[k], send) for k, send in enumerate((s1, s2, s3))], sems)
 
 
 def early_kernel(a0, ef, warm, inner, fed, lines):
@@ -161,25 +170,31 @@
         err[:, cols] = total.astype(BF16)
 
 
-def input_kernel(w, og, r1, r2, r3, h0, h1, h2, h3, c0, c1, c2, c3, o0, o1, o2, o3, weights, feats):
+def input_kernel(w, og, r1, r2, r3, h0, h1, h2, h3, c0, c1, c2, c3, *rest):
+    *outs, rv, hv, cv, weights, feats, total, sems = rest
     t, y, core = lax.axis_index("t"), lax.axis_index("y"), lax.axis_index("core")
-    weights[0:128, :] = w[:, pl.ds(pl.multiple_of(t * PART, PART), PART)]
-    feats[:, 0:128] = og[...]
-    for k, r in enumerate((r1, r2, r3), 1):
+    mine = w.at[:, pl.ds(pl.multiple_of(t * PART, PART), PART)]
+    pairs = [(mine, weights.at[pl.ds(0, 128), :]), (og, feats.at[:, pl.ds(0, 128)])]
+    pairs += [(r, rv.at[k]) for k, r in enumerate((r1, r2, r3))]
+    pairs += [(h, hv.at[j]) for j, h in enumerate((h0, h1, h2, h3))]
+    pairs += [(c, cv.at[j]) for j, c in enumerate((c0, c1, c2, c3))]
+    fetched(pairs, sems)
+    for k in range(1, TENSOR):
         for m in range(8):
-            feats[16 * m : 16 * m + 16, 128 * k : 128 * k + 128] = r[
-                CUT : 2 * CUT, 128 * m : 128 * m + 128
+            feats[16 * m : 16 * m + 16, 128 * k : 128 * k + 128] = rv[
+                k - 1, CUT : 2 * CUT, 128 * m : 128 * m + 128
             ]
-        for j, (h, c) in enumerate(((h0, c0), (h1, c1), (h2, c2), (h3, c3))):
+        for j in range(4):
             first = 128 * k + 2 * CUT * lax.rem(y - j + 4, 4)
             here = pl.ds(pl.multiple_of(first + CUT * core, CUT), CUT)
             there = pl.ds(pl.multiple_of(first + CUT * (1 - core), CUT), CUT)
-            weights[here, :] = h[CUT * (k - 1) : CUT * k, :]
-            weights[there, :] = c[CUT * (k - 1) : CUT * k, :]
-    for k, out in enumerate((o0, o1, o2, o3)):
+            weights[here, :] = hv[j, CUT * (k - 1) : CUT * k, :]
+            weights[there, :] = cv[j, CUT * (k - 1) : CUT * k, :]
+    for k in range(TENSOR):
         target = lax.rem(t + k, TENSOR)
         rows = feats[pl.ds(pl.multiple_of(target * OWN, OWN), OWN), :]
-        out[...] = jnp.dot(rows, weights[...], preferred_element_type=F32).astype(BF16)
+        total[k] = jnp.dot(rows, weights[...], preferred_element_type=F32).astype(BF16)
+    fetched([(total.at[k], out) for k, out in enumerate(outs)], sems)
 
 
 def moved(x, k, axis="t"):
@@ -199,10 +214,24 @@
     ef = error_feedback[0, 0]
     warm = warm_right[0, 0].T
 
-    sends = call(pack_kernel, [((2 * CUT, PART), BF16)] * 3)(weight, og)
+    sends = call(
+        pack_kernel,
+        [((2 * CUT, PART), BF16)] * 3,
+        [
+            pltpu.VMEM((CUT, WIDE), BF16),
+            pltpu.VMEM((128, HEAD), BF16),
+            pltpu.VMEM((3, 2 * CUT, PART), BF16),
+            pltpu.SemaphoreType.DMA((3,)),
+        ],
+        space=pltpu.MemorySpace.HBM,
+        dest=pltpu.MemorySpace.HBM,
+        room=60,
+    )(weight, og)
     got = [moved(x, k) for k, x in zip((1, 2, 3), sends)]
-    act, got = lax.optimization_barrier((act, got))
     acts = [act] + [moved(act, k) for k in (1, 2, 3)]
+    shares = [jnp.concatenate([g[:CUT] for g in got], axis=0)]
+    shares += [moved(shares[0], j, "y") for j in (1, 2, 3)]
+    traded = [swapped(x) for x in shares]
     inner, fed, lines = call(
         early_kernel,
         [((RANK, OWN), F32), ((RANK, HEAD), F32), ((RANK, WIDE), BF16)],
@@ -210,25 +239,34 @@
         moved=0,
     )(act, ef, warm)
 
-    shares = [jnp.concatenate([g[:CUT] for g in got], axis=0)]
-    shares += [moved(shares[0], j, "y") for j in (1, 2, 3)]
-    outs = call(
-        input_kernel,
-        [((OWN, PART), BF16)] * 4,
-        [pltpu.VMEM((512, PART), BF16), pltpu.VMEM((128, 512), BF16)],
-        flops=0,
-        moved=0,
-    )(weight, og, *got, *shares, *[swapped(x) for x in shares])
-    inputs = [outs[0]] + [moved(o, k) for k, o in zip((1, 2, 3), outs[1:])]
-
     half = ((HALF, HEAD), F32)
     left_keep, left_send = call(
         left_kernel, [half, half], [pltpu.VMEM((RANK, HEAD), F32)], flops=5 * 10**7, moved=10**6
     )(*acts[1:], og, lines, inner, fed)
+    left_send, traded, shares = lax.optimization_barrier((left_send, traded, shares))
 
     left_half = left_keep + swapped(left_send)
-    left_half, inputs = lax.optimization_barrier((left_half, inputs))
     pieces = exchanged(jnp.broadcast_to(left_half[None], (N_CHIPS, HALF, HEAD)), CHIPS)
+    outs = call(
+        input_kernel,
+        [((OWN, PART), BF16)] * 4,
+        [
+            pltpu.VMEM((3, 2 * CUT, PART), BF16),
+            pltpu.VMEM((4, 3 * CUT, PART), BF16),
+            pltpu.VMEM((4, 3 * CUT, PART), BF16),
+            pltpu.VMEM((512, PART), BF16),
+            pltpu.VMEM((128, 512), BF16),
+            pltpu.VMEM((4, OWN, PART), BF16),
+            pltpu.SemaphoreType.DMA((13,)),
+        ],
+        flops=2 * 10**8,
+        moved=2 * 10**6,
+        space=pltpu.MemorySpace.HBM,
+        dest=pltpu.MemorySpace.HBM,
+        room=60,
+    )(weight, og, *got, *shares, *traded)
+    inputs = [outs[0]] + [moved(o, k) for k, o in zip((1, 2, 3), outs[1:])]
+    pieces, outs = lax.optimization_barrier((pieces, outs))
     left_own = jnp.sum(pieces, axis=0)
     left_other = swapped(left_own)
 
@@ -242,8 +280,10 @@
     )(left_own, left_other, *acts, og, ef)
 
     pieces = exchanged(right_keep + swapped(right_send), CHIPS)
+    pieces, inputs[1] = lax.optimization_barrier((pieces, inputs[1]))
     (mean,) = call(spread_kernel, [block])(pieces)
     right_own = exchanged(mean, CHIPS)
+    right_own, inputs = lax.optimization_barrier((right_own, inputs))
     right_other = swapped(right_own)
 
     err, fac, igrad = call(

time: 113 us -> 108 us (0.956)
  blocking collectives: 41.5 us -> 0 us
  starting transfers between devices: 43.8 us -> 59.3 us
  waiting for transfers between devices: 16.9 us -> 31.4 us
  Pallas kernels: 7.29 us -> 11.8 us
  local copies, waits for them, and re-layouts: 2.03 us -> 3.16 us
    all_to_all x3 -> x0, blocking collectives: 41.5 us -> none  [exchanged(): return lax.all_to_all(x, axes, 0, 0, tiled=True)]
    all_to_all x0 -> x3, starting transfers between devices: none -> 15.7 us  [exchanged(): return lax.all_to_all(x, axes, 0, 0, tiled=True)]
    ppermute x12, waiting for transfers between devices: 11.6 us -> 21.8 us  [moved(): return lax.ppermute(x, axis, [(i, (i + k) % 4) for i in range(4)])]
    ppermute x12, starting transfers between devices: 29.2 us -> 22.7 us  [moved(): return lax.ppermute(x, axis, [(i, (i + k) % 4) for i in range(4)])]
    ppermute x8, starting transfers between devices: 14.6 us -> 21 us  [swapped(): return lax.ppermute(x, 'core', [(0, 1), (1, 0)])]
    all_to_all x0 -> x3, waiting for transfers between devices: none -> 5.34 us  [exchanged(): return lax.all_to_all(x, axes, 0, 0, tiled=True)]
    pallas_call x7, Pallas kernels: 7.29 us -> 11.8 us  [run(): pl.pallas_call(kernel, out_shape=[jax.ShapeDtypeStruct(s, d) for s, d in...]
    unnamed x14 -> x42, local copies, waits for them, and re-layouts: 2 us -> 2.42 us
  transfers between devices with their start and end apart: 20 -> 23, of which waited for: 12 -> 11; matrix products, arithmetic and copies ran while one was open for 0% -> 0% of each run, Pallas kernels for 2% -> 4%
where the time goes in v6:
time: 108 us; the launch traced here: 107 us
  starting transfers between devices  59.3 us (55%)
  waiting for transfers between devices  31.4 us (29%)
  Pallas kernels  11.8 us (11%)
  local copies, waits for them, and re-layouts  3.16 us (3%)
    ppermute x12, starting transfers between devices, moved(): return lax.ppermute(x, axis, [(i, (i + k) % 4) for i in range(4)])  22.7 us
    ppermute x12, waiting for transfers between devices, moved(): return lax.ppermute(x, axis, [(i, (i + k) % 4) for i in range(4)])  21.8 us
    ppermute x8, starting transfers between devices, swapped(): return lax.ppermute(x, 'core', [(0, 1), (1, 0)])  21 us
    all_to_all x3, starting transfers between devices, exchanged(): return lax.all_to_all(x, axes, 0, 0, tiled=True)  15.7 us
    pallas_call x7, Pallas kernels, run(): pl.pallas_call(kernel, out_shape=[jax.ShapeDtypeStruct(s, d) for s, d in...  11.8 us
    all_to_all x3, waiting for transfers between devices, exchanged(): return lax.all_to_all(x, axes, 0, 0, tiled=True)  5.34 us
    ppermute x8, waiting for transfers between devices, swapped(): return lax.ppermute(x, 'core', [(0, 1), (1, 0)])  4.27 us
    unnamed x42, local copies, waits for them, and re-layouts  2.42 us
  transfers between devices with their start and end apart: 23, of which 11 were waited for; matrix products, arithmetic and copies ran while one was open for 0% of the time, Pallas kernels for 4%

profile of v6, /device:TPU:1, one launch (start us, length us, event | category | flops | bytes accessed | tf_op | source)
XLA Modules:
  0.0 107.4 jit_solution(17960338361984213071)
XLA Ops:
  0.6 1.7 %shard_map.86 = (bf16[32,1024]{1,0:T(8,128)(2,1)}, bf16[32,1024]{1,0:T(8,128)(2,1)}, bf16[32,1024]{1,0:T(8,128)(2,1)}) custom-call(bf16[128,4096]{1,0:T(8,128)(2,1)} %bitcast.31, bf16[128,128]{1,0:T(8,128)(2,1)} %bitcast.24), custom_call_target="tpu_custom_call" | custom-call | flops 1000000 | bytes 1000000 | tf_op jit(solution)/shard_map/pallas_call | solution.py:51
  2.4 0.0 copy-start.1
  2.4 3.9 %collective-permute-start.3 = (bf16[32,1024]{1,0:T(8,128)(2,1)}, bf16[32,1024]{1,0:T(8,128)(2,1)S(1)}, u32[]{:S(2)}, u32[]{:S(2)}) collective-permute-start(bf16[32,1024]{1,0:T(8,128)(2,1)} %get-tuple-element.44), channel_id=1, source_target_pairs={{0,1},{1,2},{2,3},{3,0},{4,5},{5,6},{6,7},{7,4},{8,9},{9,10},{10,1... | collective-permute-start | bytes 196616 | tf_op jit(solution)/shard_map/ppermute | solution.py:201
  6.3 5.1 %collective-permute-start.4 = (bf16[32,1024]{1,0:T(8,128)(2,1)}, bf16[32,1024]{1,0:T(8,128)(2,1)S(1)}, u32[]{:S(2)}, u32[]{:S(2)}) collective-permute-start(bf16[32,1024]{1,0:T(8,128)(2,1)} %get-tuple-element.45), channel_id=1, source_target_pairs={{0,2},{1,3},{2,0},{3,1},{4,6},{5,7},{6,4},{7,5},{8,10},{9,11},{10,... | collective-permute-start | bytes 196616 | tf_op jit(solution)/shard_map/ppermute | solution.py:201
  11.4 2.4 %collective-permute-start.5 = (bf16[32,1024]{1,0:T(8,128)(2,1)}, bf16[32,1024]{1,0:T(8,128)(2,1)S(1)}, u32[]{:S(2)}, u32[]{:S(2)}) collective-permute-start(bf16[32,1024]{1,0:T(8,128)(2,1)} %get-tuple-element.46), channel_id=1, source_target_pairs={{0,3},{1,0},{2,1},{3,2},{4,7},{5,4},{6,5},{7,6},{8,11},{9,8},{10,9... | collective-permute-start | bytes 196616 | tf_op jit(solution)/shard_map/ppermute | solution.py:201
  13.8 0.0 collective-permute-start.2
  13.8 3.2 %collective-permute-start.1 = (bf16[32,4096]{1,0:T(8,128)(2,1)}, bf16[32,4096]{1,0:T(8,128)(2,1)S(1)}, u32[]{:S(2)}, u32[]{:S(2)}) collective-permute-start(bf16[32,4096]{1,0:T(8,128)(2,1)} %bitcast.19), channel_id=1, source_target_pairs={{0,2},{1,3},{2,0},{3,1},{4,6},{5,7},{6,4},{7,5},{8,10},{9,11},{10,... | collective-permute-start | bytes 786440 | tf_op jit(solution)/shard_map/ppermute | solution.py:201
  17.1 0.0 collective-permute-done.3.r1
  17.1 0.0 collective-permute-done.4.r2
  17.1 0.6 copy-done.8
  17.7 5.0 %collective-permute-done.5.r3 = bf16[32,1024]{1,0:T(8,128)(2,1)S(1)} collective-permute-done((bf16[32,1024]{1,0:T(8,128)(2,1)}, bf16[32,1024]{1,0:T(8,128)(2,1)S(1)}, u32[]{:S(2)}, u32[]{:S(2)}) %collective-permute-start.5) | collective-permute-done | bytes 65568 | tf_op jit(solution)/shard_map/ppermute | solution.py:201
  22.7 0.6 copy-done.10
  23.3 2.7 %collective-permute-start.11 = (bf16[48,1024]{1,0:T(8,128)(2,1)S(1)}, bf16[48,1024]{1,0:T(8,128)(2,1)S(1)}, u32[]{:S(2)}, u32[]{:S(2)}) collective-permute-start(bf16[48,1024]{1,0:T(8,128)(2,1)S(1)} %pad_maximum_fusion.h0), channel_id=1, source_target_pairs={{0,24},{8,0},{16,8},{24,16},{1,25},{9,1},{17,9},{25,17},{2,26},{10... | collective-permute-start | bytes 294920 | tf_op jit(solution)/shard_map/ppermute | solution.py:201
  26.0 0.0 collective-permute-start
  26.0 0.4 collective-permute-start.9
  26.4 1.3 %collective-permute-done.11.h3 = bf16[48,1024]{1,0:T(8,128)(2,1)S(1)} collective-permute-done((bf16[48,1024]{1,0:T(8,128)(2,1)S(1)}, bf16[48,1024]{1,0:T(8,128)(2,1)S(1)}, u32[]{:S(2)}, u32[]{:S(2)}) %collective-permute-start.11) | collective-permute-done | bytes 98336 | tf_op jit(solution)/shard_map/ppermute | solution.py:201
  27.6 0.7 collective-permute-start.7
  28.3 2.7 %collective-permute-done.9.h2 = bf16[48,1024]{1,0:T(8,128)(2,1)S(1)} collective-permute-done((bf16[48,1024]{1,0:T(8,128)(2,1)S(1)}, bf16[48,1024]{1,0:T(8,128)(2,1)S(1)}, u32[]{:S(2)}, u32[]{:S(2)}) %collective-permute-start.9) | collective-permute-done | bytes 98336 | tf_op jit(solution)/shard_map/ppermute | solution.py:201
  31.0 11.8 %collective-permute-start.6 = (bf16[48,1024]{1,0:T(8,128)(2,1)S(1)}, bf16[48,1024]{1,0:T(8,128)(2,1)S(1)}, u32[]{:S(2)}, u32[]{:S(2)}) collective-permute-start(bf16[48,1024]{1,0:T(8,128)(2,1)S(1)} %pad_maximum_fusion.h0), channel_id=1, source_target_pairs={{0,4},{4,0},{1,5},{5,1},{2,6},{6,2},{3,7},{7,3},{8,12},{12,8},{9,1... | collective-permute-start | bytes 294920 | tf_op jit(solution)/shard_map/ppermute | solution.py:205
  42.8 0.0 collective-permute-done.7.h1
  42.8 1.0 collective-permute-start.12
  43.8 0.0 collective-permute-done.2.a3
  43.8 0.1 collective-permute-start.10
  43.9 0.0 collective-permute-done.1.a2
  43.9 0.4 collective-permute-start.8
  44.3 0.9 copy-done.4
  45.2 0.5 shard_map.84
  45.7 0.0 copy-done.7
  45.7 0.0 copy-done.11
  45.8 0.0 collective-permute-done.a1
  45.8 0.2 copy-done.2
  46.0 0.5 shard_map.85
  46.5 0.0 collective-permute-done.6.c0
  46.5 0.0 copy-start.14
  46.6 0.0 collective-permute-done.12.c3
  46.6 0.0 collective-permute-done.10.c2
  46.6 0.0 collective-permute-done.8.c1
  46.6 0.2 collective-permute-start.13
  46.8 1.1 %collective-permute-done.13 = f32[16,128]{1,0:T(8,128)S(1)} collective-permute-done((f32[16,128]{1,0:T(8,128)S(1)}, f32[16,128]{1,0:T(8,128)S(1)}, u32[]{:S(2)}, u32[]{:S(2)}) %collective-permute-start.13) | collective-permute-done | bytes 8224 | tf_op jit(solution)/shard_map/ppermute | solution.py:205
  47.9 0.7 broadcast_in_dim.18
  48.6 0.0 copy-done.17
  48.6 5.2 %all-to-all-start = ((f32[32,16,128]{2,1,0:T(8,128)}), f32[32,16,128]{2,1,0:T(8,128)S(1)}, u32[]{:S(2)}, u32[]{:S(2)}) async-start(f32[32,16,128]{2,1,0:T(8,128)} %broadcast_in_dim.18), calls=%async_computation | async-start | bytes 524288 | tf_op jit(solution)/shard_map/all_to_all | solution.py:209
  53.8 3.0 %shard_map.87 = (bf16[32,1024]{1,0:T(8,128)(2,1)}, bf16[32,1024]{1,0:T(8,128)(2,1)}, bf16[32,1024]{1,0:T(8,128)(2,1)}, bf16[32,1024]{1,0:T(8,128)(2,1)}) custom-call(bf16[128,4096]{1,0:T(8,128)(2,1)} %bitcast.32, bf16[128,128]{1,0:T(8,128)(2,1)} %bitcast.25, bf16[32,1024]{1,0:T(8,128)(2,1)} %copy-done.8, bf16[32,1024]{1,0:T(8,128)(2,1)} %copy-done.9, ...), custom_call_target="tpu_custom_call" | custom-call | flops 200000000 | bytes 2000000 | tf_op jit(solution)/shard_map/pallas_call | solution.py:51
  56.9 5.1 %all-to-all-done = f32[32,16,128]{2,1,0:T(8,128)S(1)} async-done(((f32[32,16,128]{2,1,0:T(8,128)}), f32[32,16,128]{2,1,0:T(8,128)S(1)}, u32[]{:S(2)}, u32[]{:S(2)}) %all-to-all-start) | async-done | bytes 262176 | tf_op jit(solution)/shard_map/all_to_all | solution.py:209
  62.0 2.2 %collective-permute-start.14 = (f32[16,128]{1,0:T(8,128)S(1)}, f32[16,128]{1,0:T(8,128)S(1)}, u32[]{:S(2)}, u32[]{:S(2)}) collective-permute-start(f32[16,128]{1,0:T(8,128)S(1)} %reduce_sum.9.lown), channel_id=1, source_target_pairs={{0,4},{4,0},{1,5},{5,1},{2,6},{6,2},{3,7},{7,3},{8,12},{12,8},{9,1... | collective-permute-start | bytes 24584 | tf_op jit(solution)/shard_map/ppermute | solution.py:205
  64.2 0.8 collective-permute-done.14.loth
  65.1 3.8 %shard_map.88 = (f32[32,128]{1,0:T(8,128)}, f32[32,16,128]{2,1,0:T(8,128)S(1)}, f32[32,16,128]{2,1,0:T(8,128)S(1)}) custom-call(f32[16,128]{1,0:T(8,128)S(1)} %reduce_sum.9.lown, f32[16,128]{1,0:T(8,128)S(1)} %collective-permute-done.14.loth, bf16[32,4096]{1,0:T(8,128)(2,1)S(1)} %bitcast.22, bf16[32,4096]{1,0:T(8,128)(2,1)S(1)} %collective-permute-done.a1, ...), custom_call_target="tpu_custom_call" | custom-call | flops 100000000 | bytes 3000000 | tf_op jit(solution)/shard_map/pallas_call | solution.py:51
  68.8 0.3 collective-permute-start.15
  69.2 1.2 %collective-permute-done.15 = f32[32,16,128]{2,1,0:T(8,128)S(1)} collective-permute-done((f32[32,16,128]{2,1,0:T(8,128)S(1)}, f32[32,16,128]{2,1,0:T(8,128)S(1)}, u32[]{:S(2)}, u32[]{:S(2)}) %collective-permute-start.15) | collective-permute-done | bytes 262176 | tf_op jit(solution)/shard_map/ppermute | solution.py:205
  70.4 0.7 add.7
  71.1 4.0 %all-to-all-start.1 = ((f32[32,16,128]{2,1,0:T(8,128)}), f32[32,16,128]{2,1,0:T(8,128)S(1)}, u32[]{:S(2)}, u32[]{:S(2)}) async-start(f32[32,16,128]{2,1,0:T(8,128)} %add.7), calls=%async_computation.1 | async-start | bytes 524288 | tf_op jit(solution)/shard_map/all_to_all | solution.py:209
  75.1 1.8 %collective-permute-start.16 = (bf16[32,1024]{1,0:T(8,128)(2,1)S(1)}, bf16[32,1024]{1,0:T(8,128)(2,1)S(1)}, u32[]{:S(2)}, u32[]{:S(2)}) collective-permute-start(bf16[32,1024]{1,0:T(8,128)(2,1)S(1)} %copy-done.20), channel_id=1, source_target_pairs={{0,1},{1,2},{2,3},{3,0},{4,5},{5,6},{6,7},{7,4},{8,9},{9,10},{10,1... | collective-permute-start | bytes 196616 | tf_op jit(solution)/shard_map/ppermute | solution.py:201
  76.9 7.7 %collective-permute-done.16.i1 = bf16[32,1024]{1,0:T(8,128)(2,1)S(1)} collective-permute-done((bf16[32,1024]{1,0:T(8,128)(2,1)S(1)}, bf16[32,1024]{1,0:T(8,128)(2,1)S(1)}, u32[]{:S(2)}, u32[]{:S(2)}) %collective-permute-start.16) | collective-permute-done | bytes 65568 | tf_op jit(solution)/shard_map/ppermute | solution.py:201
  84.6 0.0 all-to-all-done.1.pieces
  84.6 0.8 shard_map.89
  85.3 6.5 %all-to-all-start.2 = ((f32[32,16,128]{2,1,0:T(8,128)}), f32[32,16,128]{2,1,0:T(8,128)S(1)}, u32[]{:S(2)}, u32[]{:S(2)}) async-start(f32[32,16,128]{2,1,0:T(8,128)} %shard_map.89), calls=%async_computation.2 | async-start | bytes 524288 | tf_op jit(solution)/shard_map/all_to_all | solution.py:209
  91.8 2.5 %collective-permute-start.17 = (bf16[32,1024]{1,0:T(8,128)(2,1)S(1)}, bf16[32,1024]{1,0:T(8,128)(2,1)S(1)}, u32[]{:S(2)}, u32[]{:S(2)}) collective-permute-start(bf16[32,1024]{1,0:T(8,128)(2,1)S(1)} %copy-done.19), channel_id=1, source_target_pairs={{0,2},{1,3},{2,0},{3,1},{4,6},{5,7},{6,4},{7,5},{8,10},{9,11},{10,... | collective-permute-start | bytes 196616 | tf_op jit(solution)/shard_map/ppermute | solution.py:201
  94.3 0.0 collective-permute-start.18
  94.3 5.2 %collective-permute-done.17.i2 = bf16[32,1024]{1,0:T(8,128)(2,1)S(1)} collective-permute-done((bf16[32,1024]{1,0:T(8,128)(2,1)S(1)}, bf16[32,1024]{1,0:T(8,128)(2,1)S(1)}, u32[]{:S(2)}, u32[]{:S(2)}) %collective-permute-start.17) | collective-permute-done | bytes 65568 | tf_op jit(solution)/shard_map/ppermute | solution.py:201
  99.5 0.0 collective-permute-done.18.i3
  99.5 0.3 all-to-all-done.2.rown
  99.8 4.9 %collective-permute-start.19 = (f32[32,16,128]{2,1,0:T(8,128)S(1)}, f32[32,16,128]{2,1,0:T(8,128)S(1)}, u32[]{:S(2)}, u32[]{:S(2)}) collective-permute-start(f32[32,16,128]{2,1,0:T(8,128)S(1)} %all-to-all-done.2.rown), channel_id=1, source_target_pairs={{0,4},{4,0},{1,5},{5,1},{2,6},{6,2},{3,7},{7,3},{8,12},{12,8},{9,1... | collective-permute-start | bytes 786440 | tf_op jit(solution)/shard_map/ppermute | solution.py:205
  104.7 1.2 %collective-permute-done.19.roth = f32[32,16,128]{2,1,0:T(8,128)S(1)} collective-permute-done((f32[32,16,128]{2,1,0:T(8,128)S(1)}, f32[32,16,128]{2,1,0:T(8,128)S(1)}, u32[]{:S(2)}, u32[]{:S(2)}) %collective-permute-start.19) | collective-permute-done | bytes 262176 | tf_op jit(solution)/shard_map/ppermute | solution.py:205
  105.9 1.5 %shard_map.90 = (bf16[128,4096]{1,0:T(8,128)(2,1)}, bf16[32,4096]{1,0:T(8,128)(2,1)}, bf16[32,4096]{1,0:T(8,128)(2,1)}) custom-call(f32[32,16,128]{2,1,0:T(8,128)S(1)} %all-to-all-done.2.rown, f32[32,16,128]{2,1,0:T(8,128)S(1)} %collective-permute-done.19.roth, f32[32,128]{1,0:T(8,128)S(1)} %copy-done.6, bf16[128,128]{1,0:T(8,128)(2,1)S(1)} %bitcast.28, ...), custom_call_target="tpu_custom_call" | custom-call | flops 300000000 | bytes 5000000 | tf_op jit(solution)/shard_map/pallas_call | solution.py:51
  (39 shorter events, 0.1 us)
Async XLA Ops:
  0.6 43.7 %copy-start = (bf16[1,1,128,4096]{3,2,1,0:T(8,128)(2,1)S(1)}, bf16[1,1,128,4096]{3,2,1,0:T(8,128)(2,1)}, u32[]{:S(2)}) copy-start(bf16[1,1,128,4096]{3,2,1,0:T(8,128)(2,1)} %param.8) | copy-start | bytes 3145732
  2.4 23.6 %copy-start.1 = (bf16[1,32,4096]{2,1,0:T(8,128)(2,1)S(1)}, bf16[1,32,4096]{2,1,0:T(8,128)(2,1)}, u32[]{:S(2)}) copy-start(bf16[1,32,4096]{2,1,0:T(8,128)(2,1)} %param.5) | copy-start | bytes 786436
  2.4 14.7 %collective-permute-start.3 = (bf16[32,1024]{1,0:T(8,128)(2,1)}, bf16[32,1024]{1,0:T(8,128)(2,1)S(1)}, u32[]{:S(2)}, u32[]{:S(2)}) collective-permute-start(bf16[32,1024]{1,0:T(8,128)(2,1)} %get-tuple-element.44), channel_id=1, source_target_pairs={{0,1},{1,2},{2,3},{3,0},{4,5},{5,6},{6,7},{7,4},{8,9},{9,10},{10,1... | collective-permute-start | bytes 196616 | tf_op jit(solution)/shard_map/ppermute | solution.py:201
  6.3 10.8 %collective-permute-start.4 = (bf16[32,1024]{1,0:T(8,128)(2,1)}, bf16[32,1024]{1,0:T(8,128)(2,1)S(1)}, u32[]{:S(2)}, u32[]{:S(2)}) collective-permute-start(bf16[32,1024]{1,0:T(8,128)(2,1)} %get-tuple-element.45), channel_id=1, source_target_pairs={{0,2},{1,3},{2,0},{3,1},{4,6},{5,7},{6,4},{7,5},{8,10},{9,11},{10,... | collective-permute-start | bytes 196616 | tf_op jit(solution)/shard_map/ppermute | solution.py:201
  11.4 11.2 %collective-permute-start.5 = (bf16[32,1024]{1,0:T(8,128)(2,1)}, bf16[32,1024]{1,0:T(8,128)(2,1)S(1)}, u32[]{:S(2)}, u32[]{:S(2)}) collective-permute-start(bf16[32,1024]{1,0:T(8,128)(2,1)} %get-tuple-element.46), channel_id=1, source_target_pairs={{0,3},{1,0},{2,1},{3,2},{4,7},{5,4},{6,5},{7,6},{8,11},{9,8},{10,9... | collective-permute-start | bytes 196616 | tf_op jit(solution)/shard_map/ppermute | solution.py:201
  13.8 30.0 %collective-permute-start.2 = (bf16[32,4096]{1,0:T(8,128)(2,1)}, bf16[32,4096]{1,0:T(8,128)(2,1)S(1)}, u32[]{:S(2)}, u32[]{:S(2)}) collective-permute-start(bf16[32,4096]{1,0:T(8,128)(2,1)} %bitcast.18), channel_id=1, source_target_pairs={{0,3},{1,0},{2,1},{3,2},{4,7},{5,4},{6,5},{7,6},{8,11},{9,8},{10,9... | collective-permute-start | bytes 786440 | tf_op jit(solution)/shard_map/ppermute | solution.py:201
  13.8 30.1 %collective-permute-start.1 = (bf16[32,4096]{1,0:T(8,128)(2,1)}, bf16[32,4096]{1,0:T(8,128)(2,1)S(1)}, u32[]{:S(2)}, u32[]{:S(2)}) collective-permute-start(bf16[32,4096]{1,0:T(8,128)(2,1)} %bitcast.19), channel_id=1, source_target_pairs={{0,2},{1,3},{2,0},{3,1},{4,6},{5,7},{6,4},{7,5},{8,10},{9,11},{10,... | collective-permute-start | bytes 786440 | tf_op jit(solution)/shard_map/ppermute | solution.py:201
  17.1 0.6 copy-start.8
  17.1 5.6 %copy-start.9 = (bf16[32,1024]{1,0:T(8,128)(2,1)}, bf16[32,1024]{1,0:T(8,128)(2,1)S(1)}, u32[]{:S(2)}) copy-start(bf16[32,1024]{1,0:T(8,128)(2,1)S(1)} %collective-permute-done.4.r2) | copy-start | bytes 196612
  22.6 0.6 copy-start.10
  23.3 22.5 %copy-start.7 = (bf16[48,1024]{1,0:T(8,128)(2,1)}, bf16[48,1024]{1,0:T(8,128)(2,1)S(1)}, u32[]{:S(2)}) copy-start(bf16[48,1024]{1,0:T(8,128)(2,1)S(1)} %pad_maximum_fusion.h0) | copy-start | bytes 294916
  23.3 4.4 %collective-permute-start.11 = (bf16[48,1024]{1,0:T(8,128)(2,1)S(1)}, bf16[48,1024]{1,0:T(8,128)(2,1)S(1)}, u32[]{:S(2)}, u32[]{:S(2)}) collective-permute-start(bf16[48,1024]{1,0:T(8,128)(2,1)S(1)} %pad_maximum_fusion.h0), channel_id=1, source_target_pairs={{0,24},{8,0},{16,8},{24,16},{1,25},{9,1},{17,9},{25,17},{2,26},{10... | collective-permute-start | bytes 294920 | tf_op jit(solution)/shard_map/ppermute | solution.py:201
  26.0 19.8 %collective-permute-start = (bf16[32,4096]{1,0:T(8,128)(2,1)S(1)}, bf16[32,4096]{1,0:T(8,128)(2,1)S(1)}, u32[]{:S(2)}, u32[]{:S(2)}) collective-permute-start(bf16[32,4096]{1,0:T(8,128)(2,1)S(1)} %bitcast.20), channel_id=1, source_target_pairs={{0,1},{1,2},{2,3},{3,0},{4,5},{5,6},{6,7},{7,4},{8,9},{9,10},{10,1... | collective-permute-start | bytes 786440 | tf_op jit(solution)/shard_map/ppermute | solution.py:201
  26.0 5.0 %collective-permute-start.9 = (bf16[48,1024]{1,0:T(8,128)(2,1)S(1)}, bf16[48,1024]{1,0:T(8,128)(2,1)S(1)}, u32[]{:S(2)}, u32[]{:S(2)}) collective-permute-start(bf16[48,1024]{1,0:T(8,128)(2,1)S(1)} %pad_maximum_fusion.h0), channel_id=1, source_target_pairs={{0,16},{8,24},{16,0},{24,8},{1,17},{9,25},{17,1},{25,9},{2,18},{10... | collective-permute-start | bytes 294920 | tf_op jit(solution)/shard_map/ppermute | solution.py:201
  27.6 18.1 %copy-start.11 = (bf16[48,1024]{1,0:T(8,128)(2,1)}, bf16[48,1024]{1,0:T(8,128)(2,1)S(1)}, u32[]{:S(2)}) copy-start(bf16[48,1024]{1,0:T(8,128)(2,1)S(1)} %collective-permute-done.11.h3) | copy-start | bytes 294916
  27.6 15.2 %collective-permute-start.7 = (bf16[48,1024]{1,0:T(8,128)(2,1)S(1)}, bf16[48,1024]{1,0:T(8,128)(2,1)S(1)}, u32[]{:S(2)}, u32[]{:S(2)}) collective-permute-start(bf16[48,1024]{1,0:T(8,128)(2,1)S(1)} %pad_maximum_fusion.h0), channel_id=1, source_target_pairs={{0,8},{8,16},{16,24},{24,0},{1,9},{9,17},{17,25},{25,1},{2,10},{10... | collective-permute-start | bytes 294920 | tf_op jit(solution)/shard_map/ppermute | solution.py:201
  31.0 14.8 %copy-start.12 = (bf16[48,1024]{1,0:T(8,128)(2,1)}, bf16[48,1024]{1,0:T(8,128)(2,1)S(1)}, u32[]{:S(2)}) copy-start(bf16[48,1024]{1,0:T(8,128)(2,1)S(1)} %collective-permute-done.9.h2) | copy-start | bytes 294916
  31.0 15.6 %collective-permute-start.6 = (bf16[48,1024]{1,0:T(8,128)(2,1)S(1)}, bf16[48,1024]{1,0:T(8,128)(2,1)S(1)}, u32[]{:S(2)}, u32[]{:S(2)}) collective-permute-start(bf16[48,1024]{1,0:T(8,128)(2,1)S(1)} %pad_maximum_fusion.h0), channel_id=1, source_target_pairs={{0,4},{4,0},{1,5},{5,1},{2,6},{6,2},{3,7},{7,3},{8,12},{12,8},{9,1... | collective-permute-start | bytes 294920 | tf_op jit(solution)/shard_map/ppermute | solution.py:205
  42.8 3.0 %copy-start.13 = (bf16[48,1024]{1,0:T(8,128)(2,1)}, bf16[48,1024]{1,0:T(8,128)(2,1)S(1)}, u32[]{:S(2)}) copy-start(bf16[48,1024]{1,0:T(8,128)(2,1)S(1)} %collective-permute-done.7.h1) | copy-start | bytes 294916
  42.8 3.8 %collective-permute-start.12 = (bf16[48,1024]{1,0:T(8,128)(2,1)S(1)}, bf16[48,1024]{1,0:T(8,128)(2,1)S(1)}, u32[]{:S(2)}, u32[]{:S(2)}) collective-permute-start(bf16[48,1024]{1,0:T(8,128)(2,1)S(1)} %collective-permute-done.11.h3), channel_id=1, source_target_pairs={{0,4},{4,0},{1,5},{5,1},{2,6},{6,2},{3,7},{7,3},{8,12},{12,8},{9,1... | collective-permute-start | bytes 294920 | tf_op jit(solution)/shard_map/ppermute | solution.py:205
  43.8 2.8 %collective-permute-start.10 = (bf16[48,1024]{1,0:T(8,128)(2,1)S(1)}, bf16[48,1024]{1,0:T(8,128)(2,1)S(1)}, u32[]{:S(2)}, u32[]{:S(2)}) collective-permute-start(bf16[48,1024]{1,0:T(8,128)(2,1)S(1)} %collective-permute-done.9.h2), channel_id=1, source_target_pairs={{0,4},{4,0},{1,5},{5,1},{2,6},{6,2},{3,7},{7,3},{8,12},{12,8},{9,1... | collective-permute-start | bytes 294920 | tf_op jit(solution)/shard_map/ppermute | solution.py:205
  43.9 2.7 %collective-permute-start.8 = (bf16[48,1024]{1,0:T(8,128)(2,1)S(1)}, bf16[48,1024]{1,0:T(8,128)(2,1)S(1)}, u32[]{:S(2)}, u32[]{:S(2)}) collective-permute-start(bf16[48,1024]{1,0:T(8,128)(2,1)S(1)} %collective-permute-done.7.h1), channel_id=1, source_target_pairs={{0,4},{4,0},{1,5},{5,1},{2,6},{6,2},{3,7},{7,3},{8,12},{12,8},{9,1... | collective-permute-start | bytes 294920 | tf_op jit(solution)/shard_map/ppermute | solution.py:205
  44.3 1.0 copy-start.4
  45.2 0.8 copy-start.2
  46.5 2.1 %copy-start.14 = (bf16[48,1024]{1,0:T(8,128)(2,1)}, bf16[48,1024]{1,0:T(8,128)(2,1)S(1)}, u32[]{:S(2)}) copy-start(bf16[48,1024]{1,0:T(8,128)(2,1)S(1)} %collective-permute-done.6.c0) | copy-start | bytes 294916
  46.6 2.0 %copy-start.15 = (bf16[48,1024]{1,0:T(8,128)(2,1)}, bf16[48,1024]{1,0:T(8,128)(2,1)S(1)}, u32[]{:S(2)}) copy-start(bf16[48,1024]{1,0:T(8,128)(2,1)S(1)} %collective-permute-done.12.c3) | copy-start | bytes 294916
  46.6 2.0 %copy-start.16 = (bf16[48,1024]{1,0:T(8,128)(2,1)}, bf16[48,1024]{1,0:T(8,128)(2,1)S(1)}, u32[]{:S(2)}) copy-start(bf16[48,1024]{1,0:T(8,128)(2,1)S(1)} %collective-permute-done.10.c2) | copy-start | bytes 294916
  46.6 2.0 %copy-start.17 = (bf16[48,1024]{1,0:T(8,128)(2,1)}, bf16[48,1024]{1,0:T(8,128)(2,1)S(1)}, u32[]{:S(2)}) copy-start(bf16[48,1024]{1,0:T(8,128)(2,1)S(1)} %collective-permute-done.8.c1) | copy-start | bytes 294916
  46.6 1.3 %collective-permute-start.13 = (f32[16,128]{1,0:T(8,128)S(1)}, f32[16,128]{1,0:T(8,128)S(1)}, u32[]{:S(2)}, u32[]{:S(2)}) collective-permute-start(f32[16,128]{1,0:T(8,128)S(1)} %get-tuple-element.47), channel_id=1, source_target_pairs={{0,4},{4,0},{1,5},{5,1},{2,6},{6,2},{3,7},{7,3},{8,12},{12,8},{9,1... | collective-permute-start | bytes 24584 | tf_op jit(solution)/shard_map/ppermute | solution.py:205
  48.6 13.3 %all-to-all-start = ((f32[32,16,128]{2,1,0:T(8,128)}), f32[32,16,128]{2,1,0:T(8,128)S(1)}, u32[]{:S(2)}, u32[]{:S(2)}) async-start(f32[32,16,128]{2,1,0:T(8,128)} %broadcast_in_dim.18), calls=%async_computation | async-start | bytes 524288 | tf_op jit(solution)/shard_map/all_to_all | solution.py:209
  61.9 3.1 %copy-start.3 = (bf16[1,128,128]{2,1,0:T(8,128)(2,1)S(1)}, bf16[1,128,128]{2,1,0:T(8,128)(2,1)}, u32[]{:S(2)}) copy-start(bf16[1,128,128]{2,1,0:T(8,128)(2,1)} %param.6) | copy-start | bytes 98308
  62.0 3.1 %collective-permute-start.14 = (f32[16,128]{1,0:T(8,128)S(1)}, f32[16,128]{1,0:T(8,128)S(1)}, u32[]{:S(2)}, u32[]{:S(2)}) collective-permute-start(f32[16,128]{1,0:T(8,128)S(1)} %reduce_sum.9.lown), channel_id=1, source_target_pairs={{0,4},{4,0},{1,5},{5,1},{2,6},{6,2},{3,7},{7,3},{8,12},{12,8},{9,1... | collective-permute-start | bytes 24584 | tf_op jit(solution)/shard_map/ppermute | solution.py:205
  68.8 1.5 %collective-permute-start.15 = (f32[32,16,128]{2,1,0:T(8,128)S(1)}, f32[32,16,128]{2,1,0:T(8,128)S(1)}, u32[]{:S(2)}, u32[]{:S(2)}) collective-permute-start(f32[32,16,128]{2,1,0:T(8,128)S(1)} %get-tuple-element.62), channel_id=1, source_target_pairs={{0,4},{4,0},{1,5},{5,1},{2,6},{6,2},{3,7},{7,3},{8,12},{12,8},{9,1... | collective-permute-start | bytes 786440 | tf_op jit(solution)/shard_map/ppermute | solution.py:205
  71.1 4.0 %copy-start.20 = (bf16[32,1024]{1,0:T(8,128)(2,1)S(1)}, bf16[32,1024]{1,0:T(8,128)(2,1)}, u32[]{:S(2)}) copy-start(bf16[32,1024]{1,0:T(8,128)(2,1)} %get-tuple-element.57) | copy-start | bytes 196612
  71.1 13.5 %all-to-all-start.1 = ((f32[32,16,128]{2,1,0:T(8,128)}), f32[32,16,128]{2,1,0:T(8,128)S(1)}, u32[]{:S(2)}, u32[]{:S(2)}) async-start(f32[32,16,128]{2,1,0:T(8,128)} %add.7), calls=%async_computation.1 | async-start | bytes 524288 | tf_op jit(solution)/shard_map/all_to_all | solution.py:209
  75.1 9.5 %collective-permute-start.16 = (bf16[32,1024]{1,0:T(8,128)(2,1)S(1)}, bf16[32,1024]{1,0:T(8,128)(2,1)S(1)}, u32[]{:S(2)}, u32[]{:S(2)}) collective-permute-start(bf16[32,1024]{1,0:T(8,128)(2,1)S(1)} %copy-done.20), channel_id=1, source_target_pairs={{0,1},{1,2},{2,3},{3,0},{4,5},{5,6},{6,7},{7,4},{8,9},{9,10},{10,1... | collective-permute-start | bytes 196616 | tf_op jit(solution)/shard_map/ppermute | solution.py:201
  85.3 6.5 %copy-start.19 = (bf16[32,1024]{1,0:T(8,128)(2,1)S(1)}, bf16[32,1024]{1,0:T(8,128)(2,1)}, u32[]{:S(2)}) copy-start(bf16[32,1024]{1,0:T(8,128)(2,1)} %get-tuple-element.58) | copy-start | bytes 196612
  85.3 9.0 %copy-start.18 = (bf16[32,1024]{1,0:T(8,128)(2,1)S(1)}, bf16[32,1024]{1,0:T(8,128)(2,1)}, u32[]{:S(2)}) copy-start(bf16[32,1024]{1,0:T(8,128)(2,1)} %get-tuple-element.59) | copy-start | bytes 196612
  85.3 20.5 %copy-start.5 = (bf16[32,1024]{1,0:T(8,128)(2,1)S(1)}, bf16[32,1024]{1,0:T(8,128)(2,1)}, u32[]{:S(2)}) copy-start(bf16[32,1024]{1,0:T(8,128)(2,1)} %get-tuple-element.67.i0) | copy-start | bytes 196612
  85.3 20.5 %copy-start.6 = (f32[32,128]{1,0:T(8,128)S(1)}, f32[32,128]{1,0:T(8,128)}, u32[]{:S(2)}) copy-start(f32[32,128]{1,0:T(8,128)} %get-tuple-element.66.qt) | copy-start | bytes 49156
  85.3 14.5 %all-to-all-start.2 = ((f32[32,16,128]{2,1,0:T(8,128)}), f32[32,16,128]{2,1,0:T(8,128)S(1)}, u32[]{:S(2)}, u32[]{:S(2)}) async-start(f32[32,16,128]{2,1,0:T(8,128)} %shard_map.89), calls=%async_computation.2 | async-start | bytes 524288 | tf_op jit(solution)/shard_map/all_to_all | solution.py:209
  91.8 7.7 %collective-permute-start.17 = (bf16[32,1024]{1,0:T(8,128)(2,1)S(1)}, bf16[32,1024]{1,0:T(8,128)(2,1)S(1)}, u32[]{:S(2)}, u32[]{:S(2)}) collective-permute-start(bf16[32,1024]{1,0:T(8,128)(2,1)S(1)} %copy-done.19), channel_id=1, source_target_pairs={{0,2},{1,3},{2,0},{3,1},{4,6},{5,7},{6,4},{7,5},{8,10},{9,11},{10,... | collective-permute-start | bytes 196616 | tf_op jit(solution)/shard_map/ppermute | solution.py:201
  94.3 5.2 %collective-permute-start.18 = (bf16[32,1024]{1,0:T(8,128)(2,1)S(1)}, bf16[32,1024]{1,0:T(8,128)(2,1)S(1)}, u32[]{:S(2)}, u32[]{:S(2)}) collective-permute-start(bf16[32,1024]{1,0:T(8,128)(2,1)S(1)} %copy-done.18), channel_id=1, source_target_pairs={{0,3},{1,0},{2,1},{3,2},{4,7},{5,4},{6,5},{7,6},{8,11},{9,8},{10,9... | collective-permute-start | bytes 196616 | tf_op jit(solution)/shard_map/ppermute | solution.py:201
  99.8 6.1 %collective-permute-start.19 = (f32[32,16,128]{2,1,0:T(8,128)S(1)}, f32[32,16,128]{2,1,0:T(8,128)S(1)}, u32[]{:S(2)}, u32[]{:S(2)}) collective-permute-start(f32[32,16,128]{2,1,0:T(8,128)S(1)} %all-to-all-done.2.rown), channel_id=1, source_target_pairs={{0,4},{4,0},{1,5},{5,1},{2,6},{6,2},{3,7},{7,3},{8,12},{12,8},{9,1... | collective-permute-start | bytes 786440 | tf_op jit(solution)/shard_map/ppermute | solution.py:205

commit v7 on v6

--- a/solution.py
+++ b/solution.py
@@ -20,8 +20,8 @@
 RANK = 32
 HALF = RANK // 2
 OWN = 32
-CUT = 16
-PART = WIDE // TENSOR
+CUT = 256
+PLANE = 16
 N_CHIPS = REPLICAS // 2
 STEP = 512
 NT = (((1,), (1,)), ((), ()))
@@ -69,16 +69,33 @@
         copy.wait()
 
 
+def plane():
+    return 4 * lax.axis_index("x") + lax.axis_index("y")
+
+
 def pack_kernel(w, og, s1, s2, s3, lines, feats, packed, sems):
-    t, y, core = lax.axis_index("t"), lax.axis_index("y"), lax.axis_index("core")
-    rows = pl.ds(pl.multiple_of((2 * y + core) * CUT, CUT), CUT)
-    fetched([(w.at[rows, :], lines), (og, feats)], sems)
+    t = lax.axis_index("t")
+    cols = pl.ds(pl.multiple_of(plane() * CUT, CUT), CUT)
+    fetched([(w.at[:, cols], lines), (og, feats)], sems)
     for k in range(1, TENSOR):
-        target = lax.rem(t + k, TENSOR)
-        packed[k - 1, 0:CUT, :] = lines[:, pl.ds(pl.multiple_of(target * PART, PART), PART)]
-        for m in range(8):
-            packed[k - 1, CUT : 2 * CUT, 128 * m : 128 * m + 128] = feats[16 * m : 16 * m + 16, :]
+        first = OWN * lax.rem(t + k, TENSOR)
+        packed[k - 1, 0:HEAD, :] = lines[...]
+        for h in range(2):
+            rows = pl.ds(pl.multiple_of(first + 16 * h, 16), 16)
+            packed[k - 1, HEAD : HEAD + 16, 128 * h : 128 * h + 128] = feats[rows, :]
     fetched([(packed.at[k], send) for k, send in enumerate((s1, s2, s3))], sems)
+
+
+def rows_kernel(og, r1, r2, r3, out, held):
+    t = lax.axis_index("t")
+    held[:, 0:128] = og[pl.ds(pl.multiple_of(OWN * t, OWN), OWN), :]
+    for k, r in enumerate((r1, r2, r3), 1):
+        for h in range(2):
+            held[16 * h : 16 * h + 16, 128 * k : 128 * k + 128] = r[
+                HEAD : HEAD + 16, 128 * h : 128 * h + 128
+            ]
+    for g in range(PLANE):
+        out[g] = held[...]
 
 
 def early_kernel(a0, ef, warm, inner, fed, lines):
@@ -141,18 +158,25 @@
             send[chip] = r[HALF:, 128 * j : 128 * j + 128]
 
 
-def spread_kernel(pieces, out):
-    total = jnp.sum(pieces[...], axis=0) * (1.0 / REPLICAS)
-    out[...] = jnp.broadcast_to(total[None], out.shape)
-
-
-def finish_kernel(rown, roth, qt, og, a0, a1, a2, a3, ef, i0, i1, i2, i3, err, fac, igrad):
+def spread_kernel(pieces, inputs, out):
+    hi, mid = split2(jnp.sum(pieces[...], axis=0) * (1.0 / REPLICAS))
+    for chip in range(N_CHIPS):
+        g = chip // 8 * 4 + chip % 4
+        out[chip, 0:16, :] = hi
+        out[chip, 16:32, :] = mid
+        out[chip, 32:64, :] = inputs[g, :, 0:128]
+        out[chip, 64:96, :] = inputs[g, :, 128:256]
+
+
+def finish_kernel(mixed, roth, qt, og, a0, a1, a2, a3, ef, err, fac, igrad):
     t, core = lax.axis_index("t"), lax.axis_index("core")
+    zl = lax.axis_index("zl")
     mine = pl.ds(pl.multiple_of(core * HALF, HALF), HALF)
     other = pl.ds(pl.multiple_of((1 - core) * HALF, HALF), HALF)
-    for k, block in enumerate((i0, i1, i2, i3)):
-        source = lax.rem(t - k + TENSOR, TENSOR)
-        igrad[:, pl.ds(pl.multiple_of(source * PART, PART), PART)] = block[...]
+    for g in range(PLANE):
+        chip = g // 4 * 8 + 4 * zl + g % 4
+        igrad[:, CUT * g : CUT * g + 128] = mixed[chip, 32:64, :]
+        igrad[:, CUT * g + 128 : CUT * g + 256] = mixed[chip, 64:96, :]
     q = jnp.concatenate([qt[mine, :], qt[other, :]], axis=0)
     hi, mid = split2(q)
     hi, mid = hi.astype(F32), mid.astype(F32)
@@ -160,41 +184,34 @@
     lhs = jnp.concatenate([ogp, -hi, -hi, -mid, -mid], axis=0).T.astype(BF16)
     for c in range(0, WIDE, STEP):
         cols = slice(c, c + STEP)
-        ro = jnp.concatenate([rown[c // 128 + j] for j in range(STEP // 128)], axis=1)
-        rt = jnp.concatenate([roth[c // 128 + j] for j in range(STEP // 128)], axis=1)
-        fac[mine, cols] = ro.astype(BF16)
-        fac[other, cols] = rt.astype(BF16)
-        rhi, rmid = split2(jnp.concatenate([ro, rt], axis=0))
-        rhs = jnp.concatenate([a[:, cols] for a in (a0, a1, a2, a3)] + [rhi, rmid, rhi, rmid], axis=0)
+        chips = range(c // 128, (c + STEP) // 128)
+        own = jnp.concatenate([mixed[j, 0:32, :] for j in chips], axis=1)
+        oth = jnp.concatenate([roth[j] for j in chips], axis=1)
+        fac[mine, cols] = own[0:16]
+        fac[other, cols] = oth[0:16]
+        high = jnp.concatenate([own[0:16], oth[0:16]], axis=0)
+        low = jnp.concatenate([own[16:32], oth[16:32]], axis=0)
+        rhs = jnp.concatenate(
+            [a[:, cols] for a in (a0, a1, a2, a3)] + [high, low, high, low], axis=0
+        )
         total = jnp.dot(lhs, rhs, preferred_element_type=F32) + ef[:, cols].astype(F32)
         err[:, cols] = total.astype(BF16)
 
 
-def input_kernel(w, og, r1, r2, r3, h0, h1, h2, h3, c0, c1, c2, c3, *rest):
-    *outs, rv, hv, cv, weights, feats, total, sems = rest
-    t, y, core = lax.axis_index("t"), lax.axis_index("y"), lax.axis_index("core")
-    mine = w.at[:, pl.ds(pl.multiple_of(t * PART, PART), PART)]
-    pairs = [(mine, weights.at[pl.ds(0, 128), :]), (og, feats.at[:, pl.ds(0, 128)])]
-    pairs += [(r, rv.at[k]) for k, r in enumerate((r1, r2, r3))]
-    pairs += [(h, hv.at[j]) for j, h in enumerate((h0, h1, h2, h3))]
-    pairs += [(c, cv.at[j]) for j, c in enumerate((c0, c1, c2, c3))]
+def input_kernel(w, feats, r1, r2, r3, out, fv, weights, total, sems):
+    cols = pl.ds(pl.multiple_of(plane() * CUT, CUT), CUT)
+    pairs = [(w.at[:, cols], weights.at[pl.ds(0, HEAD), :]), (feats, fv)]
+    pairs += [
+        (r.at[pl.ds(0, HEAD), :], weights.at[pl.ds(HEAD * k, HEAD), :])
+        for k, r in enumerate((r1, r2, r3), 1)
+    ]
     fetched(pairs, sems)
-    for k in range(1, TENSOR):
-        for m in range(8):
-            feats[16 * m : 16 * m + 16, 128 * k : 128 * k + 128] = rv[
-                k - 1, CUT : 2 * CUT, 128 * m : 128 * m + 128
-            ]
-        for j in range(4):
-            first = 128 * k + 2 * CUT * lax.rem(y - j + 4, 4)
-            here = pl.ds(pl.multiple_of(first + CUT * core, CUT), CUT)
-            there = pl.ds(pl.multiple_of(first + CUT * (1 - core), CUT), CUT)
-            weights[here, :] = hv[j, CUT * (k - 1) : CUT * k, :]
-            weights[there, :] = cv[j, CUT * (k - 1) : CUT * k, :]
-    for k in range(TENSOR):
-        target = lax.rem(t + k, TENSOR)
-        rows = feats[pl.ds(pl.multiple_of(target * OWN, OWN), OWN), :]
-        total[k] = jnp.dot(rows, weights[...], preferred_element_type=F32).astype(BF16)
-    fetched([(total.at[k], out) for k, out in enumerate(outs)], sems)
+    for g in range(0, PLANE, 4):
+        rows = jnp.concatenate([fv[g + i] for i in range(4)], axis=0)
+        part = jnp.dot(rows, weights[...], preferred_element_type=F32).astype(BF16)
+        for i in range(4):
+            total[g + i] = part[OWN * i : OWN * i + OWN]
+    fetched([(total, out)], sems)
 
 
 def moved(x, k, axis="t"):
@@ -216,11 +233,11 @@
 
     sends = call(
         pack_kernel,
-        [((2 * CUT, PART), BF16)] * 3,
+        [((HEAD + 16, CUT), BF16)] * 3,
         [
-            pltpu.VMEM((CUT, WIDE), BF16),
+            pltpu.VMEM((HEAD, CUT), BF16),
             pltpu.VMEM((128, HEAD), BF16),
-            pltpu.VMEM((3, 2 * CUT, PART), BF16),
+            pltpu.VMEM((3, HEAD + 16, CUT), BF16),
             pltpu.SemaphoreType.DMA((3,)),
         ],
         space=pltpu.MemorySpace.HBM,
@@ -229,44 +246,39 @@
     )(weight, og)
     got = [moved(x, k) for k, x in zip((1, 2, 3), sends)]
     acts = [act] + [moved(act, k) for k in (1, 2, 3)]
-    shares = [jnp.concatenate([g[:CUT] for g in got], axis=0)]
-    shares += [moved(shares[0], j, "y") for j in (1, 2, 3)]
-    traded = [swapped(x) for x in shares]
+    (rows,) = call(rows_kernel, [((PLANE, OWN, 512), BF16)], [pltpu.VMEM((OWN, 512), BF16)])(og, *got)
+    feats = exchanged(rows, ("x", "y"))
     inner, fed, lines = call(
         early_kernel,
         [((RANK, OWN), F32), ((RANK, HEAD), F32), ((RANK, WIDE), BF16)],
-        flops=0,
-        moved=0,
+        flops=10**10,
+        moved=10**8,
     )(act, ef, warm)
 
     half = ((HALF, HEAD), F32)
     left_keep, left_send = call(
         left_kernel, [half, half], [pltpu.VMEM((RANK, HEAD), F32)], flops=5 * 10**7, moved=10**6
     )(*acts[1:], og, lines, inner, fed)
-    left_send, traded, shares = lax.optimization_barrier((left_send, traded, shares))
+    left_send, feats = lax.optimization_barrier((left_send, feats))
 
     left_half = left_keep + swapped(left_send)
     pieces = exchanged(jnp.broadcast_to(left_half[None], (N_CHIPS, HALF, HEAD)), CHIPS)
-    outs = call(
+    (inputs,) = call(
         input_kernel,
-        [((OWN, PART), BF16)] * 4,
+        [((PLANE, OWN, CUT), BF16)],
         [
-            pltpu.VMEM((3, 2 * CUT, PART), BF16),
-            pltpu.VMEM((4, 3 * CUT, PART), BF16),
-            pltpu.VMEM((4, 3 * CUT, PART), BF16),
-            pltpu.VMEM((512, PART), BF16),
-            pltpu.VMEM((128, 512), BF16),
-            pltpu.VMEM((4, OWN, PART), BF16),
-            pltpu.SemaphoreType.DMA((13,)),
+            pltpu.VMEM((PLANE, OWN, 512), BF16),
+            pltpu.VMEM((512, CUT), BF16),
+            pltpu.VMEM((PLANE, OWN, CUT), BF16),
+            pltpu.SemaphoreType.DMA((5,)),
         ],
         flops=2 * 10**8,
         moved=2 * 10**6,
         space=pltpu.MemorySpace.HBM,
         dest=pltpu.MemorySpace.HBM,
         room=60,
-    )(weight, og, *got, *shares, *traded)
-    inputs = [outs[0]] + [moved(o, k) for k, o in zip((1, 2, 3), outs[1:])]
-    pieces, outs = lax.optimization_barrier((pieces, outs))
+    )(weight, feats, *got)
+    pieces, inputs = lax.optimization_barrier((pieces, inputs))
     left_own = jnp.sum(pieces, axis=0)
     left_other = swapped(left_own)
 
@@ -280,18 +292,16 @@
     )(left_own, left_other, *acts, og, ef)
 
     pieces = exchanged(right_keep + swapped(right_send), CHIPS)
-    pieces, inputs[1] = lax.optimization_barrier((pieces, inputs[1]))
-    (mean,) = call(spread_kernel, [block])(pieces)
-    right_own = exchanged(mean, CHIPS)
-    right_own, inputs = lax.optimization_barrier((right_own, inputs))
-    right_other = swapped(right_own)
+    (mixed,) = call(spread_kernel, [((N_CHIPS, 96, 128), BF16)])(pieces, inputs)
+    mixed = exchanged(mixed, CHIPS)
+    right_other = swapped(mixed[:, 0:32])
 
     err, fac, igrad = call(
         finish_kernel,
         [((HEAD, WIDE), BF16), ((RANK, WIDE), BF16), ((OWN, WIDE), BF16)],
         flops=3 * 10**8,
         moved=5 * 10**6,
-    )(right_own, right_other, basis, og, *acts, ef, *inputs)
+    )(mixed, right_other, basis, og, *acts, ef)
 
     return (err[None, None], basis.T[None], fac.T[None, None], igrad[None])
 

time: 108 us -> 104 us (0.963)
  blocking collectives: 0 us -> 27.1 us
  starting transfers between devices: 59.3 us -> 34 us
  local copies, waits for them, and re-layouts: 3.16 us -> 0.78 us
  waiting for transfers between devices: 31.4 us -> 29.4 us
    all_to_all x0 -> x2, blocking collectives: none -> 27.1 us  [exchanged(): return lax.all_to_all(x, axes, 0, 0, tiled=True)]
    ppermute x8 -> x4, starting transfers between devices: 21 us -> 7.82 us  [swapped(): return lax.ppermute(x, 'core', [(0, 1), (1, 0)])]
    ppermute x12 -> x6, starting transfers between devices: 22.7 us -> 14.8 us  [moved(): return lax.ppermute(x, axis, [(i, (i + k) % 4) for i in range(4)])]
    ppermute x12 -> x6, waiting for transfers between devices: 21.8 us -> 16.9 us  [moved(): return lax.ppermute(x, axis, [(i, (i + k) % 4) for i in range(4)])]
    all_to_all x3 -> x2, starting transfers between devices: 15.7 us -> 11.4 us  [exchanged(): return lax.all_to_all(x, axes, 0, 0, tiled=True)]
    all_to_all x3 -> x2, waiting for transfers between devices: 5.34 us -> 8.47 us  [exchanged(): return lax.all_to_all(x, axes, 0, 0, tiled=True)]
    unnamed x42 -> x20, local copies, waits for them, and re-layouts: 2.42 us -> 0.04 us
    pallas_call x7 -> x8, Pallas kernels: 11.8 us -> 11.1 us  [run(): pl.pallas_call(kernel, out_shape=[jax.ShapeDtypeStruct(s, d) for s, d in...]
  transfers between devices with their start and end apart: 23 -> 12, of which waited for: 11 -> 8; matrix products, arithmetic and copies ran while one was open for 0% -> 0% of each run, Pallas kernels for 4% -> 4%
where the time goes in v7:
time: 104 us; the launch traced here: 103 us
  starting transfers between devices  34 us (33%)
  waiting for transfers between devices  29.4 us (28%)
  blocking collectives  27.1 us (26%)
  Pallas kernels  11.1 us (11%)
    all_to_all x2, blocking collectives, exchanged(): return lax.all_to_all(x, axes, 0, 0, tiled=True)  27.1 us
    ppermute x6, waiting for transfers between devices, moved(): return lax.ppermute(x, axis, [(i, (i + k) % 4) for i in range(4)])  16.9 us
    ppermute x6, starting transfers between devices, moved(): return lax.ppermute(x, axis, [(i, (i + k) % 4) for i in range(4)])  14.8 us
    all_to_all x2, starting transfers between devices, exchanged(): return lax.all_to_all(x, axes, 0, 0, tiled=True)  11.4 us
    pallas_call x8, Pallas kernels, run(): pl.pallas_call(kernel, out_shape=[jax.ShapeDtypeStruct(s, d) for s, d in...  11.1 us
    all_to_all x2, waiting for transfers between devices, exchanged(): return lax.all_to_all(x, axes, 0, 0, tiled=True)  8.47 us
    ppermute x4, starting transfers between devices, swapped(): return lax.ppermute(x, 'core', [(0, 1), (1, 0)])  7.82 us
    ppermute x4, waiting for transfers between devices, swapped(): return lax.ppermute(x, 'core', [(0, 1), (1, 0)])  4.01 us
  transfers between devices with their start and end apart: 12, of which 8 were waited for; matrix products, arithmetic and copies ran while one was open for 0% of the time, Pallas kernels for 4%

profile of v7, /device:TPU:1, one launch (start us, length us, event | category | flops | bytes accessed | tf_op | source)
XLA Modules:
  0.0 103.2 jit_solution(12163112217047246729)
XLA Ops:
  0.6 0.0 copy-start.1
  0.6 0.0 copy-start.3
  0.7 1.6 %shard_map.86 = (bf16[144,256]{1,0:T(8,128)(2,1)}, bf16[144,256]{1,0:T(8,128)(2,1)}, bf16[144,256]{1,0:T(8,128)(2,1)}) custom-call(bf16[128,4096]{1,0:T(8,128)(2,1)} %bitcast.31, bf16[128,128]{1,0:T(8,128)(2,1)} %bitcast.24), custom_call_target="tpu_custom_call" | custom-call | flops 1000000 | bytes 1000000 | tf_op jit(solution)/shard_map/pallas_call | solution.py:51
  2.3 0.0 copy-start
  2.3 3.9 %collective-permute-start.3 = (bf16[144,256]{1,0:T(8,128)(2,1)}, bf16[144,256]{1,0:T(8,128)(2,1)S(1)}, u32[]{:S(2)}, u32[]{:S(2)}) collective-permute-start(bf16[144,256]{1,0:T(8,128)(2,1)} %get-tuple-element.27), channel_id=1, source_target_pairs={{0,1},{1,2},{2,3},{3,0},{4,5},{5,6},{6,7},{7,4},{8,9},{9,10},{10,1... | collective-permute-start | bytes 221192 | tf_op jit(solution)/shard_map/ppermute | solution.py:218
  6.2 5.1 %collective-permute-start.4 = (bf16[144,256]{1,0:T(8,128)(2,1)}, bf16[144,256]{1,0:T(8,128)(2,1)S(1)}, u32[]{:S(2)}, u32[]{:S(2)}) collective-permute-start(bf16[144,256]{1,0:T(8,128)(2,1)} %get-tuple-element.28), channel_id=1, source_target_pairs={{0,2},{1,3},{2,0},{3,1},{4,6},{5,7},{6,4},{7,5},{8,10},{9,11},{10,... | collective-permute-start | bytes 221192 | tf_op jit(solution)/shard_map/ppermute | solution.py:218
  11.3 2.4 %collective-permute-start.5 = (bf16[144,256]{1,0:T(8,128)(2,1)}, bf16[144,256]{1,0:T(8,128)(2,1)S(1)}, u32[]{:S(2)}, u32[]{:S(2)}) collective-permute-start(bf16[144,256]{1,0:T(8,128)(2,1)} %get-tuple-element.29), channel_id=1, source_target_pairs={{0,3},{1,0},{2,1},{3,2},{4,7},{5,4},{6,5},{7,6},{8,11},{9,8},{10,9... | collective-permute-start | bytes 221192 | tf_op jit(solution)/shard_map/ppermute | solution.py:218
  13.7 0.0 copy-done.1
  13.7 0.0 collective-permute-start.2
  13.7 3.2 %collective-permute-start.1 = (bf16[32,4096]{1,0:T(8,128)(2,1)S(1)}, bf16[32,4096]{1,0:T(8,128)(2,1)S(1)}, u32[]{:S(2)}, u32[]{:S(2)}) collective-permute-start(bf16[32,4096]{1,0:T(8,128)(2,1)S(1)} %bitcast.19), channel_id=1, source_target_pairs={{0,2},{1,3},{2,0},{3,1},{4,6},{5,7},{6,4},{7,5},{8,10},{9,11},{10,... | collective-permute-start | bytes 786440 | tf_op jit(solution)/shard_map/ppermute | solution.py:218
  17.0 0.0 collective-permute-done.3.r1
  17.0 0.0 copy-start.4
  17.0 0.1 collective-permute-start
  17.1 0.0 collective-permute-done.4.r2
  17.1 0.0 copy-start.5
  17.1 10.2 %collective-permute-done.5.r3 = bf16[144,256]{1,0:T(8,128)(2,1)S(1)} collective-permute-done((bf16[144,256]{1,0:T(8,128)(2,1)}, bf16[144,256]{1,0:T(8,128)(2,1)S(1)}, u32[]{:S(2)}, u32[]{:S(2)}) %collective-permute-start.5) | collective-permute-done | bytes 73760 | tf_op jit(solution)/shard_map/ppermute | solution.py:218
  27.3 0.0 copy-done.3
  27.3 0.0 copy-start.6
  27.3 0.9 shard_map.87
  28.1 0.0 copy-done.4
  28.1 0.0 copy-done.5
  28.2 0.0 copy-done.6
  28.2 0.0 copy-start.8
  28.2 6.9 %all-to-all-start = ((bf16[16,32,512]{2,1,0:T(8,128)(2,1)}), bf16[16,32,512]{2,1,0:T(8,128)(2,1)S(1)}, u32[]{:S(2)}, u32[]{:S(2)}) async-start(bf16[16,32,512]{2,1,0:T(8,128)(2,1)} %shard_map.87), calls=%async_computation | async-start | bytes 1048576 | tf_op jit(solution)/shard_map/all_to_all | solution.py:226
  35.1 0.0 copy-done
  35.1 0.0 copy-done.8
  35.1 0.5 shard_map.84
  35.6 6.7 %collective-permute-done.2.a3 = bf16[32,4096]{1,0:T(8,128)(2,1)S(1)} collective-permute-done((bf16[32,4096]{1,0:T(8,128)(2,1)S(1)}, bf16[32,4096]{1,0:T(8,128)(2,1)S(1)}, u32[]{:S(2)}, u32[]{:S(2)}) %collective-permute-start.2) | collective-permute-done | bytes 262176 | tf_op jit(solution)/shard_map/ppermute | solution.py:218
  42.3 0.0 collective-permute-done.1.a2
  42.3 0.0 collective-permute-done.a1
  42.3 0.6 shard_map.85
  42.8 2.5 %all-to-all-done.feats = bf16[16,32,512]{2,1,0:T(8,128)(2,1)S(1)} async-done(((bf16[16,32,512]{2,1,0:T(8,128)(2,1)}), bf16[16,32,512]{2,1,0:T(8,128)(2,1)S(1)}, u32[]{:S(2)}, u32[]{:S(2)}) %all-to-all-start) | async-done | bytes 524320 | tf_op jit(solution)/shard_map/all_to_all | solution.py:226
  45.4 0.0 copy-start.9
  45.4 2.1 %collective-permute-start.6 = (f32[16,128]{1,0:T(8,128)S(1)}, f32[16,128]{1,0:T(8,128)S(1)}, u32[]{:S(2)}, u32[]{:S(2)}) collective-permute-start(f32[16,128]{1,0:T(8,128)S(1)} %get-tuple-element.30), channel_id=1, source_target_pairs={{0,4},{4,0},{1,5},{5,1},{2,6},{6,2},{3,7},{7,3},{8,12},{12,8},{9,1... | collective-permute-start | bytes 24584 | tf_op jit(solution)/shard_map/ppermute | solution.py:222
  47.5 0.8 collective-permute-done.6
  48.3 0.7 broadcast_in_dim.18
  49.1 4.5 %all-to-all-start.1 = ((f32[32,16,128]{2,1,0:T(8,128)}), f32[32,16,128]{2,1,0:T(8,128)S(1)}, u32[]{:S(2)}, u32[]{:S(2)}) async-start(f32[32,16,128]{2,1,0:T(8,128)} %broadcast_in_dim.18), calls=%async_computation.1 | async-start | bytes 524288 | tf_op jit(solution)/shard_map/all_to_all | solution.py:226
  53.6 0.0 copy-done.9
  53.6 2.2 %shard_map.88.inputs = bf16[16,32,256]{2,1,0:T(8,128)(2,1)} custom-call(bf16[128,4096]{1,0:T(8,128)(2,1)} %bitcast.32, bf16[16,32,512]{2,1,0:T(8,128)(2,1)} %copy-done.9, bf16[144,256]{1,0:T(8,128)(2,1)} %copy-done.4, bf16[144,256]{1,0:T(8,128)(2,1)} %copy-done.5, bf16[144,256]{1,0:T(8,128)(2,1)} %copy-done.6), custom_call_target="tpu_custom_call" | custom-call | flops 200000000 | bytes 2000000 | tf_op jit(solution)/shard_map/pallas_call | solution.py:51
  55.8 5.9 %all-to-all-done.1 = f32[32,16,128]{2,1,0:T(8,128)S(1)} async-done(((f32[32,16,128]{2,1,0:T(8,128)}), f32[32,16,128]{2,1,0:T(8,128)S(1)}, u32[]{:S(2)}, u32[]{:S(2)}) %all-to-all-start.1) | async-done | bytes 262176 | tf_op jit(solution)/shard_map/all_to_all | solution.py:226
  61.7 2.1 %collective-permute-start.7 = (f32[16,128]{1,0:T(8,128)S(1)}, f32[16,128]{1,0:T(8,128)S(1)}, u32[]{:S(2)}, u32[]{:S(2)}) collective-permute-start(f32[16,128]{1,0:T(8,128)S(1)} %reduce_sum.9.lown), channel_id=1, source_target_pairs={{0,4},{4,0},{1,5},{5,1},{2,6},{6,2},{3,7},{7,3},{8,12},{12,8},{9,1... | collective-permute-start | bytes 24584 | tf_op jit(solution)/shard_map/ppermute | solution.py:222
  63.8 0.8 collective-permute-done.7.loth
  64.6 3.8 %shard_map.89 = (f32[32,128]{1,0:T(8,128)}, f32[32,16,128]{2,1,0:T(8,128)S(1)}, f32[32,16,128]{2,1,0:T(8,128)S(1)}) custom-call(f32[16,128]{1,0:T(8,128)S(1)} %reduce_sum.9.lown, f32[16,128]{1,0:T(8,128)S(1)} %collective-permute-done.7.loth, bf16[32,4096]{1,0:T(8,128)(2,1)S(1)} %bitcast.22, bf16[32,4096]{1,0:T(8,128)(2,1)S(1)} %collective-permute-done.a1, ...), custom_call_target="tpu_custom_call" | custom-call | flops 100000000 | bytes 3000000 | tf_op jit(solution)/shard_map/pallas_call | solution.py:51
  68.4 0.3 collective-permute-start.8
  68.7 1.2 %collective-permute-done.8 = f32[32,16,128]{2,1,0:T(8,128)S(1)} collective-permute-done((f32[32,16,128]{2,1,0:T(8,128)S(1)}, f32[32,16,128]{2,1,0:T(8,128)S(1)}, u32[]{:S(2)}, u32[]{:S(2)}) %collective-permute-start.8) | collective-permute-done | bytes 262176 | tf_op jit(solution)/shard_map/ppermute | solution.py:222
  70.0 0.0 copy-start.2
  70.0 11.5 %all_to_all.20.pieces = f32[32,16,128]{2,1,0:T(8,128)S(1)} all-to-all(f32[32,16,128]{2,1,0:T(8,128)S(1)} %add.7), channel_id=1, replica_groups=mesh['x'=4,'zl'=2,'y'=4,'core'=2,'t'=4] {'x','zl','y'}, dimensions={0} | all-to-all | bytes 524288 | tf_op jit(solution)/shard_map/all_to_all | solution.py:226
  81.5 0.0 copy-done.2
  81.5 0.1 shard_map.90
  81.6 15.5 %all_to_all.21.mixed = bf16[32,96,128]{2,1,0:T(8,128)(2,1)S(1)} all-to-all(bf16[32,96,128]{2,1,0:T(8,128)(2,1)S(1)} %shard_map.90), channel_id=1, replica_groups=mesh['x'=4,'zl'=2,'y'=4,'core'=2,'t'=4] {'x','zl','y'}, dimensions={0} | all-to-all | bytes 1572864 | tf_op jit(solution)/shard_map/all_to_all | solution.py:226
  97.2 0.0 copy-start.7
  97.2 3.3 %collective-permute-start.9 = (bf16[32,32,128]{2,1,0:T(8,128)(2,1)S(1)}, bf16[32,32,128]{2,1,0:T(8,128)(2,1)S(1)}, u32[]{:S(2)}, u32[]{:S(2)}) collective-permute-start(bf16[32,32,128]{2,1,0:T(8,128)(2,1)S(1)} %slice.4), channel_id=1, source_target_pairs={{0,4},{4,0},{1,5},{5,1},{2,6},{6,2},{3,7},{7,3},{8,12},{12,8},{9,1... | collective-permute-start | bytes 786440 | tf_op jit(solution)/shard_map/ppermute | solution.py:222
  100.5 1.2 %collective-permute-done.9.roth = bf16[32,32,128]{2,1,0:T(8,128)(2,1)S(1)} collective-permute-done((bf16[32,32,128]{2,1,0:T(8,128)(2,1)S(1)}, bf16[32,32,128]{2,1,0:T(8,128)(2,1)S(1)}, u32[]{:S(2)}, u32[]{:S(2)}) %collective-permute-start.9) | collective-permute-done | bytes 262176 | tf_op jit(solution)/shard_map/ppermute | solution.py:222
  101.6 0.0 copy-done.7
  101.6 1.6 %shard_map.91 = (bf16[128,4096]{1,0:T(8,128)(2,1)}, bf16[32,4096]{1,0:T(8,128)(2,1)}, bf16[32,4096]{1,0:T(8,128)(2,1)}) custom-call(bf16[32,96,128]{2,1,0:T(8,128)(2,1)S(1)} %all_to_all.21.mixed, bf16[32,32,128]{2,1,0:T(8,128)(2,1)S(1)} %collective-permute-done.9.roth, f32[32,128]{1,0:T(8,128)S(1)} %copy-done.7, bf16[128,128]{1,0:T(8,128)(2,1)S(1)} %bitcast.28, ...), custom_call_target="tpu_custom_call" | custom-call | flops 300000000 | bytes 5000000 | tf_op jit(solution)/shard_map/pallas_call | solution.py:51
  (4 shorter events, 0.1 us)
Async XLA Ops:
  0.6 13.1 %copy-start.1 = (bf16[1,32,4096]{2,1,0:T(8,128)(2,1)S(1)}, bf16[1,32,4096]{2,1,0:T(8,128)(2,1)}, u32[]{:S(2)}) copy-start(bf16[1,32,4096]{2,1,0:T(8,128)(2,1)} %param.5) | copy-start | bytes 786436
  0.6 26.6 %copy-start.3 = (bf16[1,128,128]{2,1,0:T(8,128)(2,1)S(1)}, bf16[1,128,128]{2,1,0:T(8,128)(2,1)}, u32[]{:S(2)}) copy-start(bf16[1,128,128]{2,1,0:T(8,128)(2,1)} %param.6) | copy-start | bytes 98308
  2.3 32.8 %copy-start = (bf16[1,1,128,4096]{3,2,1,0:T(8,128)(2,1)S(1)}, bf16[1,1,128,4096]{3,2,1,0:T(8,128)(2,1)}, u32[]{:S(2)}) copy-start(bf16[1,1,128,4096]{3,2,1,0:T(8,128)(2,1)} %param.8) | copy-start | bytes 3145732
  2.3 14.7 %collective-permute-start.3 = (bf16[144,256]{1,0:T(8,128)(2,1)}, bf16[144,256]{1,0:T(8,128)(2,1)S(1)}, u32[]{:S(2)}, u32[]{:S(2)}) collective-permute-start(bf16[144,256]{1,0:T(8,128)(2,1)} %get-tuple-element.27), channel_id=1, source_target_pairs={{0,1},{1,2},{2,3},{3,0},{4,5},{5,6},{6,7},{7,4},{8,9},{9,10},{10,1... | collective-permute-start | bytes 221192 | tf_op jit(solution)/shard_map/ppermute | solution.py:218
  6.2 10.9 %collective-permute-start.4 = (bf16[144,256]{1,0:T(8,128)(2,1)}, bf16[144,256]{1,0:T(8,128)(2,1)S(1)}, u32[]{:S(2)}, u32[]{:S(2)}) collective-permute-start(bf16[144,256]{1,0:T(8,128)(2,1)} %get-tuple-element.28), channel_id=1, source_target_pairs={{0,2},{1,3},{2,0},{3,1},{4,6},{5,7},{6,4},{7,5},{8,10},{9,11},{10,... | collective-permute-start | bytes 221192 | tf_op jit(solution)/shard_map/ppermute | solution.py:218
  11.3 16.0 %collective-permute-start.5 = (bf16[144,256]{1,0:T(8,128)(2,1)}, bf16[144,256]{1,0:T(8,128)(2,1)S(1)}, u32[]{:S(2)}, u32[]{:S(2)}) collective-permute-start(bf16[144,256]{1,0:T(8,128)(2,1)} %get-tuple-element.29), channel_id=1, source_target_pairs={{0,3},{1,0},{2,1},{3,2},{4,7},{5,4},{6,5},{7,6},{8,11},{9,8},{10,9... | collective-permute-start | bytes 221192 | tf_op jit(solution)/shard_map/ppermute | solution.py:218
  13.7 28.6 %collective-permute-start.2 = (bf16[32,4096]{1,0:T(8,128)(2,1)S(1)}, bf16[32,4096]{1,0:T(8,128)(2,1)S(1)}, u32[]{:S(2)}, u32[]{:S(2)}) collective-permute-start(bf16[32,4096]{1,0:T(8,128)(2,1)S(1)} %bitcast.18), channel_id=1, source_target_pairs={{0,3},{1,0},{2,1},{3,2},{4,7},{5,4},{6,5},{7,6},{8,11},{9,8},{10,9... | collective-permute-start | bytes 786440 | tf_op jit(solution)/shard_map/ppermute | solution.py:218
  13.7 28.6 %collective-permute-start.1 = (bf16[32,4096]{1,0:T(8,128)(2,1)S(1)}, bf16[32,4096]{1,0:T(8,128)(2,1)S(1)}, u32[]{:S(2)}, u32[]{:S(2)}) collective-permute-start(bf16[32,4096]{1,0:T(8,128)(2,1)S(1)} %bitcast.19), channel_id=1, source_target_pairs={{0,2},{1,3},{2,0},{3,1},{4,6},{5,7},{6,4},{7,5},{8,10},{9,11},{10,... | collective-permute-start | bytes 786440 | tf_op jit(solution)/shard_map/ppermute | solution.py:218
  17.0 11.2 %copy-start.4 = (bf16[144,256]{1,0:T(8,128)(2,1)}, bf16[144,256]{1,0:T(8,128)(2,1)S(1)}, u32[]{:S(2)}) copy-start(bf16[144,256]{1,0:T(8,128)(2,1)S(1)} %collective-permute-done.3.r1) | copy-start | bytes 221188
  17.0 25.3 %collective-permute-start = (bf16[32,4096]{1,0:T(8,128)(2,1)S(1)}, bf16[32,4096]{1,0:T(8,128)(2,1)S(1)}, u32[]{:S(2)}, u32[]{:S(2)}) collective-permute-start(bf16[32,4096]{1,0:T(8,128)(2,1)S(1)} %bitcast.20), channel_id=1, source_target_pairs={{0,1},{1,2},{2,3},{3,0},{4,5},{5,6},{6,7},{7,4},{8,9},{9,10},{10,1... | collective-permute-start | bytes 786440 | tf_op jit(solution)/shard_map/ppermute | solution.py:218
  17.1 11.1 %copy-start.5 = (bf16[144,256]{1,0:T(8,128)(2,1)}, bf16[144,256]{1,0:T(8,128)(2,1)S(1)}, u32[]{:S(2)}) copy-start(bf16[144,256]{1,0:T(8,128)(2,1)S(1)} %collective-permute-done.4.r2) | copy-start | bytes 221188
  27.3 0.9 copy-start.6
  28.2 6.9 %copy-start.8 = (bf16[1,1,4096,32]{2,3,1,0:T(8,128)(2,1)S(1)}, bf16[1,1,4096,32]{2,3,1,0:T(8,128)(2,1)}, u32[]{:S(2)}) copy-start(bf16[1,1,4096,32]{2,3,1,0:T(8,128)(2,1)} %param.9) | copy-start | bytes 786436
  28.2 17.2 %all-to-all-start = ((bf16[16,32,512]{2,1,0:T(8,128)(2,1)}), bf16[16,32,512]{2,1,0:T(8,128)(2,1)S(1)}, u32[]{:S(2)}, u32[]{:S(2)}) async-start(bf16[16,32,512]{2,1,0:T(8,128)(2,1)} %shard_map.87), calls=%async_computation | async-start | bytes 1048576 | tf_op jit(solution)/shard_map/all_to_all | solution.py:226
  45.4 8.2 %copy-start.9 = (bf16[16,32,512]{2,1,0:T(8,128)(2,1)}, bf16[16,32,512]{2,1,0:T(8,128)(2,1)S(1)}, u32[]{:S(2)}) copy-start(bf16[16,32,512]{2,1,0:T(8,128)(2,1)S(1)} %all-to-all-done.feats) | copy-start | bytes 1572868
  45.4 3.0 %collective-permute-start.6 = (f32[16,128]{1,0:T(8,128)S(1)}, f32[16,128]{1,0:T(8,128)S(1)}, u32[]{:S(2)}, u32[]{:S(2)}) collective-permute-start(f32[16,128]{1,0:T(8,128)S(1)} %get-tuple-element.30), channel_id=1, source_target_pairs={{0,4},{4,0},{1,5},{5,1},{2,6},{6,2},{3,7},{7,3},{8,12},{12,8},{9,1... | collective-permute-start | bytes 24584 | tf_op jit(solution)/shard_map/ppermute | solution.py:222
  49.1 12.6 %all-to-all-start.1 = ((f32[32,16,128]{2,1,0:T(8,128)}), f32[32,16,128]{2,1,0:T(8,128)S(1)}, u32[]{:S(2)}, u32[]{:S(2)}) async-start(f32[32,16,128]{2,1,0:T(8,128)} %broadcast_in_dim.18), calls=%async_computation.1 | async-start | bytes 524288 | tf_op jit(solution)/shard_map/all_to_all | solution.py:226
  61.7 2.9 %collective-permute-start.7 = (f32[16,128]{1,0:T(8,128)S(1)}, f32[16,128]{1,0:T(8,128)S(1)}, u32[]{:S(2)}, u32[]{:S(2)}) collective-permute-start(f32[16,128]{1,0:T(8,128)S(1)} %reduce_sum.9.lown), channel_id=1, source_target_pairs={{0,4},{4,0},{1,5},{5,1},{2,6},{6,2},{3,7},{7,3},{8,12},{12,8},{9,1... | collective-permute-start | bytes 24584 | tf_op jit(solution)/shard_map/ppermute | solution.py:222
  68.4 1.5 %collective-permute-start.8 = (f32[32,16,128]{2,1,0:T(8,128)S(1)}, f32[32,16,128]{2,1,0:T(8,128)S(1)}, u32[]{:S(2)}, u32[]{:S(2)}) collective-permute-start(f32[32,16,128]{2,1,0:T(8,128)S(1)} %get-tuple-element.34), channel_id=1, source_target_pairs={{0,4},{4,0},{1,5},{5,1},{2,6},{6,2},{3,7},{7,3},{8,12},{12,8},{9,1... | collective-permute-start | bytes 786440 | tf_op jit(solution)/shard_map/ppermute | solution.py:222
  70.0 11.6 %copy-start.2 = (bf16[16,32,256]{2,1,0:T(8,128)(2,1)S(1)}, bf16[16,32,256]{2,1,0:T(8,128)(2,1)}, u32[]{:S(2)}) copy-start(bf16[16,32,256]{2,1,0:T(8,128)(2,1)} %shard_map.88.inputs) | copy-start | bytes 786436
  97.2 4.5 %copy-start.7 = (f32[32,128]{1,0:T(8,128)S(1)}, f32[32,128]{1,0:T(8,128)}, u32[]{:S(2)}) copy-start(f32[32,128]{1,0:T(8,128)} %get-tuple-element.36.qt) | copy-start | bytes 49156
  97.2 4.4 %collective-permute-start.9 = (bf16[32,32,128]{2,1,0:T(8,128)(2,1)S(1)}, bf16[32,32,128]{2,1,0:T(8,128)(2,1)S(1)}, u32[]{:S(2)}, u32[]{:S(2)}) collective-permute-start(bf16[32,32,128]{2,1,0:T(8,128)(2,1)S(1)} %slice.4), channel_id=1, source_target_pairs={{0,4},{4,0},{1,5},{5,1},{2,6},{6,2},{3,7},{7,3},{8,12},{12,8},{9,1... | collective-permute-start | bytes 786440 | tf_op jit(solution)/shard_map/ppermute | solution.py:222

commit v8 on v7

--- a/solution.py
+++ b/solution.py
@@ -73,17 +73,17 @@
     return 4 * lax.axis_index("x") + lax.axis_index("y")
 
 
-def pack_kernel(w, og, s1, s2, s3, lines, feats, packed, sems):
-    t = lax.axis_index("t")
+def pack_kernel(w, og, s1, s2, s3, feats, sems):
+    t, core = lax.axis_index("t"), lax.axis_index("core")
     cols = pl.ds(pl.multiple_of(plane() * CUT, CUT), CUT)
-    fetched([(w.at[:, cols], lines), (og, feats)], sems)
-    for k in range(1, TENSOR):
+    part = w.at[pl.ds(pl.multiple_of(core * 64, 64), 64), cols]
+    sends = (s1, s2, s3)
+    fetched([(part, s.at[pl.ds(0, 64), :]) for s in sends] + [(og, feats)], sems)
+    for k, send in enumerate(sends, 1):
         first = OWN * lax.rem(t + k, TENSOR)
-        packed[k - 1, 0:HEAD, :] = lines[...]
         for h in range(2):
             rows = pl.ds(pl.multiple_of(first + 16 * h, 16), 16)
-            packed[k - 1, HEAD : HEAD + 16, 128 * h : 128 * h + 128] = feats[rows, :]
-    fetched([(packed.at[k], send) for k, send in enumerate((s1, s2, s3))], sems)
+            send[64:80, 128 * h : 128 * h + 128] = feats[rows, :]
 
 
 def rows_kernel(og, r1, r2, r3, out, held):
@@ -92,7 +92,7 @@
     for k, r in enumerate((r1, r2, r3), 1):
         for h in range(2):
             held[16 * h : 16 * h + 16, 128 * k : 128 * k + 128] = r[
-                HEAD : HEAD + 16, 128 * h : 128 * h + 128
+                64:80, 128 * h : 128 * h + 128
             ]
     for g in range(PLANE):
         out[g] = held[...]
@@ -198,13 +198,14 @@
         err[:, cols] = total.astype(BF16)
 
 
-def input_kernel(w, feats, r1, r2, r3, out, fv, weights, total, sems):
+def input_kernel(w, feats, r1, r2, r3, c1, c2, c3, out, fv, weights, total, sems):
+    core = lax.axis_index("core")
     cols = pl.ds(pl.multiple_of(plane() * CUT, CUT), CUT)
     pairs = [(w.at[:, cols], weights.at[pl.ds(0, HEAD), :]), (feats, fv)]
-    pairs += [
-        (r.at[pl.ds(0, HEAD), :], weights.at[pl.ds(HEAD * k, HEAD), :])
-        for k, r in enumerate((r1, r2, r3), 1)
-    ]
+    for k, (r, c) in enumerate(((r1, c1), (r2, c2), (r3, c3)), 1):
+        for source, side in ((r, core), (c, 1 - core)):
+            rows = pl.ds(pl.multiple_of(HEAD * k + 64 * side, 64), 64)
+            pairs.append((source.at[pl.ds(0, 64), :], weights.at[rows, :]))
     fetched(pairs, sems)
     for g in range(0, PLANE, 4):
         rows = jnp.concatenate([fv[g + i] for i in range(4)], axis=0)
@@ -233,21 +234,16 @@
 
     sends = call(
         pack_kernel,
-        [((HEAD + 16, CUT), BF16)] * 3,
-        [
-            pltpu.VMEM((HEAD, CUT), BF16),
-            pltpu.VMEM((128, HEAD), BF16),
-            pltpu.VMEM((3, HEAD + 16, CUT), BF16),
-            pltpu.SemaphoreType.DMA((3,)),
-        ],
+        [((80, CUT), BF16)] * 3,
+        [pltpu.VMEM((128, HEAD), BF16), pltpu.SemaphoreType.DMA((4,))],
         space=pltpu.MemorySpace.HBM,
-        dest=pltpu.MemorySpace.HBM,
         room=60,
     )(weight, og)
     got = [moved(x, k) for k, x in zip((1, 2, 3), sends)]
     acts = [act] + [moved(act, k) for k in (1, 2, 3)]
     (rows,) = call(rows_kernel, [((PLANE, OWN, 512), BF16)], [pltpu.VMEM((OWN, 512), BF16)])(og, *got)
     feats = exchanged(rows, ("x", "y"))
+    traded = [swapped(g) for g in got]
     inner, fed, lines = call(
         early_kernel,
         [((RANK, OWN), F32), ((RANK, HEAD), F32), ((RANK, WIDE), BF16)],
@@ -259,7 +255,7 @@
     left_keep, left_send = call(
         left_kernel, [half, half], [pltpu.VMEM((RANK, HEAD), F32)], flops=5 * 10**7, moved=10**6
     )(*acts[1:], og, lines, inner, fed)
-    left_send, feats = lax.optimization_barrier((left_send, feats))
+    left_send, feats, traded = lax.optimization_barrier((left_send, feats, traded))
 
     left_half = left_keep + swapped(left_send)
     pieces = exchanged(jnp.broadcast_to(left_half[None], (N_CHIPS, HALF, HEAD)), CHIPS)
@@ -270,14 +266,14 @@
             pltpu.VMEM((PLANE, OWN, 512), BF16),
             pltpu.VMEM((512, CUT), BF16),
             pltpu.VMEM((PLANE, OWN, CUT), BF16),
-            pltpu.SemaphoreType.DMA((5,)),
+            pltpu.SemaphoreType.DMA((8,)),
         ],
         flops=2 * 10**8,
         moved=2 * 10**6,
         space=pltpu.MemorySpace.HBM,
         dest=pltpu.MemorySpace.HBM,
         room=60,
-    )(weight, feats, *got)
+    )(weight, feats, *got, *traded)
     pieces, inputs = lax.optimization_barrier((pieces, inputs))
     left_own = jnp.sum(pieces, axis=0)
     left_other = swapped(left_own)

time: 104 us -> 108 us (1.038)
  starting transfers between devices: 34 us -> 56.9 us
  waiting for transfers between devices: 29.4 us -> 11.2 us
    ppermute x4 -> x7, starting transfers between devices: 7.82 us -> 30.2 us  [swapped(): return lax.ppermute(x, 'core', [(0, 1), (1, 0)])]
    ppermute x6, waiting for transfers between devices: 16.9 us -> 1.23 us  [moved(): return lax.ppermute(x, axis, [(i, (i + k) % 4) for i in range(4)])]
    all_to_all x2, waiting for transfers between devices: 8.47 us -> 5.94 us  [exchanged(): return lax.all_to_all(x, axes, 0, 0, tiled=True)]
    ppermute x6, starting transfers between devices: 14.8 us -> 15.9 us  [moved(): return lax.ppermute(x, axis, [(i, (i + k) % 4) for i in range(4)])]
    ppermute x4 -> x7, waiting for transfers between devices: 4.01 us -> 4.02 us  [swapped(): return lax.ppermute(x, 'core', [(0, 1), (1, 0)])]
  transfers between devices with their start and end apart: 12 -> 15, of which waited for: 8 -> 6; matrix products, arithmetic and copies ran while one was open for 0% -> 0% of each run, Pallas kernels for 4% -> 5%
where the time goes in v8:
time: 108 us
  starting transfers between devices  56.9 us (53%)
  blocking collectives  27.1 us (25%)
  waiting for transfers between devices  11.2 us (10%)
  Pallas kernels  11.1 us (10%)
    ppermute x7, starting transfers between devices, swapped(): return lax.ppermute(x, 'core', [(0, 1), (1, 0)])  30.2 us
    all_to_all x2, blocking collectives, exchanged(): return lax.all_to_all(x, axes, 0, 0, tiled=True)  27.1 us
    ppermute x6, starting transfers between devices, moved(): return lax.ppermute(x, axis, [(i, (i + k) % 4) for i in range(4)])  15.9 us
    pallas_call x8, Pallas kernels, run(): pl.pallas_call(kernel, out_shape=[jax.ShapeDtypeStruct(s, d) for s, d in...  11.1 us
    all_to_all x2, starting transfers between devices, exchanged(): return lax.all_to_all(x, axes, 0, 0, tiled=True)  10.8 us
    all_to_all x2, waiting for transfers between devices, exchanged(): return lax.all_to_all(x, axes, 0, 0, tiled=True)  5.94 us
    ppermute x7, waiting for transfers between devices, swapped(): return lax.ppermute(x, 'core', [(0, 1), (1, 0)])  4.02 us
  transfers between devices with their start and end apart: 15, of which 6 were waited for; matrix products, arithmetic and copies ran while one was open for 0% of the time, Pallas kernels for 5%

profile of v8, /device:TPU:1, one launch (start us, length us, event | category | flops | bytes accessed | tf_op | source)
XLA Modules:
  0.0 108.0 jit_solution(3424877429636074604)
XLA Ops:
  0.6 6.9 %collective-permute-start.2 = (bf16[32,4096]{1,0:T(8,128)(2,1)}, bf16[32,4096]{1,0:T(8,128)(2,1)S(1)}, u32[]{:S(2)}, u32[]{:S(2)}) collective-permute-start(bf16[32,4096]{1,0:T(8,128)(2,1)} %bitcast.18), channel_id=1, source_target_pairs={{0,3},{1,0},{2,1},{3,2},{4,7},{5,4},{6,5},{7,6},{8,11},{9,8},{10,9... | collective-permute-start | bytes 786440 | tf_op jit(solution)/shard_map/ppermute | solution.py:219
  7.6 0.0 copy-start.1
  7.6 0.0 copy-start.3
  7.6 1.6 %shard_map.86 = (bf16[80,256]{1,0:T(8,128)(2,1)}, bf16[80,256]{1,0:T(8,128)(2,1)}, bf16[80,256]{1,0:T(8,128)(2,1)}) custom-call(bf16[128,4096]{1,0:T(8,128)(2,1)} %bitcast.31, bf16[128,128]{1,0:T(8,128)(2,1)} %bitcast.24), custom_call_target="tpu_custom_call" | custom-call | flops 1000000 | bytes 1000000 | tf_op jit(solution)/shard_map/pallas_call | solution.py:51
  9.1 0.0 copy-start
  9.1 0.1 collective-permute-start.3
  9.2 3.2 %collective-permute-start.4 = (bf16[80,256]{1,0:T(8,128)(2,1)}, bf16[80,256]{1,0:T(8,128)(2,1)S(1)}, u32[]{:S(2)}, u32[]{:S(2)}) collective-permute-start(bf16[80,256]{1,0:T(8,128)(2,1)} %get-tuple-element.31), channel_id=1, source_target_pairs={{0,2},{1,3},{2,0},{3,1},{4,6},{5,7},{6,4},{7,5},{8,10},{9,11},{10,... | collective-permute-start | bytes 122888 | tf_op jit(solution)/shard_map/ppermute | solution.py:219
  12.5 1.3 %collective-permute-start.5 = (bf16[80,256]{1,0:T(8,128)(2,1)}, bf16[80,256]{1,0:T(8,128)(2,1)S(1)}, u32[]{:S(2)}, u32[]{:S(2)}) collective-permute-start(bf16[80,256]{1,0:T(8,128)(2,1)} %get-tuple-element.32), channel_id=1, source_target_pairs={{0,3},{1,0},{2,1},{3,2},{4,7},{5,4},{6,5},{7,6},{8,11},{9,8},{10,9... | collective-permute-start | bytes 122888 | tf_op jit(solution)/shard_map/ppermute | solution.py:219
  13.7 0.0 copy-done.1
  13.7 4.4 %collective-permute-start.1 = (bf16[32,4096]{1,0:T(8,128)(2,1)S(1)}, bf16[32,4096]{1,0:T(8,128)(2,1)S(1)}, u32[]{:S(2)}, u32[]{:S(2)}) collective-permute-start(bf16[32,4096]{1,0:T(8,128)(2,1)S(1)} %bitcast.19), channel_id=1, source_target_pairs={{0,2},{1,3},{2,0},{3,1},{4,6},{5,7},{6,4},{7,5},{8,10},{9,11},{10,... | collective-permute-start | bytes 786440 | tf_op jit(solution)/shard_map/ppermute | solution.py:219
  18.2 0.0 collective-permute-done.3.r1
  18.2 0.0 copy-start.4
  18.2 0.0 collective-permute-start
  18.2 0.0 collective-permute-done.4.r2
  18.2 0.0 copy-start.5
  18.2 1.2 %collective-permute-done.5.r3 = bf16[80,256]{1,0:T(8,128)(2,1)S(1)} collective-permute-done((bf16[80,256]{1,0:T(8,128)(2,1)}, bf16[80,256]{1,0:T(8,128)(2,1)S(1)}, u32[]{:S(2)}, u32[]{:S(2)}) %collective-permute-start.5) | collective-permute-done | bytes 40992 | tf_op jit(solution)/shard_map/ppermute | solution.py:219
  19.4 0.0 copy-done.3
  19.4 0.9 shard_map.87
  20.3 6.9 %all-to-all-start = ((bf16[16,32,512]{2,1,0:T(8,128)(2,1)}), bf16[16,32,512]{2,1,0:T(8,128)(2,1)S(1)}, u32[]{:S(2)}, u32[]{:S(2)}) async-start(bf16[16,32,512]{2,1,0:T(8,128)(2,1)} %shard_map.87), calls=%async_computation | async-start | bytes 1048576 | tf_op jit(solution)/shard_map/all_to_all | solution.py:227
  27.2 0.0 copy-done.4
  27.2 15.8 %collective-permute-start.6 = (bf16[80,256]{1,0:T(8,128)(2,1)S(1)}, bf16[80,256]{1,0:T(8,128)(2,1)S(1)}, u32[]{:S(2)}, u32[]{:S(2)}) collective-permute-start(bf16[80,256]{1,0:T(8,128)(2,1)S(1)} %collective-permute-done.3.r1), channel_id=1, source_target_pairs={{0,4},{4,0},{1,5},{5,1},{2,6},{6,2},{3,7},{7,3},{8,12},{12,8},{9,1... | collective-permute-start | bytes 122888 | tf_op jit(solution)/shard_map/ppermute | solution.py:223
  42.9 0.0 copy-done.5
  42.9 0.1 collective-permute-start.7
  43.0 0.0 collective-permute-done.2.a3
  43.0 0.0 copy-done.6
  43.0 0.4 collective-permute-start.8
  43.4 0.0 copy-done
  43.5 0.0 copy-done.8
  43.5 0.5 shard_map.84
  43.9 0.0 collective-permute-done.1.a2
  44.0 0.0 collective-permute-done.a1
  44.0 0.6 shard_map.85
  44.5 0.0 collective-permute-done.6.c1
  44.6 0.0 copy-start.10
  44.6 0.0 collective-permute-done.7.c2
  44.6 0.0 copy-start.11
  44.6 0.0 collective-permute-done.8.c3
  44.6 0.0 copy-start.12
  44.6 0.0 all-to-all-done.feats
  44.6 0.0 copy-start.9
  44.6 8.3 %collective-permute-start.9 = (f32[16,128]{1,0:T(8,128)S(1)}, f32[16,128]{1,0:T(8,128)S(1)}, u32[]{:S(2)}, u32[]{:S(2)}) collective-permute-start(f32[16,128]{1,0:T(8,128)S(1)} %get-tuple-element.33), channel_id=1, source_target_pairs={{0,4},{4,0},{1,5},{5,1},{2,6},{6,2},{3,7},{7,3},{8,12},{12,8},{9,1... | collective-permute-start | bytes 24584 | tf_op jit(solution)/shard_map/ppermute | solution.py:223
  52.9 0.8 collective-permute-done.9
  53.8 0.7 broadcast_in_dim.18
  54.5 0.0 copy-done.10
  54.5 0.0 copy-done.11
  54.5 0.0 copy-done.12
  54.5 3.9 %all-to-all-start.1 = ((f32[32,16,128]{2,1,0:T(8,128)}), f32[32,16,128]{2,1,0:T(8,128)S(1)}, u32[]{:S(2)}, u32[]{:S(2)}) async-start(f32[32,16,128]{2,1,0:T(8,128)} %broadcast_in_dim.18), calls=%async_computation.1 | async-start | bytes 524288 | tf_op jit(solution)/shard_map/all_to_all | solution.py:227
  58.4 0.0 copy-done.9
  58.4 2.2 %shard_map.88.inputs = bf16[16,32,256]{2,1,0:T(8,128)(2,1)} custom-call(bf16[128,4096]{1,0:T(8,128)(2,1)} %bitcast.32, bf16[16,32,512]{2,1,0:T(8,128)(2,1)} %copy-done.9, bf16[80,256]{1,0:T(8,128)(2,1)} %copy-done.4, bf16[80,256]{1,0:T(8,128)(2,1)} %copy-done.5, bf16[80,256]{1,0:T(8,128)(2,1)} %copy-done.6, bf16[80,256]{1,0:T(8,128)(2,1)} %copy-done.10, ...), custom_call_target="tpu_custom_call" | custom-call | flops 200000000 | bytes 2000000 | tf_op jit(solution)/shard_map/pallas_call | solution.py:51
  60.6 5.9 %all-to-all-done.1 = f32[32,16,128]{2,1,0:T(8,128)S(1)} async-done(((f32[32,16,128]{2,1,0:T(8,128)}), f32[32,16,128]{2,1,0:T(8,128)S(1)}, u32[]{:S(2)}, u32[]{:S(2)}) %all-to-all-start.1) | async-done | bytes 262176 | tf_op jit(solution)/shard_map/all_to_all | solution.py:227
  66.6 2.0 %collective-permute-start.10 = (f32[16,128]{1,0:T(8,128)S(1)}, f32[16,128]{1,0:T(8,128)S(1)}, u32[]{:S(2)}, u32[]{:S(2)}) collective-permute-start(f32[16,128]{1,0:T(8,128)S(1)} %reduce_sum.9.lown), channel_id=1, source_target_pairs={{0,4},{4,0},{1,5},{5,1},{2,6},{6,2},{3,7},{7,3},{8,12},{12,8},{9,1... | collective-permute-start | bytes 24584 | tf_op jit(solution)/shard_map/ppermute | solution.py:223
  68.6 0.8 collective-permute-done.10.loth
  69.4 3.8 %shard_map.89 = (f32[32,128]{1,0:T(8,128)}, f32[32,16,128]{2,1,0:T(8,128)S(1)}, f32[32,16,128]{2,1,0:T(8,128)S(1)}) custom-call(f32[16,128]{1,0:T(8,128)S(1)} %reduce_sum.9.lown, f32[16,128]{1,0:T(8,128)S(1)} %collective-permute-done.10.loth, bf16[32,4096]{1,0:T(8,128)(2,1)S(1)} %bitcast.22, bf16[32,4096]{1,0:T(8,128)(2,1)S(1)} %collective-permute-done.a1, ...), custom_call_target="tpu_custom_call" | custom-call | flops 100000000 | bytes 3000000 | tf_op jit(solution)/shard_map/pallas_call | solution.py:51
  73.2 0.3 collective-permute-start.11
  73.5 1.2 %collective-permute-done.11 = f32[32,16,128]{2,1,0:T(8,128)S(1)} collective-permute-done((f32[32,16,128]{2,1,0:T(8,128)S(1)}, f32[32,16,128]{2,1,0:T(8,128)S(1)}, u32[]{:S(2)}, u32[]{:S(2)}) %collective-permute-start.11) | collective-permute-done | bytes 262176 | tf_op jit(solution)/shard_map/ppermute | solution.py:223
  74.8 0.0 copy-start.2
  74.8 11.6 %all_to_all.20.pieces = f32[32,16,128]{2,1,0:T(8,128)S(1)} all-to-all(f32[32,16,128]{2,1,0:T(8,128)S(1)} %add.7), channel_id=1, replica_groups=mesh['x'=4,'zl'=2,'y'=4,'core'=2,'t'=4] {'x','zl','y'}, dimensions={0} | all-to-all | bytes 524288 | tf_op jit(solution)/shard_map/all_to_all | solution.py:227
  86.4 0.0 copy-done.2
  86.4 0.1 shard_map.90
  86.5 15.5 %all_to_all.21.mixed = bf16[32,96,128]{2,1,0:T(8,128)(2,1)S(1)} all-to-all(bf16[32,96,128]{2,1,0:T(8,128)(2,1)S(1)} %shard_map.90), channel_id=1, replica_groups=mesh['x'=4,'zl'=2,'y'=4,'core'=2,'t'=4] {'x','zl','y'}, dimensions={0} | all-to-all | bytes 1572864 | tf_op jit(solution)/shard_map/all_to_all | solution.py:227
  102.0 3.3 %collective-permute-start.12 = (bf16[32,32,128]{2,1,0:T(8,128)(2,1)S(1)}, bf16[32,32,128]{2,1,0:T(8,128)(2,1)S(1)}, u32[]{:S(2)}, u32[]{:S(2)}) collective-permute-start(bf16[32,32,128]{2,1,0:T(8,128)(2,1)S(1)} %slice.4), channel_id=1, source_target_pairs={{0,4},{4,0},{1,5},{5,1},{2,6},{6,2},{3,7},{7,3},{8,12},{12,8},{9,1... | collective-permute-start | bytes 786440 | tf_op jit(solution)/shard_map/ppermute | solution.py:223
  105.3 1.2 %collective-permute-done.12.roth = bf16[32,32,128]{2,1,0:T(8,128)(2,1)S(1)} collective-permute-done((bf16[32,32,128]{2,1,0:T(8,128)(2,1)S(1)}, bf16[32,32,128]{2,1,0:T(8,128)(2,1)S(1)}, u32[]{:S(2)}, u32[]{:S(2)}) %collective-permute-start.12) | collective-permute-done | bytes 262176 | tf_op jit(solution)/shard_map/ppermute | solution.py:223
  106.4 0.0 copy-done.7
  106.4 1.5 %shard_map.91 = (bf16[128,4096]{1,0:T(8,128)(2,1)}, bf16[32,4096]{1,0:T(8,128)(2,1)}, bf16[32,4096]{1,0:T(8,128)(2,1)}) custom-call(bf16[32,96,128]{2,1,0:T(8,128)(2,1)S(1)} %all_to_all.21.mixed, bf16[32,32,128]{2,1,0:T(8,128)(2,1)S(1)} %collective-permute-done.12.roth, f32[32,128]{1,0:T(8,128)S(1)} %copy-done.7, bf16[128,128]{1,0:T(8,128)(2,1)S(1)} %bitcast.28, ...), custom_call_target="tpu_custom_call" | custom-call | flops 300000000 | bytes 5000000 | tf_op jit(solution)/shard_map/pallas_call | solution.py:51
  (7 shorter events, 0.1 us)
Async XLA Ops:
  0.6 42.4 %collective-permute-start.2 = (bf16[32,4096]{1,0:T(8,128)(2,1)}, bf16[32,4096]{1,0:T(8,128)(2,1)S(1)}, u32[]{:S(2)}, u32[]{:S(2)}) collective-permute-start(bf16[32,4096]{1,0:T(8,128)(2,1)} %bitcast.18), channel_id=1, source_target_pairs={{0,3},{1,0},{2,1},{3,2},{4,7},{5,4},{6,5},{7,6},{8,11},{9,8},{10,9... | collective-permute-start | bytes 786440 | tf_op jit(solution)/shard_map/ppermute | solution.py:219
  7.6 6.2 %copy-start.1 = (bf16[1,32,4096]{2,1,0:T(8,128)(2,1)S(1)}, bf16[1,32,4096]{2,1,0:T(8,128)(2,1)}, u32[]{:S(2)}) copy-start(bf16[1,32,4096]{2,1,0:T(8,128)(2,1)} %param.5) | copy-start | bytes 786436
  7.6 11.9 %copy-start.3 = (bf16[1,128,128]{2,1,0:T(8,128)(2,1)S(1)}, bf16[1,128,128]{2,1,0:T(8,128)(2,1)}, u32[]{:S(2)}) copy-start(bf16[1,128,128]{2,1,0:T(8,128)(2,1)} %param.6) | copy-start | bytes 98308
  9.1 34.3 %copy-start = (bf16[1,1,128,4096]{3,2,1,0:T(8,128)(2,1)S(1)}, bf16[1,1,128,4096]{3,2,1,0:T(8,128)(2,1)}, u32[]{:S(2)}) copy-start(bf16[1,1,128,4096]{3,2,1,0:T(8,128)(2,1)} %param.8) | copy-start | bytes 3145732
  9.1 9.0 %collective-permute-start.3 = (bf16[80,256]{1,0:T(8,128)(2,1)}, bf16[80,256]{1,0:T(8,128)(2,1)S(1)}, u32[]{:S(2)}, u32[]{:S(2)}) collective-permute-start(bf16[80,256]{1,0:T(8,128)(2,1)} %get-tuple-element.30), channel_id=1, source_target_pairs={{0,1},{1,2},{2,3},{3,0},{4,5},{5,6},{6,7},{7,4},{8,9},{9,10},{10,1... | collective-permute-start | bytes 122888 | tf_op jit(solution)/shard_map/ppermute | solution.py:219
  9.2 9.0 %collective-permute-start.4 = (bf16[80,256]{1,0:T(8,128)(2,1)}, bf16[80,256]{1,0:T(8,128)(2,1)S(1)}, u32[]{:S(2)}, u32[]{:S(2)}) collective-permute-start(bf16[80,256]{1,0:T(8,128)(2,1)} %get-tuple-element.31), channel_id=1, source_target_pairs={{0,2},{1,3},{2,0},{3,1},{4,6},{5,7},{6,4},{7,5},{8,10},{9,11},{10,... | collective-permute-start | bytes 122888 | tf_op jit(solution)/shard_map/ppermute | solution.py:219
  12.5 6.9 %collective-permute-start.5 = (bf16[80,256]{1,0:T(8,128)(2,1)}, bf16[80,256]{1,0:T(8,128)(2,1)S(1)}, u32[]{:S(2)}, u32[]{:S(2)}) collective-permute-start(bf16[80,256]{1,0:T(8,128)(2,1)} %get-tuple-element.32), channel_id=1, source_target_pairs={{0,3},{1,0},{2,1},{3,2},{4,7},{5,4},{6,5},{7,6},{8,11},{9,8},{10,9... | collective-permute-start | bytes 122888 | tf_op jit(solution)/shard_map/ppermute | solution.py:219
  13.7 30.2 %collective-permute-start.1 = (bf16[32,4096]{1,0:T(8,128)(2,1)S(1)}, bf16[32,4096]{1,0:T(8,128)(2,1)S(1)}, u32[]{:S(2)}, u32[]{:S(2)}) collective-permute-start(bf16[32,4096]{1,0:T(8,128)(2,1)S(1)} %bitcast.19), channel_id=1, source_target_pairs={{0,2},{1,3},{2,0},{3,1},{4,6},{5,7},{6,4},{7,5},{8,10},{9,11},{10,... | collective-permute-start | bytes 786440 | tf_op jit(solution)/shard_map/ppermute | solution.py:219
  18.2 9.0 %copy-start.4 = (bf16[80,256]{1,0:T(8,128)(2,1)}, bf16[80,256]{1,0:T(8,128)(2,1)S(1)}, u32[]{:S(2)}) copy-start(bf16[80,256]{1,0:T(8,128)(2,1)S(1)} %collective-permute-done.3.r1) | copy-start | bytes 122884
  18.2 25.8 %collective-permute-start = (bf16[32,4096]{1,0:T(8,128)(2,1)S(1)}, bf16[32,4096]{1,0:T(8,128)(2,1)S(1)}, u32[]{:S(2)}, u32[]{:S(2)}) collective-permute-start(bf16[32,4096]{1,0:T(8,128)(2,1)S(1)} %bitcast.20), channel_id=1, source_target_pairs={{0,1},{1,2},{2,3},{3,0},{4,5},{5,6},{6,7},{7,4},{8,9},{9,10},{10,1... | collective-permute-start | bytes 786440 | tf_op jit(solution)/shard_map/ppermute | solution.py:219
  18.2 24.7 %copy-start.5 = (bf16[80,256]{1,0:T(8,128)(2,1)}, bf16[80,256]{1,0:T(8,128)(2,1)S(1)}, u32[]{:S(2)}) copy-start(bf16[80,256]{1,0:T(8,128)(2,1)S(1)} %collective-permute-done.4.r2) | copy-start | bytes 122884
  19.4 23.6 %copy-start.6 = (bf16[80,256]{1,0:T(8,128)(2,1)}, bf16[80,256]{1,0:T(8,128)(2,1)S(1)}, u32[]{:S(2)}) copy-start(bf16[80,256]{1,0:T(8,128)(2,1)S(1)} %collective-permute-done.5.r3) | copy-start | bytes 122884
  20.3 23.2 %copy-start.8 = (bf16[1,1,4096,32]{2,3,1,0:T(8,128)(2,1)S(1)}, bf16[1,1,4096,32]{2,3,1,0:T(8,128)(2,1)}, u32[]{:S(2)}) copy-start(bf16[1,1,4096,32]{2,3,1,0:T(8,128)(2,1)} %param.9) | copy-start | bytes 786436
  20.3 24.3 %all-to-all-start = ((bf16[16,32,512]{2,1,0:T(8,128)(2,1)}), bf16[16,32,512]{2,1,0:T(8,128)(2,1)S(1)}, u32[]{:S(2)}, u32[]{:S(2)}) async-start(bf16[16,32,512]{2,1,0:T(8,128)(2,1)} %shard_map.87), calls=%async_computation | async-start | bytes 1048576 | tf_op jit(solution)/shard_map/all_to_all | solution.py:227
  27.2 17.4 %collective-permute-start.6 = (bf16[80,256]{1,0:T(8,128)(2,1)S(1)}, bf16[80,256]{1,0:T(8,128)(2,1)S(1)}, u32[]{:S(2)}, u32[]{:S(2)}) collective-permute-start(bf16[80,256]{1,0:T(8,128)(2,1)S(1)} %collective-permute-done.3.r1), channel_id=1, source_target_pairs={{0,4},{4,0},{1,5},{5,1},{2,6},{6,2},{3,7},{7,3},{8,12},{12,8},{9,1... | collective-permute-start | bytes 122888 | tf_op jit(solution)/shard_map/ppermute | solution.py:223
  42.9 1.6 %collective-permute-start.7 = (bf16[80,256]{1,0:T(8,128)(2,1)S(1)}, bf16[80,256]{1,0:T(8,128)(2,1)S(1)}, u32[]{:S(2)}, u32[]{:S(2)}) collective-permute-start(bf16[80,256]{1,0:T(8,128)(2,1)S(1)} %collective-permute-done.4.r2), channel_id=1, source_target_pairs={{0,4},{4,0},{1,5},{5,1},{2,6},{6,2},{3,7},{7,3},{8,12},{12,8},{9,1... | collective-permute-start | bytes 122888 | tf_op jit(solution)/shard_map/ppermute | solution.py:223
  43.0 1.5 %collective-permute-start.8 = (bf16[80,256]{1,0:T(8,128)(2,1)S(1)}, bf16[80,256]{1,0:T(8,128)(2,1)S(1)}, u32[]{:S(2)}, u32[]{:S(2)}) collective-permute-start(bf16[80,256]{1,0:T(8,128)(2,1)S(1)} %collective-permute-done.5.r3), channel_id=1, source_target_pairs={{0,4},{4,0},{1,5},{5,1},{2,6},{6,2},{3,7},{7,3},{8,12},{12,8},{9,1... | collective-permute-start | bytes 122888 | tf_op jit(solution)/shard_map/ppermute | solution.py:223
  44.6 9.9 %copy-start.10 = (bf16[80,256]{1,0:T(8,128)(2,1)}, bf16[80,256]{1,0:T(8,128)(2,1)S(1)}, u32[]{:S(2)}) copy-start(bf16[80,256]{1,0:T(8,128)(2,1)S(1)} %collective-permute-done.6.c1) | copy-start | bytes 122884
  44.6 9.9 %copy-start.11 = (bf16[80,256]{1,0:T(8,128)(2,1)}, bf16[80,256]{1,0:T(8,128)(2,1)S(1)}, u32[]{:S(2)}) copy-start(bf16[80,256]{1,0:T(8,128)(2,1)S(1)} %collective-permute-done.7.c2) | copy-start | bytes 122884
  44.6 9.9 %copy-start.12 = (bf16[80,256]{1,0:T(8,128)(2,1)}, bf16[80,256]{1,0:T(8,128)(2,1)S(1)}, u32[]{:S(2)}) copy-start(bf16[80,256]{1,0:T(8,128)(2,1)S(1)} %collective-permute-done.8.c3) | copy-start | bytes 122884
  44.6 13.8 %copy-start.9 = (bf16[16,32,512]{2,1,0:T(8,128)(2,1)}, bf16[16,32,512]{2,1,0:T(8,128)(2,1)S(1)}, u32[]{:S(2)}) copy-start(bf16[16,32,512]{2,1,0:T(8,128)(2,1)S(1)} %all-to-all-done.feats) | copy-start | bytes 1572868
  44.6 9.1 %collective-permute-start.9 = (f32[16,128]{1,0:T(8,128)S(1)}, f32[16,128]{1,0:T(8,128)S(1)}, u32[]{:S(2)}, u32[]{:S(2)}) collective-permute-start(f32[16,128]{1,0:T(8,128)S(1)} %get-tuple-element.33), channel_id=1, source_target_pairs={{0,4},{4,0},{1,5},{5,1},{2,6},{6,2},{3,7},{7,3},{8,12},{12,8},{9,1... | collective-permute-start | bytes 24584 | tf_op jit(solution)/shard_map/ppermute | solution.py:223
  54.5 12.0 %all-to-all-start.1 = ((f32[32,16,128]{2,1,0:T(8,128)}), f32[32,16,128]{2,1,0:T(8,128)S(1)}, u32[]{:S(2)}, u32[]{:S(2)}) async-start(f32[32,16,128]{2,1,0:T(8,128)} %broadcast_in_dim.18), calls=%async_computation.1 | async-start | bytes 524288 | tf_op jit(solution)/shard_map/all_to_all | solution.py:227
  66.6 2.9 %collective-permute-start.10 = (f32[16,128]{1,0:T(8,128)S(1)}, f32[16,128]{1,0:T(8,128)S(1)}, u32[]{:S(2)}, u32[]{:S(2)}) collective-permute-start(f32[16,128]{1,0:T(8,128)S(1)} %reduce_sum.9.lown), channel_id=1, source_target_pairs={{0,4},{4,0},{1,5},{5,1},{2,6},{6,2},{3,7},{7,3},{8,12},{12,8},{9,1... | collective-permute-start | bytes 24584 | tf_op jit(solution)/shard_map/ppermute | solution.py:223
  73.2 1.5 %collective-permute-start.11 = (f32[32,16,128]{2,1,0:T(8,128)S(1)}, f32[32,16,128]{2,1,0:T(8,128)S(1)}, u32[]{:S(2)}, u32[]{:S(2)}) collective-permute-start(f32[32,16,128]{2,1,0:T(8,128)S(1)} %get-tuple-element.40), channel_id=1, source_target_pairs={{0,4},{4,0},{1,5},{5,1},{2,6},{6,2},{3,7},{7,3},{8,12},{12,8},{9,1... | collective-permute-start | bytes 786440 | tf_op jit(solution)/shard_map/ppermute | solution.py:223
  74.8 11.6 %copy-start.2 = (bf16[16,32,256]{2,1,0:T(8,128)(2,1)S(1)}, bf16[16,32,256]{2,1,0:T(8,128)(2,1)}, u32[]{:S(2)}) copy-start(bf16[16,32,256]{2,1,0:T(8,128)(2,1)} %shard_map.88.inputs) | copy-start | bytes 786436
  102.0 4.5 %copy-start.7 = (f32[32,128]{1,0:T(8,128)S(1)}, f32[32,128]{1,0:T(8,128)}, u32[]{:S(2)}) copy-start(f32[32,128]{1,0:T(8,128)} %get-tuple-element.42.qt) | copy-start | bytes 49156
  102.0 4.4 %collective-permute-start.12 = (bf16[32,32,128]{2,1,0:T(8,128)(2,1)S(1)}, bf16[32,32,128]{2,1,0:T(8,128)(2,1)S(1)}, u32[]{:S(2)}, u32[]{:S(2)}) collective-permute-start(bf16[32,32,128]{2,1,0:T(8,128)(2,1)S(1)} %slice.4), channel_id=1, source_target_pairs={{0,4},{4,0},{1,5},{5,1},{2,6},{6,2},{3,7},{7,3},{8,12},{12,8},{9,1... | collective-permute-start | bytes 786440 | tf_op jit(solution)/shard_map/ppermute | solution.py:223

commit v9 on v7

--- a/solution.py
+++ b/solution.py
@@ -73,17 +73,16 @@
     return 4 * lax.axis_index("x") + lax.axis_index("y")
 
 
-def pack_kernel(w, og, s1, s2, s3, lines, feats, packed, sems):
+def pack_kernel(w, og, s1, s2, s3, feats, sems):
     t = lax.axis_index("t")
-    cols = pl.ds(pl.multiple_of(plane() * CUT, CUT), CUT)
-    fetched([(w.at[:, cols], lines), (og, feats)], sems)
-    for k in range(1, TENSOR):
+    part = w.at[:, pl.ds(pl.multiple_of(plane() * CUT, CUT), CUT)]
+    sends = (s1, s2, s3)
+    fetched([(part, s.at[pl.ds(0, HEAD), :]) for s in sends] + [(og, feats)], sems)
+    for k, send in enumerate(sends, 1):
         first = OWN * lax.rem(t + k, TENSOR)
-        packed[k - 1, 0:HEAD, :] = lines[...]
         for h in range(2):
             rows = pl.ds(pl.multiple_of(first + 16 * h, 16), 16)
-            packed[k - 1, HEAD : HEAD + 16, 128 * h : 128 * h + 128] = feats[rows, :]
-    fetched([(packed.at[k], send) for k, send in enumerate((s1, s2, s3))], sems)
+            send[HEAD : HEAD + 16, 128 * h : 128 * h + 128] = feats[rows, :]
 
 
 def rows_kernel(og, r1, r2, r3, out, held):
@@ -234,17 +233,12 @@
     sends = call(
         pack_kernel,
         [((HEAD + 16, CUT), BF16)] * 3,
-        [
-            pltpu.VMEM((HEAD, CUT), BF16),
-            pltpu.VMEM((128, HEAD), BF16),
-            pltpu.VMEM((3, HEAD + 16, CUT), BF16),
-            pltpu.SemaphoreType.DMA((3,)),
-        ],
+        [pltpu.VMEM((128, HEAD), BF16), pltpu.SemaphoreType.DMA((4,))],
         space=pltpu.MemorySpace.HBM,
-        dest=pltpu.MemorySpace.HBM,
         room=60,
     )(weight, og)
     got = [moved(x, k) for k, x in zip((1, 2, 3), sends)]
+    act, got = lax.optimization_barrier((act, got))
     acts = [act] + [moved(act, k) for k in (1, 2, 3)]
     (rows,) = call(rows_kernel, [((PLANE, OWN, 512), BF16)], [pltpu.VMEM((OWN, 512), BF16)])(og, *got)
     feats = exchanged(rows, ("x", "y"))

time: 104 us -> 109 us (1.048)
  starting transfers between devices: 34 us -> 37.3 us
  waiting for transfers between devices: 29.4 us -> 31.4 us
    ppermute x6, waiting for transfers between devices: 16.9 us -> 21.4 us  [moved(): return lax.ppermute(x, axis, [(i, (i + k) % 4) for i in range(4)])]
    all_to_all x2, starting transfers between devices: 11.4 us -> 14.1 us  [exchanged(): return lax.all_to_all(x, axes, 0, 0, tiled=True)]
    all_to_all x2, waiting for transfers between devices: 8.47 us -> 5.94 us  [exchanged(): return lax.all_to_all(x, axes, 0, 0, tiled=True)]
    ppermute x6, starting transfers between devices: 14.8 us -> 16.8 us  [moved(): return lax.ppermute(x, axis, [(i, (i + k) % 4) for i in range(4)])]
    ppermute x4, starting transfers between devices: 7.82 us -> 6.46 us  [swapped(): return lax.ppermute(x, 'core', [(0, 1), (1, 0)])]
  transfers between devices with their start and end apart: 12 -> 12, of which waited for: 8 -> 9; matrix products, arithmetic and copies ran while one was open for 0% -> 0% of each run, Pallas kernels for 4% -> 4%
where the time goes in v9:
time: 109 us
  starting transfers between devices  37.3 us (34%)
  waiting for transfers between devices  31.4 us (29%)
  blocking collectives  27.1 us (25%)
  Pallas kernels  11.1 us (10%)
    all_to_all x2, blocking collectives, exchanged(): return lax.all_to_all(x, axes, 0, 0, tiled=True)  27.1 us
    ppermute x6, waiting for transfers between devices, moved(): return lax.ppermute(x, axis, [(i, (i + k) % 4) for i in range(4)])  21.4 us
    ppermute x6, starting transfers between devices, moved(): return lax.ppermute(x, axis, [(i, (i + k) % 4) for i in range(4)])  16.8 us
    all_to_all x2, starting transfers between devices, exchanged(): return lax.all_to_all(x, axes, 0, 0, tiled=True)  14.1 us
    pallas_call x8, Pallas kernels, run(): pl.pallas_call(kernel, out_shape=[jax.ShapeDtypeStruct(s, d) for s, d in...  11.1 us
    ppermute x4, starting transfers between devices, swapped(): return lax.ppermute(x, 'core', [(0, 1), (1, 0)])  6.46 us
    all_to_all x2, waiting for transfers between devices, exchanged(): return lax.all_to_all(x, axes, 0, 0, tiled=True)  5.94 us
    ppermute x4, waiting for transfers between devices, swapped(): return lax.ppermute(x, 'core', [(0, 1), (1, 0)])  4.01 us
  transfers between devices with their start and end apart: 12, of which 9 were waited for; matrix products, arithmetic and copies ran while one was open for 0% of the time, Pallas kernels for 4%

profile of v9, /device:TPU:1, one launch (start us, length us, event | category | flops | bytes accessed | tf_op | source)
XLA Modules:
  0.0 108.6 jit_solution(6535353247184115584)
XLA Ops:
  0.6 0.0 copy-start.1
  0.6 0.0 copy-start.3
  0.7 1.7 %shard_map.84 = (bf16[144,256]{1,0:T(8,128)(2,1)}, bf16[144,256]{1,0:T(8,128)(2,1)}, bf16[144,256]{1,0:T(8,128)(2,1)}) custom-call(bf16[128,4096]{1,0:T(8,128)(2,1)} %bitcast.31, bf16[128,128]{1,0:T(8,128)(2,1)} %bitcast.24), custom_call_target="tpu_custom_call" | custom-call | flops 1000000 | bytes 1000000 | tf_op jit(solution)/shard_map/pallas_call | solution.py:51
  2.3 0.0 copy-start
  2.4 3.9 %collective-permute-start = (bf16[144,256]{1,0:T(8,128)(2,1)}, bf16[144,256]{1,0:T(8,128)(2,1)S(1)}, u32[]{:S(2)}, u32[]{:S(2)}) collective-permute-start(bf16[144,256]{1,0:T(8,128)(2,1)} %get-tuple-element.26), channel_id=1, source_target_pairs={{0,1},{1,2},{2,3},{3,0},{4,5},{5,6},{6,7},{7,4},{8,9},{9,10},{10,1... | collective-permute-start | bytes 221192 | tf_op jit(solution)/shard_map/ppermute | solution.py:217
  6.3 5.1 %collective-permute-start.1 = (bf16[144,256]{1,0:T(8,128)(2,1)}, bf16[144,256]{1,0:T(8,128)(2,1)S(1)}, u32[]{:S(2)}, u32[]{:S(2)}) collective-permute-start(bf16[144,256]{1,0:T(8,128)(2,1)} %get-tuple-element.27), channel_id=1, source_target_pairs={{0,2},{1,3},{2,0},{3,1},{4,6},{5,7},{6,4},{7,5},{8,10},{9,11},{10,... | collective-permute-start | bytes 221192 | tf_op jit(solution)/shard_map/ppermute | solution.py:217
  11.4 2.4 %collective-permute-start.2 = (bf16[144,256]{1,0:T(8,128)(2,1)}, bf16[144,256]{1,0:T(8,128)(2,1)S(1)}, u32[]{:S(2)}, u32[]{:S(2)}) collective-permute-start(bf16[144,256]{1,0:T(8,128)(2,1)} %get-tuple-element.28), channel_id=1, source_target_pairs={{0,3},{1,0},{2,1},{3,2},{4,7},{5,4},{6,5},{7,6},{8,11},{9,8},{10,9... | collective-permute-start | bytes 221192 | tf_op jit(solution)/shard_map/ppermute | solution.py:217
  13.7 0.0 collective-permute-done.r1
  13.8 0.0 copy-start.4
  13.8 2.2 %collective-permute-done.1.r2 = bf16[144,256]{1,0:T(8,128)(2,1)S(1)} collective-permute-done((bf16[144,256]{1,0:T(8,128)(2,1)}, bf16[144,256]{1,0:T(8,128)(2,1)S(1)}, u32[]{:S(2)}, u32[]{:S(2)}) %collective-permute-start.1) | collective-permute-done | bytes 73760 | tf_op jit(solution)/shard_map/ppermute | solution.py:217
  15.9 0.0 copy-start.5
  15.9 3.9 %collective-permute-done.2.r3 = bf16[144,256]{1,0:T(8,128)(2,1)S(1)} collective-permute-done((bf16[144,256]{1,0:T(8,128)(2,1)}, bf16[144,256]{1,0:T(8,128)(2,1)S(1)}, u32[]{:S(2)}, u32[]{:S(2)}) %collective-permute-start.2) | collective-permute-done | bytes 73760 | tf_op jit(solution)/shard_map/ppermute | solution.py:217
  19.9 0.0 copy-start.6
  19.9 0.0 copy-done.1
  19.9 3.0 %collective-permute-start.5 = (bf16[32,4096]{1,0:T(8,128)(2,1)S(1)}, bf16[32,4096]{1,0:T(8,128)(2,1)S(1)}, u32[]{:S(2)}, u32[]{:S(2)}) collective-permute-start(bf16[32,4096]{1,0:T(8,128)(2,1)S(1)} %bitcast.18), channel_id=1, source_target_pairs={{0,3},{1,0},{2,1},{3,2},{4,7},{5,4},{6,5},{7,6},{8,11},{9,8},{10,9... | collective-permute-start | bytes 786440 | tf_op jit(solution)/shard_map/ppermute | solution.py:217
  22.9 0.7 collective-permute-start.4
  23.6 1.6 %collective-permute-start.3 = (bf16[32,4096]{1,0:T(8,128)(2,1)S(1)}, bf16[32,4096]{1,0:T(8,128)(2,1)S(1)}, u32[]{:S(2)}, u32[]{:S(2)}) collective-permute-start(bf16[32,4096]{1,0:T(8,128)(2,1)S(1)} %bitcast.20), channel_id=1, source_target_pairs={{0,1},{1,2},{2,3},{3,0},{4,5},{5,6},{6,7},{7,4},{8,9},{9,10},{10,1... | collective-permute-start | bytes 786440 | tf_op jit(solution)/shard_map/ppermute | solution.py:217
  25.2 0.0 copy-done.3
  25.2 0.9 shard_map.87
  26.1 0.0 copy-done.4
  26.1 0.0 copy-done.5
  26.1 0.0 copy-done.6
  26.1 0.0 copy-start.8
  26.1 7.0 %all-to-all-start = ((bf16[16,32,512]{2,1,0:T(8,128)(2,1)}), bf16[16,32,512]{2,1,0:T(8,128)(2,1)S(1)}, u32[]{:S(2)}, u32[]{:S(2)}) async-start(bf16[16,32,512]{2,1,0:T(8,128)(2,1)} %shard_map.87), calls=%async_computation | async-start | bytes 1048576 | tf_op jit(solution)/shard_map/all_to_all | solution.py:225
  33.1 0.0 copy-done
  33.1 0.0 copy-done.8
  33.1 0.5 shard_map.85
  33.6 7.4 %collective-permute-done.5.a3 = bf16[32,4096]{1,0:T(8,128)(2,1)S(1)} collective-permute-done((bf16[32,4096]{1,0:T(8,128)(2,1)S(1)}, bf16[32,4096]{1,0:T(8,128)(2,1)S(1)}, u32[]{:S(2)}, u32[]{:S(2)}) %collective-permute-start.5) | collective-permute-done | bytes 262176 | tf_op jit(solution)/shard_map/ppermute | solution.py:217
  41.0 0.0 collective-permute-done.4.a2
  41.0 8.0 %collective-permute-done.3.a1 = bf16[32,4096]{1,0:T(8,128)(2,1)S(1)} collective-permute-done((bf16[32,4096]{1,0:T(8,128)(2,1)S(1)}, bf16[32,4096]{1,0:T(8,128)(2,1)S(1)}, u32[]{:S(2)}, u32[]{:S(2)}) %collective-permute-start.3) | collective-permute-done | bytes 262176 | tf_op jit(solution)/shard_map/ppermute | solution.py:217
  49.0 0.5 shard_map.86
  49.5 0.0 all-to-all-done.feats
  49.5 0.0 copy-start.9
  49.5 0.8 collective-permute-start.6
  50.3 0.8 collective-permute-done.6
  51.1 0.7 broadcast_in_dim.18
  51.9 7.1 %all-to-all-start.1 = ((f32[32,16,128]{2,1,0:T(8,128)}), f32[32,16,128]{2,1,0:T(8,128)S(1)}, u32[]{:S(2)}, u32[]{:S(2)}) async-start(f32[32,16,128]{2,1,0:T(8,128)} %broadcast_in_dim.18), calls=%async_computation.1 | async-start | bytes 524288 | tf_op jit(solution)/shard_map/all_to_all | solution.py:225
  59.0 0.0 copy-done.9
  59.0 2.2 %shard_map.88.inputs = bf16[16,32,256]{2,1,0:T(8,128)(2,1)} custom-call(bf16[128,4096]{1,0:T(8,128)(2,1)} %bitcast.32, bf16[16,32,512]{2,1,0:T(8,128)(2,1)} %copy-done.9, bf16[144,256]{1,0:T(8,128)(2,1)} %copy-done.4, bf16[144,256]{1,0:T(8,128)(2,1)} %copy-done.5, bf16[144,256]{1,0:T(8,128)(2,1)} %copy-done.6), custom_call_target="tpu_custom_call" | custom-call | flops 200000000 | bytes 2000000 | tf_op jit(solution)/shard_map/pallas_call | solution.py:51
  61.1 5.9 %all-to-all-done.1 = f32[32,16,128]{2,1,0:T(8,128)S(1)} async-done(((f32[32,16,128]{2,1,0:T(8,128)}), f32[32,16,128]{2,1,0:T(8,128)S(1)}, u32[]{:S(2)}, u32[]{:S(2)}) %all-to-all-start.1) | async-done | bytes 262176 | tf_op jit(solution)/shard_map/all_to_all | solution.py:225
  67.1 2.1 %collective-permute-start.7 = (f32[16,128]{1,0:T(8,128)S(1)}, f32[16,128]{1,0:T(8,128)S(1)}, u32[]{:S(2)}, u32[]{:S(2)}) collective-permute-start(f32[16,128]{1,0:T(8,128)S(1)} %reduce_sum.9.lown), channel_id=1, source_target_pairs={{0,4},{4,0},{1,5},{5,1},{2,6},{6,2},{3,7},{7,3},{8,12},{12,8},{9,1... | collective-permute-start | bytes 24584 | tf_op jit(solution)/shard_map/ppermute | solution.py:221
  69.2 0.8 collective-permute-done.7.loth
  70.0 3.8 %shard_map.89 = (f32[32,128]{1,0:T(8,128)}, f32[32,16,128]{2,1,0:T(8,128)S(1)}, f32[32,16,128]{2,1,0:T(8,128)S(1)}) custom-call(f32[16,128]{1,0:T(8,128)S(1)} %reduce_sum.9.lown, f32[16,128]{1,0:T(8,128)S(1)} %collective-permute-done.7.loth, bf16[32,4096]{1,0:T(8,128)(2,1)S(1)} %bitcast.22, bf16[32,4096]{1,0:T(8,128)(2,1)S(1)} %collective-permute-done.3.a1, ...), custom_call_target="tpu_custom_call" | custom-call | flops 100000000 | bytes 3000000 | tf_op jit(solution)/shard_map/pallas_call | solution.py:51
  73.8 0.3 collective-permute-start.8
  74.1 1.2 %collective-permute-done.8 = f32[32,16,128]{2,1,0:T(8,128)S(1)} collective-permute-done((f32[32,16,128]{2,1,0:T(8,128)S(1)}, f32[32,16,128]{2,1,0:T(8,128)S(1)}, u32[]{:S(2)}, u32[]{:S(2)}) %collective-permute-start.8) | collective-permute-done | bytes 262176 | tf_op jit(solution)/shard_map/ppermute | solution.py:221
  75.4 0.0 copy-start.2
  75.4 11.6 %all_to_all.20.pieces = f32[32,16,128]{2,1,0:T(8,128)S(1)} all-to-all(f32[32,16,128]{2,1,0:T(8,128)S(1)} %add.7), channel_id=1, replica_groups=mesh['x'=4,'zl'=2,'y'=4,'core'=2,'t'=4] {'x','zl','y'}, dimensions={0} | all-to-all | bytes 524288 | tf_op jit(solution)/shard_map/all_to_all | solution.py:225
  86.9 0.0 copy-done.2
  86.9 0.1 shard_map.90
  87.0 15.5 %all_to_all.21.mixed = bf16[32,96,128]{2,1,0:T(8,128)(2,1)S(1)} all-to-all(bf16[32,96,128]{2,1,0:T(8,128)(2,1)S(1)} %shard_map.90), channel_id=1, replica_groups=mesh['x'=4,'zl'=2,'y'=4,'core'=2,'t'=4] {'x','zl','y'}, dimensions={0} | all-to-all | bytes 1572864 | tf_op jit(solution)/shard_map/all_to_all | solution.py:225
  102.6 0.0 copy-start.7
  102.6 3.3 %collective-permute-start.9 = (bf16[32,32,128]{2,1,0:T(8,128)(2,1)S(1)}, bf16[32,32,128]{2,1,0:T(8,128)(2,1)S(1)}, u32[]{:S(2)}, u32[]{:S(2)}) collective-permute-start(bf16[32,32,128]{2,1,0:T(8,128)(2,1)S(1)} %slice.4), channel_id=1, source_target_pairs={{0,4},{4,0},{1,5},{5,1},{2,6},{6,2},{3,7},{7,3},{8,12},{12,8},{9,1... | collective-permute-start | bytes 786440 | tf_op jit(solution)/shard_map/ppermute | solution.py:221
  105.9 1.2 %collective-permute-done.9.roth = bf16[32,32,128]{2,1,0:T(8,128)(2,1)S(1)} collective-permute-done((bf16[32,32,128]{2,1,0:T(8,128)(2,1)S(1)}, bf16[32,32,128]{2,1,0:T(8,128)(2,1)S(1)}, u32[]{:S(2)}, u32[]{:S(2)}) %collective-permute-start.9) | collective-permute-done | bytes 262176 | tf_op jit(solution)/shard_map/ppermute | solution.py:221
  107.0 0.0 copy-done.7
  107.0 1.5 %shard_map.91 = (bf16[128,4096]{1,0:T(8,128)(2,1)}, bf16[32,4096]{1,0:T(8,128)(2,1)}, bf16[32,4096]{1,0:T(8,128)(2,1)}) custom-call(bf16[32,96,128]{2,1,0:T(8,128)(2,1)S(1)} %all_to_all.21.mixed, bf16[32,32,128]{2,1,0:T(8,128)(2,1)S(1)} %collective-permute-done.9.roth, f32[32,128]{1,0:T(8,128)S(1)} %copy-done.7, bf16[128,128]{1,0:T(8,128)(2,1)S(1)} %bitcast.28, ...), custom_call_target="tpu_custom_call" | custom-call | flops 300000000 | bytes 5000000 | tf_op jit(solution)/shard_map/pallas_call | solution.py:51
  (4 shorter events, 0.1 us)
Async XLA Ops:
  0.6 19.2 %copy-start.1 = (bf16[1,32,4096]{2,1,0:T(8,128)(2,1)S(1)}, bf16[1,32,4096]{2,1,0:T(8,128)(2,1)}, u32[]{:S(2)}) copy-start(bf16[1,32,4096]{2,1,0:T(8,128)(2,1)} %param.5) | copy-start | bytes 786436
  0.6 24.6 %copy-start.3 = (bf16[1,128,128]{2,1,0:T(8,128)(2,1)S(1)}, bf16[1,128,128]{2,1,0:T(8,128)(2,1)}, u32[]{:S(2)}) copy-start(bf16[1,128,128]{2,1,0:T(8,128)(2,1)} %param.6) | copy-start | bytes 98308
  2.3 30.8 %copy-start = (bf16[1,1,128,4096]{3,2,1,0:T(8,128)(2,1)S(1)}, bf16[1,1,128,4096]{3,2,1,0:T(8,128)(2,1)}, u32[]{:S(2)}) copy-start(bf16[1,1,128,4096]{3,2,1,0:T(8,128)(2,1)} %param.8) | copy-start | bytes 3145732
  2.4 11.4 %collective-permute-start = (bf16[144,256]{1,0:T(8,128)(2,1)}, bf16[144,256]{1,0:T(8,128)(2,1)S(1)}, u32[]{:S(2)}, u32[]{:S(2)}) collective-permute-start(bf16[144,256]{1,0:T(8,128)(2,1)} %get-tuple-element.26), channel_id=1, source_target_pairs={{0,1},{1,2},{2,3},{3,0},{4,5},{5,6},{6,7},{7,4},{8,9},{9,10},{10,1... | collective-permute-start | bytes 221192 | tf_op jit(solution)/shard_map/ppermute | solution.py:217
  6.3 9.7 %collective-permute-start.1 = (bf16[144,256]{1,0:T(8,128)(2,1)}, bf16[144,256]{1,0:T(8,128)(2,1)S(1)}, u32[]{:S(2)}, u32[]{:S(2)}) collective-permute-start(bf16[144,256]{1,0:T(8,128)(2,1)} %get-tuple-element.27), channel_id=1, source_target_pairs={{0,2},{1,3},{2,0},{3,1},{4,6},{5,7},{6,4},{7,5},{8,10},{9,11},{10,... | collective-permute-start | bytes 221192 | tf_op jit(solution)/shard_map/ppermute | solution.py:217
  11.4 8.5 %collective-permute-start.2 = (bf16[144,256]{1,0:T(8,128)(2,1)}, bf16[144,256]{1,0:T(8,128)(2,1)S(1)}, u32[]{:S(2)}, u32[]{:S(2)}) collective-permute-start(bf16[144,256]{1,0:T(8,128)(2,1)} %get-tuple-element.28), channel_id=1, source_target_pairs={{0,3},{1,0},{2,1},{3,2},{4,7},{5,4},{6,5},{7,6},{8,11},{9,8},{10,9... | collective-permute-start | bytes 221192 | tf_op jit(solution)/shard_map/ppermute | solution.py:217
  13.8 12.4 %copy-start.4 = (bf16[144,256]{1,0:T(8,128)(2,1)}, bf16[144,256]{1,0:T(8,128)(2,1)S(1)}, u32[]{:S(2)}) copy-start(bf16[144,256]{1,0:T(8,128)(2,1)S(1)} %collective-permute-done.r1) | copy-start | bytes 221188
  15.9 10.2 %copy-start.5 = (bf16[144,256]{1,0:T(8,128)(2,1)}, bf16[144,256]{1,0:T(8,128)(2,1)S(1)}, u32[]{:S(2)}) copy-start(bf16[144,256]{1,0:T(8,128)(2,1)S(1)} %collective-permute-done.1.r2) | copy-start | bytes 221188
  19.9 6.2 %copy-start.6 = (bf16[144,256]{1,0:T(8,128)(2,1)}, bf16[144,256]{1,0:T(8,128)(2,1)S(1)}, u32[]{:S(2)}) copy-start(bf16[144,256]{1,0:T(8,128)(2,1)S(1)} %collective-permute-done.2.r3) | copy-start | bytes 221188
  19.9 21.1 %collective-permute-start.5 = (bf16[32,4096]{1,0:T(8,128)(2,1)S(1)}, bf16[32,4096]{1,0:T(8,128)(2,1)S(1)}, u32[]{:S(2)}, u32[]{:S(2)}) collective-permute-start(bf16[32,4096]{1,0:T(8,128)(2,1)S(1)} %bitcast.18), channel_id=1, source_target_pairs={{0,3},{1,0},{2,1},{3,2},{4,7},{5,4},{6,5},{7,6},{8,11},{9,8},{10,9... | collective-permute-start | bytes 786440 | tf_op jit(solution)/shard_map/ppermute | solution.py:217
  22.9 18.1 %collective-permute-start.4 = (bf16[32,4096]{1,0:T(8,128)(2,1)S(1)}, bf16[32,4096]{1,0:T(8,128)(2,1)S(1)}, u32[]{:S(2)}, u32[]{:S(2)}) collective-permute-start(bf16[32,4096]{1,0:T(8,128)(2,1)S(1)} %bitcast.19), channel_id=1, source_target_pairs={{0,2},{1,3},{2,0},{3,1},{4,6},{5,7},{6,4},{7,5},{8,10},{9,11},{10,... | collective-permute-start | bytes 786440 | tf_op jit(solution)/shard_map/ppermute | solution.py:217
  23.6 25.3 %collective-permute-start.3 = (bf16[32,4096]{1,0:T(8,128)(2,1)S(1)}, bf16[32,4096]{1,0:T(8,128)(2,1)S(1)}, u32[]{:S(2)}, u32[]{:S(2)}) collective-permute-start(bf16[32,4096]{1,0:T(8,128)(2,1)S(1)} %bitcast.20), channel_id=1, source_target_pairs={{0,1},{1,2},{2,3},{3,0},{4,5},{5,6},{6,7},{7,4},{8,9},{9,10},{10,1... | collective-permute-start | bytes 786440 | tf_op jit(solution)/shard_map/ppermute | solution.py:217
  26.1 7.0 %copy-start.8 = (bf16[1,1,4096,32]{2,3,1,0:T(8,128)(2,1)S(1)}, bf16[1,1,4096,32]{2,3,1,0:T(8,128)(2,1)}, u32[]{:S(2)}) copy-start(bf16[1,1,4096,32]{2,3,1,0:T(8,128)(2,1)} %param.9) | copy-start | bytes 786436
  26.1 23.4 %all-to-all-start = ((bf16[16,32,512]{2,1,0:T(8,128)(2,1)}), bf16[16,32,512]{2,1,0:T(8,128)(2,1)S(1)}, u32[]{:S(2)}, u32[]{:S(2)}) async-start(bf16[16,32,512]{2,1,0:T(8,128)(2,1)} %shard_map.87), calls=%async_computation | async-start | bytes 1048576 | tf_op jit(solution)/shard_map/all_to_all | solution.py:225
  49.5 9.5 %copy-start.9 = (bf16[16,32,512]{2,1,0:T(8,128)(2,1)}, bf16[16,32,512]{2,1,0:T(8,128)(2,1)S(1)}, u32[]{:S(2)}) copy-start(bf16[16,32,512]{2,1,0:T(8,128)(2,1)S(1)} %all-to-all-done.feats) | copy-start | bytes 1572868
  49.5 1.6 %collective-permute-start.6 = (f32[16,128]{1,0:T(8,128)S(1)}, f32[16,128]{1,0:T(8,128)S(1)}, u32[]{:S(2)}, u32[]{:S(2)}) collective-permute-start(f32[16,128]{1,0:T(8,128)S(1)} %get-tuple-element.38), channel_id=1, source_target_pairs={{0,4},{4,0},{1,5},{5,1},{2,6},{6,2},{3,7},{7,3},{8,12},{12,8},{9,1... | collective-permute-start | bytes 24584 | tf_op jit(solution)/shard_map/ppermute | solution.py:221
  51.9 15.2 %all-to-all-start.1 = ((f32[32,16,128]{2,1,0:T(8,128)}), f32[32,16,128]{2,1,0:T(8,128)S(1)}, u32[]{:S(2)}, u32[]{:S(2)}) async-start(f32[32,16,128]{2,1,0:T(8,128)} %broadcast_in_dim.18), calls=%async_computation.1 | async-start | bytes 524288 | tf_op jit(solution)/shard_map/all_to_all | solution.py:225
  67.1 2.9 %collective-permute-start.7 = (f32[16,128]{1,0:T(8,128)S(1)}, f32[16,128]{1,0:T(8,128)S(1)}, u32[]{:S(2)}, u32[]{:S(2)}) collective-permute-start(f32[16,128]{1,0:T(8,128)S(1)} %reduce_sum.9.lown), channel_id=1, source_target_pairs={{0,4},{4,0},{1,5},{5,1},{2,6},{6,2},{3,7},{7,3},{8,12},{12,8},{9,1... | collective-permute-start | bytes 24584 | tf_op jit(solution)/shard_map/ppermute | solution.py:221
  73.8 1.5 %collective-permute-start.8 = (f32[32,16,128]{2,1,0:T(8,128)S(1)}, f32[32,16,128]{2,1,0:T(8,128)S(1)}, u32[]{:S(2)}, u32[]{:S(2)}) collective-permute-start(f32[32,16,128]{2,1,0:T(8,128)S(1)} %get-tuple-element.42), channel_id=1, source_target_pairs={{0,4},{4,0},{1,5},{5,1},{2,6},{6,2},{3,7},{7,3},{8,12},{12,8},{9,1... | collective-permute-start | bytes 786440 | tf_op jit(solution)/shard_map/ppermute | solution.py:221
  75.4 11.6 %copy-start.2 = (bf16[16,32,256]{2,1,0:T(8,128)(2,1)S(1)}, bf16[16,32,256]{2,1,0:T(8,128)(2,1)}, u32[]{:S(2)}) copy-start(bf16[16,32,256]{2,1,0:T(8,128)(2,1)} %shard_map.88.inputs) | copy-start | bytes 786436
  102.6 4.5 %copy-start.7 = (f32[32,128]{1,0:T(8,128)S(1)}, f32[32,128]{1,0:T(8,128)}, u32[]{:S(2)}) copy-start(f32[32,128]{1,0:T(8,128)} %get-tuple-element.44.qt) | copy-start | bytes 49156
  102.6 4.4 %collective-permute-start.9 = (bf16[32,32,128]{2,1,0:T(8,128)(2,1)S(1)}, bf16[32,32,128]{2,1,0:T(8,128)(2,1)S(1)}, u32[]{:S(2)}, u32[]{:S(2)}) collective-permute-start(bf16[32,32,128]{2,1,0:T(8,128)(2,1)S(1)} %slice.4), channel_id=1, source_target_pairs={{0,4},{4,0},{1,5},{5,1},{2,6},{6,2},{3,7},{7,3},{8,12},{12,8},{9,1... | collective-permute-start | bytes 786440 | tf_op jit(solution)/shard_map/ppermute | solution.py:221

commit v10 on v7

--- a/solution.py
+++ b/solution.py
@@ -255,14 +255,6 @@
         moved=10**8,
     )(act, ef, warm)
 
-    half = ((HALF, HEAD), F32)
-    left_keep, left_send = call(
-        left_kernel, [half, half], [pltpu.VMEM((RANK, HEAD), F32)], flops=5 * 10**7, moved=10**6
-    )(*acts[1:], og, lines, inner, fed)
-    left_send, feats = lax.optimization_barrier((left_send, feats))
-
-    left_half = left_keep + swapped(left_send)
-    pieces = exchanged(jnp.broadcast_to(left_half[None], (N_CHIPS, HALF, HEAD)), CHIPS)
     (inputs,) = call(
         input_kernel,
         [((PLANE, OWN, CUT), BF16)],
@@ -278,7 +270,14 @@
         dest=pltpu.MemorySpace.HBM,
         room=60,
     )(weight, feats, *got)
-    pieces, inputs = lax.optimization_barrier((pieces, inputs))
+    lines, inputs = lax.optimization_barrier((lines, inputs))
+    half = ((HALF, HEAD), F32)
+    left_keep, left_send = call(
+        left_kernel, [half, half], [pltpu.VMEM((RANK, HEAD), F32)], flops=5 * 10**7, moved=10**6
+    )(*acts[1:], og, lines, inner, fed)
+
+    left_half = left_keep + swapped(left_send)
+    pieces = exchanged(jnp.broadcast_to(left_half[None], (N_CHIPS, HALF, HEAD)), CHIPS)
     left_own = jnp.sum(pieces, axis=0)
     left_other = swapped(left_own)
 

time: 104 us -> 105 us (level)
  blocking collectives: 27.1 us -> 38.5 us
  waiting for transfers between devices: 29.4 us -> 24 us
  starting transfers between devices: 34 us -> 29.5 us
    all_to_all x2 -> x3, blocking collectives: 27.1 us -> 38.5 us  [exchanged(): return lax.all_to_all(x, axes, 0, 0, tiled=True)]
    ppermute x6, waiting for transfers between devices: 16.9 us -> 10.2 us  [moved(): return lax.ppermute(x, axis, [(i, (i + k) % 4) for i in range(4)])]
    all_to_all x2 -> x1, starting transfers between devices: 11.4 us -> 6.9 us  [exchanged(): return lax.all_to_all(x, axes, 0, 0, tiled=True)]
    all_to_all x2 -> x1, waiting for transfers between devices: 8.47 us -> 9.78 us  [exchanged(): return lax.all_to_all(x, axes, 0, 0, tiled=True)]
  transfers between devices with their start and end apart: 12 -> 11, of which waited for: 8 -> 6; matrix products, arithmetic and copies ran while one was open for 0% -> 0% of each run, Pallas kernels for 4% -> 3%
where the time goes in v10:
time: 105 us
  blocking collectives  38.5 us (37%)
  starting transfers between devices  29.5 us (28%)
  waiting for transfers between devices  24 us (23%)
  Pallas kernels  11.1 us (11%)
    all_to_all x3, blocking collectives, exchanged(): return lax.all_to_all(x, axes, 0, 0, tiled=True)  38.5 us
    ppermute x6, starting transfers between devices, moved(): return lax.ppermute(x, axis, [(i, (i + k) % 4) for i in range(4)])  14.8 us
    pallas_call x8, Pallas kernels, run(): pl.pallas_call(kernel, out_shape=[jax.ShapeDtypeStruct(s, d) for s, d in...  11.1 us
    ppermute x6, waiting for transfers between devices, moved(): return lax.ppermute(x, axis, [(i, (i + k) % 4) for i in range(4)])  10.2 us
    all_to_all x1, waiting for transfers between devices, exchanged(): return lax.all_to_all(x, axes, 0, 0, tiled=True)  9.78 us
    ppermute x4, starting transfers between devices, swapped(): return lax.ppermute(x, 'core', [(0, 1), (1, 0)])  7.85 us
    all_to_all x1, starting transfers between devices, exchanged(): return lax.all_to_all(x, axes, 0, 0, tiled=True)  6.9 us
    ppermute x4, waiting for transfers between devices, swapped(): return lax.ppermute(x, 'core', [(0, 1), (1, 0)])  4.01 us
  transfers between devices with their start and end apart: 11, of which 6 were waited for; matrix products, arithmetic and copies ran while one was open for 0% of the time, Pallas kernels for 3%

profile of v10, /device:TPU:1, one launch (start us, length us, event | category | flops | bytes accessed | tf_op | source)
XLA Modules:
  0.0 104.8 jit_solution(8579168726649491821)
XLA Ops:
  0.6 0.0 copy-start.1
  0.6 0.0 copy-start.3
  0.7 1.6 %shard_map.85 = (bf16[144,256]{1,0:T(8,128)(2,1)}, bf16[144,256]{1,0:T(8,128)(2,1)}, bf16[144,256]{1,0:T(8,128)(2,1)}) custom-call(bf16[128,4096]{1,0:T(8,128)(2,1)} %bitcast.31, bf16[128,128]{1,0:T(8,128)(2,1)} %bitcast.24), custom_call_target="tpu_custom_call" | custom-call | flops 1000000 | bytes 1000000 | tf_op jit(solution)/shard_map/pallas_call | solution.py:51
  2.3 0.0 copy-start
  2.3 3.9 %collective-permute-start.3 = (bf16[144,256]{1,0:T(8,128)(2,1)}, bf16[144,256]{1,0:T(8,128)(2,1)S(1)}, u32[]{:S(2)}, u32[]{:S(2)}) collective-permute-start(bf16[144,256]{1,0:T(8,128)(2,1)} %get-tuple-element.21), channel_id=1, source_target_pairs={{0,1},{1,2},{2,3},{3,0},{4,5},{5,6},{6,7},{7,4},{8,9},{9,10},{10,1... | collective-permute-start | bytes 221192 | tf_op jit(solution)/shard_map/ppermute | solution.py:218
  6.2 5.1 %collective-permute-start.4 = (bf16[144,256]{1,0:T(8,128)(2,1)}, bf16[144,256]{1,0:T(8,128)(2,1)S(1)}, u32[]{:S(2)}, u32[]{:S(2)}) collective-permute-start(bf16[144,256]{1,0:T(8,128)(2,1)} %get-tuple-element.22), channel_id=1, source_target_pairs={{0,2},{1,3},{2,0},{3,1},{4,6},{5,7},{6,4},{7,5},{8,10},{9,11},{10,... | collective-permute-start | bytes 221192 | tf_op jit(solution)/shard_map/ppermute | solution.py:218
  11.3 2.4 %collective-permute-start.5 = (bf16[144,256]{1,0:T(8,128)(2,1)}, bf16[144,256]{1,0:T(8,128)(2,1)S(1)}, u32[]{:S(2)}, u32[]{:S(2)}) collective-permute-start(bf16[144,256]{1,0:T(8,128)(2,1)} %get-tuple-element.23), channel_id=1, source_target_pairs={{0,3},{1,0},{2,1},{3,2},{4,7},{5,4},{6,5},{7,6},{8,11},{9,8},{10,9... | collective-permute-start | bytes 221192 | tf_op jit(solution)/shard_map/ppermute | solution.py:218
  13.7 0.0 copy-done.1
  13.7 0.0 collective-permute-start.2
  13.7 3.2 %collective-permute-start.1 = (bf16[32,4096]{1,0:T(8,128)(2,1)S(1)}, bf16[32,4096]{1,0:T(8,128)(2,1)S(1)}, u32[]{:S(2)}, u32[]{:S(2)}) collective-permute-start(bf16[32,4096]{1,0:T(8,128)(2,1)S(1)} %bitcast.19), channel_id=1, source_target_pairs={{0,2},{1,3},{2,0},{3,1},{4,6},{5,7},{6,4},{7,5},{8,10},{9,11},{10,... | collective-permute-start | bytes 786440 | tf_op jit(solution)/shard_map/ppermute | solution.py:218
  17.0 0.0 collective-permute-done.3.r1
  17.0 0.0 copy-start.4
  17.0 0.1 collective-permute-start
  17.1 0.0 collective-permute-done.4.r2
  17.1 0.0 copy-start.5
  17.1 10.2 %collective-permute-done.5.r3 = bf16[144,256]{1,0:T(8,128)(2,1)S(1)} collective-permute-done((bf16[144,256]{1,0:T(8,128)(2,1)}, bf16[144,256]{1,0:T(8,128)(2,1)S(1)}, u32[]{:S(2)}, u32[]{:S(2)}) %collective-permute-start.5) | collective-permute-done | bytes 73760 | tf_op jit(solution)/shard_map/ppermute | solution.py:218
  27.3 0.0 copy-done.3
  27.3 0.0 copy-start.6
  27.3 0.9 shard_map.86
  28.1 0.0 copy-done.4
  28.1 0.0 copy-done.5
  28.2 0.0 copy-done.6
  28.2 0.0 copy-start.8
  28.2 6.9 %all-to-all-start = ((bf16[16,32,512]{2,1,0:T(8,128)(2,1)}), bf16[16,32,512]{2,1,0:T(8,128)(2,1)S(1)}, u32[]{:S(2)}, u32[]{:S(2)}) async-start(bf16[16,32,512]{2,1,0:T(8,128)(2,1)} %shard_map.86), calls=%async_computation | async-start | bytes 1048576 | tf_op jit(solution)/shard_map/all_to_all | solution.py:226
  35.1 0.0 copy-done
  35.1 0.0 copy-done.8
  35.1 0.5 shard_map.84
  35.6 9.8 %all-to-all-done.feats = bf16[16,32,512]{2,1,0:T(8,128)(2,1)S(1)} async-done(((bf16[16,32,512]{2,1,0:T(8,128)(2,1)}), bf16[16,32,512]{2,1,0:T(8,128)(2,1)S(1)}, u32[]{:S(2)}, u32[]{:S(2)}) %all-to-all-start) | async-done | bytes 524320 | tf_op jit(solution)/shard_map/all_to_all | solution.py:226
  45.4 0.0 copy-start.9
  45.4 0.8 copy-done.9
  46.2 2.1 %shard_map.87.inputs = bf16[16,32,256]{2,1,0:T(8,128)(2,1)} custom-call(bf16[128,4096]{1,0:T(8,128)(2,1)} %bitcast.32, bf16[16,32,512]{2,1,0:T(8,128)(2,1)} %copy-done.9, bf16[144,256]{1,0:T(8,128)(2,1)} %copy-done.4, bf16[144,256]{1,0:T(8,128)(2,1)} %copy-done.5, bf16[144,256]{1,0:T(8,128)(2,1)} %copy-done.6), custom_call_target="tpu_custom_call" | custom-call | flops 200000000 | bytes 2000000 | tf_op jit(solution)/shard_map/pallas_call | solution.py:51
  48.3 0.0 collective-permute-done.2.a3
  48.3 0.0 collective-permute-done.1.a2
  48.3 0.0 collective-permute-done.a1
  48.3 0.6 shard_map.88
  48.9 2.2 %collective-permute-start.6 = (f32[16,128]{1,0:T(8,128)S(1)}, f32[16,128]{1,0:T(8,128)S(1)}, u32[]{:S(2)}, u32[]{:S(2)}) collective-permute-start(f32[16,128]{1,0:T(8,128)S(1)} %get-tuple-element.28), channel_id=1, source_target_pairs={{0,4},{4,0},{1,5},{5,1},{2,6},{6,2},{3,7},{7,3},{8,12},{12,8},{9,1... | collective-permute-start | bytes 24584 | tf_op jit(solution)/shard_map/ppermute | solution.py:222
  51.1 0.8 collective-permute-done.6
  51.9 11.4 %all_to_all.20 = f32[32,16,128]{2,1,0:T(8,128)S(1)} all-to-all(f32[32,16,128]{2,1,0:T(8,128)S(1)} %broadcast_in_dim.18), channel_id=1, replica_groups=mesh['x'=4,'zl'=2,'y'=4,'core'=2,'t'=4] {'x','zl','y'}, dimensions={0} | all-to-all | bytes 524288 | tf_op jit(solution)/shard_map/all_to_all | solution.py:226
  63.4 2.1 %collective-permute-start.7 = (f32[16,128]{1,0:T(8,128)S(1)}, f32[16,128]{1,0:T(8,128)S(1)}, u32[]{:S(2)}, u32[]{:S(2)}) collective-permute-start(f32[16,128]{1,0:T(8,128)S(1)} %reduce_sum.9.lown), channel_id=1, source_target_pairs={{0,4},{4,0},{1,5},{5,1},{2,6},{6,2},{3,7},{7,3},{8,12},{12,8},{9,1... | collective-permute-start | bytes 24584 | tf_op jit(solution)/shard_map/ppermute | solution.py:222
  65.4 0.8 collective-permute-done.7.loth
  66.3 3.8 %shard_map.89 = (f32[32,128]{1,0:T(8,128)}, f32[32,16,128]{2,1,0:T(8,128)S(1)}, f32[32,16,128]{2,1,0:T(8,128)S(1)}) custom-call(f32[16,128]{1,0:T(8,128)S(1)} %reduce_sum.9.lown, f32[16,128]{1,0:T(8,128)S(1)} %collective-permute-done.7.loth, bf16[32,4096]{1,0:T(8,128)(2,1)S(1)} %bitcast.22, bf16[32,4096]{1,0:T(8,128)(2,1)S(1)} %collective-permute-done.a1, ...), custom_call_target="tpu_custom_call" | custom-call | flops 100000000 | bytes 3000000 | tf_op jit(solution)/shard_map/pallas_call | solution.py:51
  70.0 0.3 collective-permute-start.8
  70.4 1.2 %collective-permute-done.8 = f32[32,16,128]{2,1,0:T(8,128)S(1)} collective-permute-done((f32[32,16,128]{2,1,0:T(8,128)S(1)}, f32[32,16,128]{2,1,0:T(8,128)S(1)}, u32[]{:S(2)}, u32[]{:S(2)}) %collective-permute-start.8) | collective-permute-done | bytes 262176 | tf_op jit(solution)/shard_map/ppermute | solution.py:222
  71.6 0.0 copy-start.2
  71.6 11.6 %all_to_all.21.pieces = f32[32,16,128]{2,1,0:T(8,128)S(1)} all-to-all(f32[32,16,128]{2,1,0:T(8,128)S(1)} %add.7), channel_id=1, replica_groups=mesh['x'=4,'zl'=2,'y'=4,'core'=2,'t'=4] {'x','zl','y'}, dimensions={0} | all-to-all | bytes 524288 | tf_op jit(solution)/shard_map/all_to_all | solution.py:226
  83.2 0.0 copy-done.2
  83.2 0.1 shard_map.90
  83.3 15.5 %all_to_all.22.mixed = bf16[32,96,128]{2,1,0:T(8,128)(2,1)S(1)} all-to-all(bf16[32,96,128]{2,1,0:T(8,128)(2,1)S(1)} %shard_map.90), channel_id=1, replica_groups=mesh['x'=4,'zl'=2,'y'=4,'core'=2,'t'=4] {'x','zl','y'}, dimensions={0} | all-to-all | bytes 1572864 | tf_op jit(solution)/shard_map/all_to_all | solution.py:226
  98.8 0.0 copy-start.7
  98.8 3.3 %collective-permute-start.9 = (bf16[32,32,128]{2,1,0:T(8,128)(2,1)S(1)}, bf16[32,32,128]{2,1,0:T(8,128)(2,1)S(1)}, u32[]{:S(2)}, u32[]{:S(2)}) collective-permute-start(bf16[32,32,128]{2,1,0:T(8,128)(2,1)S(1)} %slice.4), channel_id=1, source_target_pairs={{0,4},{4,0},{1,5},{5,1},{2,6},{6,2},{3,7},{7,3},{8,12},{12,8},{9,1... | collective-permute-start | bytes 786440 | tf_op jit(solution)/shard_map/ppermute | solution.py:222
  102.1 1.2 %collective-permute-done.9.roth = bf16[32,32,128]{2,1,0:T(8,128)(2,1)S(1)} collective-permute-done((bf16[32,32,128]{2,1,0:T(8,128)(2,1)S(1)}, bf16[32,32,128]{2,1,0:T(8,128)(2,1)S(1)}, u32[]{:S(2)}, u32[]{:S(2)}) %collective-permute-start.9) | collective-permute-done | bytes 262176 | tf_op jit(solution)/shard_map/ppermute | solution.py:222
  103.3 0.0 copy-done.7
  103.3 1.5 %shard_map.91 = (bf16[128,4096]{1,0:T(8,128)(2,1)}, bf16[32,4096]{1,0:T(8,128)(2,1)}, bf16[32,4096]{1,0:T(8,128)(2,1)}) custom-call(bf16[32,96,128]{2,1,0:T(8,128)(2,1)S(1)} %all_to_all.22.mixed, bf16[32,32,128]{2,1,0:T(8,128)(2,1)S(1)} %collective-permute-done.9.roth, f32[32,128]{1,0:T(8,128)S(1)} %copy-done.7, bf16[128,128]{1,0:T(8,128)(2,1)S(1)} %bitcast.28, ...), custom_call_target="tpu_custom_call" | custom-call | flops 300000000 | bytes 5000000 | tf_op jit(solution)/shard_map/pallas_call | solution.py:51
  (5 shorter events, 0.1 us)
Async XLA Ops:
  0.6 13.1 %copy-start.1 = (bf16[1,32,4096]{2,1,0:T(8,128)(2,1)S(1)}, bf16[1,32,4096]{2,1,0:T(8,128)(2,1)}, u32[]{:S(2)}) copy-start(bf16[1,32,4096]{2,1,0:T(8,128)(2,1)} %param.5) | copy-start | bytes 786436
  0.6 26.6 %copy-start.3 = (bf16[1,128,128]{2,1,0:T(8,128)(2,1)S(1)}, bf16[1,128,128]{2,1,0:T(8,128)(2,1)}, u32[]{:S(2)}) copy-start(bf16[1,128,128]{2,1,0:T(8,128)(2,1)} %param.6) | copy-start | bytes 98308
  2.3 32.8 %copy-start = (bf16[1,1,128,4096]{3,2,1,0:T(8,128)(2,1)S(1)}, bf16[1,1,128,4096]{3,2,1,0:T(8,128)(2,1)}, u32[]{:S(2)}) copy-start(bf16[1,1,128,4096]{3,2,1,0:T(8,128)(2,1)} %param.8) | copy-start | bytes 3145732
  2.3 14.7 %collective-permute-start.3 = (bf16[144,256]{1,0:T(8,128)(2,1)}, bf16[144,256]{1,0:T(8,128)(2,1)S(1)}, u32[]{:S(2)}, u32[]{:S(2)}) collective-permute-start(bf16[144,256]{1,0:T(8,128)(2,1)} %get-tuple-element.21), channel_id=1, source_target_pairs={{0,1},{1,2},{2,3},{3,0},{4,5},{5,6},{6,7},{7,4},{8,9},{9,10},{10,1... | collective-permute-start | bytes 221192 | tf_op jit(solution)/shard_map/ppermute | solution.py:218
  6.2 10.9 %collective-permute-start.4 = (bf16[144,256]{1,0:T(8,128)(2,1)}, bf16[144,256]{1,0:T(8,128)(2,1)S(1)}, u32[]{:S(2)}, u32[]{:S(2)}) collective-permute-start(bf16[144,256]{1,0:T(8,128)(2,1)} %get-tuple-element.22), channel_id=1, source_target_pairs={{0,2},{1,3},{2,0},{3,1},{4,6},{5,7},{6,4},{7,5},{8,10},{9,11},{10,... | collective-permute-start | bytes 221192 | tf_op jit(solution)/shard_map/ppermute | solution.py:218
  11.3 16.0 %collective-permute-start.5 = (bf16[144,256]{1,0:T(8,128)(2,1)}, bf16[144,256]{1,0:T(8,128)(2,1)S(1)}, u32[]{:S(2)}, u32[]{:S(2)}) collective-permute-start(bf16[144,256]{1,0:T(8,128)(2,1)} %get-tuple-element.23), channel_id=1, source_target_pairs={{0,3},{1,0},{2,1},{3,2},{4,7},{5,4},{6,5},{7,6},{8,11},{9,8},{10,9... | collective-permute-start | bytes 221192 | tf_op jit(solution)/shard_map/ppermute | solution.py:218
  13.7 34.6 %collective-permute-start.2 = (bf16[32,4096]{1,0:T(8,128)(2,1)S(1)}, bf16[32,4096]{1,0:T(8,128)(2,1)S(1)}, u32[]{:S(2)}, u32[]{:S(2)}) collective-permute-start(bf16[32,4096]{1,0:T(8,128)(2,1)S(1)} %bitcast.18), channel_id=1, source_target_pairs={{0,3},{1,0},{2,1},{3,2},{4,7},{5,4},{6,5},{7,6},{8,11},{9,8},{10,9... | collective-permute-start | bytes 786440 | tf_op jit(solution)/shard_map/ppermute | solution.py:218
  13.7 34.6 %collective-permute-start.1 = (bf16[32,4096]{1,0:T(8,128)(2,1)S(1)}, bf16[32,4096]{1,0:T(8,128)(2,1)S(1)}, u32[]{:S(2)}, u32[]{:S(2)}) collective-permute-start(bf16[32,4096]{1,0:T(8,128)(2,1)S(1)} %bitcast.19), channel_id=1, source_target_pairs={{0,2},{1,3},{2,0},{3,1},{4,6},{5,7},{6,4},{7,5},{8,10},{9,11},{10,... | collective-permute-start | bytes 786440 | tf_op jit(solution)/shard_map/ppermute | solution.py:218
  17.0 11.2 %copy-start.4 = (bf16[144,256]{1,0:T(8,128)(2,1)}, bf16[144,256]{1,0:T(8,128)(2,1)S(1)}, u32[]{:S(2)}) copy-start(bf16[144,256]{1,0:T(8,128)(2,1)S(1)} %collective-permute-done.3.r1) | copy-start | bytes 221188
  17.0 31.4 %collective-permute-start = (bf16[32,4096]{1,0:T(8,128)(2,1)S(1)}, bf16[32,4096]{1,0:T(8,128)(2,1)S(1)}, u32[]{:S(2)}, u32[]{:S(2)}) collective-permute-start(bf16[32,4096]{1,0:T(8,128)(2,1)S(1)} %bitcast.20), channel_id=1, source_target_pairs={{0,1},{1,2},{2,3},{3,0},{4,5},{5,6},{6,7},{7,4},{8,9},{9,10},{10,1... | collective-permute-start | bytes 786440 | tf_op jit(solution)/shard_map/ppermute | solution.py:218
  17.1 11.1 %copy-start.5 = (bf16[144,256]{1,0:T(8,128)(2,1)}, bf16[144,256]{1,0:T(8,128)(2,1)S(1)}, u32[]{:S(2)}) copy-start(bf16[144,256]{1,0:T(8,128)(2,1)S(1)} %collective-permute-done.4.r2) | copy-start | bytes 221188
  27.3 0.9 copy-start.6
  28.2 6.9 %copy-start.8 = (bf16[1,1,4096,32]{2,3,1,0:T(8,128)(2,1)S(1)}, bf16[1,1,4096,32]{2,3,1,0:T(8,128)(2,1)}, u32[]{:S(2)}) copy-start(bf16[1,1,4096,32]{2,3,1,0:T(8,128)(2,1)} %param.9) | copy-start | bytes 786436
  28.2 17.2 %all-to-all-start = ((bf16[16,32,512]{2,1,0:T(8,128)(2,1)}), bf16[16,32,512]{2,1,0:T(8,128)(2,1)S(1)}, u32[]{:S(2)}, u32[]{:S(2)}) async-start(bf16[16,32,512]{2,1,0:T(8,128)(2,1)} %shard_map.86), calls=%async_computation | async-start | bytes 1048576 | tf_op jit(solution)/shard_map/all_to_all | solution.py:226
  45.4 0.8 copy-start.9
  48.9 3.0 %collective-permute-start.6 = (f32[16,128]{1,0:T(8,128)S(1)}, f32[16,128]{1,0:T(8,128)S(1)}, u32[]{:S(2)}, u32[]{:S(2)}) collective-permute-start(f32[16,128]{1,0:T(8,128)S(1)} %get-tuple-element.28), channel_id=1, source_target_pairs={{0,4},{4,0},{1,5},{5,1},{2,6},{6,2},{3,7},{7,3},{8,12},{12,8},{9,1... | collective-permute-start | bytes 24584 | tf_op jit(solution)/shard_map/ppermute | solution.py:222
  63.4 2.9 %collective-permute-start.7 = (f32[16,128]{1,0:T(8,128)S(1)}, f32[16,128]{1,0:T(8,128)S(1)}, u32[]{:S(2)}, u32[]{:S(2)}) collective-permute-start(f32[16,128]{1,0:T(8,128)S(1)} %reduce_sum.9.lown), channel_id=1, source_target_pairs={{0,4},{4,0},{1,5},{5,1},{2,6},{6,2},{3,7},{7,3},{8,12},{12,8},{9,1... | collective-permute-start | bytes 24584 | tf_op jit(solution)/shard_map/ppermute | solution.py:222
  70.0 1.5 %collective-permute-start.8 = (f32[32,16,128]{2,1,0:T(8,128)S(1)}, f32[32,16,128]{2,1,0:T(8,128)S(1)}, u32[]{:S(2)}, u32[]{:S(2)}) collective-permute-start(f32[32,16,128]{2,1,0:T(8,128)S(1)} %get-tuple-element.30), channel_id=1, source_target_pairs={{0,4},{4,0},{1,5},{5,1},{2,6},{6,2},{3,7},{7,3},{8,12},{12,8},{9,1... | collective-permute-start | bytes 786440 | tf_op jit(solution)/shard_map/ppermute | solution.py:222
  71.6 11.6 %copy-start.2 = (bf16[16,32,256]{2,1,0:T(8,128)(2,1)S(1)}, bf16[16,32,256]{2,1,0:T(8,128)(2,1)}, u32[]{:S(2)}) copy-start(bf16[16,32,256]{2,1,0:T(8,128)(2,1)} %shard_map.87.inputs) | copy-start | bytes 786436
  98.8 4.5 %copy-start.7 = (f32[32,128]{1,0:T(8,128)S(1)}, f32[32,128]{1,0:T(8,128)}, u32[]{:S(2)}) copy-start(f32[32,128]{1,0:T(8,128)} %get-tuple-element.32.qt) | copy-start | bytes 49156
  98.8 4.4 %collective-permute-start.9 = (bf16[32,32,128]{2,1,0:T(8,128)(2,1)S(1)}, bf16[32,32,128]{2,1,0:T(8,128)(2,1)S(1)}, u32[]{:S(2)}, u32[]{:S(2)}) collective-permute-start(bf16[32,32,128]{2,1,0:T(8,128)(2,1)S(1)} %slice.4), channel_id=1, source_target_pairs={{0,4},{4,0},{1,5},{5,1},{2,6},{6,2},{3,7},{7,3},{8,12},{12,8},{9,1... | collective-permute-start | bytes 786440 | tf_op jit(solution)/shard_map/ppermute | solution.py:222

commit v11 on v8

--- a/solution.py
+++ b/solution.py
@@ -243,7 +243,6 @@
     acts = [act] + [moved(act, k) for k in (1, 2, 3)]
     (rows,) = call(rows_kernel, [((PLANE, OWN, 512), BF16)], [pltpu.VMEM((OWN, 512), BF16)])(og, *got)
     feats = exchanged(rows, ("x", "y"))
-    traded = [swapped(g) for g in got]
     inner, fed, lines = call(
         early_kernel,
         [((RANK, OWN), F32), ((RANK, HEAD), F32), ((RANK, WIDE), BF16)],
@@ -255,9 +254,11 @@
     left_keep, left_send = call(
         left_kernel, [half, half], [pltpu.VMEM((RANK, HEAD), F32)], flops=5 * 10**7, moved=10**6
     )(*acts[1:], og, lines, inner, fed)
-    left_send, feats, traded = lax.optimization_barrier((left_send, feats, traded))
+    left_send, feats = lax.optimization_barrier((left_send, feats))
 
     left_half = left_keep + swapped(left_send)
+    left_half, got = lax.optimization_barrier((left_half, got))
+    traded = [swapped(g) for g in got]
     pieces = exchanged(jnp.broadcast_to(left_half[None], (N_CHIPS, HALF, HEAD)), CHIPS)
     (inputs,) = call(
         input_kernel,

time: 108 us -> 104 us (0.963)
  starting transfers between devices: 56.9 us -> 42 us
  waiting for transfers between devices: 11.2 us -> 19.9 us
    ppermute x7, starting transfers between devices: 30.2 us -> 8.02 us  [swapped(): return lax.ppermute(x, 'core', [(0, 1), (1, 0)])]
    ppermute x6, waiting for transfers between devices: 1.23 us -> 12.3 us  [moved(): return lax.ppermute(x, axis, [(i, (i + k) % 4) for i in range(4)])]
    all_to_all x2, starting transfers between devices: 10.8 us -> 19.2 us  [exchanged(): return lax.all_to_all(x, axes, 0, 0, tiled=True)]
    all_to_all x2, waiting for transfers between devices: 5.94 us -> 2.76 us  [exchanged(): return lax.all_to_all(x, axes, 0, 0, tiled=True)]
    ppermute x6, starting transfers between devices: 15.9 us -> 14.8 us  [moved(): return lax.ppermute(x, axis, [(i, (i + k) % 4) for i in range(4)])]
  transfers between devices with their start and end apart: 15 -> 15, of which waited for: 6 -> 9; matrix products, arithmetic and copies ran while one was open for 0% -> 0% of each run, Pallas kernels for 5% -> 4%
where the time goes in v11:
time: 104 us; the launch traced here: 103 us
  starting transfers between devices  42 us (40%)
  blocking collectives  27.6 us (27%)
  waiting for transfers between devices  19.9 us (19%)
  Pallas kernels  11.1 us (11%)
  local copies, waits for them, and re-layouts  1.85 us (2%)
    all_to_all x2, blocking collectives, exchanged(): return lax.all_to_all(x, axes, 0, 0, tiled=True)  27.6 us
    all_to_all x2, starting transfers between devices, exchanged(): return lax.all_to_all(x, axes, 0, 0, tiled=True)  19.2 us
    ppermute x6, starting transfers between devices, moved(): return lax.ppermute(x, axis, [(i, (i + k) % 4) for i in range(4)])  14.8 us
    ppermute x6, waiting for transfers between devices, moved(): return lax.ppermute(x, axis, [(i, (i + k) % 4) for i in range(4)])  12.3 us
    pallas_call x8, Pallas kernels, run(): pl.pallas_call(kernel, out_shape=[jax.ShapeDtypeStruct(s, d) for s, d in...  11.1 us
    ppermute x7, starting transfers between devices, swapped(): return lax.ppermute(x, 'core', [(0, 1), (1, 0)])  8.02 us
    ppermute x7, waiting for transfers between devices, swapped(): return lax.ppermute(x, 'core', [(0, 1), (1, 0)])  4.88 us
    all_to_all x2, waiting for transfers between devices, exchanged(): return lax.all_to_all(x, axes, 0, 0, tiled=True)  2.76 us
  transfers between devices with their start and end apart: 15, of which 9 were waited for; matrix products, arithmetic and copies ran while one was open for 0% of the time, Pallas kernels for 4%

profile of v11, /device:TPU:1, one launch (start us, length us, event | category | flops | bytes accessed | tf_op | source)
XLA Modules:
  0.0 103.2 jit_solution(4271437582341232733)
XLA Ops:
  0.6 0.0 copy-start.1
  0.6 0.0 copy-start.3
  0.7 1.6 %shard_map.86 = (bf16[80,256]{1,0:T(8,128)(2,1)}, bf16[80,256]{1,0:T(8,128)(2,1)}, bf16[80,256]{1,0:T(8,128)(2,1)}) custom-call(bf16[128,4096]{1,0:T(8,128)(2,1)} %bitcast.31, bf16[128,128]{1,0:T(8,128)(2,1)} %bitcast.24), custom_call_target="tpu_custom_call" | custom-call | flops 1000000 | bytes 1000000 | tf_op jit(solution)/shard_map/pallas_call | solution.py:51
  2.2 0.0 copy-start
  2.2 3.9 %collective-permute-start.3 = (bf16[80,256]{1,0:T(8,128)(2,1)}, bf16[80,256]{1,0:T(8,128)(2,1)S(1)}, u32[]{:S(2)}, u32[]{:S(2)}) collective-permute-start(bf16[80,256]{1,0:T(8,128)(2,1)} %get-tuple-element.31), channel_id=1, source_target_pairs={{0,1},{1,2},{2,3},{3,0},{4,5},{5,6},{6,7},{7,4},{8,9},{9,10},{10,1... | collective-permute-start | bytes 122888 | tf_op jit(solution)/shard_map/ppermute | solution.py:219
  6.1 5.1 %collective-permute-start.4 = (bf16[80,256]{1,0:T(8,128)(2,1)}, bf16[80,256]{1,0:T(8,128)(2,1)S(1)}, u32[]{:S(2)}, u32[]{:S(2)}) collective-permute-start(bf16[80,256]{1,0:T(8,128)(2,1)} %get-tuple-element.32), channel_id=1, source_target_pairs={{0,2},{1,3},{2,0},{3,1},{4,6},{5,7},{6,4},{7,5},{8,10},{9,11},{10,... | collective-permute-start | bytes 122888 | tf_op jit(solution)/shard_map/ppermute | solution.py:219
  11.2 2.4 %collective-permute-start.5 = (bf16[80,256]{1,0:T(8,128)(2,1)}, bf16[80,256]{1,0:T(8,128)(2,1)S(1)}, u32[]{:S(2)}, u32[]{:S(2)}) collective-permute-start(bf16[80,256]{1,0:T(8,128)(2,1)} %get-tuple-element.33), channel_id=1, source_target_pairs={{0,3},{1,0},{2,1},{3,2},{4,7},{5,4},{6,5},{7,6},{8,11},{9,8},{10,9... | collective-permute-start | bytes 122888 | tf_op jit(solution)/shard_map/ppermute | solution.py:219
  13.6 0.0 copy-done.1
  13.6 0.0 collective-permute-start.2
  13.7 3.2 %collective-permute-start.1 = (bf16[32,4096]{1,0:T(8,128)(2,1)S(1)}, bf16[32,4096]{1,0:T(8,128)(2,1)S(1)}, u32[]{:S(2)}, u32[]{:S(2)}) collective-permute-start(bf16[32,4096]{1,0:T(8,128)(2,1)S(1)} %bitcast.19), channel_id=1, source_target_pairs={{0,2},{1,3},{2,0},{3,1},{4,6},{5,7},{6,4},{7,5},{8,10},{9,11},{10,... | collective-permute-start | bytes 786440 | tf_op jit(solution)/shard_map/ppermute | solution.py:219
  16.9 0.0 collective-permute-done.3.r1
  16.9 0.0 copy-start.4
  16.9 0.1 collective-permute-start
  17.0 0.0 collective-permute-done.4.r2
  17.0 0.0 copy-start.5
  17.0 0.0 collective-permute-done.5.r3
  17.0 0.0 copy-done.3
  17.0 0.0 copy-start.6
  17.0 0.9 shard_map.87
  17.9 0.0 copy-start.8
  17.9 6.9 %all-to-all-start = ((bf16[16,32,512]{2,1,0:T(8,128)(2,1)}), bf16[16,32,512]{2,1,0:T(8,128)(2,1)S(1)}, u32[]{:S(2)}, u32[]{:S(2)}) async-start(bf16[16,32,512]{2,1,0:T(8,128)(2,1)} %shard_map.87), calls=%async_computation | async-start | bytes 1048576 | tf_op jit(solution)/shard_map/all_to_all | solution.py:227
  24.8 0.0 copy-done
  24.8 0.0 copy-done.8
  24.9 0.5 shard_map.84
  25.4 12.3 %collective-permute-done.2.a3 = bf16[32,4096]{1,0:T(8,128)(2,1)S(1)} collective-permute-done((bf16[32,4096]{1,0:T(8,128)(2,1)S(1)}, bf16[32,4096]{1,0:T(8,128)(2,1)S(1)}, u32[]{:S(2)}, u32[]{:S(2)}) %collective-permute-start.2) | collective-permute-done | bytes 262176 | tf_op jit(solution)/shard_map/ppermute | solution.py:219
  37.6 0.0 collective-permute-done.1.a2
  37.6 0.0 collective-permute-done.a1
  37.6 0.6 shard_map.85
  38.2 0.0 all-to-all-done.feats
  38.2 0.0 copy-start.9
  38.2 1.3 %collective-permute-start.6 = (f32[16,128]{1,0:T(8,128)S(1)}, f32[16,128]{1,0:T(8,128)S(1)}, u32[]{:S(2)}, u32[]{:S(2)}) collective-permute-start(f32[16,128]{1,0:T(8,128)S(1)} %get-tuple-element.34), channel_id=1, source_target_pairs={{0,4},{4,0},{1,5},{5,1},{2,6},{6,2},{3,7},{7,3},{8,12},{12,8},{9,1... | collective-permute-start | bytes 24584 | tf_op jit(solution)/shard_map/ppermute | solution.py:223
  39.5 0.8 collective-permute-done.6
  40.4 0.7 broadcast_in_dim.18
  41.1 12.3 %all-to-all-start.1 = ((f32[32,16,128]{2,1,0:T(8,128)}), f32[32,16,128]{2,1,0:T(8,128)S(1)}, u32[]{:S(2)}, u32[]{:S(2)}) async-start(f32[32,16,128]{2,1,0:T(8,128)} %broadcast_in_dim.18), calls=%async_computation.1 | async-start | bytes 524288 | tf_op jit(solution)/shard_map/all_to_all | solution.py:227
  53.3 0.0 copy-done.4
  53.4 0.7 collective-permute-start.7
  54.1 0.0 copy-done.5
  54.1 0.1 collective-permute-start.8
  54.2 0.0 copy-done.6
  54.2 0.4 collective-permute-start.9
  54.6 0.4 collective-permute-done.7.c1
  54.9 0.0 copy-start.10
  54.9 0.3 collective-permute-done.8.c2
  55.3 0.2 collective-permute-done.9.c3
  55.5 0.0 copy-done.9
  55.5 0.1 copy-done.10
  55.6 0.4 copy-done.11
  55.9 0.6 copy-done.12
  56.5 2.2 %shard_map.88.inputs = bf16[16,32,256]{2,1,0:T(8,128)(2,1)} custom-call(bf16[128,4096]{1,0:T(8,128)(2,1)} %bitcast.32, bf16[16,32,512]{2,1,0:T(8,128)(2,1)} %copy-done.9, bf16[80,256]{1,0:T(8,128)(2,1)} %copy-done.4, bf16[80,256]{1,0:T(8,128)(2,1)} %copy-done.5, bf16[80,256]{1,0:T(8,128)(2,1)} %copy-done.6, bf16[80,256]{1,0:T(8,128)(2,1)} %copy-done.10, ...), custom_call_target="tpu_custom_call" | custom-call | flops 200000000 | bytes 2000000 | tf_op jit(solution)/shard_map/pallas_call | solution.py:51
  58.7 2.8 %all-to-all-done.1 = f32[32,16,128]{2,1,0:T(8,128)S(1)} async-done(((f32[32,16,128]{2,1,0:T(8,128)}), f32[32,16,128]{2,1,0:T(8,128)S(1)}, u32[]{:S(2)}, u32[]{:S(2)}) %all-to-all-start.1) | async-done | bytes 262176 | tf_op jit(solution)/shard_map/all_to_all | solution.py:227
  61.5 2.1 %collective-permute-start.10 = (f32[16,128]{1,0:T(8,128)S(1)}, f32[16,128]{1,0:T(8,128)S(1)}, u32[]{:S(2)}, u32[]{:S(2)}) collective-permute-start(f32[16,128]{1,0:T(8,128)S(1)} %reduce_sum.9.lown), channel_id=1, source_target_pairs={{0,4},{4,0},{1,5},{5,1},{2,6},{6,2},{3,7},{7,3},{8,12},{12,8},{9,1... | collective-permute-start | bytes 24584 | tf_op jit(solution)/shard_map/ppermute | solution.py:223
  63.6 0.8 collective-permute-done.10.loth
  64.4 3.8 %shard_map.89 = (f32[32,128]{1,0:T(8,128)}, f32[32,16,128]{2,1,0:T(8,128)S(1)}, f32[32,16,128]{2,1,0:T(8,128)S(1)}) custom-call(f32[16,128]{1,0:T(8,128)S(1)} %reduce_sum.9.lown, f32[16,128]{1,0:T(8,128)S(1)} %collective-permute-done.10.loth, bf16[32,4096]{1,0:T(8,128)(2,1)S(1)} %bitcast.22, bf16[32,4096]{1,0:T(8,128)(2,1)S(1)} %collective-permute-done.a1, ...), custom_call_target="tpu_custom_call" | custom-call | flops 100000000 | bytes 3000000 | tf_op jit(solution)/shard_map/pallas_call | solution.py:51
  68.2 0.3 collective-permute-start.11
  68.5 1.2 %collective-permute-done.11 = f32[32,16,128]{2,1,0:T(8,128)S(1)} collective-permute-done((f32[32,16,128]{2,1,0:T(8,128)S(1)}, f32[32,16,128]{2,1,0:T(8,128)S(1)}, u32[]{:S(2)}, u32[]{:S(2)}) %collective-permute-start.11) | collective-permute-done | bytes 262176 | tf_op jit(solution)/shard_map/ppermute | solution.py:223
  69.7 0.0 copy-start.2
  69.7 11.7 %all_to_all.20.pieces = f32[32,16,128]{2,1,0:T(8,128)S(1)} all-to-all(f32[32,16,128]{2,1,0:T(8,128)S(1)} %add.7), channel_id=1, replica_groups=mesh['x'=4,'zl'=2,'y'=4,'core'=2,'t'=4] {'x','zl','y'}, dimensions={0} | all-to-all | bytes 524288 | tf_op jit(solution)/shard_map/all_to_all | solution.py:227
  81.4 0.0 copy-done.2
  81.4 0.1 shard_map.90
  81.5 15.9 %all_to_all.21.mixed = bf16[32,96,128]{2,1,0:T(8,128)(2,1)S(1)} all-to-all(bf16[32,96,128]{2,1,0:T(8,128)(2,1)S(1)} %shard_map.90), channel_id=1, replica_groups=mesh['x'=4,'zl'=2,'y'=4,'core'=2,'t'=4] {'x','zl','y'}, dimensions={0} | all-to-all | bytes 1572864 | tf_op jit(solution)/shard_map/all_to_all | solution.py:227
  97.4 3.1 %collective-permute-start.12 = (bf16[32,32,128]{2,1,0:T(8,128)(2,1)S(1)}, bf16[32,32,128]{2,1,0:T(8,128)(2,1)S(1)}, u32[]{:S(2)}, u32[]{:S(2)}) collective-permute-start(bf16[32,32,128]{2,1,0:T(8,128)(2,1)S(1)} %slice.4), channel_id=1, source_target_pairs={{0,4},{4,0},{1,5},{5,1},{2,6},{6,2},{3,7},{7,3},{8,12},{12,8},{9,1... | collective-permute-start | bytes 786440 | tf_op jit(solution)/shard_map/ppermute | solution.py:223
  100.5 1.2 %collective-permute-done.12.roth = bf16[32,32,128]{2,1,0:T(8,128)(2,1)S(1)} collective-permute-done((bf16[32,32,128]{2,1,0:T(8,128)(2,1)S(1)}, bf16[32,32,128]{2,1,0:T(8,128)(2,1)S(1)}, u32[]{:S(2)}, u32[]{:S(2)}) %collective-permute-start.12) | collective-permute-done | bytes 262176 | tf_op jit(solution)/shard_map/ppermute | solution.py:223
  101.7 0.0 copy-done.7
  101.7 1.5 %shard_map.91 = (bf16[128,4096]{1,0:T(8,128)(2,1)}, bf16[32,4096]{1,0:T(8,128)(2,1)}, bf16[32,4096]{1,0:T(8,128)(2,1)}) custom-call(bf16[32,96,128]{2,1,0:T(8,128)(2,1)S(1)} %all_to_all.21.mixed, bf16[32,32,128]{2,1,0:T(8,128)(2,1)S(1)} %collective-permute-done.12.roth, f32[32,128]{1,0:T(8,128)S(1)} %copy-done.7, bf16[128,128]{1,0:T(8,128)(2,1)S(1)} %bitcast.28, ...), custom_call_target="tpu_custom_call" | custom-call | flops 300000000 | bytes 5000000 | tf_op jit(solution)/shard_map/pallas_call | solution.py:51
  (7 shorter events, 0.1 us)
Async XLA Ops:
  0.6 13.0 %copy-start.1 = (bf16[1,32,4096]{2,1,0:T(8,128)(2,1)S(1)}, bf16[1,32,4096]{2,1,0:T(8,128)(2,1)}, u32[]{:S(2)}) copy-start(bf16[1,32,4096]{2,1,0:T(8,128)(2,1)} %param.5) | copy-start | bytes 786436
  0.6 16.4 %copy-start.3 = (bf16[1,128,128]{2,1,0:T(8,128)(2,1)S(1)}, bf16[1,128,128]{2,1,0:T(8,128)(2,1)}, u32[]{:S(2)}) copy-start(bf16[1,128,128]{2,1,0:T(8,128)(2,1)} %param.6) | copy-start | bytes 98308
  2.2 22.6 %copy-start = (bf16[1,1,128,4096]{3,2,1,0:T(8,128)(2,1)S(1)}, bf16[1,1,128,4096]{3,2,1,0:T(8,128)(2,1)}, u32[]{:S(2)}) copy-start(bf16[1,1,128,4096]{3,2,1,0:T(8,128)(2,1)} %param.8) | copy-start | bytes 3145732
  2.2 14.7 %collective-permute-start.3 = (bf16[80,256]{1,0:T(8,128)(2,1)}, bf16[80,256]{1,0:T(8,128)(2,1)S(1)}, u32[]{:S(2)}, u32[]{:S(2)}) collective-permute-start(bf16[80,256]{1,0:T(8,128)(2,1)} %get-tuple-element.31), channel_id=1, source_target_pairs={{0,1},{1,2},{2,3},{3,0},{4,5},{5,6},{6,7},{7,4},{8,9},{9,10},{10,1... | collective-permute-start | bytes 122888 | tf_op jit(solution)/shard_map/ppermute | solution.py:219
  6.1 10.9 %collective-permute-start.4 = (bf16[80,256]{1,0:T(8,128)(2,1)}, bf16[80,256]{1,0:T(8,128)(2,1)S(1)}, u32[]{:S(2)}, u32[]{:S(2)}) collective-permute-start(bf16[80,256]{1,0:T(8,128)(2,1)} %get-tuple-element.32), channel_id=1, source_target_pairs={{0,2},{1,3},{2,0},{3,1},{4,6},{5,7},{6,4},{7,5},{8,10},{9,11},{10,... | collective-permute-start | bytes 122888 | tf_op jit(solution)/shard_map/ppermute | solution.py:219
  11.2 5.8 %collective-permute-start.5 = (bf16[80,256]{1,0:T(8,128)(2,1)}, bf16[80,256]{1,0:T(8,128)(2,1)S(1)}, u32[]{:S(2)}, u32[]{:S(2)}) collective-permute-start(bf16[80,256]{1,0:T(8,128)(2,1)} %get-tuple-element.33), channel_id=1, source_target_pairs={{0,3},{1,0},{2,1},{3,2},{4,7},{5,4},{6,5},{7,6},{8,11},{9,8},{10,9... | collective-permute-start | bytes 122888 | tf_op jit(solution)/shard_map/ppermute | solution.py:219
  13.6 24.0 %collective-permute-start.2 = (bf16[32,4096]{1,0:T(8,128)(2,1)S(1)}, bf16[32,4096]{1,0:T(8,128)(2,1)S(1)}, u32[]{:S(2)}, u32[]{:S(2)}) collective-permute-start(bf16[32,4096]{1,0:T(8,128)(2,1)S(1)} %bitcast.18), channel_id=1, source_target_pairs={{0,3},{1,0},{2,1},{3,2},{4,7},{5,4},{6,5},{7,6},{8,11},{9,8},{10,9... | collective-permute-start | bytes 786440 | tf_op jit(solution)/shard_map/ppermute | solution.py:219
  13.7 24.0 %collective-permute-start.1 = (bf16[32,4096]{1,0:T(8,128)(2,1)S(1)}, bf16[32,4096]{1,0:T(8,128)(2,1)S(1)}, u32[]{:S(2)}, u32[]{:S(2)}) collective-permute-start(bf16[32,4096]{1,0:T(8,128)(2,1)S(1)} %bitcast.19), channel_id=1, source_target_pairs={{0,2},{1,3},{2,0},{3,1},{4,6},{5,7},{6,4},{7,5},{8,10},{9,11},{10,... | collective-permute-start | bytes 786440 | tf_op jit(solution)/shard_map/ppermute | solution.py:219
  16.9 36.4 %copy-start.4 = (bf16[80,256]{1,0:T(8,128)(2,1)}, bf16[80,256]{1,0:T(8,128)(2,1)S(1)}, u32[]{:S(2)}) copy-start(bf16[80,256]{1,0:T(8,128)(2,1)S(1)} %collective-permute-done.3.r1) | copy-start | bytes 122884
  16.9 20.7 %collective-permute-start = (bf16[32,4096]{1,0:T(8,128)(2,1)S(1)}, bf16[32,4096]{1,0:T(8,128)(2,1)S(1)}, u32[]{:S(2)}, u32[]{:S(2)}) collective-permute-start(bf16[32,4096]{1,0:T(8,128)(2,1)S(1)} %bitcast.20), channel_id=1, source_target_pairs={{0,1},{1,2},{2,3},{3,0},{4,5},{5,6},{6,7},{7,4},{8,9},{9,10},{10,1... | collective-permute-start | bytes 786440 | tf_op jit(solution)/shard_map/ppermute | solution.py:219
  17.0 37.1 %copy-start.5 = (bf16[80,256]{1,0:T(8,128)(2,1)}, bf16[80,256]{1,0:T(8,128)(2,1)S(1)}, u32[]{:S(2)}) copy-start(bf16[80,256]{1,0:T(8,128)(2,1)S(1)} %collective-permute-done.4.r2) | copy-start | bytes 122884
  17.0 37.1 %copy-start.6 = (bf16[80,256]{1,0:T(8,128)(2,1)}, bf16[80,256]{1,0:T(8,128)(2,1)S(1)}, u32[]{:S(2)}) copy-start(bf16[80,256]{1,0:T(8,128)(2,1)S(1)} %collective-permute-done.5.r3) | copy-start | bytes 122884
  17.9 6.9 %copy-start.8 = (bf16[1,1,4096,32]{2,3,1,0:T(8,128)(2,1)S(1)}, bf16[1,1,4096,32]{2,3,1,0:T(8,128)(2,1)}, u32[]{:S(2)}) copy-start(bf16[1,1,4096,32]{2,3,1,0:T(8,128)(2,1)} %param.9) | copy-start | bytes 786436
  17.9 20.3 %all-to-all-start = ((bf16[16,32,512]{2,1,0:T(8,128)(2,1)}), bf16[16,32,512]{2,1,0:T(8,128)(2,1)S(1)}, u32[]{:S(2)}, u32[]{:S(2)}) async-start(bf16[16,32,512]{2,1,0:T(8,128)(2,1)} %shard_map.87), calls=%async_computation | async-start | bytes 1048576 | tf_op jit(solution)/shard_map/all_to_all | solution.py:227
  38.2 17.2 %copy-start.9 = (bf16[16,32,512]{2,1,0:T(8,128)(2,1)}, bf16[16,32,512]{2,1,0:T(8,128)(2,1)S(1)}, u32[]{:S(2)}) copy-start(bf16[16,32,512]{2,1,0:T(8,128)(2,1)S(1)} %all-to-all-done.feats) | copy-start | bytes 1572868
  38.2 2.1 %collective-permute-start.6 = (f32[16,128]{1,0:T(8,128)S(1)}, f32[16,128]{1,0:T(8,128)S(1)}, u32[]{:S(2)}, u32[]{:S(2)}) collective-permute-start(f32[16,128]{1,0:T(8,128)S(1)} %get-tuple-element.34), channel_id=1, source_target_pairs={{0,4},{4,0},{1,5},{5,1},{2,6},{6,2},{3,7},{7,3},{8,12},{12,8},{9,1... | collective-permute-start | bytes 24584 | tf_op jit(solution)/shard_map/ppermute | solution.py:223
  41.1 20.4 %all-to-all-start.1 = ((f32[32,16,128]{2,1,0:T(8,128)}), f32[32,16,128]{2,1,0:T(8,128)S(1)}, u32[]{:S(2)}, u32[]{:S(2)}) async-start(f32[32,16,128]{2,1,0:T(8,128)} %broadcast_in_dim.18), calls=%async_computation.1 | async-start | bytes 524288 | tf_op jit(solution)/shard_map/all_to_all | solution.py:227
  53.4 1.6 %collective-permute-start.7 = (bf16[80,256]{1,0:T(8,128)(2,1)S(1)}, bf16[80,256]{1,0:T(8,128)(2,1)S(1)}, u32[]{:S(2)}, u32[]{:S(2)}) collective-permute-start(bf16[80,256]{1,0:T(8,128)(2,1)S(1)} %collective-permute-done.3.r1), channel_id=1, source_target_pairs={{0,4},{4,0},{1,5},{5,1},{2,6},{6,2},{3,7},{7,3},{8,12},{12,8},{9,1... | collective-permute-start | bytes 122888 | tf_op jit(solution)/shard_map/ppermute | solution.py:223
  54.1 1.2 %collective-permute-start.8 = (bf16[80,256]{1,0:T(8,128)(2,1)S(1)}, bf16[80,256]{1,0:T(8,128)(2,1)S(1)}, u32[]{:S(2)}, u32[]{:S(2)}) collective-permute-start(bf16[80,256]{1,0:T(8,128)(2,1)S(1)} %collective-permute-done.4.r2), channel_id=1, source_target_pairs={{0,4},{4,0},{1,5},{5,1},{2,6},{6,2},{3,7},{7,3},{8,12},{12,8},{9,1... | collective-permute-start | bytes 122888 | tf_op jit(solution)/shard_map/ppermute | solution.py:223
  54.2 1.3 %collective-permute-start.9 = (bf16[80,256]{1,0:T(8,128)(2,1)S(1)}, bf16[80,256]{1,0:T(8,128)(2,1)S(1)}, u32[]{:S(2)}, u32[]{:S(2)}) collective-permute-start(bf16[80,256]{1,0:T(8,128)(2,1)S(1)} %collective-permute-done.5.r3), channel_id=1, source_target_pairs={{0,4},{4,0},{1,5},{5,1},{2,6},{6,2},{3,7},{7,3},{8,12},{12,8},{9,1... | collective-permute-start | bytes 122888 | tf_op jit(solution)/shard_map/ppermute | solution.py:223
  54.9 0.6 copy-start.10
  55.3 0.6 copy-start.11
  55.9 0.6 copy-start.12
  61.5 2.9 %collective-permute-start.10 = (f32[16,128]{1,0:T(8,128)S(1)}, f32[16,128]{1,0:T(8,128)S(1)}, u32[]{:S(2)}, u32[]{:S(2)}) collective-permute-start(f32[16,128]{1,0:T(8,128)S(1)} %reduce_sum.9.lown), channel_id=1, source_target_pairs={{0,4},{4,0},{1,5},{5,1},{2,6},{6,2},{3,7},{7,3},{8,12},{12,8},{9,1... | collective-permute-start | bytes 24584 | tf_op jit(solution)/shard_map/ppermute | solution.py:223
  68.2 1.5 %collective-permute-start.11 = (f32[32,16,128]{2,1,0:T(8,128)S(1)}, f32[32,16,128]{2,1,0:T(8,128)S(1)}, u32[]{:S(2)}, u32[]{:S(2)}) collective-permute-start(f32[32,16,128]{2,1,0:T(8,128)S(1)} %get-tuple-element.42), channel_id=1, source_target_pairs={{0,4},{4,0},{1,5},{5,1},{2,6},{6,2},{3,7},{7,3},{8,12},{12,8},{9,1... | collective-permute-start | bytes 786440 | tf_op jit(solution)/shard_map/ppermute | solution.py:223
  69.7 11.7 %copy-start.2 = (bf16[16,32,256]{2,1,0:T(8,128)(2,1)S(1)}, bf16[16,32,256]{2,1,0:T(8,128)(2,1)}, u32[]{:S(2)}) copy-start(bf16[16,32,256]{2,1,0:T(8,128)(2,1)} %shard_map.88.inputs) | copy-start | bytes 786436
  97.4 4.3 %copy-start.7 = (f32[32,128]{1,0:T(8,128)S(1)}, f32[32,128]{1,0:T(8,128)}, u32[]{:S(2)}) copy-start(f32[32,128]{1,0:T(8,128)} %get-tuple-element.44.qt) | copy-start | bytes 49156
  97.4 4.3 %collective-permute-start.12 = (bf16[32,32,128]{2,1,0:T(8,128)(2,1)S(1)}, bf16[32,32,128]{2,1,0:T(8,128)(2,1)S(1)}, u32[]{:S(2)}, u32[]{:S(2)}) collective-permute-start(bf16[32,32,128]{2,1,0:T(8,128)(2,1)S(1)} %slice.4), channel_id=1, source_target_pairs={{0,4},{4,0},{1,5},{5,1},{2,6},{6,2},{3,7},{7,3},{8,12},{12,8},{9,1... | collective-permute-start | bytes 786440 | tf_op jit(solution)/shard_map/ppermute | solution.py:223

commit v12 on v11

--- a/solution.py
+++ b/solution.py
@@ -250,16 +250,8 @@
         moved=10**8,
     )(act, ef, warm)
 
-    half = ((HALF, HEAD), F32)
-    left_keep, left_send = call(
-        left_kernel, [half, half], [pltpu.VMEM((RANK, HEAD), F32)], flops=5 * 10**7, moved=10**6
-    )(*acts[1:], og, lines, inner, fed)
-    left_send, feats = lax.optimization_barrier((left_send, feats))
-
-    left_half = left_keep + swapped(left_send)
-    left_half, got = lax.optimization_barrier((left_half, got))
+    got, inner = lax.optimization_barrier((got, inner))
     traded = [swapped(g) for g in got]
-    pieces = exchanged(jnp.broadcast_to(left_half[None], (N_CHIPS, HALF, HEAD)), CHIPS)
     (inputs,) = call(
         input_kernel,
         [((PLANE, OWN, CUT), BF16)],
@@ -275,7 +267,14 @@
         dest=pltpu.MemorySpace.HBM,
         room=60,
     )(weight, feats, *got, *traded)
-    pieces, inputs = lax.optimization_barrier((pieces, inputs))
+    lines, inputs = lax.optimization_barrier((lines, inputs))
+    half = ((HALF, HEAD), F32)
+    left_keep, left_send = call(
+        left_kernel, [half, half], [pltpu.VMEM((RANK, HEAD), F32)], flops=5 * 10**7, moved=10**6
+    )(*acts[1:], og, lines, inner, fed)
+
+    left_half = left_keep + swapped(left_send)
+    pieces = exchanged(jnp.broadcast_to(left_half[None], (N_CHIPS, HALF, HEAD)), CHIPS)
     left_own = jnp.sum(pieces, axis=0)
     left_other = swapped(left_own)
 

time: 104 us -> 102 us (0.981)
  blocking collectives: 27.6 us -> 44.9 us
  waiting for transfers between devices: 19.9 us -> 9.46 us
  starting transfers between devices: 42 us -> 34.8 us
    all_to_all x2 -> x3, blocking collectives: 27.6 us -> 44.9 us  [exchanged(): return lax.all_to_all(x, axes, 0, 0, tiled=True)]
    all_to_all x2 -> x1, starting transfers between devices: 19.2 us -> 6.92 us  [exchanged(): return lax.all_to_all(x, axes, 0, 0, tiled=True)]
    ppermute x6, waiting for transfers between devices: 12.3 us -> 0.88 us  [moved(): return lax.ppermute(x, axis, [(i, (i + k) % 4) for i in range(4)])]
    ppermute x7, starting transfers between devices: 8.02 us -> 13.1 us  [swapped(): return lax.ppermute(x, 'core', [(0, 1), (1, 0)])]
    all_to_all x2 -> x1, waiting for transfers between devices: 2.76 us -> 2.94 us  [exchanged(): return lax.all_to_all(x, axes, 0, 0, tiled=True)]
  transfers between devices with their start and end apart: 15 -> 14, of which waited for: 9 -> 8; matrix products, arithmetic and copies ran while one was open for 0% -> 0% of each run, Pallas kernels for 4% -> 3%
where the time goes in v12:
time: 102 us
  blocking collectives  44.9 us (44%)
  starting transfers between devices  34.8 us (34%)
  Pallas kernels  11.1 us (11%)
  waiting for transfers between devices  9.46 us (9%)
    all_to_all x3, blocking collectives, exchanged(): return lax.all_to_all(x, axes, 0, 0, tiled=True)  44.9 us
    ppermute x6, starting transfers between devices, moved(): return lax.ppermute(x, axis, [(i, (i + k) % 4) for i in range(4)])  14.8 us
    ppermute x7, starting transfers between devices, swapped(): return lax.ppermute(x, 'core', [(0, 1), (1, 0)])  13.1 us
    pallas_call x8, Pallas kernels, run(): pl.pallas_call(kernel, out_shape=[jax.ShapeDtypeStruct(s, d) for s, d in...  11.1 us
    all_to_all x1, starting transfers between devices, exchanged(): return lax.all_to_all(x, axes, 0, 0, tiled=True)  6.92 us
    ppermute x7, waiting for transfers between devices, swapped(): return lax.ppermute(x, 'core', [(0, 1), (1, 0)])  5.64 us
    all_to_all x1, waiting for transfers between devices, exchanged(): return lax.all_to_all(x, axes, 0, 0, tiled=True)  2.94 us
  transfers between devices with their start and end apart: 14, of which 8 were waited for; matrix products, arithmetic and copies ran while one was open for 0% of the time, Pallas kernels for 3%

profile of v12, /device:TPU:1, one launch (start us, length us, event | category | flops | bytes accessed | tf_op | source)
XLA Modules:
  0.0 102.0 jit_solution(12345300264600080122)
XLA Ops:
  0.6 0.0 copy-start.1
  0.6 0.0 copy-start.3
  0.7 1.6 %shard_map.85 = (bf16[80,256]{1,0:T(8,128)(2,1)}, bf16[80,256]{1,0:T(8,128)(2,1)}, bf16[80,256]{1,0:T(8,128)(2,1)}) custom-call(bf16[128,4096]{1,0:T(8,128)(2,1)} %bitcast.31, bf16[128,128]{1,0:T(8,128)(2,1)} %bitcast.24), custom_call_target="tpu_custom_call" | custom-call | flops 1000000 | bytes 1000000 | tf_op jit(solution)/shard_map/pallas_call | solution.py:51
  2.2 0.0 copy-start
  2.2 3.9 %collective-permute-start.3 = (bf16[80,256]{1,0:T(8,128)(2,1)}, bf16[80,256]{1,0:T(8,128)(2,1)S(1)}, u32[]{:S(2)}, u32[]{:S(2)}) collective-permute-start(bf16[80,256]{1,0:T(8,128)(2,1)} %get-tuple-element.25), channel_id=1, source_target_pairs={{0,1},{1,2},{2,3},{3,0},{4,5},{5,6},{6,7},{7,4},{8,9},{9,10},{10,1... | collective-permute-start | bytes 122888 | tf_op jit(solution)/shard_map/ppermute | solution.py:219
  6.1 5.1 %collective-permute-start.4 = (bf16[80,256]{1,0:T(8,128)(2,1)}, bf16[80,256]{1,0:T(8,128)(2,1)S(1)}, u32[]{:S(2)}, u32[]{:S(2)}) collective-permute-start(bf16[80,256]{1,0:T(8,128)(2,1)} %get-tuple-element.26), channel_id=1, source_target_pairs={{0,2},{1,3},{2,0},{3,1},{4,6},{5,7},{6,4},{7,5},{8,10},{9,11},{10,... | collective-permute-start | bytes 122888 | tf_op jit(solution)/shard_map/ppermute | solution.py:219
  11.2 2.4 %collective-permute-start.5 = (bf16[80,256]{1,0:T(8,128)(2,1)}, bf16[80,256]{1,0:T(8,128)(2,1)S(1)}, u32[]{:S(2)}, u32[]{:S(2)}) collective-permute-start(bf16[80,256]{1,0:T(8,128)(2,1)} %get-tuple-element.27), channel_id=1, source_target_pairs={{0,3},{1,0},{2,1},{3,2},{4,7},{5,4},{6,5},{7,6},{8,11},{9,8},{10,9... | collective-permute-start | bytes 122888 | tf_op jit(solution)/shard_map/ppermute | solution.py:219
  13.6 0.0 copy-done.1
  13.6 0.0 collective-permute-start.2
  13.7 3.2 %collective-permute-start.1 = (bf16[32,4096]{1,0:T(8,128)(2,1)S(1)}, bf16[32,4096]{1,0:T(8,128)(2,1)S(1)}, u32[]{:S(2)}, u32[]{:S(2)}) collective-permute-start(bf16[32,4096]{1,0:T(8,128)(2,1)S(1)} %bitcast.19), channel_id=1, source_target_pairs={{0,2},{1,3},{2,0},{3,1},{4,6},{5,7},{6,4},{7,5},{8,10},{9,11},{10,... | collective-permute-start | bytes 786440 | tf_op jit(solution)/shard_map/ppermute | solution.py:219
  16.9 0.0 collective-permute-done.3.r1
  16.9 0.1 collective-permute-start
  17.0 0.0 collective-permute-done.4.r2
  17.0 0.0 copy-start.5
  17.0 0.0 collective-permute-done.5.r3
  17.0 0.0 copy-done.3
  17.0 0.0 copy-start.6
  17.0 0.9 shard_map.86
  17.9 0.0 copy-start.8
  17.9 6.9 %all-to-all-start = ((bf16[16,32,512]{2,1,0:T(8,128)(2,1)}), bf16[16,32,512]{2,1,0:T(8,128)(2,1)S(1)}, u32[]{:S(2)}, u32[]{:S(2)}) async-start(bf16[16,32,512]{2,1,0:T(8,128)(2,1)} %shard_map.86), calls=%async_computation | async-start | bytes 1048576 | tf_op jit(solution)/shard_map/all_to_all | solution.py:227
  24.8 0.0 copy-done
  24.8 0.0 copy-done.8
  24.9 0.5 shard_map.84
  25.4 0.0 copy-done.4
  25.4 3.4 %collective-permute-start.6 = (bf16[80,256]{1,0:T(8,128)(2,1)S(1)}, bf16[80,256]{1,0:T(8,128)(2,1)S(1)}, u32[]{:S(2)}, u32[]{:S(2)}) collective-permute-start(bf16[80,256]{1,0:T(8,128)(2,1)S(1)} %collective-permute-done.3.r1), channel_id=1, source_target_pairs={{0,4},{4,0},{1,5},{5,1},{2,6},{6,2},{3,7},{7,3},{8,12},{12,8},{9,1... | collective-permute-start | bytes 122888 | tf_op jit(solution)/shard_map/ppermute | solution.py:223
  28.7 0.0 copy-done.5
  28.7 0.1 collective-permute-start.7
  28.9 0.8 collective-permute-done.6.c1
  29.6 0.0 copy-done.6
  29.6 0.0 copy-start.10
  29.6 0.3 collective-permute-start.8
  30.0 0.0 collective-permute-done.7.c2
  30.0 0.0 copy-start.11
  30.0 0.9 collective-permute-done.8.c3
  30.8 0.0 copy-start.12
  30.8 2.9 %all-to-all-done.feats = bf16[16,32,512]{2,1,0:T(8,128)(2,1)S(1)} async-done(((bf16[16,32,512]{2,1,0:T(8,128)(2,1)}), bf16[16,32,512]{2,1,0:T(8,128)(2,1)S(1)}, u32[]{:S(2)}, u32[]{:S(2)}) %all-to-all-start) | async-done | bytes 524320 | tf_op jit(solution)/shard_map/all_to_all | solution.py:227
  33.8 0.0 copy-done.10
  33.8 0.0 copy-done.11
  33.8 0.0 copy-done.12
  33.8 0.0 copy-start.9
  33.8 0.8 copy-done.9
  34.6 2.2 %shard_map.87.inputs = bf16[16,32,256]{2,1,0:T(8,128)(2,1)} custom-call(bf16[128,4096]{1,0:T(8,128)(2,1)} %bitcast.32, bf16[16,32,512]{2,1,0:T(8,128)(2,1)} %copy-done.9, bf16[80,256]{1,0:T(8,128)(2,1)} %copy-done.4, bf16[80,256]{1,0:T(8,128)(2,1)} %copy-done.5, bf16[80,256]{1,0:T(8,128)(2,1)} %copy-done.6, bf16[80,256]{1,0:T(8,128)(2,1)} %copy-done.10, ...), custom_call_target="tpu_custom_call" | custom-call | flops 200000000 | bytes 2000000 | tf_op jit(solution)/shard_map/pallas_call | solution.py:51
  36.8 0.9 collective-permute-done.2.a3
  37.6 0.0 collective-permute-done.1.a2
  37.6 0.0 collective-permute-done.a1
  37.6 0.6 shard_map.88
  38.2 3.6 %collective-permute-start.9 = (f32[16,128]{1,0:T(8,128)S(1)}, f32[16,128]{1,0:T(8,128)S(1)}, u32[]{:S(2)}, u32[]{:S(2)}) collective-permute-start(f32[16,128]{1,0:T(8,128)S(1)} %get-tuple-element.36), channel_id=1, source_target_pairs={{0,4},{4,0},{1,5},{5,1},{2,6},{6,2},{3,7},{7,3},{8,12},{12,8},{9,1... | collective-permute-start | bytes 24584 | tf_op jit(solution)/shard_map/ppermute | solution.py:223
  41.8 0.8 collective-permute-done.9
  42.7 17.8 %all_to_all.20 = f32[32,16,128]{2,1,0:T(8,128)S(1)} all-to-all(f32[32,16,128]{2,1,0:T(8,128)S(1)} %broadcast_in_dim.18), channel_id=1, replica_groups=mesh['x'=4,'zl'=2,'y'=4,'core'=2,'t'=4] {'x','zl','y'}, dimensions={0} | all-to-all | bytes 524288 | tf_op jit(solution)/shard_map/all_to_all | solution.py:227
  60.5 2.1 %collective-permute-start.10 = (f32[16,128]{1,0:T(8,128)S(1)}, f32[16,128]{1,0:T(8,128)S(1)}, u32[]{:S(2)}, u32[]{:S(2)}) collective-permute-start(f32[16,128]{1,0:T(8,128)S(1)} %reduce_sum.9.lown), channel_id=1, source_target_pairs={{0,4},{4,0},{1,5},{5,1},{2,6},{6,2},{3,7},{7,3},{8,12},{12,8},{9,1... | collective-permute-start | bytes 24584 | tf_op jit(solution)/shard_map/ppermute | solution.py:223
  62.6 0.8 collective-permute-done.10.loth
  63.4 3.8 %shard_map.89 = (f32[32,128]{1,0:T(8,128)}, f32[32,16,128]{2,1,0:T(8,128)S(1)}, f32[32,16,128]{2,1,0:T(8,128)S(1)}) custom-call(f32[16,128]{1,0:T(8,128)S(1)} %reduce_sum.9.lown, f32[16,128]{1,0:T(8,128)S(1)} %collective-permute-done.10.loth, bf16[32,4096]{1,0:T(8,128)(2,1)S(1)} %bitcast.22, bf16[32,4096]{1,0:T(8,128)(2,1)S(1)} %collective-permute-done.a1, ...), custom_call_target="tpu_custom_call" | custom-call | flops 100000000 | bytes 3000000 | tf_op jit(solution)/shard_map/pallas_call | solution.py:51
  67.2 0.3 collective-permute-start.11
  67.5 1.2 %collective-permute-done.11 = f32[32,16,128]{2,1,0:T(8,128)S(1)} collective-permute-done((f32[32,16,128]{2,1,0:T(8,128)S(1)}, f32[32,16,128]{2,1,0:T(8,128)S(1)}, u32[]{:S(2)}, u32[]{:S(2)}) %collective-permute-start.11) | collective-permute-done | bytes 262176 | tf_op jit(solution)/shard_map/ppermute | solution.py:223
  68.7 0.0 copy-start.2
  68.7 11.6 %all_to_all.21.pieces = f32[32,16,128]{2,1,0:T(8,128)S(1)} all-to-all(f32[32,16,128]{2,1,0:T(8,128)S(1)} %add.7), channel_id=1, replica_groups=mesh['x'=4,'zl'=2,'y'=4,'core'=2,'t'=4] {'x','zl','y'}, dimensions={0} | all-to-all | bytes 524288 | tf_op jit(solution)/shard_map/all_to_all | solution.py:227
  80.3 0.0 copy-done.2
  80.3 0.1 shard_map.90
  80.4 15.5 %all_to_all.22.mixed = bf16[32,96,128]{2,1,0:T(8,128)(2,1)S(1)} all-to-all(bf16[32,96,128]{2,1,0:T(8,128)(2,1)S(1)} %shard_map.90), channel_id=1, replica_groups=mesh['x'=4,'zl'=2,'y'=4,'core'=2,'t'=4] {'x','zl','y'}, dimensions={0} | all-to-all | bytes 1572864 | tf_op jit(solution)/shard_map/all_to_all | solution.py:227
  95.9 0.0 copy-start.7
  96.0 3.3 %collective-permute-start.12 = (bf16[32,32,128]{2,1,0:T(8,128)(2,1)S(1)}, bf16[32,32,128]{2,1,0:T(8,128)(2,1)S(1)}, u32[]{:S(2)}, u32[]{:S(2)}) collective-permute-start(bf16[32,32,128]{2,1,0:T(8,128)(2,1)S(1)} %slice.4), channel_id=1, source_target_pairs={{0,4},{4,0},{1,5},{5,1},{2,6},{6,2},{3,7},{7,3},{8,12},{12,8},{9,1... | collective-permute-start | bytes 786440 | tf_op jit(solution)/shard_map/ppermute | solution.py:223
  99.2 1.2 %collective-permute-done.12.roth = bf16[32,32,128]{2,1,0:T(8,128)(2,1)S(1)} collective-permute-done((bf16[32,32,128]{2,1,0:T(8,128)(2,1)S(1)}, bf16[32,32,128]{2,1,0:T(8,128)(2,1)S(1)}, u32[]{:S(2)}, u32[]{:S(2)}) %collective-permute-start.12) | collective-permute-done | bytes 262176 | tf_op jit(solution)/shard_map/ppermute | solution.py:223
  100.4 0.0 copy-done.7
  100.4 1.6 %shard_map.91 = (bf16[128,4096]{1,0:T(8,128)(2,1)}, bf16[32,4096]{1,0:T(8,128)(2,1)}, bf16[32,4096]{1,0:T(8,128)(2,1)}) custom-call(bf16[32,96,128]{2,1,0:T(8,128)(2,1)S(1)} %all_to_all.22.mixed, bf16[32,32,128]{2,1,0:T(8,128)(2,1)S(1)} %collective-permute-done.12.roth, f32[32,128]{1,0:T(8,128)S(1)} %copy-done.7, bf16[128,128]{1,0:T(8,128)(2,1)S(1)} %bitcast.28, ...), custom_call_target="tpu_custom_call" | custom-call | flops 300000000 | bytes 5000000 | tf_op jit(solution)/shard_map/pallas_call | solution.py:51
  (6 shorter events, 0.1 us)
Async XLA Ops:
  0.6 13.0 %copy-start.1 = (bf16[1,32,4096]{2,1,0:T(8,128)(2,1)S(1)}, bf16[1,32,4096]{2,1,0:T(8,128)(2,1)}, u32[]{:S(2)}) copy-start(bf16[1,32,4096]{2,1,0:T(8,128)(2,1)} %param.5) | copy-start | bytes 786436
  0.6 16.4 %copy-start.3 = (bf16[1,128,128]{2,1,0:T(8,128)(2,1)S(1)}, bf16[1,128,128]{2,1,0:T(8,128)(2,1)}, u32[]{:S(2)}) copy-start(bf16[1,128,128]{2,1,0:T(8,128)(2,1)} %param.6) | copy-start | bytes 98308
  2.2 22.6 %copy-start = (bf16[1,1,128,4096]{3,2,1,0:T(8,128)(2,1)S(1)}, bf16[1,1,128,4096]{3,2,1,0:T(8,128)(2,1)}, u32[]{:S(2)}) copy-start(bf16[1,1,128,4096]{3,2,1,0:T(8,128)(2,1)} %param.8) | copy-start | bytes 3145732
  2.2 14.7 %collective-permute-start.3 = (bf16[80,256]{1,0:T(8,128)(2,1)}, bf16[80,256]{1,0:T(8,128)(2,1)S(1)}, u32[]{:S(2)}, u32[]{:S(2)}) collective-permute-start(bf16[80,256]{1,0:T(8,128)(2,1)} %get-tuple-element.25), channel_id=1, source_target_pairs={{0,1},{1,2},{2,3},{3,0},{4,5},{5,6},{6,7},{7,4},{8,9},{9,10},{10,1... | collective-permute-start | bytes 122888 | tf_op jit(solution)/shard_map/ppermute | solution.py:219
  6.1 10.9 %collective-permute-start.4 = (bf16[80,256]{1,0:T(8,128)(2,1)}, bf16[80,256]{1,0:T(8,128)(2,1)S(1)}, u32[]{:S(2)}, u32[]{:S(2)}) collective-permute-start(bf16[80,256]{1,0:T(8,128)(2,1)} %get-tuple-element.26), channel_id=1, source_target_pairs={{0,2},{1,3},{2,0},{3,1},{4,6},{5,7},{6,4},{7,5},{8,10},{9,11},{10,... | collective-permute-start | bytes 122888 | tf_op jit(solution)/shard_map/ppermute | solution.py:219
  11.2 5.8 %collective-permute-start.5 = (bf16[80,256]{1,0:T(8,128)(2,1)}, bf16[80,256]{1,0:T(8,128)(2,1)S(1)}, u32[]{:S(2)}, u32[]{:S(2)}) collective-permute-start(bf16[80,256]{1,0:T(8,128)(2,1)} %get-tuple-element.27), channel_id=1, source_target_pairs={{0,3},{1,0},{2,1},{3,2},{4,7},{5,4},{6,5},{7,6},{8,11},{9,8},{10,9... | collective-permute-start | bytes 122888 | tf_op jit(solution)/shard_map/ppermute | solution.py:219
  13.6 24.0 %collective-permute-start.2 = (bf16[32,4096]{1,0:T(8,128)(2,1)S(1)}, bf16[32,4096]{1,0:T(8,128)(2,1)S(1)}, u32[]{:S(2)}, u32[]{:S(2)}) collective-permute-start(bf16[32,4096]{1,0:T(8,128)(2,1)S(1)} %bitcast.18), channel_id=1, source_target_pairs={{0,3},{1,0},{2,1},{3,2},{4,7},{5,4},{6,5},{7,6},{8,11},{9,8},{10,9... | collective-permute-start | bytes 786440 | tf_op jit(solution)/shard_map/ppermute | solution.py:219
  13.7 24.0 %collective-permute-start.1 = (bf16[32,4096]{1,0:T(8,128)(2,1)S(1)}, bf16[32,4096]{1,0:T(8,128)(2,1)S(1)}, u32[]{:S(2)}, u32[]{:S(2)}) collective-permute-start(bf16[32,4096]{1,0:T(8,128)(2,1)S(1)} %bitcast.19), channel_id=1, source_target_pairs={{0,2},{1,3},{2,0},{3,1},{4,6},{5,7},{6,4},{7,5},{8,10},{9,11},{10,... | collective-permute-start | bytes 786440 | tf_op jit(solution)/shard_map/ppermute | solution.py:219
  16.9 8.4 %copy-start.4 = (bf16[80,256]{1,0:T(8,128)(2,1)}, bf16[80,256]{1,0:T(8,128)(2,1)S(1)}, u32[]{:S(2)}) copy-start(bf16[80,256]{1,0:T(8,128)(2,1)S(1)} %collective-permute-done.3.r1) | copy-start | bytes 122884
  16.9 20.7 %collective-permute-start = (bf16[32,4096]{1,0:T(8,128)(2,1)S(1)}, bf16[32,4096]{1,0:T(8,128)(2,1)S(1)}, u32[]{:S(2)}, u32[]{:S(2)}) collective-permute-start(bf16[32,4096]{1,0:T(8,128)(2,1)S(1)} %bitcast.20), channel_id=1, source_target_pairs={{0,1},{1,2},{2,3},{3,0},{4,5},{5,6},{6,7},{7,4},{8,9},{9,10},{10,1... | collective-permute-start | bytes 786440 | tf_op jit(solution)/shard_map/ppermute | solution.py:219
  17.0 11.7 %copy-start.5 = (bf16[80,256]{1,0:T(8,128)(2,1)}, bf16[80,256]{1,0:T(8,128)(2,1)S(1)}, u32[]{:S(2)}) copy-start(bf16[80,256]{1,0:T(8,128)(2,1)S(1)} %collective-permute-done.4.r2) | copy-start | bytes 122884
  17.0 12.6 %copy-start.6 = (bf16[80,256]{1,0:T(8,128)(2,1)}, bf16[80,256]{1,0:T(8,128)(2,1)S(1)}, u32[]{:S(2)}) copy-start(bf16[80,256]{1,0:T(8,128)(2,1)S(1)} %collective-permute-done.5.r3) | copy-start | bytes 122884
  17.9 6.9 %copy-start.8 = (bf16[1,1,4096,32]{2,3,1,0:T(8,128)(2,1)S(1)}, bf16[1,1,4096,32]{2,3,1,0:T(8,128)(2,1)}, u32[]{:S(2)}) copy-start(bf16[1,1,4096,32]{2,3,1,0:T(8,128)(2,1)} %param.9) | copy-start | bytes 786436
  17.9 15.9 %all-to-all-start = ((bf16[16,32,512]{2,1,0:T(8,128)(2,1)}), bf16[16,32,512]{2,1,0:T(8,128)(2,1)S(1)}, u32[]{:S(2)}, u32[]{:S(2)}) async-start(bf16[16,32,512]{2,1,0:T(8,128)(2,1)} %shard_map.86), calls=%async_computation | async-start | bytes 1048576 | tf_op jit(solution)/shard_map/all_to_all | solution.py:227
  25.4 4.3 %collective-permute-start.6 = (bf16[80,256]{1,0:T(8,128)(2,1)S(1)}, bf16[80,256]{1,0:T(8,128)(2,1)S(1)}, u32[]{:S(2)}, u32[]{:S(2)}) collective-permute-start(bf16[80,256]{1,0:T(8,128)(2,1)S(1)} %collective-permute-done.3.r1), channel_id=1, source_target_pairs={{0,4},{4,0},{1,5},{5,1},{2,6},{6,2},{3,7},{7,3},{8,12},{12,8},{9,1... | collective-permute-start | bytes 122888 | tf_op jit(solution)/shard_map/ppermute | solution.py:223
  28.7 1.2 %collective-permute-start.7 = (bf16[80,256]{1,0:T(8,128)(2,1)S(1)}, bf16[80,256]{1,0:T(8,128)(2,1)S(1)}, u32[]{:S(2)}, u32[]{:S(2)}) collective-permute-start(bf16[80,256]{1,0:T(8,128)(2,1)S(1)} %collective-permute-done.4.r2), channel_id=1, source_target_pairs={{0,4},{4,0},{1,5},{5,1},{2,6},{6,2},{3,7},{7,3},{8,12},{12,8},{9,1... | collective-permute-start | bytes 122888 | tf_op jit(solution)/shard_map/ppermute | solution.py:223
  29.6 4.2 %copy-start.10 = (bf16[80,256]{1,0:T(8,128)(2,1)}, bf16[80,256]{1,0:T(8,128)(2,1)S(1)}, u32[]{:S(2)}) copy-start(bf16[80,256]{1,0:T(8,128)(2,1)S(1)} %collective-permute-done.6.c1) | copy-start | bytes 122884
  29.6 1.2 %collective-permute-start.8 = (bf16[80,256]{1,0:T(8,128)(2,1)S(1)}, bf16[80,256]{1,0:T(8,128)(2,1)S(1)}, u32[]{:S(2)}, u32[]{:S(2)}) collective-permute-start(bf16[80,256]{1,0:T(8,128)(2,1)S(1)} %collective-permute-done.5.r3), channel_id=1, source_target_pairs={{0,4},{4,0},{1,5},{5,1},{2,6},{6,2},{3,7},{7,3},{8,12},{12,8},{9,1... | collective-permute-start | bytes 122888 | tf_op jit(solution)/shard_map/ppermute | solution.py:223
  30.0 3.8 %copy-start.11 = (bf16[80,256]{1,0:T(8,128)(2,1)}, bf16[80,256]{1,0:T(8,128)(2,1)S(1)}, u32[]{:S(2)}) copy-start(bf16[80,256]{1,0:T(8,128)(2,1)S(1)} %collective-permute-done.7.c2) | copy-start | bytes 122884
  30.8 3.0 %copy-start.12 = (bf16[80,256]{1,0:T(8,128)(2,1)}, bf16[80,256]{1,0:T(8,128)(2,1)S(1)}, u32[]{:S(2)}) copy-start(bf16[80,256]{1,0:T(8,128)(2,1)S(1)} %collective-permute-done.8.c3) | copy-start | bytes 122884
  33.8 0.8 copy-start.9
  38.2 4.4 %collective-permute-start.9 = (f32[16,128]{1,0:T(8,128)S(1)}, f32[16,128]{1,0:T(8,128)S(1)}, u32[]{:S(2)}, u32[]{:S(2)}) collective-permute-start(f32[16,128]{1,0:T(8,128)S(1)} %get-tuple-element.36), channel_id=1, source_target_pairs={{0,4},{4,0},{1,5},{5,1},{2,6},{6,2},{3,7},{7,3},{8,12},{12,8},{9,1... | collective-permute-start | bytes 24584 | tf_op jit(solution)/shard_map/ppermute | solution.py:223
  60.5 2.9 %collective-permute-start.10 = (f32[16,128]{1,0:T(8,128)S(1)}, f32[16,128]{1,0:T(8,128)S(1)}, u32[]{:S(2)}, u32[]{:S(2)}) collective-permute-start(f32[16,128]{1,0:T(8,128)S(1)} %reduce_sum.9.lown), channel_id=1, source_target_pairs={{0,4},{4,0},{1,5},{5,1},{2,6},{6,2},{3,7},{7,3},{8,12},{12,8},{9,1... | collective-permute-start | bytes 24584 | tf_op jit(solution)/shard_map/ppermute | solution.py:223
  67.2 1.5 %collective-permute-start.11 = (f32[32,16,128]{2,1,0:T(8,128)S(1)}, f32[32,16,128]{2,1,0:T(8,128)S(1)}, u32[]{:S(2)}, u32[]{:S(2)}) collective-permute-start(f32[32,16,128]{2,1,0:T(8,128)S(1)} %get-tuple-element.38), channel_id=1, source_target_pairs={{0,4},{4,0},{1,5},{5,1},{2,6},{6,2},{3,7},{7,3},{8,12},{12,8},{9,1... | collective-permute-start | bytes 786440 | tf_op jit(solution)/shard_map/ppermute | solution.py:223
  68.7 11.6 %copy-start.2 = (bf16[16,32,256]{2,1,0:T(8,128)(2,1)S(1)}, bf16[16,32,256]{2,1,0:T(8,128)(2,1)}, u32[]{:S(2)}) copy-start(bf16[16,32,256]{2,1,0:T(8,128)(2,1)} %shard_map.87.inputs) | copy-start | bytes 786436
  95.9 4.5 %copy-start.7 = (f32[32,128]{1,0:T(8,128)S(1)}, f32[32,128]{1,0:T(8,128)}, u32[]{:S(2)}) copy-start(f32[32,128]{1,0:T(8,128)} %get-tuple-element.40.qt) | copy-start | bytes 49156
  96.0 4.4 %collective-permute-start.12 = (bf16[32,32,128]{2,1,0:T(8,128)(2,1)S(1)}, bf16[32,32,128]{2,1,0:T(8,128)(2,1)S(1)}, u32[]{:S(2)}, u32[]{:S(2)}) collective-permute-start(bf16[32,32,128]{2,1,0:T(8,128)(2,1)S(1)} %slice.4), channel_id=1, source_target_pairs={{0,4},{4,0},{1,5},{5,1},{2,6},{6,2},{3,7},{7,3},{8,12},{12,8},{9,1... | collective-permute-start | bytes 786440 | tf_op jit(solution)/shard_map/ppermute | solution.py:223

commit v13 on v12

--- a/solution.py
+++ b/solution.py
@@ -126,12 +126,19 @@
     left = held[...]
     gram = lax.dot_general(left, left, NT, precision=HIGH, preferred_element_type=F32)
     row = lax.broadcasted_iota(jnp.int32, (RANK, 1), 0)
-    for k in range(RANK - 1):
+    for k in range(0, RANK, 2):
+        first_g, first_l = gram[k : k + 1, :], left[k : k + 1, :]
+        corner = gram[k : k + 1, k + 1 : k + 2]
         scale = 1.0 / gram[k : k + 1, k : k + 1]
-        factor = jnp.where(row > k, gram[:, k : k + 1] * scale, 0.0)
-        pivot_g, pivot_l = gram[k : k + 1, :], left[k : k + 1, :]
-        gram = gram - factor * pivot_g
-        left = left - factor * pivot_l
+        ratio = corner * scale
+        pivot = 1.0 / (gram[k + 1 : k + 2, k + 1 : k + 2] - ratio * corner)
+        column = gram[:, k : k + 1]
+        one = jnp.where(row > k, column * scale, 0.0)
+        two = jnp.where(row > k + 1, (gram[:, k + 1 : k + 2] - column * ratio) * pivot, 0.0)
+        second_g = gram[k + 1 : k + 2, :] - ratio * first_g
+        second_l = left[k + 1 : k + 2, :] - ratio * first_l
+        gram = gram - one * first_g - two * second_g
+        left = left - one * first_l - two * second_l
     eye = row == lax.broadcasted_iota(jnp.int32, (RANK, RANK), 1)
     diagonal = jnp.sum(jnp.where(eye, gram, 0.0), axis=1, keepdims=True)
     basis = left * (1.0 / jnp.sqrt(diagonal))

time: 102 us -> 104 us (1.020)
  Pallas kernels: 11.1 us -> 13 us
    pallas_call x8, Pallas kernels: 11.1 us -> 13 us  [run(): pl.pallas_call(kernel, out_shape=[jax.ShapeDtypeStruct(s, d) for s, d in...]
where the time goes in v13:
time: 104 us
  blocking collectives  44.8 us (43%)
  starting transfers between devices  34.8 us (33%)
  Pallas kernels  13 us (12%)
  waiting for transfers between devices  9.46 us (9%)
    all_to_all x3, blocking collectives, exchanged(): return lax.all_to_all(x, axes, 0, 0, tiled=True)  44.8 us
    ppermute x6, starting transfers between devices, moved(): return lax.ppermute(x, axis, [(i, (i + k) % 4) for i in range(4)])  14.8 us
    ppermute x7, starting transfers between devices, swapped(): return lax.ppermute(x, 'core', [(0, 1), (1, 0)])  13.2 us
    pallas_call x8, Pallas kernels, run(): pl.pallas_call(kernel, out_shape=[jax.ShapeDtypeStruct(s, d) for s, d in...  13 us
    all_to_all x1, starting transfers between devices, exchanged(): return lax.all_to_all(x, axes, 0, 0, tiled=True)  6.92 us
    ppermute x7, waiting for transfers between devices, swapped(): return lax.ppermute(x, 'core', [(0, 1), (1, 0)])  5.64 us
    all_to_all x1, waiting for transfers between devices, exchanged(): return lax.all_to_all(x, axes, 0, 0, tiled=True)  2.94 us
  transfers between devices with their start and end apart: 14, of which 8 were waited for; matrix products, arithmetic and copies ran while one was open for 0% of the time, Pallas kernels for 3%

profile of v13, /device:TPU:1, one launch (start us, length us, event | category | flops | bytes accessed | tf_op | source)
XLA Modules:
  0.0 103.8 jit_solution(5026728975130412855)
XLA Ops:
  0.6 0.0 copy-start.1
  0.6 0.0 copy-start.3
  0.7 1.6 %shard_map.85 = (bf16[80,256]{1,0:T(8,128)(2,1)}, bf16[80,256]{1,0:T(8,128)(2,1)}, bf16[80,256]{1,0:T(8,128)(2,1)}) custom-call(bf16[128,4096]{1,0:T(8,128)(2,1)} %bitcast.31, bf16[128,128]{1,0:T(8,128)(2,1)} %bitcast.24), custom_call_target="tpu_custom_call" | custom-call | flops 1000000 | bytes 1000000 | tf_op jit(solution)/shard_map/pallas_call | solution.py:51
  2.2 0.0 copy-start
  2.2 3.9 %collective-permute-start.3 = (bf16[80,256]{1,0:T(8,128)(2,1)}, bf16[80,256]{1,0:T(8,128)(2,1)S(1)}, u32[]{:S(2)}, u32[]{:S(2)}) collective-permute-start(bf16[80,256]{1,0:T(8,128)(2,1)} %get-tuple-element.25), channel_id=1, source_target_pairs={{0,1},{1,2},{2,3},{3,0},{4,5},{5,6},{6,7},{7,4},{8,9},{9,10},{10,1... | collective-permute-start | bytes 122888 | tf_op jit(solution)/shard_map/ppermute | solution.py:226
  6.1 5.1 %collective-permute-start.4 = (bf16[80,256]{1,0:T(8,128)(2,1)}, bf16[80,256]{1,0:T(8,128)(2,1)S(1)}, u32[]{:S(2)}, u32[]{:S(2)}) collective-permute-start(bf16[80,256]{1,0:T(8,128)(2,1)} %get-tuple-element.26), channel_id=1, source_target_pairs={{0,2},{1,3},{2,0},{3,1},{4,6},{5,7},{6,4},{7,5},{8,10},{9,11},{10,... | collective-permute-start | bytes 122888 | tf_op jit(solution)/shard_map/ppermute | solution.py:226
  11.2 2.4 %collective-permute-start.5 = (bf16[80,256]{1,0:T(8,128)(2,1)}, bf16[80,256]{1,0:T(8,128)(2,1)S(1)}, u32[]{:S(2)}, u32[]{:S(2)}) collective-permute-start(bf16[80,256]{1,0:T(8,128)(2,1)} %get-tuple-element.27), channel_id=1, source_target_pairs={{0,3},{1,0},{2,1},{3,2},{4,7},{5,4},{6,5},{7,6},{8,11},{9,8},{10,9... | collective-permute-start | bytes 122888 | tf_op jit(solution)/shard_map/ppermute | solution.py:226
  13.6 0.0 copy-done.1
  13.6 0.0 collective-permute-start.2
  13.7 3.2 %collective-permute-start.1 = (bf16[32,4096]{1,0:T(8,128)(2,1)S(1)}, bf16[32,4096]{1,0:T(8,128)(2,1)S(1)}, u32[]{:S(2)}, u32[]{:S(2)}) collective-permute-start(bf16[32,4096]{1,0:T(8,128)(2,1)S(1)} %bitcast.19), channel_id=1, source_target_pairs={{0,2},{1,3},{2,0},{3,1},{4,6},{5,7},{6,4},{7,5},{8,10},{9,11},{10,... | collective-permute-start | bytes 786440 | tf_op jit(solution)/shard_map/ppermute | solution.py:226
  16.9 0.0 collective-permute-done.3.r1
  16.9 0.0 copy-start.4
  16.9 0.1 collective-permute-start
  17.0 0.0 collective-permute-done.4.r2
  17.0 0.0 copy-start.5
  17.0 0.0 collective-permute-done.5.r3
  17.0 0.0 copy-done.3
  17.0 0.0 copy-start.6
  17.0 0.9 shard_map.86
  17.9 0.0 copy-start.8
  17.9 6.9 %all-to-all-start = ((bf16[16,32,512]{2,1,0:T(8,128)(2,1)}), bf16[16,32,512]{2,1,0:T(8,128)(2,1)S(1)}, u32[]{:S(2)}, u32[]{:S(2)}) async-start(bf16[16,32,512]{2,1,0:T(8,128)(2,1)} %shard_map.86), calls=%async_computation | async-start | bytes 1048576 | tf_op jit(solution)/shard_map/all_to_all | solution.py:234
  24.8 0.0 copy-done
  24.8 0.0 copy-done.8
  24.9 0.5 shard_map.84
  25.4 0.0 copy-done.4
  25.4 3.4 %collective-permute-start.6 = (bf16[80,256]{1,0:T(8,128)(2,1)S(1)}, bf16[80,256]{1,0:T(8,128)(2,1)S(1)}, u32[]{:S(2)}, u32[]{:S(2)}) collective-permute-start(bf16[80,256]{1,0:T(8,128)(2,1)S(1)} %collective-permute-done.3.r1), channel_id=1, source_target_pairs={{0,4},{4,0},{1,5},{5,1},{2,6},{6,2},{3,7},{7,3},{8,12},{12,8},{9,1... | collective-permute-start | bytes 122888 | tf_op jit(solution)/shard_map/ppermute | solution.py:230
  28.7 0.0 copy-done.5
  28.7 0.1 collective-permute-start.7
  28.9 0.8 collective-permute-done.6.c1
  29.6 0.0 copy-done.6
  29.6 0.0 copy-start.10
  29.6 0.3 collective-permute-start.8
  30.0 0.0 collective-permute-done.7.c2
  30.0 0.0 copy-start.11
  30.0 0.9 collective-permute-done.8.c3
  30.8 0.0 copy-start.12
  30.8 2.9 %all-to-all-done.feats = bf16[16,32,512]{2,1,0:T(8,128)(2,1)S(1)} async-done(((bf16[16,32,512]{2,1,0:T(8,128)(2,1)}), bf16[16,32,512]{2,1,0:T(8,128)(2,1)S(1)}, u32[]{:S(2)}, u32[]{:S(2)}) %all-to-all-start) | async-done | bytes 524320 | tf_op jit(solution)/shard_map/all_to_all | solution.py:234
  33.8 0.0 copy-done.10
  33.8 0.0 copy-done.11
  33.8 0.0 copy-done.12
  33.8 0.0 copy-start.9
  33.8 0.8 copy-done.9
  34.6 2.2 %shard_map.87.inputs = bf16[16,32,256]{2,1,0:T(8,128)(2,1)} custom-call(bf16[128,4096]{1,0:T(8,128)(2,1)} %bitcast.32, bf16[16,32,512]{2,1,0:T(8,128)(2,1)} %copy-done.9, bf16[80,256]{1,0:T(8,128)(2,1)} %copy-done.4, bf16[80,256]{1,0:T(8,128)(2,1)} %copy-done.5, bf16[80,256]{1,0:T(8,128)(2,1)} %copy-done.6, bf16[80,256]{1,0:T(8,128)(2,1)} %copy-done.10, ...), custom_call_target="tpu_custom_call" | custom-call | flops 200000000 | bytes 2000000 | tf_op jit(solution)/shard_map/pallas_call | solution.py:51
  36.8 0.9 collective-permute-done.2.a3
  37.6 0.0 collective-permute-done.1.a2
  37.6 0.0 collective-permute-done.a1
  37.6 0.6 shard_map.88
  38.2 3.6 %collective-permute-start.9 = (f32[16,128]{1,0:T(8,128)S(1)}, f32[16,128]{1,0:T(8,128)S(1)}, u32[]{:S(2)}, u32[]{:S(2)}) collective-permute-start(f32[16,128]{1,0:T(8,128)S(1)} %get-tuple-element.36), channel_id=1, source_target_pairs={{0,4},{4,0},{1,5},{5,1},{2,6},{6,2},{3,7},{7,3},{8,12},{12,8},{9,1... | collective-permute-start | bytes 24584 | tf_op jit(solution)/shard_map/ppermute | solution.py:230
  41.8 0.8 collective-permute-done.9
  42.7 17.8 %all_to_all.20 = f32[32,16,128]{2,1,0:T(8,128)S(1)} all-to-all(f32[32,16,128]{2,1,0:T(8,128)S(1)} %broadcast_in_dim.18), channel_id=1, replica_groups=mesh['x'=4,'zl'=2,'y'=4,'core'=2,'t'=4] {'x','zl','y'}, dimensions={0} | all-to-all | bytes 524288 | tf_op jit(solution)/shard_map/all_to_all | solution.py:234
  60.5 2.1 %collective-permute-start.10 = (f32[16,128]{1,0:T(8,128)S(1)}, f32[16,128]{1,0:T(8,128)S(1)}, u32[]{:S(2)}, u32[]{:S(2)}) collective-permute-start(f32[16,128]{1,0:T(8,128)S(1)} %reduce_sum.9.lown), channel_id=1, source_target_pairs={{0,4},{4,0},{1,5},{5,1},{2,6},{6,2},{3,7},{7,3},{8,12},{12,8},{9,1... | collective-permute-start | bytes 24584 | tf_op jit(solution)/shard_map/ppermute | solution.py:230
  62.6 0.8 collective-permute-done.10.loth
  63.4 5.7 %shard_map.89 = (f32[32,128]{1,0:T(8,128)}, f32[32,16,128]{2,1,0:T(8,128)S(1)}, f32[32,16,128]{2,1,0:T(8,128)S(1)}) custom-call(f32[16,128]{1,0:T(8,128)S(1)} %reduce_sum.9.lown, f32[16,128]{1,0:T(8,128)S(1)} %collective-permute-done.10.loth, bf16[32,4096]{1,0:T(8,128)(2,1)S(1)} %bitcast.22, bf16[32,4096]{1,0:T(8,128)(2,1)S(1)} %collective-permute-done.a1, ...), custom_call_target="tpu_custom_call" | custom-call | flops 100000000 | bytes 3000000 | tf_op jit(solution)/shard_map/pallas_call | solution.py:51
  69.1 0.3 collective-permute-start.11
  69.4 1.2 %collective-permute-done.11 = f32[32,16,128]{2,1,0:T(8,128)S(1)} collective-permute-done((f32[32,16,128]{2,1,0:T(8,128)S(1)}, f32[32,16,128]{2,1,0:T(8,128)S(1)}, u32[]{:S(2)}, u32[]{:S(2)}) %collective-permute-start.11) | collective-permute-done | bytes 262176 | tf_op jit(solution)/shard_map/ppermute | solution.py:230
  70.6 0.0 copy-start.2
  70.6 11.6 %all_to_all.21.pieces = f32[32,16,128]{2,1,0:T(8,128)S(1)} all-to-all(f32[32,16,128]{2,1,0:T(8,128)S(1)} %add.7), channel_id=1, replica_groups=mesh['x'=4,'zl'=2,'y'=4,'core'=2,'t'=4] {'x','zl','y'}, dimensions={0} | all-to-all | bytes 524288 | tf_op jit(solution)/shard_map/all_to_all | solution.py:234
  82.2 0.0 copy-done.2
  82.2 0.1 shard_map.90
  82.3 15.5 %all_to_all.22.mixed = bf16[32,96,128]{2,1,0:T(8,128)(2,1)S(1)} all-to-all(bf16[32,96,128]{2,1,0:T(8,128)(2,1)S(1)} %shard_map.90), channel_id=1, replica_groups=mesh['x'=4,'zl'=2,'y'=4,'core'=2,'t'=4] {'x','zl','y'}, dimensions={0} | all-to-all | bytes 1572864 | tf_op jit(solution)/shard_map/all_to_all | solution.py:234
  97.8 3.3 %collective-permute-start.12 = (bf16[32,32,128]{2,1,0:T(8,128)(2,1)S(1)}, bf16[32,32,128]{2,1,0:T(8,128)(2,1)S(1)}, u32[]{:S(2)}, u32[]{:S(2)}) collective-permute-start(bf16[32,32,128]{2,1,0:T(8,128)(2,1)S(1)} %slice.4), channel_id=1, source_target_pairs={{0,4},{4,0},{1,5},{5,1},{2,6},{6,2},{3,7},{7,3},{8,12},{12,8},{9,1... | collective-permute-start | bytes 786440 | tf_op jit(solution)/shard_map/ppermute | solution.py:230
  101.1 1.2 %collective-permute-done.12.roth = bf16[32,32,128]{2,1,0:T(8,128)(2,1)S(1)} collective-permute-done((bf16[32,32,128]{2,1,0:T(8,128)(2,1)S(1)}, bf16[32,32,128]{2,1,0:T(8,128)(2,1)S(1)}, u32[]{:S(2)}, u32[]{:S(2)}) %collective-permute-start.12) | collective-permute-done | bytes 262176 | tf_op jit(solution)/shard_map/ppermute | solution.py:230
  102.3 0.0 copy-done.7
  102.3 1.5 %shard_map.91 = (bf16[128,4096]{1,0:T(8,128)(2,1)}, bf16[32,4096]{1,0:T(8,128)(2,1)}, bf16[32,4096]{1,0:T(8,128)(2,1)}) custom-call(bf16[32,96,128]{2,1,0:T(8,128)(2,1)S(1)} %all_to_all.22.mixed, bf16[32,32,128]{2,1,0:T(8,128)(2,1)S(1)} %collective-permute-done.12.roth, f32[32,128]{1,0:T(8,128)S(1)} %copy-done.7, bf16[128,128]{1,0:T(8,128)(2,1)S(1)} %bitcast.28, ...), custom_call_target="tpu_custom_call" | custom-call | flops 300000000 | bytes 5000000 | tf_op jit(solution)/shard_map/pallas_call | solution.py:51
  (6 shorter events, 0.1 us)
Async XLA Ops:
  0.6 13.0 %copy-start.1 = (bf16[1,32,4096]{2,1,0:T(8,128)(2,1)S(1)}, bf16[1,32,4096]{2,1,0:T(8,128)(2,1)}, u32[]{:S(2)}) copy-start(bf16[1,32,4096]{2,1,0:T(8,128)(2,1)} %param.5) | copy-start | bytes 786436
  0.6 16.4 %copy-start.3 = (bf16[1,128,128]{2,1,0:T(8,128)(2,1)S(1)}, bf16[1,128,128]{2,1,0:T(8,128)(2,1)}, u32[]{:S(2)}) copy-start(bf16[1,128,128]{2,1,0:T(8,128)(2,1)} %param.6) | copy-start | bytes 98308
  2.2 22.6 %copy-start = (bf16[1,1,128,4096]{3,2,1,0:T(8,128)(2,1)S(1)}, bf16[1,1,128,4096]{3,2,1,0:T(8,128)(2,1)}, u32[]{:S(2)}) copy-start(bf16[1,1,128,4096]{3,2,1,0:T(8,128)(2,1)} %param.8) | copy-start | bytes 3145732
  2.2 14.7 %collective-permute-start.3 = (bf16[80,256]{1,0:T(8,128)(2,1)}, bf16[80,256]{1,0:T(8,128)(2,1)S(1)}, u32[]{:S(2)}, u32[]{:S(2)}) collective-permute-start(bf16[80,256]{1,0:T(8,128)(2,1)} %get-tuple-element.25), channel_id=1, source_target_pairs={{0,1},{1,2},{2,3},{3,0},{4,5},{5,6},{6,7},{7,4},{8,9},{9,10},{10,1... | collective-permute-start | bytes 122888 | tf_op jit(solution)/shard_map/ppermute | solution.py:226
  6.1 10.9 %collective-permute-start.4 = (bf16[80,256]{1,0:T(8,128)(2,1)}, bf16[80,256]{1,0:T(8,128)(2,1)S(1)}, u32[]{:S(2)}, u32[]{:S(2)}) collective-permute-start(bf16[80,256]{1,0:T(8,128)(2,1)} %get-tuple-element.26), channel_id=1, source_target_pairs={{0,2},{1,3},{2,0},{3,1},{4,6},{5,7},{6,4},{7,5},{8,10},{9,11},{10,... | collective-permute-start | bytes 122888 | tf_op jit(solution)/shard_map/ppermute | solution.py:226
  11.2 5.8 %collective-permute-start.5 = (bf16[80,256]{1,0:T(8,128)(2,1)}, bf16[80,256]{1,0:T(8,128)(2,1)S(1)}, u32[]{:S(2)}, u32[]{:S(2)}) collective-permute-start(bf16[80,256]{1,0:T(8,128)(2,1)} %get-tuple-element.27), channel_id=1, source_target_pairs={{0,3},{1,0},{2,1},{3,2},{4,7},{5,4},{6,5},{7,6},{8,11},{9,8},{10,9... | collective-permute-start | bytes 122888 | tf_op jit(solution)/shard_map/ppermute | solution.py:226
  13.6 24.0 %collective-permute-start.2 = (bf16[32,4096]{1,0:T(8,128)(2,1)S(1)}, bf16[32,4096]{1,0:T(8,128)(2,1)S(1)}, u32[]{:S(2)}, u32[]{:S(2)}) collective-permute-start(bf16[32,4096]{1,0:T(8,128)(2,1)S(1)} %bitcast.18), channel_id=1, source_target_pairs={{0,3},{1,0},{2,1},{3,2},{4,7},{5,4},{6,5},{7,6},{8,11},{9,8},{10,9... | collective-permute-start | bytes 786440 | tf_op jit(solution)/shard_map/ppermute | solution.py:226
  13.7 24.0 %collective-permute-start.1 = (bf16[32,4096]{1,0:T(8,128)(2,1)S(1)}, bf16[32,4096]{1,0:T(8,128)(2,1)S(1)}, u32[]{:S(2)}, u32[]{:S(2)}) collective-permute-start(bf16[32,4096]{1,0:T(8,128)(2,1)S(1)} %bitcast.19), channel_id=1, source_target_pairs={{0,2},{1,3},{2,0},{3,1},{4,6},{5,7},{6,4},{7,5},{8,10},{9,11},{10,... | collective-permute-start | bytes 786440 | tf_op jit(solution)/shard_map/ppermute | solution.py:226
  16.9 8.4 %copy-start.4 = (bf16[80,256]{1,0:T(8,128)(2,1)}, bf16[80,256]{1,0:T(8,128)(2,1)S(1)}, u32[]{:S(2)}) copy-start(bf16[80,256]{1,0:T(8,128)(2,1)S(1)} %collective-permute-done.3.r1) | copy-start | bytes 122884
  16.9 20.7 %collective-permute-start = (bf16[32,4096]{1,0:T(8,128)(2,1)S(1)}, bf16[32,4096]{1,0:T(8,128)(2,1)S(1)}, u32[]{:S(2)}, u32[]{:S(2)}) collective-permute-start(bf16[32,4096]{1,0:T(8,128)(2,1)S(1)} %bitcast.20), channel_id=1, source_target_pairs={{0,1},{1,2},{2,3},{3,0},{4,5},{5,6},{6,7},{7,4},{8,9},{9,10},{10,1... | collective-permute-start | bytes 786440 | tf_op jit(solution)/shard_map/ppermute | solution.py:226
  17.0 11.7 %copy-start.5 = (bf16[80,256]{1,0:T(8,128)(2,1)}, bf16[80,256]{1,0:T(8,128)(2,1)S(1)}, u32[]{:S(2)}) copy-start(bf16[80,256]{1,0:T(8,128)(2,1)S(1)} %collective-permute-done.4.r2) | copy-start | bytes 122884
  17.0 12.6 %copy-start.6 = (bf16[80,256]{1,0:T(8,128)(2,1)}, bf16[80,256]{1,0:T(8,128)(2,1)S(1)}, u32[]{:S(2)}) copy-start(bf16[80,256]{1,0:T(8,128)(2,1)S(1)} %collective-permute-done.5.r3) | copy-start | bytes 122884
  17.9 6.9 %copy-start.8 = (bf16[1,1,4096,32]{2,3,1,0:T(8,128)(2,1)S(1)}, bf16[1,1,4096,32]{2,3,1,0:T(8,128)(2,1)}, u32[]{:S(2)}) copy-start(bf16[1,1,4096,32]{2,3,1,0:T(8,128)(2,1)} %param.9) | copy-start | bytes 786436
  17.9 15.9 %all-to-all-start = ((bf16[16,32,512]{2,1,0:T(8,128)(2,1)}), bf16[16,32,512]{2,1,0:T(8,128)(2,1)S(1)}, u32[]{:S(2)}, u32[]{:S(2)}) async-start(bf16[16,32,512]{2,1,0:T(8,128)(2,1)} %shard_map.86), calls=%async_computation | async-start | bytes 1048576 | tf_op jit(solution)/shard_map/all_to_all | solution.py:234
  25.4 4.3 %collective-permute-start.6 = (bf16[80,256]{1,0:T(8,128)(2,1)S(1)}, bf16[80,256]{1,0:T(8,128)(2,1)S(1)}, u32[]{:S(2)}, u32[]{:S(2)}) collective-permute-start(bf16[80,256]{1,0:T(8,128)(2,1)S(1)} %collective-permute-done.3.r1), channel_id=1, source_target_pairs={{0,4},{4,0},{1,5},{5,1},{2,6},{6,2},{3,7},{7,3},{8,12},{12,8},{9,1... | collective-permute-start | bytes 122888 | tf_op jit(solution)/shard_map/ppermute | solution.py:230
  28.7 1.2 %collective-permute-start.7 = (bf16[80,256]{1,0:T(8,128)(2,1)S(1)}, bf16[80,256]{1,0:T(8,128)(2,1)S(1)}, u32[]{:S(2)}, u32[]{:S(2)}) collective-permute-start(bf16[80,256]{1,0:T(8,128)(2,1)S(1)} %collective-permute-done.4.r2), channel_id=1, source_target_pairs={{0,4},{4,0},{1,5},{5,1},{2,6},{6,2},{3,7},{7,3},{8,12},{12,8},{9,1... | collective-permute-start | bytes 122888 | tf_op jit(solution)/shard_map/ppermute | solution.py:230
  29.6 4.2 %copy-start.10 = (bf16[80,256]{1,0:T(8,128)(2,1)}, bf16[80,256]{1,0:T(8,128)(2,1)S(1)}, u32[]{:S(2)}) copy-start(bf16[80,256]{1,0:T(8,128)(2,1)S(1)} %collective-permute-done.6.c1) | copy-start | bytes 122884
  29.6 1.2 %collective-permute-start.8 = (bf16[80,256]{1,0:T(8,128)(2,1)S(1)}, bf16[80,256]{1,0:T(8,128)(2,1)S(1)}, u32[]{:S(2)}, u32[]{:S(2)}) collective-permute-start(bf16[80,256]{1,0:T(8,128)(2,1)S(1)} %collective-permute-done.5.r3), channel_id=1, source_target_pairs={{0,4},{4,0},{1,5},{5,1},{2,6},{6,2},{3,7},{7,3},{8,12},{12,8},{9,1... | collective-permute-start | bytes 122888 | tf_op jit(solution)/shard_map/ppermute | solution.py:230
  30.0 3.8 %copy-start.11 = (bf16[80,256]{1,0:T(8,128)(2,1)}, bf16[80,256]{1,0:T(8,128)(2,1)S(1)}, u32[]{:S(2)}) copy-start(bf16[80,256]{1,0:T(8,128)(2,1)S(1)} %collective-permute-done.7.c2) | copy-start | bytes 122884
  30.8 3.0 %copy-start.12 = (bf16[80,256]{1,0:T(8,128)(2,1)}, bf16[80,256]{1,0:T(8,128)(2,1)S(1)}, u32[]{:S(2)}) copy-start(bf16[80,256]{1,0:T(8,128)(2,1)S(1)} %collective-permute-done.8.c3) | copy-start | bytes 122884
  33.8 0.8 copy-start.9
  38.2 4.4 %collective-permute-start.9 = (f32[16,128]{1,0:T(8,128)S(1)}, f32[16,128]{1,0:T(8,128)S(1)}, u32[]{:S(2)}, u32[]{:S(2)}) collective-permute-start(f32[16,128]{1,0:T(8,128)S(1)} %get-tuple-element.36), channel_id=1, source_target_pairs={{0,4},{4,0},{1,5},{5,1},{2,6},{6,2},{3,7},{7,3},{8,12},{12,8},{9,1... | collective-permute-start | bytes 24584 | tf_op jit(solution)/shard_map/ppermute | solution.py:230
  60.5 2.9 %collective-permute-start.10 = (f32[16,128]{1,0:T(8,128)S(1)}, f32[16,128]{1,0:T(8,128)S(1)}, u32[]{:S(2)}, u32[]{:S(2)}) collective-permute-start(f32[16,128]{1,0:T(8,128)S(1)} %reduce_sum.9.lown), channel_id=1, source_target_pairs={{0,4},{4,0},{1,5},{5,1},{2,6},{6,2},{3,7},{7,3},{8,12},{12,8},{9,1... | collective-permute-start | bytes 24584 | tf_op jit(solution)/shard_map/ppermute | solution.py:230
  69.1 1.5 %collective-permute-start.11 = (f32[32,16,128]{2,1,0:T(8,128)S(1)}, f32[32,16,128]{2,1,0:T(8,128)S(1)}, u32[]{:S(2)}, u32[]{:S(2)}) collective-permute-start(f32[32,16,128]{2,1,0:T(8,128)S(1)} %get-tuple-element.38), channel_id=1, source_target_pairs={{0,4},{4,0},{1,5},{5,1},{2,6},{6,2},{3,7},{7,3},{8,12},{12,8},{9,1... | collective-permute-start | bytes 786440 | tf_op jit(solution)/shard_map/ppermute | solution.py:230
  70.6 11.6 %copy-start.2 = (bf16[16,32,256]{2,1,0:T(8,128)(2,1)S(1)}, bf16[16,32,256]{2,1,0:T(8,128)(2,1)}, u32[]{:S(2)}) copy-start(bf16[16,32,256]{2,1,0:T(8,128)(2,1)} %shard_map.87.inputs) | copy-start | bytes 786436
  97.8 4.5 %copy-start.7 = (f32[32,128]{1,0:T(8,128)S(1)}, f32[32,128]{1,0:T(8,128)}, u32[]{:S(2)}) copy-start(f32[32,128]{1,0:T(8,128)} %get-tuple-element.40.qt) | copy-start | bytes 49156
  97.8 4.4 %collective-permute-start.12 = (bf16[32,32,128]{2,1,0:T(8,128)(2,1)S(1)}, bf16[32,32,128]{2,1,0:T(8,128)(2,1)S(1)}, u32[]{:S(2)}, u32[]{:S(2)}) collective-permute-start(bf16[32,32,128]{2,1,0:T(8,128)(2,1)S(1)} %slice.4), channel_id=1, source_target_pairs={{0,4},{4,0},{1,5},{5,1},{2,6},{6,2},{3,7},{7,3},{8,12},{12,8},{9,1... | collective-permute-start | bytes 786440 | tf_op jit(solution)/shard_map/ppermute | solution.py:230

commit v14 on v12

--- a/solution.py
+++ b/solution.py
@@ -128,7 +128,7 @@
     row = lax.broadcasted_iota(jnp.int32, (RANK, 1), 0)
     for k in range(RANK - 1):
         scale = 1.0 / gram[k : k + 1, k : k + 1]
-        factor = jnp.where(row > k, gram[:, k : k + 1] * scale, 0.0)
+        factor = jnp.where(row > k, gram[:, k : k + 1], 0.0) * scale
         pivot_g, pivot_l = gram[k : k + 1, :], left[k : k + 1, :]
         gram = gram - factor * pivot_g
         left = left - factor * pivot_l

time: 102 us -> 102 us (level)
  no operation moved by 1% of the time
where the time goes in v14:
time: 102 us
  blocking collectives  44.9 us (44%)
  starting transfers between devices  34.8 us (34%)
  Pallas kernels  11.1 us (11%)
  waiting for transfers between devices  9.46 us (9%)
    all_to_all x3, blocking collectives, exchanged(): return lax.all_to_all(x, axes, 0, 0, tiled=True)  44.9 us
    ppermute x6, starting transfers between devices, moved(): return lax.ppermute(x, axis, [(i, (i + k) % 4) for i in range(4)])  14.8 us
    ppermute x7, starting transfers between devices, swapped(): return lax.ppermute(x, 'core', [(0, 1), (1, 0)])  13.1 us
    pallas_call x8, Pallas kernels, run(): pl.pallas_call(kernel, out_shape=[jax.ShapeDtypeStruct(s, d) for s, d in...  11.1 us
    all_to_all x1, starting transfers between devices, exchanged(): return lax.all_to_all(x, axes, 0, 0, tiled=True)  6.92 us
    ppermute x7, waiting for transfers between devices, swapped(): return lax.ppermute(x, 'core', [(0, 1), (1, 0)])  5.64 us
    all_to_all x1, waiting for transfers between devices, exchanged(): return lax.all_to_all(x, axes, 0, 0, tiled=True)  2.94 us
  transfers between devices with their start and end apart: 14, of which 8 were waited for; matrix products, arithmetic and copies ran while one was open for 0% of the time, Pallas kernels for 3%

profile of v14, /device:TPU:1, one launch (start us, length us, event | category | flops | bytes accessed | tf_op | source)
XLA Modules:
  0.0 102.0 jit_solution(3881699864305927366)
XLA Ops:
  0.6 0.0 copy-start.1
  0.6 0.0 copy-start.3
  0.7 1.6 %shard_map.85 = (bf16[80,256]{1,0:T(8,128)(2,1)}, bf16[80,256]{1,0:T(8,128)(2,1)}, bf16[80,256]{1,0:T(8,128)(2,1)}) custom-call(bf16[128,4096]{1,0:T(8,128)(2,1)} %bitcast.31, bf16[128,128]{1,0:T(8,128)(2,1)} %bitcast.24), custom_call_target="tpu_custom_call" | custom-call | flops 1000000 | bytes 1000000 | tf_op jit(solution)/shard_map/pallas_call | solution.py:51
  2.2 0.0 copy-start
  2.2 3.9 %collective-permute-start.3 = (bf16[80,256]{1,0:T(8,128)(2,1)}, bf16[80,256]{1,0:T(8,128)(2,1)S(1)}, u32[]{:S(2)}, u32[]{:S(2)}) collective-permute-start(bf16[80,256]{1,0:T(8,128)(2,1)} %get-tuple-element.25), channel_id=1, source_target_pairs={{0,1},{1,2},{2,3},{3,0},{4,5},{5,6},{6,7},{7,4},{8,9},{9,10},{10,1... | collective-permute-start | bytes 122888 | tf_op jit(solution)/shard_map/ppermute | solution.py:219
  6.1 5.1 %collective-permute-start.4 = (bf16[80,256]{1,0:T(8,128)(2,1)}, bf16[80,256]{1,0:T(8,128)(2,1)S(1)}, u32[]{:S(2)}, u32[]{:S(2)}) collective-permute-start(bf16[80,256]{1,0:T(8,128)(2,1)} %get-tuple-element.26), channel_id=1, source_target_pairs={{0,2},{1,3},{2,0},{3,1},{4,6},{5,7},{6,4},{7,5},{8,10},{9,11},{10,... | collective-permute-start | bytes 122888 | tf_op jit(solution)/shard_map/ppermute | solution.py:219
  11.2 2.4 %collective-permute-start.5 = (bf16[80,256]{1,0:T(8,128)(2,1)}, bf16[80,256]{1,0:T(8,128)(2,1)S(1)}, u32[]{:S(2)}, u32[]{:S(2)}) collective-permute-start(bf16[80,256]{1,0:T(8,128)(2,1)} %get-tuple-element.27), channel_id=1, source_target_pairs={{0,3},{1,0},{2,1},{3,2},{4,7},{5,4},{6,5},{7,6},{8,11},{9,8},{10,9... | collective-permute-start | bytes 122888 | tf_op jit(solution)/shard_map/ppermute | solution.py:219
  13.6 0.0 copy-done.1
  13.6 0.0 collective-permute-start.2
  13.7 3.2 %collective-permute-start.1 = (bf16[32,4096]{1,0:T(8,128)(2,1)S(1)}, bf16[32,4096]{1,0:T(8,128)(2,1)S(1)}, u32[]{:S(2)}, u32[]{:S(2)}) collective-permute-start(bf16[32,4096]{1,0:T(8,128)(2,1)S(1)} %bitcast.19), channel_id=1, source_target_pairs={{0,2},{1,3},{2,0},{3,1},{4,6},{5,7},{6,4},{7,5},{8,10},{9,11},{10,... | collective-permute-start | bytes 786440 | tf_op jit(solution)/shard_map/ppermute | solution.py:219
  16.9 0.0 collective-permute-done.3.r1
  16.9 0.0 copy-start.4
  16.9 0.1 collective-permute-start
  17.0 0.0 collective-permute-done.4.r2
  17.0 0.0 copy-start.5
  17.0 0.0 collective-permute-done.5.r3
  17.0 0.0 copy-done.3
  17.0 0.0 copy-start.6
  17.0 0.9 shard_map.86
  17.9 0.0 copy-start.8
  17.9 6.9 %all-to-all-start = ((bf16[16,32,512]{2,1,0:T(8,128)(2,1)}), bf16[16,32,512]{2,1,0:T(8,128)(2,1)S(1)}, u32[]{:S(2)}, u32[]{:S(2)}) async-start(bf16[16,32,512]{2,1,0:T(8,128)(2,1)} %shard_map.86), calls=%async_computation | async-start | bytes 1048576 | tf_op jit(solution)/shard_map/all_to_all | solution.py:227
  24.8 0.0 copy-done
  24.8 0.0 copy-done.8
  24.9 0.5 shard_map.84
  25.4 0.0 copy-done.4
  25.4 3.4 %collective-permute-start.6 = (bf16[80,256]{1,0:T(8,128)(2,1)S(1)}, bf16[80,256]{1,0:T(8,128)(2,1)S(1)}, u32[]{:S(2)}, u32[]{:S(2)}) collective-permute-start(bf16[80,256]{1,0:T(8,128)(2,1)S(1)} %collective-permute-done.3.r1), channel_id=1, source_target_pairs={{0,4},{4,0},{1,5},{5,1},{2,6},{6,2},{3,7},{7,3},{8,12},{12,8},{9,1... | collective-permute-start | bytes 122888 | tf_op jit(solution)/shard_map/ppermute | solution.py:223
  28.7 0.0 copy-done.5
  28.7 0.1 collective-permute-start.7
  28.9 0.8 collective-permute-done.6.c1
  29.6 0.0 copy-done.6
  29.6 0.0 copy-start.10
  29.6 0.3 collective-permute-start.8
  30.0 0.0 collective-permute-done.7.c2
  30.0 0.0 copy-start.11
  30.0 0.9 collective-permute-done.8.c3
  30.8 0.0 copy-start.12
  30.8 2.9 %all-to-all-done.feats = bf16[16,32,512]{2,1,0:T(8,128)(2,1)S(1)} async-done(((bf16[16,32,512]{2,1,0:T(8,128)(2,1)}), bf16[16,32,512]{2,1,0:T(8,128)(2,1)S(1)}, u32[]{:S(2)}, u32[]{:S(2)}) %all-to-all-start) | async-done | bytes 524320 | tf_op jit(solution)/shard_map/all_to_all | solution.py:227
  33.8 0.0 copy-done.10
  33.8 0.0 copy-done.11
  33.8 0.0 copy-done.12
  33.8 0.0 copy-start.9
  33.8 0.8 copy-done.9
  34.6 2.2 %shard_map.87.inputs = bf16[16,32,256]{2,1,0:T(8,128)(2,1)} custom-call(bf16[128,4096]{1,0:T(8,128)(2,1)} %bitcast.32, bf16[16,32,512]{2,1,0:T(8,128)(2,1)} %copy-done.9, bf16[80,256]{1,0:T(8,128)(2,1)} %copy-done.4, bf16[80,256]{1,0:T(8,128)(2,1)} %copy-done.5, bf16[80,256]{1,0:T(8,128)(2,1)} %copy-done.6, bf16[80,256]{1,0:T(8,128)(2,1)} %copy-done.10, ...), custom_call_target="tpu_custom_call" | custom-call | flops 200000000 | bytes 2000000 | tf_op jit(solution)/shard_map/pallas_call | solution.py:51
  36.8 0.9 collective-permute-done.2.a3
  37.6 0.0 collective-permute-done.1.a2
  37.6 0.0 collective-permute-done.a1
  37.6 0.6 shard_map.88
  38.2 3.6 %collective-permute-start.9 = (f32[16,128]{1,0:T(8,128)S(1)}, f32[16,128]{1,0:T(8,128)S(1)}, u32[]{:S(2)}, u32[]{:S(2)}) collective-permute-start(f32[16,128]{1,0:T(8,128)S(1)} %get-tuple-element.36), channel_id=1, source_target_pairs={{0,4},{4,0},{1,5},{5,1},{2,6},{6,2},{3,7},{7,3},{8,12},{12,8},{9,1... | collective-permute-start | bytes 24584 | tf_op jit(solution)/shard_map/ppermute | solution.py:223
  41.8 0.8 collective-permute-done.9
  42.7 17.8 %all_to_all.20 = f32[32,16,128]{2,1,0:T(8,128)S(1)} all-to-all(f32[32,16,128]{2,1,0:T(8,128)S(1)} %broadcast_in_dim.18), channel_id=1, replica_groups=mesh['x'=4,'zl'=2,'y'=4,'core'=2,'t'=4] {'x','zl','y'}, dimensions={0} | all-to-all | bytes 524288 | tf_op jit(solution)/shard_map/all_to_all | solution.py:227
  60.5 2.1 %collective-permute-start.10 = (f32[16,128]{1,0:T(8,128)S(1)}, f32[16,128]{1,0:T(8,128)S(1)}, u32[]{:S(2)}, u32[]{:S(2)}) collective-permute-start(f32[16,128]{1,0:T(8,128)S(1)} %reduce_sum.9.lown), channel_id=1, source_target_pairs={{0,4},{4,0},{1,5},{5,1},{2,6},{6,2},{3,7},{7,3},{8,12},{12,8},{9,1... | collective-permute-start | bytes 24584 | tf_op jit(solution)/shard_map/ppermute | solution.py:223
  62.6 0.8 collective-permute-done.10.loth
  63.4 3.8 %shard_map.89 = (f32[32,128]{1,0:T(8,128)}, f32[32,16,128]{2,1,0:T(8,128)S(1)}, f32[32,16,128]{2,1,0:T(8,128)S(1)}) custom-call(f32[16,128]{1,0:T(8,128)S(1)} %reduce_sum.9.lown, f32[16,128]{1,0:T(8,128)S(1)} %collective-permute-done.10.loth, bf16[32,4096]{1,0:T(8,128)(2,1)S(1)} %bitcast.22, bf16[32,4096]{1,0:T(8,128)(2,1)S(1)} %collective-permute-done.a1, ...), custom_call_target="tpu_custom_call" | custom-call | flops 100000000 | bytes 3000000 | tf_op jit(solution)/shard_map/pallas_call | solution.py:51
  67.2 0.3 collective-permute-start.11
  67.5 1.2 %collective-permute-done.11 = f32[32,16,128]{2,1,0:T(8,128)S(1)} collective-permute-done((f32[32,16,128]{2,1,0:T(8,128)S(1)}, f32[32,16,128]{2,1,0:T(8,128)S(1)}, u32[]{:S(2)}, u32[]{:S(2)}) %collective-permute-start.11) | collective-permute-done | bytes 262176 | tf_op jit(solution)/shard_map/ppermute | solution.py:223
  68.7 0.0 copy-start.2
  68.7 11.6 %all_to_all.21.pieces = f32[32,16,128]{2,1,0:T(8,128)S(1)} all-to-all(f32[32,16,128]{2,1,0:T(8,128)S(1)} %add.7), channel_id=1, replica_groups=mesh['x'=4,'zl'=2,'y'=4,'core'=2,'t'=4] {'x','zl','y'}, dimensions={0} | all-to-all | bytes 524288 | tf_op jit(solution)/shard_map/all_to_all | solution.py:227
  80.3 0.0 copy-done.2
  80.3 0.1 shard_map.90
  80.4 15.5 %all_to_all.22.mixed = bf16[32,96,128]{2,1,0:T(8,128)(2,1)S(1)} all-to-all(bf16[32,96,128]{2,1,0:T(8,128)(2,1)S(1)} %shard_map.90), channel_id=1, replica_groups=mesh['x'=4,'zl'=2,'y'=4,'core'=2,'t'=4] {'x','zl','y'}, dimensions={0} | all-to-all | bytes 1572864 | tf_op jit(solution)/shard_map/all_to_all | solution.py:227
  96.0 3.3 %collective-permute-start.12 = (bf16[32,32,128]{2,1,0:T(8,128)(2,1)S(1)}, bf16[32,32,128]{2,1,0:T(8,128)(2,1)S(1)}, u32[]{:S(2)}, u32[]{:S(2)}) collective-permute-start(bf16[32,32,128]{2,1,0:T(8,128)(2,1)S(1)} %slice.4), channel_id=1, source_target_pairs={{0,4},{4,0},{1,5},{5,1},{2,6},{6,2},{3,7},{7,3},{8,12},{12,8},{9,1... | collective-permute-start | bytes 786440 | tf_op jit(solution)/shard_map/ppermute | solution.py:223
  99.2 1.2 %collective-permute-done.12.roth = bf16[32,32,128]{2,1,0:T(8,128)(2,1)S(1)} collective-permute-done((bf16[32,32,128]{2,1,0:T(8,128)(2,1)S(1)}, bf16[32,32,128]{2,1,0:T(8,128)(2,1)S(1)}, u32[]{:S(2)}, u32[]{:S(2)}) %collective-permute-start.12) | collective-permute-done | bytes 262176 | tf_op jit(solution)/shard_map/ppermute | solution.py:223
  100.4 0.0 copy-done.7
  100.4 1.6 %shard_map.91 = (bf16[128,4096]{1,0:T(8,128)(2,1)}, bf16[32,4096]{1,0:T(8,128)(2,1)}, bf16[32,4096]{1,0:T(8,128)(2,1)}) custom-call(bf16[32,96,128]{2,1,0:T(8,128)(2,1)S(1)} %all_to_all.22.mixed, bf16[32,32,128]{2,1,0:T(8,128)(2,1)S(1)} %collective-permute-done.12.roth, f32[32,128]{1,0:T(8,128)S(1)} %copy-done.7, bf16[128,128]{1,0:T(8,128)(2,1)S(1)} %bitcast.28, ...), custom_call_target="tpu_custom_call" | custom-call | flops 300000000 | bytes 5000000 | tf_op jit(solution)/shard_map/pallas_call | solution.py:51
  (6 shorter events, 0.1 us)
Async XLA Ops:
  0.6 13.0 %copy-start.1 = (bf16[1,32,4096]{2,1,0:T(8,128)(2,1)S(1)}, bf16[1,32,4096]{2,1,0:T(8,128)(2,1)}, u32[]{:S(2)}) copy-start(bf16[1,32,4096]{2,1,0:T(8,128)(2,1)} %param.5) | copy-start | bytes 786436
  0.6 16.4 %copy-start.3 = (bf16[1,128,128]{2,1,0:T(8,128)(2,1)S(1)}, bf16[1,128,128]{2,1,0:T(8,128)(2,1)}, u32[]{:S(2)}) copy-start(bf16[1,128,128]{2,1,0:T(8,128)(2,1)} %param.6) | copy-start | bytes 98308
  2.2 22.6 %copy-start = (bf16[1,1,128,4096]{3,2,1,0:T(8,128)(2,1)S(1)}, bf16[1,1,128,4096]{3,2,1,0:T(8,128)(2,1)}, u32[]{:S(2)}) copy-start(bf16[1,1,128,4096]{3,2,1,0:T(8,128)(2,1)} %param.8) | copy-start | bytes 3145732
  2.2 14.7 %collective-permute-start.3 = (bf16[80,256]{1,0:T(8,128)(2,1)}, bf16[80,256]{1,0:T(8,128)(2,1)S(1)}, u32[]{:S(2)}, u32[]{:S(2)}) collective-permute-start(bf16[80,256]{1,0:T(8,128)(2,1)} %get-tuple-element.25), channel_id=1, source_target_pairs={{0,1},{1,2},{2,3},{3,0},{4,5},{5,6},{6,7},{7,4},{8,9},{9,10},{10,1... | collective-permute-start | bytes 122888 | tf_op jit(solution)/shard_map/ppermute | solution.py:219
  6.1 10.9 %collective-permute-start.4 = (bf16[80,256]{1,0:T(8,128)(2,1)}, bf16[80,256]{1,0:T(8,128)(2,1)S(1)}, u32[]{:S(2)}, u32[]{:S(2)}) collective-permute-start(bf16[80,256]{1,0:T(8,128)(2,1)} %get-tuple-element.26), channel_id=1, source_target_pairs={{0,2},{1,3},{2,0},{3,1},{4,6},{5,7},{6,4},{7,5},{8,10},{9,11},{10,... | collective-permute-start | bytes 122888 | tf_op jit(solution)/shard_map/ppermute | solution.py:219
  11.2 5.8 %collective-permute-start.5 = (bf16[80,256]{1,0:T(8,128)(2,1)}, bf16[80,256]{1,0:T(8,128)(2,1)S(1)}, u32[]{:S(2)}, u32[]{:S(2)}) collective-permute-start(bf16[80,256]{1,0:T(8,128)(2,1)} %get-tuple-element.27), channel_id=1, source_target_pairs={{0,3},{1,0},{2,1},{3,2},{4,7},{5,4},{6,5},{7,6},{8,11},{9,8},{10,9... | collective-permute-start | bytes 122888 | tf_op jit(solution)/shard_map/ppermute | solution.py:219
  13.6 24.0 %collective-permute-start.2 = (bf16[32,4096]{1,0:T(8,128)(2,1)S(1)}, bf16[32,4096]{1,0:T(8,128)(2,1)S(1)}, u32[]{:S(2)}, u32[]{:S(2)}) collective-permute-start(bf16[32,4096]{1,0:T(8,128)(2,1)S(1)} %bitcast.18), channel_id=1, source_target_pairs={{0,3},{1,0},{2,1},{3,2},{4,7},{5,4},{6,5},{7,6},{8,11},{9,8},{10,9... | collective-permute-start | bytes 786440 | tf_op jit(solution)/shard_map/ppermute | solution.py:219
  13.7 24.0 %collective-permute-start.1 = (bf16[32,4096]{1,0:T(8,128)(2,1)S(1)}, bf16[32,4096]{1,0:T(8,128)(2,1)S(1)}, u32[]{:S(2)}, u32[]{:S(2)}) collective-permute-start(bf16[32,4096]{1,0:T(8,128)(2,1)S(1)} %bitcast.19), channel_id=1, source_target_pairs={{0,2},{1,3},{2,0},{3,1},{4,6},{5,7},{6,4},{7,5},{8,10},{9,11},{10,... | collective-permute-start | bytes 786440 | tf_op jit(solution)/shard_map/ppermute | solution.py:219
  16.9 8.4 %copy-start.4 = (bf16[80,256]{1,0:T(8,128)(2,1)}, bf16[80,256]{1,0:T(8,128)(2,1)S(1)}, u32[]{:S(2)}) copy-start(bf16[80,256]{1,0:T(8,128)(2,1)S(1)} %collective-permute-done.3.r1) | copy-start | bytes 122884
  16.9 20.7 %collective-permute-start = (bf16[32,4096]{1,0:T(8,128)(2,1)S(1)}, bf16[32,4096]{1,0:T(8,128)(2,1)S(1)}, u32[]{:S(2)}, u32[]{:S(2)}) collective-permute-start(bf16[32,4096]{1,0:T(8,128)(2,1)S(1)} %bitcast.20), channel_id=1, source_target_pairs={{0,1},{1,2},{2,3},{3,0},{4,5},{5,6},{6,7},{7,4},{8,9},{9,10},{10,1... | collective-permute-start | bytes 786440 | tf_op jit(solution)/shard_map/ppermute | solution.py:219
  17.0 11.7 %copy-start.5 = (bf16[80,256]{1,0:T(8,128)(2,1)}, bf16[80,256]{1,0:T(8,128)(2,1)S(1)}, u32[]{:S(2)}) copy-start(bf16[80,256]{1,0:T(8,128)(2,1)S(1)} %collective-permute-done.4.r2) | copy-start | bytes 122884
  17.0 12.6 %copy-start.6 = (bf16[80,256]{1,0:T(8,128)(2,1)}, bf16[80,256]{1,0:T(8,128)(2,1)S(1)}, u32[]{:S(2)}) copy-start(bf16[80,256]{1,0:T(8,128)(2,1)S(1)} %collective-permute-done.5.r3) | copy-start | bytes 122884
  17.9 6.9 %copy-start.8 = (bf16[1,1,4096,32]{2,3,1,0:T(8,128)(2,1)S(1)}, bf16[1,1,4096,32]{2,3,1,0:T(8,128)(2,1)}, u32[]{:S(2)}) copy-start(bf16[1,1,4096,32]{2,3,1,0:T(8,128)(2,1)} %param.9) | copy-start | bytes 786436
  17.9 15.9 %all-to-all-start = ((bf16[16,32,512]{2,1,0:T(8,128)(2,1)}), bf16[16,32,512]{2,1,0:T(8,128)(2,1)S(1)}, u32[]{:S(2)}, u32[]{:S(2)}) async-start(bf16[16,32,512]{2,1,0:T(8,128)(2,1)} %shard_map.86), calls=%async_computation | async-start | bytes 1048576 | tf_op jit(solution)/shard_map/all_to_all | solution.py:227
  25.4 4.3 %collective-permute-start.6 = (bf16[80,256]{1,0:T(8,128)(2,1)S(1)}, bf16[80,256]{1,0:T(8,128)(2,1)S(1)}, u32[]{:S(2)}, u32[]{:S(2)}) collective-permute-start(bf16[80,256]{1,0:T(8,128)(2,1)S(1)} %collective-permute-done.3.r1), channel_id=1, source_target_pairs={{0,4},{4,0},{1,5},{5,1},{2,6},{6,2},{3,7},{7,3},{8,12},{12,8},{9,1... | collective-permute-start | bytes 122888 | tf_op jit(solution)/shard_map/ppermute | solution.py:223
  28.7 1.2 %collective-permute-start.7 = (bf16[80,256]{1,0:T(8,128)(2,1)S(1)}, bf16[80,256]{1,0:T(8,128)(2,1)S(1)}, u32[]{:S(2)}, u32[]{:S(2)}) collective-permute-start(bf16[80,256]{1,0:T(8,128)(2,1)S(1)} %collective-permute-done.4.r2), channel_id=1, source_target_pairs={{0,4},{4,0},{1,5},{5,1},{2,6},{6,2},{3,7},{7,3},{8,12},{12,8},{9,1... | collective-permute-start | bytes 122888 | tf_op jit(solution)/shard_map/ppermute | solution.py:223
  29.6 4.2 %copy-start.10 = (bf16[80,256]{1,0:T(8,128)(2,1)}, bf16[80,256]{1,0:T(8,128)(2,1)S(1)}, u32[]{:S(2)}) copy-start(bf16[80,256]{1,0:T(8,128)(2,1)S(1)} %collective-permute-done.6.c1) | copy-start | bytes 122884
  29.6 1.2 %collective-permute-start.8 = (bf16[80,256]{1,0:T(8,128)(2,1)S(1)}, bf16[80,256]{1,0:T(8,128)(2,1)S(1)}, u32[]{:S(2)}, u32[]{:S(2)}) collective-permute-start(bf16[80,256]{1,0:T(8,128)(2,1)S(1)} %collective-permute-done.5.r3), channel_id=1, source_target_pairs={{0,4},{4,0},{1,5},{5,1},{2,6},{6,2},{3,7},{7,3},{8,12},{12,8},{9,1... | collective-permute-start | bytes 122888 | tf_op jit(solution)/shard_map/ppermute | solution.py:223
  30.0 3.8 %copy-start.11 = (bf16[80,256]{1,0:T(8,128)(2,1)}, bf16[80,256]{1,0:T(8,128)(2,1)S(1)}, u32[]{:S(2)}) copy-start(bf16[80,256]{1,0:T(8,128)(2,1)S(1)} %collective-permute-done.7.c2) | copy-start | bytes 122884
  30.8 3.0 %copy-start.12 = (bf16[80,256]{1,0:T(8,128)(2,1)}, bf16[80,256]{1,0:T(8,128)(2,1)S(1)}, u32[]{:S(2)}) copy-start(bf16[80,256]{1,0:T(8,128)(2,1)S(1)} %collective-permute-done.8.c3) | copy-start | bytes 122884
  33.8 0.8 copy-start.9
  38.2 4.4 %collective-permute-start.9 = (f32[16,128]{1,0:T(8,128)S(1)}, f32[16,128]{1,0:T(8,128)S(1)}, u32[]{:S(2)}, u32[]{:S(2)}) collective-permute-start(f32[16,128]{1,0:T(8,128)S(1)} %get-tuple-element.36), channel_id=1, source_target_pairs={{0,4},{4,0},{1,5},{5,1},{2,6},{6,2},{3,7},{7,3},{8,12},{12,8},{9,1... | collective-permute-start | bytes 24584 | tf_op jit(solution)/shard_map/ppermute | solution.py:223
  60.5 2.9 %collective-permute-start.10 = (f32[16,128]{1,0:T(8,128)S(1)}, f32[16,128]{1,0:T(8,128)S(1)}, u32[]{:S(2)}, u32[]{:S(2)}) collective-permute-start(f32[16,128]{1,0:T(8,128)S(1)} %reduce_sum.9.lown), channel_id=1, source_target_pairs={{0,4},{4,0},{1,5},{5,1},{2,6},{6,2},{3,7},{7,3},{8,12},{12,8},{9,1... | collective-permute-start | bytes 24584 | tf_op jit(solution)/shard_map/ppermute | solution.py:223
  67.2 1.5 %collective-permute-start.11 = (f32[32,16,128]{2,1,0:T(8,128)S(1)}, f32[32,16,128]{2,1,0:T(8,128)S(1)}, u32[]{:S(2)}, u32[]{:S(2)}) collective-permute-start(f32[32,16,128]{2,1,0:T(8,128)S(1)} %get-tuple-element.38), channel_id=1, source_target_pairs={{0,4},{4,0},{1,5},{5,1},{2,6},{6,2},{3,7},{7,3},{8,12},{12,8},{9,1... | collective-permute-start | bytes 786440 | tf_op jit(solution)/shard_map/ppermute | solution.py:223
  68.7 11.6 %copy-start.2 = (bf16[16,32,256]{2,1,0:T(8,128)(2,1)S(1)}, bf16[16,32,256]{2,1,0:T(8,128)(2,1)}, u32[]{:S(2)}) copy-start(bf16[16,32,256]{2,1,0:T(8,128)(2,1)} %shard_map.87.inputs) | copy-start | bytes 786436
  95.9 4.5 %copy-start.7 = (f32[32,128]{1,0:T(8,128)S(1)}, f32[32,128]{1,0:T(8,128)}, u32[]{:S(2)}) copy-start(f32[32,128]{1,0:T(8,128)} %get-tuple-element.40.qt) | copy-start | bytes 49156
  96.0 4.4 %collective-permute-start.12 = (bf16[32,32,128]{2,1,0:T(8,128)(2,1)S(1)}, bf16[32,32,128]{2,1,0:T(8,128)(2,1)S(1)}, u32[]{:S(2)}, u32[]{:S(2)}) collective-permute-start(bf16[32,32,128]{2,1,0:T(8,128)(2,1)S(1)} %slice.4), channel_id=1, source_target_pairs={{0,4},{4,0},{1,5},{5,1},{2,6},{6,2},{3,7},{7,3},{8,12},{12,8},{9,1... | collective-permute-start | bytes 786440 | tf_op jit(solution)/shard_map/ppermute | solution.py:223
